TPU v7x, 32 devices: a whole 2x2x4 slice. The times are simulated.
32 devices in a mesh: section: 2 (over core), seq: 4 (over y, x), head: 4 (over z).
Axes of the slice: x: 2, y: 2, z: 4, core: 2. Of those that a mesh axis runs over, the one named last changes fastest.
Arguments:
- inputs: bfloat16 [2, 2048, 2048], P(None, ('seq', 'head')), may hold values from -6 to 6
- cotangent: bfloat16 [2, 2048, 2048], P(None, ('seq', 'head')), may hold values from -6 to 6
- starts: int32 [2, 2048], P(None, 'seq'), may hold values from 0 to 1, as said below
- live: int32 [2, 2048], P(None, 'seq'), may hold values from 0 to 1, as said below
- norm_gain: float32 [2, 2048], P('section'), may hold values from 0.5 to 1.5
- w_gate: bfloat16 [2, 2048, 4096], P('section', None, 'head'), may hold values from -0.125 to 0.125
- w_in: bfloat16 [2, 2048, 4096], P('section', None, 'head'), may hold values from -0.125 to 0.125
- w_bc: bfloat16 [2, 2048, 256], P('section'), may hold values from -0.125 to 0.125
- w_dt: bfloat16 [2, 2048, 64], P('section', None, 'head'), may hold values from -0.125 to 0.125
- conv_x: bfloat16 [2, 4, 4096], P('section', None, 'head'), may hold values from -3 to 3
- conv_x_bias: float32 [2, 4096], P('section', 'head'), may hold values from -3 to 3
- conv_bc: bfloat16 [2, 4, 256], P('section'), may hold values from -3 to 3
- conv_bc_bias: float32 [2, 256], P('section'), may hold values from -3 to 3
- dt_bias: float32 [2, 64], P('section', 'head'), may hold values from -7 to -1
- a_log: float32 [2, 64], P('section', 'head'), may hold values from -4.5 to 2
- skip: float32 [2, 64], P('section', 'head'), may hold values from 0.5 to 1.5
- gate_gain: float32 [2, 4096], P('section', 'head'), may hold values from 0.5 to 1.5
- w_out: bfloat16 [2, 4096, 2048], P('section', 'head'), may hold values from -0.09375 to 0.09375
Outputs:
- acts: float32 [2, 2, 2048, 2048], P('section', None, ('seq', 'head'))
- in_grads: float32 [2, 2, 2048, 2048], P('section', None, ('seq', 'head'))
- g_norm_gain: float32 [2, 2048], P('section')
- g_w_gate: float32 [2, 2048, 4096], P('section', None, 'head')
- g_w_in: float32 [2, 2048, 4096], P('section', None, 'head')
- g_w_bc: float32 [2, 2048, 256], P('section')
- g_w_dt: float32 [2, 2048, 64], P('section', None, 'head')
- g_conv_x: float32 [2, 4, 4096], P('section', None, 'head')
- g_conv_x_bias: float32 [2, 4096], P('section', 'head')
- g_conv_bc: float32 [2, 4, 256], P('section')
- g_conv_bc_bias: float32 [2, 256], P('section')
- g_dt_bias: float32 [2, 64], P('section', 'head')
- g_a_log: float32 [2, 64], P('section', 'head')
- g_skip: float32 [2, 64], P('section', 'head')
- g_gate_gain: float32 [2, 4096], P('section', 'head')
- g_w_out: float32 [2, 4096, 2048], P('section', 'head')
Inputs may be any that keep to these rules, and one draw needn't show every extreme that they name: A micro-batch of even index holds three sequences in three buckets: the first begins at position 0, the first two hold 512 to 682 positions each, the third the rest; one of odd index holds one sequence in one bucket; starts is 1 exactly at each bucket's first position. In each bucket live is 1 on a leading run of half of its positions or more and 0 after it; in every micro-batch of even index one bucket is live throughout.
All inputs are finite; a program needn't handle non-finite values.
Results may differ from a plain program's by a relative error of at most 0.019.
Values may be sent and summed in bfloat16 or wider, within the bound.
A program may use at most 320 MiB of HBM per device.

v0:
```python
from functools import partial

import jax
import jax.numpy as jnp
from jax import lax
from jax.sharding import PartitionSpec as P

DI = 4096
P_SIZE = 64
N = 128
KW = 4
SCAN_BLOCK = 256


norm_eps = 1e-05
far_below = -1e30
highest = lax.Precision.HIGHEST


def shifted(value, axis, by):
    count = lax.axis_size(axis)
    pairs = [(i, i + by) for i in range(count) if 0 <= i + by < count]
    return lax.ppermute(value, axis, pairs)


def entering(value, axis, combine, identity):
    count, mine = (lax.axis_size(axis), lax.axis_index(axis))
    everything = jax.tree.map(lambda part: lax.all_gather(part, axis), value)
    start = jax.tree.map(
        lambda part, zero: jnp.broadcast_to(jnp.asarray(zero, part.dtype), part.shape),
        value,
        identity,
    )

    def lap(k, before):
        reached = k < mine
        new = combine(before, jax.tree.map(lambda part: part[k], everything))
        return jax.tree.map(lambda a, b: jnp.where(reached, a, b), new, before)

    return lax.fori_loop(0, count, lap, start)


def entering_2(value, axis, join, neutral):
    count = lax.axis_size(axis)
    place = lax.axis_index(axis)
    ahead = count - 1 - place
    gathered = jax.tree.map(
        lambda a, kind: lax.all_gather(a.astype(kind), axis),
        value,
        jax.tree.map(lambda a: jnp.bfloat16 if a.dtype == jnp.float32 else a.dtype, value),
    )
    state = jax.tree.map(lambda a, e: jnp.zeros_like(a) + jnp.asarray(e, a.dtype), value, neutral)

    def one(lap, state):
        source = count - 1 - lap
        return join(
            state,
            jax.tree.map(
                lambda a, own: lax.dynamic_index_in_dim(a, source, 0, False).astype(own.dtype),
                gathered,
                value,
            ),
        )

    return lax.fori_loop(0, ahead, one, state)


def rms_scale(values):
    return lax.rsqrt(jnp.mean(values * values, axis=-1, keepdims=True) + norm_eps)


def silu_slope(values):
    logistic = jax.nn.sigmoid(values)
    return logistic * (1.0 + values * (1.0 - logistic))


def causal_conv(extended, marks_ext, weight, conv_bias):
    tap_count = weight.shape[0]
    length = extended.shape[0] - tap_count + 1
    counts = jnp.cumsum(marks_ext)
    conv_sum = jnp.zeros((length, extended.shape[1]), jnp.float32) + conv_bias
    for tap_index in range(tap_count):
        linked = (counts[tap_count - 1 :] == counts[tap_index : tap_index + length]).astype(
            jnp.float32
        )
        conv_sum = (
            conv_sum
            + linked[:, None] * weight[tap_index] * extended[tap_index : tap_index + length]
        )
    return conv_sum


def prepare(extended, dt_pre, marks_ext, alive_mask, conv_weight, conv_bias, dt_bias, a_log):
    inner_width = dt_pre.shape[1] * P_SIZE
    activated = jax.nn.silu(causal_conv(extended, marks_ext, conv_weight, conv_bias))
    inner_act = activated[:, :inner_width] * alive_mask[:, None]
    b_mat = activated[:, inner_width : inner_width + N]
    c_mat = activated[:, inner_width + N :]
    step_size = jax.nn.softplus(dt_pre + dt_bias) * alive_mask[:, None]
    log_decay = -step_size * jnp.exp(a_log)
    return (inner_act, step_size, log_decay, b_mat, c_mat)


def block_terms(inner_act, step_size, log_decay, b_mat, start_marks):
    blocks = inner_act.shape[0] // SCAN_BLOCK
    head_count = step_size.shape[1]
    x_blocks = inner_act.reshape(blocks, SCAN_BLOCK, head_count, P_SIZE)
    dt_blocks = step_size.reshape(blocks, SCAN_BLOCK, head_count)
    cum_decay = jnp.cumsum(log_decay.reshape(blocks, SCAN_BLOCK, head_count), axis=1)
    mark_count = jnp.cumsum(start_marks.reshape(blocks, SCAN_BLOCK), axis=1)
    b_blocks = b_mat.reshape(blocks, SCAN_BLOCK, N)
    last_cum = cum_decay[:, -1]
    last_mark = mark_count[:, -1]
    same_end = (mark_count == last_mark[:, None]).astype(jnp.float32)
    end_weight = jnp.exp(last_cum[:, None, :] - cum_decay) * same_end[:, :, None] * dt_blocks
    block_states = jnp.einsum(
        "cjh,cjhp,cjn->chpn", end_weight, x_blocks, b_blocks, precision=highest
    )
    block_decay = jnp.exp(last_cum) * (last_mark == 0).astype(jnp.float32)[:, None]
    return (block_decay, block_states, cum_decay, mark_count, x_blocks, dt_blocks)


def compose_blocks(block_decay, block_states, start_state):

    def advance(chain_state, block_item):
        factor, fresh_state = block_item
        return (factor[:, None, None] * chain_state + fresh_state, chain_state)

    return lax.scan(advance, start_state, (block_decay, block_states))


def block_output(block_parts, b_mat, c_mat, skip, incoming):
    block_decay, block_states, cum_decay, mark_count, x_blocks, dt_blocks = block_parts
    blocks = cum_decay.shape[0]
    head_count = cum_decay.shape[2]
    b_blocks = b_mat.reshape(blocks, SCAN_BLOCK, N)
    c_blocks = c_mat.reshape(blocks, SCAN_BLOCK, N)
    inner_prod = jnp.einsum("cin,cjn->cij", c_blocks, b_blocks, precision=highest)
    arange_pos = jnp.arange(SCAN_BLOCK)
    linked = (arange_pos[:, None] >= arange_pos[None, :])[None] & (
        mark_count[:, :, None] == mark_count[:, None, :]
    )
    spread = jnp.where(
        linked[..., None], cum_decay[:, :, None, :] - cum_decay[:, None, :, :], far_below
    )
    weights = jnp.exp(spread) * inner_prod[..., None] * dt_blocks[:, None, :, :]
    y_intra = jnp.einsum("cijh,cjhp->cihp", weights, x_blocks, precision=highest)
    carry_in = jnp.exp(cum_decay) * (mark_count == 0).astype(jnp.float32)[:, :, None]
    y_inter = (
        jnp.einsum("cin,chpn->cihp", c_blocks, incoming, precision=highest) * carry_in[..., None]
    )
    mixed_out = y_intra + y_inter + skip[None, None, :, None] * x_blocks
    return mixed_out.reshape(blocks * SCAN_BLOCK, head_count * P_SIZE)


def local_front(marks_ext, alive_mask, extended, dt_pre, conv_weight, conv_bias, dt_bias, a_log):
    inner_act, step_size, log_decay, b_mat, c_mat = prepare(
        extended, dt_pre, marks_ext, alive_mask, conv_weight, conv_bias, dt_bias, a_log
    )
    block_parts = block_terms(inner_act, step_size, log_decay, b_mat, marks_ext[KW - 1 :])
    zero_state = jnp.zeros(block_parts[1].shape[1:], jnp.float32)
    total_state, _ = compose_blocks(block_parts[0], block_parts[1], zero_state)
    total_decay = jnp.prod(block_parts[0], axis=0)
    return (block_parts, b_mat, c_mat, total_decay, total_state)


def local_rear(block_parts, b_mat, c_mat, skip, start_state):
    _, incoming = compose_blocks(block_parts[0], block_parts[1], start_state)
    return block_output(block_parts, b_mat, c_mat, skip, incoming)


def local_pass(
    marks_ext,
    alive_mask,
    extended,
    dt_pre,
    conv_weight,
    conv_bias,
    dt_bias,
    a_log,
    skip,
    start_state,
):
    block_parts, b_mat, c_mat, total_decay, total_state = local_front(
        marks_ext, alive_mask, extended, dt_pre, conv_weight, conv_bias, dt_bias, a_log
    )
    return (local_rear(block_parts, b_mat, c_mat, skip, start_state), total_decay, total_state)


def chain_combine(earlier, later):
    return (earlier[0] * later[0], later[0][:, None, None] * earlier[1] + later[1])


def extend(pre_conv, start_marks, edge_rows, edge_marks):
    extended = jnp.concatenate([edge_rows, pre_conv], axis=0)
    marks_ext = jnp.concatenate([edge_marks.astype(jnp.int32), start_marks], axis=0)
    return (extended, marks_ext)


def mixer_state(stream, start_marks, alive_mask, layer_weights):
    (
        norm_gain,
        w_main,
        w_low,
        w_bc,
        conv_weight,
        conv_bias,
        dt_bias,
        a_log,
        skip,
        gate_gain,
        w_out,
    ) = layer_weights
    inner_width = w_out.shape[0]
    normed = (stream * rms_scale(stream) * norm_gain).astype(jnp.bfloat16)
    gathered = lax.all_gather(normed, "head", axis=0, tiled=True)
    projected = jnp.dot(gathered, w_main, preferred_element_type=jnp.float32)
    pre_conv = projected[:, inner_width : 2 * inner_width + 2 * N]
    dt_pre = projected[:, 2 * inner_width + 2 * N :]
    marks_float = start_marks.astype(jnp.float32)
    tail_from = pre_conv.shape[0] - KW + 1
    edge_parts = shifted((pre_conv[tail_from:], marks_float[tail_from:]), "seq", 1)
    extended, marks_ext = extend(pre_conv, start_marks, edge_parts[0], edge_parts[1])
    block_parts, b_mat, c_mat, total_decay, total_state = local_front(
        marks_ext, alive_mask, extended, dt_pre, conv_weight, conv_bias, dt_bias, a_log
    )
    neutral = (jnp.ones_like(total_decay), jnp.zeros_like(total_state))
    prefix = entering((total_decay, total_state), "seq", chain_combine, neutral)
    start_state = prefix[1]
    mixed_out = local_rear(block_parts, b_mat, c_mat, skip, start_state)
    gated_mix = mixed_out * jax.nn.silu(projected[:, :inner_width])
    square_total = lax.psum(jnp.sum(gated_mix * gated_mix, axis=-1), "head")
    return (
        (gathered, projected, edge_parts[0], edge_parts[1], start_state, square_total),
        gated_mix,
    )


def mixer_output(gated_mix, square_total, gate_gain, w_out):
    scale_out = lax.rsqrt(square_total / DI + norm_eps)
    normed_out = (gated_mix * scale_out[:, None] * gate_gain).astype(jnp.bfloat16)
    return lax.psum_scatter(
        jnp.dot(normed_out, w_out, preferred_element_type=jnp.float32),
        "head",
        scatter_dimension=0,
        tiled=True,
    )


def mixer_backward(stream, grad_next, start_marks, alive_mask, layer_weights, saved_parts):
    (
        norm_gain,
        w_main,
        w_low,
        w_bc,
        conv_weight,
        conv_bias,
        dt_bias,
        a_log,
        skip,
        gate_gain,
        w_out,
    ) = layer_weights
    gathered, projected, edge_rows, edge_marks, start_state, square_total = saved_parts
    inner_width = w_out.shape[0]
    gate_pre = projected[:, :inner_width]
    pre_conv = projected[:, inner_width : 2 * inner_width + 2 * N]
    dt_pre = projected[:, 2 * inner_width + 2 * N :]
    extended, marks_ext = extend(pre_conv, start_marks, edge_rows, edge_marks)
    local_fn = partial(local_pass, marks_ext, alive_mask)
    primal, pull_back = jax.vjp(
        local_fn, extended, dt_pre, conv_weight, conv_bias, dt_bias, a_log, skip, start_state
    )
    mixed_out, total_decay, total_state = primal
    silu_gate = jax.nn.silu(gate_pre)
    gated_mix = mixed_out * silu_gate
    scale_out = lax.rsqrt(square_total / DI + norm_eps)
    normed_out = (gated_mix * scale_out[:, None] * gate_gain).astype(jnp.bfloat16)
    grad_branch = grad_next.astype(jnp.bfloat16)
    shard_rows = lax.all_gather(grad_branch, "head", axis=0, tiled=True)
    out_grad = lax.dot_general(
        normed_out, shard_rows, (((0,), (0,)), ((), ())), preferred_element_type=jnp.float32
    )
    back_rows = lax.dot_general(
        shard_rows, w_out, (((1,), (1,)), ((), ())), preferred_element_type=jnp.float32
    )
    grad_normed = back_rows
    g_w_out, grad_normed = (out_grad, grad_normed)
    weighted = grad_normed * gate_gain
    g_gate_gain = jnp.sum(grad_normed * gated_mix * scale_out[:, None], axis=0)
    cross_sum = lax.psum(jnp.sum(weighted * gated_mix, axis=-1), "head")
    grad_gated = (
        scale_out[:, None] * weighted - gated_mix * (scale_out**3 * cross_sum / DI)[:, None]
    )
    grad_mixed = grad_gated * silu_gate
    grad_gate = (grad_gated * mixed_out * silu_slope(gate_pre)).astype(jnp.bfloat16)
    zero_decay = jnp.zeros_like(total_decay)
    zero_state = jnp.zeros_like(total_state)
    first_pull = pull_back((grad_mixed, zero_decay, zero_state))
    neutral = (jnp.ones_like(total_decay), zero_state)
    suffix = entering_2((total_decay, first_pull[7]), "seq", chain_combine, neutral)
    after_state = suffix[1]
    grad_decay = jnp.sum(after_state * start_state, axis=(1, 2))
    second = pull_back((jnp.zeros_like(mixed_out), grad_decay, after_state))
    summed = tuple((former + latter for former, latter in zip(first_pull[:7], second[:7])))
    grad_ext, grad_dt_pre, g_conv_w, g_conv_b, g_dt_bias, g_a_log, g_skip = summed
    returned = shifted(grad_ext[: KW - 1], "seq", -1)
    grad_pre = grad_ext[KW - 1 :]
    tail_from = grad_pre.shape[0] - KW + 1
    grad_pre = jnp.concatenate([grad_pre[:tail_from], grad_pre[tail_from:] + returned], axis=0)
    grad_inner = grad_pre[:, :inner_width].astype(jnp.bfloat16)
    grad_bc = grad_pre[:, inner_width:]
    grad_low = jnp.concatenate([grad_gate, grad_inner, grad_dt_pre.astype(jnp.bfloat16)], axis=1)
    w_bc_float = w_bc.astype(jnp.float32)
    main_term = lax.dot_general(
        grad_low, w_low, (((1,), (1,)), ((), ())), preferred_element_type=jnp.float32
    )
    side_term = lax.dot_general(
        grad_bc,
        w_bc_float,
        (((1,), (1,)), ((), ())),
        precision=highest,
        preferred_element_type=jnp.float32,
    )
    grad_normed_in = lax.psum_scatter(
        (main_term + side_term).astype(jnp.bfloat16), "head", scatter_dimension=0, tiled=True
    ).astype(jnp.float32)
    g_low = lax.dot_general(
        gathered, grad_low, (((0,), (0,)), ((), ())), preferred_element_type=jnp.float32
    )
    g_w_bc = lax.dot_general(
        gathered.astype(jnp.float32),
        grad_bc,
        (((0,), (0,)), ((), ())),
        precision=highest,
        preferred_element_type=jnp.float32,
    )
    scale_in = rms_scale(stream)
    g_norm_gain = jnp.sum(grad_normed_in * stream * scale_in, axis=0)
    weighted_in = grad_normed_in * norm_gain
    grad_stream = (
        grad_next
        + scale_in * weighted_in
        - stream * scale_in**3 * jnp.mean(weighted_in * stream, axis=-1, keepdims=True)
    )
    head_part = (
        g_low[:, :inner_width],
        g_low[:, inner_width : 2 * inner_width],
        g_low[:, 2 * inner_width :],
        g_w_out,
        g_conv_w[:, :inner_width],
        g_conv_b[:inner_width],
        g_dt_bias,
        g_a_log,
        g_skip,
        g_gate_gain,
    )
    shared_part = (g_norm_gain, g_w_bc, g_conv_w[:, inner_width:], g_conv_b[inner_width:])
    return (grad_stream, head_part, shared_part)


def reduce_grads(head_part, shared_part):
    head_sum = (
        lax.psum(head_part[0].astype(jnp.bfloat16), "seq").astype(jnp.float32),
        lax.psum(head_part[1].astype(jnp.bfloat16), "seq").astype(jnp.float32),
        lax.psum(head_part[2].astype(jnp.bfloat16), "seq").astype(jnp.float32),
        lax.psum(head_part[3].astype(jnp.bfloat16), "seq").astype(jnp.float32),
        lax.psum(head_part[4].astype(jnp.bfloat16), "seq").astype(jnp.float32),
        lax.psum(head_part[5].astype(jnp.bfloat16), "seq").astype(jnp.float32),
        lax.psum(head_part[6].astype(jnp.bfloat16), "seq").astype(jnp.float32),
        lax.psum(head_part[7].astype(jnp.bfloat16), "seq").astype(jnp.float32),
        lax.psum(head_part[8].astype(jnp.bfloat16), "seq").astype(jnp.float32),
        lax.psum(head_part[9].astype(jnp.bfloat16), "seq").astype(jnp.float32),
    )
    shared_sum = lax.psum(
        (shared_part[0], shared_part[1], shared_part[2], shared_part[3]), ("seq", "head")
    )
    return (tuple(head_sum), tuple(shared_sum))


def store_slot(buffer, value, slot_index, is_valid):
    current = lax.dynamic_index_in_dim(buffer, slot_index, 0, False)
    return lax.dynamic_update_index_in_dim(
        buffer, jnp.where(is_valid, value, current), slot_index, 0
    )


def on_device(
    inputs,
    cotangent,
    starts,
    live,
    norm_gain,
    w_gate,
    w_in,
    w_bc,
    w_dt,
    conv_x,
    conv_x_bias,
    conv_bc,
    conv_bc_bias,
    dt_bias,
    a_log,
    skip,
    gate_gain,
    w_out,
):
    section_count = lax.axis_size("section")
    section_index = lax.axis_index("section")
    micro_count = inputs.shape[0]
    tick_count = micro_count + section_count - 1
    w_main = jnp.concatenate([w_gate[0], w_in[0], w_bc[0], w_dt[0]], axis=1)
    w_low = jnp.concatenate([w_gate[0], w_in[0], w_dt[0]], axis=1)
    conv_weight = jnp.concatenate([conv_x[0], conv_bc[0]], axis=1).astype(jnp.float32)
    conv_bias = jnp.concatenate([conv_x_bias[0], conv_bc_bias[0]], axis=0)
    layer_weights = (
        norm_gain[0],
        w_main,
        w_low,
        w_bc[0],
        conv_weight,
        conv_bias,
        dt_bias[0],
        a_log[0],
        skip[0],
        gate_gain[0],
        w_out[0],
    )
    row_shape = inputs.shape[1:]
    kept_inputs = jnp.zeros((micro_count,) + row_shape, jnp.float32)
    outputs_all = jnp.zeros((micro_count,) + row_shape, jnp.float32)
    arrived = jnp.zeros(row_shape, jnp.float32)
    for tick_index in range(tick_count):
        slot_index = tick_index - section_index
        is_valid = (slot_index >= 0) & (slot_index < micro_count)
        clipped = jnp.clip(slot_index, 0, micro_count - 1)
        fresh_rows = lax.dynamic_index_in_dim(inputs, clipped, 0, False).astype(jnp.float32)
        stream = jnp.where(section_index == 0, fresh_rows, arrived)
        start_marks = lax.dynamic_index_in_dim(starts, clipped, 0, False)
        alive_mask = lax.dynamic_index_in_dim(live, clipped, 0, False).astype(jnp.float32)
        saved_parts, gated_mix = mixer_state(stream, start_marks, alive_mask, layer_weights)
        result = stream + mixer_output(
            gated_mix, saved_parts[5], layer_weights[9], layer_weights[10]
        )
        kept_inputs = store_slot(kept_inputs, stream, clipped, is_valid)
        outputs_all = store_slot(outputs_all, result, clipped, is_valid)
        if tick_index + 1 < tick_count:
            arrived = shifted(result, "section", 1)
    back_arrived = jnp.zeros(row_shape, jnp.float32)
    input_grads = jnp.zeros((micro_count,) + row_shape, jnp.float32)
    head_total = ()
    shared_total = ()
    for tick_index in range(tick_count):
        slot_index = tick_index - (section_count - 1 - section_index)
        is_valid = (slot_index >= 0) & (slot_index < micro_count)
        clipped = jnp.clip(slot_index, 0, micro_count - 1)
        outer_grad = lax.dynamic_index_in_dim(cotangent, clipped, 0, False).astype(jnp.float32)
        grad_next = jnp.where(section_index == section_count - 1, outer_grad, back_arrived)
        stream = lax.dynamic_index_in_dim(kept_inputs, clipped, 0, False)
        start_marks = lax.dynamic_index_in_dim(starts, clipped, 0, False)
        alive_mask = lax.dynamic_index_in_dim(live, clipped, 0, False).astype(jnp.float32)
        saved_parts = mixer_state(stream, start_marks, alive_mask, layer_weights)[0]
        grad_stream, head_part, shared_part = mixer_backward(
            stream, grad_next, start_marks, alive_mask, layer_weights, saved_parts
        )
        mask_value = is_valid.astype(jnp.float32)
        head_part = tuple((member * mask_value for member in head_part))
        shared_part = tuple((member * mask_value for member in shared_part))
        head_part, shared_part = reduce_grads(head_part, shared_part)
        if tick_index == 0:
            head_total = head_part
            shared_total = shared_part
        else:
            head_total = tuple((former + latter for former, latter in zip(head_total, head_part)))
            shared_total = tuple(
                (former + latter for former, latter in zip(shared_total, shared_part))
            )
        input_grads = store_slot(input_grads, grad_stream, clipped, is_valid)
        if tick_index + 1 < tick_count:
            back_arrived = shifted(grad_stream.astype(jnp.bfloat16), "section", -1).astype(
                grad_stream.dtype
            )
    return (
        outputs_all[None],
        input_grads[None],
        shared_total[0][None],
        head_total[0][None],
        head_total[1][None],
        shared_total[1][None],
        head_total[2][None],
        head_total[4][None],
        head_total[5][None],
        shared_total[2][None],
        shared_total[3][None],
        head_total[6][None],
        head_total[7][None],
        head_total[8][None],
        head_total[9][None],
        head_total[3][None],
    )


def solution(mesh):
    return jax.shard_map(
        on_device,
        mesh=mesh,
        in_specs=(
            P(None, ("seq", "head"), None),
            P(None, ("seq", "head"), None),
            P(None, "seq"),
            P(None, "seq"),
            P("section", None),
            P("section", None, "head"),
            P("section", None, "head"),
            P("section", None, None),
            P("section", None, "head"),
            P("section", None, "head"),
            P("section", "head"),
            P("section", None, None),
            P("section", None),
            P("section", "head"),
            P("section", "head"),
            P("section", "head"),
            P("section", "head"),
            P("section", "head", None),
        ),
        out_specs=(
            P("section", None, ("seq", "head"), None),
            P("section", None, ("seq", "head"), None),
            P("section", None),
            P("section", None, "head"),
            P("section", None, "head"),
            P("section", None, None),
            P("section", None, "head"),
            P("section", None, "head"),
            P("section", "head"),
            P("section", None, None),
            P("section", None),
            P("section", "head"),
            P("section", "head"),
            P("section", "head"),
            P("section", "head"),
            P("section", "head", None),
        ),
        check_vma=False,
    )
```

profile of v0, /device:TPU:0, one launch (start us, length us, event | category | flops | bytes accessed | tf_op | source)
XLA Modules:
  0.0 2883.7 jit_solution(15988698672425146854)
XLA Ops:
  27.3 9.1 pad_maximum_fusion
  37.8 21.4 all-gather.37.cloned.1.call-done
  59.3 9.2 fusion.684
  99.3 10.6 reduce-scatter.7.cloned.1.call-start
  140.0 9.4 fusion.268
  153.4 11.9 psum.357
  172.9 74.0 %reduce-scatter.7.cloned.1.call-done = f32[128,2048]{1,0:T(8,128)} async-done(((f32[512,2048]{1,0:T(8,128)}), f32[128,2048]{1,0:T(8,128)}) %reduce-scatter.7.cloned.1.call-update) | async-done | bytes 1048592 | tf_op jit(solution)/shard_map/reduce_scatter | solution.py:242
  256.6 45.9 %all-gather.39.cloned.1.call-done = bf16[512,2048]{1,0:T(8,128)(2,1)} async-done(((bf16[128,2048]{1,0:T(8,128)(2,1)}), bf16[512,2048]{1,0:T(8,128)(2,1)}) %all-gather.39.cloned.1.call-update) | async-done | bytes 2097168 | tf_op jit(solution)/shard_map/all_gather | solution.py:216
  302.5 9.2 fusion.685
  355.3 21.3 all-gather.57.cloned.1.call-done
  390.5 9.4 fusion.267
  403.9 11.9 psum.358
  427.0 70.4 %reduce-scatter.9.cloned.1.call-done = f32[128,2048]{1,0:T(8,128)} async-done(((f32[512,2048]{1,0:T(8,128)}), f32[128,2048]{1,0:T(8,128)}) %reduce-scatter.9.cloned.1.call-update) | async-done | bytes 1048592 | tf_op jit(solution)/shard_map/reduce_scatter | solution.py:242
  517.9 37.9 %all-gather.43.cloned.1.call-done = bf16[512,2048]{1,0:T(8,128)(2,1)} async-done(((bf16[128,2048]{1,0:T(8,128)(2,1)}), bf16[512,2048]{1,0:T(8,128)(2,1)}) %all-gather.43.cloned.1.call-update) | async-done | bytes 2097168 | tf_op jit(solution)/shard_map/all_gather | solution.py:216
  555.8 9.2 fusion.687
  596.1 9.6 all-reduce.93
  623.9 10.8 while.601
  657.8 11.1 fusion.265
  690.1 9.4 psum.360
  699.5 9.6 multiply_reduce_fusion.38
  709.1 9.5 psum.361
  733.6 9.1 fusion.262
  744.4 9.9 while.599
  775.1 16.4 fusion.99
  858.2 10.7 multiply_reduce_fusion.24
  873.8 9.9 add_add_fusion.2
  919.5 42.6 %reduce-scatter.13.cloned.1.call-done = bf16[128,2048]{1,0:T(8,128)(2,1)} async-done(((bf16[512,2048]{1,0:T(8,128)(2,1)}), bf16[128,2048]{1,0:T(8,128)(2,1)}) %reduce-scatter.13.cloned.1.call-update) | async-done | bytes 524304 | tf_op jit(solution)/shard_map/reduce_scatter | solution.py:325
  979.6 34.1 %all-gather.47.cloned.1.call-done = bf16[512,2048]{1,0:T(8,128)(2,1)} async-done(((bf16[128,2048]{1,0:T(8,128)(2,1)}), bf16[512,2048]{1,0:T(8,128)(2,1)}) %all-gather.47.cloned.1.call-update) | async-done | bytes 2097168 | tf_op jit(solution)/shard_map/all_gather | solution.py:216
  1013.7 9.2 fusion.690
  1025.3 35.3 %all-gather.51.cloned.1.call-done = bf16[512,2048]{1,0:T(8,128)(2,1)} async-done(((bf16[128,2048]{1,0:T(8,128)(2,1)}), bf16[512,2048]{1,0:T(8,128)(2,1)}) %all-gather.51.cloned.1.call-update) | async-done | bytes 2097168 | tf_op jit(solution)/shard_map/all_gather | solution.py:216
  1060.6 9.2 fusion.693
  1073.1 33.7 %all-gather.41.cloned.1.call-done = bf16[512,2048]{1,0:T(8,128)(2,1)} async-done(((bf16[128,2048]{1,0:T(8,128)(2,1)}), bf16[512,2048]{1,0:T(8,128)(2,1)}) %all-gather.41.cloned.1.call-update) | async-done | bytes 2097168 | tf_op jit(solution)/shard_map/all_gather | solution.py:216
  1106.8 9.2 fusion.686
  1138.8 9.0 fusion.240
  1168.3 9.4 fusion.241
  1275.1 10.8 fusion.68
  1331.9 14.0 fusion.253
  1371.2 9.6 psum.362
  1383.1 9.7 multiply_reduce_fusion.37
  1392.8 9.9 all-reduce.98
  1418.9 11.7 while.605
  1438.3 9.5 fusion.256
  1466.9 16.2 fusion.103
  1547.3 11.8 multiply_reduce_fusion.16
  1559.2 10.2 broadcast_multiply_fusion.6
  1647.1 13.2 reduce-scatter.15.cloned.1.call-done
  1677.0 19.7 all-gather.59.cloned.1.call-done
  1707.0 9.4 fusion.266
  1721.8 22.5 all-gather.53.cloned.1.call-done
  1744.2 10.1 multiply_reduce_fusion.36
  1754.4 10.0 all-reduce.97
  1778.8 10.7 fusion.250
  1796.2 16.6 fusion.107
  1882.8 10.4 multiply_reduce_fusion.8
  1898.2 10.0 add_add_fusion
  2015.0 17.1 all-reduce.100
  2044.0 75.9 %all-reduce.96 = (f32[2048]{0:T(1024)}, f32[4,256]{1,0:T(4,128)}, f32[256]{0:T(256)}) all-reduce(f32[2048]{0:T(1024)S(1)} %multiply_add_fusion.6, f32[4,256]{1,0:T(4,128)S(1)} %fusion.559, f32[256]{0:T(256)S(1)} %fusion.600), channel_id=1, replica_groups=mesh['section'=2,'seq'=4,'head'=4] {'seq','head'}, use_global_device_ids=true, to_apply=%region_223.225 | all-reduce | flops 3328 | bytes 26624 | tf_op jit(solution)/shard_map/psum | solution.py:375
  2126.0 615.0 %all-reduce.107.cloned.1.call-done = (bf16[2048,1024]{0,1:T(8,128)(2,1)}, bf16[2048,1024]{0,1:T(8,128)(2,1)}, bf16[2048,1024]{0,1:T(8,128)(2,1)}, bf16[2048,1024...) async-done(((bf16[2048,1024]{0,1:T(8,128)(2,1)}, ...) | async-done | bytes 37945360 | tf_op jit(solution)/shard_map/psum | solution.py:364
  2741.0 11.0 add_bitcast_fusion.2
  2751.9 9.2 copy.1198
  2761.1 11.1 add_bitcast_fusion.1
  2772.2 9.3 copy.1199
  2782.3 11.0 add_bitcast_fusion
  2793.3 80.7 %all-reduce.105.cloned.1.call-done = f32[2048,256]{1,0:T(8,128)} async-done(((f32[2048,256]{1,0:T(8,128)}), f32[2048,256]{1,0:T(8,128)}) %all-reduce.105.cloned.1.call-update) | async-done | bytes 2097168 | tf_op jit(solution)/shard_map/psum | solution.py:375
  (2417 shorter events, 1299.8 us)
Async XLA Ops:
  7.2 52.0 %all-gather.37.cloned.1.call-start = ((), (), s32[]{:S(2)}) async-start(), calls=%async_computation.6 | async-start | bytes 2621440 | tf_op jit(solution)/shard_map/all_gather | solution.py:216
  10.7 121.9 %all-gather.55.cloned.1.call-start = ((), (), s32[]{:S(2)}) async-start(), calls=%async_computation.21 | async-start | bytes 2621440 | tf_op jit(solution)/shard_map/all_gather | solution.py:28
  11.7 98.3 %copy-start.424 = (s32[1,512]{1,0:T(1,128)}, s32[1,512]{1,0:T(1,128)S(1)}, u32[]{:S(2)}) copy-start(s32[1,512]{1,0:T(1,128)S(1)} %get-tuple-element.4339) | copy-start | bytes 6148
  11.7 101.6 %copy-start.426 = (s32[1,512]{1,0:T(1,128)}, s32[1,512]{1,0:T(1,128)S(1)}, u32[]{:S(2)}) copy-start(s32[1,512]{1,0:T(1,128)S(1)} %get-tuple-element.4344) | copy-start | bytes 6148
  11.8 24.6 collective-permute-start
  16.7 19.7 collective-permute-start.3
  24.2 557.1 %copy-start.316 = (f32[1,512]{1,0:T(1,128)}, f32[1,512]{1,0:T(1,128)S(1)}, u32[]{:S(2)}) copy-start(f32[1,512]{1,0:T(1,128)S(1)} %get-tuple-element.4334) | copy-start | bytes 6148
  25.4 550.0 %copy-start.284 = (f32[1280]{0:T(1024)}, f32[1280]{0:T(1024)S(1)}, u32[]{:S(2)}) copy-start(f32[1280]{0:T(1024)S(1)} %pad_maximum_fusion.20) | copy-start | bytes 15364
  26.1 1142.2 %copy-start.257 = (f32[1280]{0:T(1024)}, f32[1280]{0:T(1024)S(1)}, u32[]{:S(2)}) copy-start(f32[1280]{0:T(1024)S(1)} %get-tuple-element.3656) | copy-start | bytes 15364
  26.1 1142.2 %copy-start.260 = (f32[1280]{0:T(1024)}, f32[1280]{0:T(1024)S(1)}, u32[]{:S(2)}) copy-start(f32[1280]{0:T(1024)S(1)} %get-tuple-element.3658) | copy-start | bytes 15364
  26.1 539.1 %copy-start.436 = (f32[16]{0:T(128)}, f32[16]{0:T(128)S(1)}, u32[]{:S(2)}) copy-start(f32[16]{0:T(128)S(1)} %exponential_bitcast_fusion) | copy-start | bytes 196
  72.6 8.1 collective-permute-start.1
  99.3 147.6 %reduce-scatter.7.cloned.1.call-start = ((), (), s32[]{:S(2)}) async-start(), calls=%async_computation.7 | async-start | bytes 5242880 | tf_op jit(solution)/shard_map/reduce_scatter | solution.py:242
  172.8 129.7 %all-gather.39.cloned.1.call-start = ((), (), s32[]{:S(2)}) async-start(), calls=%async_computation.8 | async-start | bytes 2621440 | tf_op jit(solution)/shard_map/all_gather | solution.py:216
  249.7 4.2 collective-permute-start.2
  255.8 120.8 %all-gather.57.cloned.1.call-start = ((), (), s32[]{:S(2)}) async-start(), calls=%async_computation.22 | async-start | bytes 2621440 | tf_op jit(solution)/shard_map/all_gather | solution.py:28
  315.8 8.7 collective-permute-start.4
  343.3 154.1 %reduce-scatter.9.cloned.1.call-start = ((), (), s32[]{:S(2)}) async-start(), calls=%async_computation.9 | async-start | bytes 5242880 | tf_op jit(solution)/shard_map/reduce_scatter | solution.py:242
  423.2 132.5 %all-gather.43.cloned.1.call-start = ((), (), s32[]{:S(2)}) async-start(), calls=%async_computation.12 | async-start | bytes 2621440 | tf_op jit(solution)/shard_map/all_gather | solution.py:216
  501.2 4.7 collective-permute-start.5
  507.9 132.1 %all-gather.61.cloned.1.call-start = ((), (), s32[]{:S(2)}) async-start(), calls=%async_computation.24 | async-start | bytes 2621440 | tf_op jit(solution)/shard_map/all_gather | solution.py:28
  508.0 8.4 collective-permute-start.6
  511.5 4.9 collective-permute-start.8
  569.1 6.0 collective-permute-start.9
  592.7 106.8 %all-gather.45.cloned.1.call-start = ((), (), s32[]{:S(2)}) async-start(), calls=%async_computation.13 | async-start | bytes 2621440 | tf_op jit(solution)/shard_map/all_gather | solution.py:280
  594.7 224.2 %all-gather.63.cloned.1.call-start = ((), (), s32[]{:S(2)}) async-start(), calls=%async_computation.25 | async-start | bytes 1310720 | tf_op jit(solution)/shard_map/all_gather | solution.py:48
  775.0 187.2 %reduce-scatter.13.cloned.1.call-start = ((), (), s32[]{:S(2)}) async-start(), calls=%async_computation.14 | async-start | bytes 2621440 | tf_op jit(solution)/shard_map/reduce_scatter | solution.py:325
  897.1 6.1 collective-permute-start.10
  919.2 94.5 %all-gather.47.cloned.1.call-start = ((), (), s32[]{:S(2)}) async-start(), calls=%async_computation.15 | async-start | bytes 2621440 | tf_op jit(solution)/shard_map/all_gather | solution.py:216
  967.6 93.1 %all-gather.51.cloned.1.call-start = ((), (), s32[]{:S(2)}) async-start(), calls=%async_computation.18 | async-start | bytes 2621440 | tf_op jit(solution)/shard_map/all_gather | solution.py:216
  968.3 138.5 %all-gather.41.cloned.1.call-start = ((), (), s32[]{:S(2)}) async-start(), calls=%async_computation.10 | async-start | bytes 2621440 | tf_op jit(solution)/shard_map/all_gather | solution.py:216
  968.5 8.9 collective-permute-start.12
  971.9 5.4 collective-permute-start.16
  976.7 156.4 %copy-start.515 = (f32[2]{0:T(128)}, f32[2]{0:T(128)S(1)}, u32[]{:S(2)}) copy-start(f32[2]{0:T(128)S(1)} %get-tuple-element.4427) | copy-start | bytes 28
  977.3 156.9 %copy-start.381 = (f32[2,256]{1,0:T(2,128)}, f32[2,256]{1,0:T(2,128)S(1)}, u32[]{:S(2)}) copy-start(f32[2,256]{1,0:T(2,128)S(1)} %get-tuple-element.4417) | copy-start | bytes 6148
  977.3 156.9 %copy-start.467 = (f32[2,256]{1,0:T(2,128)}, f32[2,256]{1,0:T(2,128)S(1)}, u32[]{:S(2)}) copy-start(f32[2,256]{1,0:T(2,128)S(1)} %get-tuple-element.4418) | copy-start | bytes 6148
  978.7 160.0 %copy-start.453 = (f32[512]{0:T(512)}, f32[512]{0:T(512)S(1)}, u32[]{:S(2)}) copy-start(f32[512]{0:T(512)S(1)} %get-tuple-element.4327) | copy-start | bytes 6148
  978.7 160.0 %copy-start.455 = (f32[512]{0:T(512)}, f32[512]{0:T(512)S(1)}, u32[]{:S(2)}) copy-start(f32[512]{0:T(512)S(1)} %get-tuple-element.4328) | copy-start | bytes 6148
  978.7 160.0 %copy-start.457 = (f32[512]{0:T(512)}, f32[512]{0:T(512)S(1)}, u32[]{:S(2)}) copy-start(f32[512]{0:T(512)S(1)} %get-tuple-element.4329) | copy-start | bytes 6148
  978.8 310.4 %all-gather.65.cloned.1.call-start = ((), (), s32[]{:S(2)}) async-start(), calls=%async_computation.26 | async-start | bytes 2621440 | tf_op jit(solution)/shard_map/all_gather | solution.py:28
  1119.7 83.3 %copy-start.222 = (f32[512,16]{0,1:T(8,128)}, f32[512,16]{0,1:T(8,128)S(1)}, u32[]{:S(2)}) copy-start(f32[512,16]{0,1:T(8,128)S(1)} %get-tuple-element.4389) | copy-start | bytes 98308
  1119.7 83.4 %copy-start.220 = (f32[512,16]{0,1:T(8,128)}, f32[512,16]{0,1:T(8,128)S(1)}, u32[]{:S(2)}) copy-start(f32[512,16]{0,1:T(8,128)S(1)} %get-tuple-element.4168) | copy-start | bytes 98308
  1123.6 14.9 collective-permute-start.13
  1128.9 38.3 %collective-permute-start.17 = (f32[3,1280]{1,0:T(4,128)}, f32[3,1280]{1,0:T(4,128)}, u32[]{:S(2)}, u32[]{:S(2)}) collective-permute-start(f32[3,1280]{1,0:T(4,128)} %copy.1131), channel_id=1, source_target_pairs={{0,4},{4,8},{8,12},{1,5},{5,9},{9,13},{2,6},{6,10},{10,14},{3,7},{... | collective-permute-start | bytes 46088 | tf_op jit(solution)/shard_map/ppermute | solution.py:23
  1162.1 136.4 %all-gather.69.cloned.1.call-start = ((), (), s32[]{:S(2)}) async-start(), calls=%async_computation.28 | async-start | bytes 2621440 | tf_op jit(solution)/shard_map/all_gather | solution.py:28
  1194.0 189.1 %all-gather.49.cloned.1.call-start = ((), (), s32[]{:S(2)}) async-start(), calls=%async_computation.16 | async-start | bytes 2621440 | tf_op jit(solution)/shard_map/all_gather | solution.py:280
  1195.5 5.8 collective-permute-start.11
  1203.0 299.9 %all-gather.67.cloned.1.call-start = ((), (), s32[]{:S(2)}) async-start(), calls=%async_computation.27 | async-start | bytes 1310720 | tf_op jit(solution)/shard_map/all_gather | solution.py:48
  1231.2 56.1 %collective-permute-start.7 = (f32[3,1280]{1,0:T(4,128)}, f32[3,1280]{1,0:T(4,128)}, u32[]{:S(2)}, u32[]{:S(2)}) collective-permute-start(f32[3,1280]{1,0:T(4,128)} %copy.986), channel_id=1, source_target_pairs={{0,4},{4,8},{8,12},{1,5},{5,9},{9,13},{2,6},{6,10},{10,14},{3,7},{... | collective-permute-start | bytes 46088 | tf_op jit(solution)/shard_map/ppermute | solution.py:23
  1248.1 113.7 %copy-start.135 = (f32[2,256,128,1]{2,1,3,0:T(8,128)}, f32[2,256,128,1]{2,1,3,0:T(8,128)S(1)}, u32[]{:S(2)}) copy-start(f32[2,256,128,1]{2,1,3,0:T(8,128)S(1)} %copy.1257) | copy-start | bytes 786436
  1466.8 193.5 %reduce-scatter.15.cloned.1.call-start = ((), (), s32[]{:S(2)}) async-start(), calls=%async_computation.17 | async-start | bytes 2621440 | tf_op jit(solution)/shard_map/reduce_scatter | solution.py:325
  1592.5 7.5 collective-permute-start.14
  1617.2 79.5 %all-gather.59.cloned.1.call-start = ((), (), s32[]{:S(2)}) async-start(), calls=%async_computation.23 | async-start | bytes 2621440 | tf_op jit(solution)/shard_map/all_gather | solution.py:28
  1637.4 106.8 %all-gather.53.cloned.1.call-start = ((), (), s32[]{:S(2)}) async-start(), calls=%async_computation.19 | async-start | bytes 2621440 | tf_op jit(solution)/shard_map/all_gather | solution.py:280
  1665.6 10.3 collective-permute-start.15
  1674.3 90.1 %copy-start.497 = (f32[512]{0:T(512)}, f32[512]{0:T(512)S(1)}, u32[]{:S(2)}) copy-start(f32[512]{0:T(512)S(1)} %add_rsqrt_fusion) | copy-start | bytes 6148
  1677.0 168.3 %all-gather.71.cloned.1.call-start = ((), (), s32[]{:S(2)}) async-start(), calls=%async_computation.29 | async-start | bytes 1310720 | tf_op jit(solution)/shard_map/all_gather | solution.py:48
  1796.1 244.9 %reduce-scatter.17.cloned.1.call-start = ((), (), s32[]{:S(2)}) async-start(), calls=%async_computation.20 | async-start | bytes 2621440 | tf_op jit(solution)/shard_map/reduce_scatter | solution.py:325
  1921.6 5.7 collective-permute-start.18
  1943.3 179.9 %reduce-scatter.11.cloned.1.call-start = ((), (), s32[]{:S(2)}) async-start(), calls=%async_computation.11 | async-start | bytes 5242880 | tf_op jit(solution)/shard_map/reduce_scatter | solution.py:242
  1956.0 784.9 %all-reduce.107.cloned.1.call-start = ((), (), s32[]{:S(2)}) async-start(), calls=%async_computation.31 | async-start | bytes 75890688 | tf_op jit(solution)/shard_map/psum | solution.py:364
  1997.8 876.1 %all-reduce.105.cloned.1.call-start = ((), (), s32[]{:S(2)}) async-start(), calls=%async_computation.30 | async-start | bytes 4194304 | tf_op jit(solution)/shard_map/psum | solution.py:375
  2040.9 79.0 %copy-start.579 = (f32[128]{0:T(128)S(1)}, f32[128]{0:T(128)}, u32[]{:S(2)}) copy-start(f32[128]{0:T(128)} %get-tuple-element.4397) | copy-start | bytes 1540
  2043.9 79.3 %copy-start.44 = (bf16[2,128,2048]{2,1,0:T(8,128)(2,1)S(1)}, bf16[2,128,2048]{2,1,0:T(8,128)(2,1)}, u32[]{:S(2)}) copy-start(bf16[2,128,2048]{2,1,0:T(8,128)(2,1)} %param.97) | copy-start | bytes 3145732
  (591 other events, 4807.9 us)
Sparse Core Ops, SparseCore 0:
  10.8 48.4 all-gather.36
  99.5 33.1 all-gather.54
  172.9 73.9 reduce-scatter.6
  255.9 46.5 all-gather.38
  343.4 33.1 all-gather.56
  423.4 73.9 reduce-scatter.8
  508.0 47.7 all-gather.42
  592.8 33.6 all-gather.60
  628.1 45.9 all-gather.44
  775.1 24.3 all-gather.62
  919.3 42.7 reduce-scatter.12
  967.7 45.9 all-gather.46
  1015.9 44.6 all-gather.50
  1062.1 44.6 all-gather.40
  1162.2 32.6 all-gather.64
  1196.7 35.2 all-gather.68
  1233.5 45.9 all-gather.48
  1466.9 24.5 all-gather.66
  1617.3 42.9 reduce-scatter.14
  1662.0 34.6 all-gather.58
  1698.3 45.9 all-gather.52
  1796.2 24.9 all-gather.70
  1943.5 42.6 reduce-scatter.16
  1989.0 76.9 reduce-scatter.10
  2072.4 668.5 all-reduce.106
  2747.2 126.6 all-reduce.104
where the time goes:
time: 2900 us; the launch traced here: 2880 us
  waiting for transfers between devices  1180 us (41%)
  matrix products  543 us (19%)
  other arithmetic  494 us (17%)
  local copies, waits for them, and re-layouts  349 us (12%)
  blocking collectives  224 us (8%)
  starting transfers between devices  67.9 us (2%)
    psum x1, waiting for transfers between devices, reduce_grads(): lax.psum(head_part[0].astype(jnp.bfloat16), 'seq').astype(jnp.float32)  615 us
    all_gather x6, waiting for transfers between devices, mixer_state(): gathered = lax.all_gather(normed, 'head', axis=0, tiled=True)  208 us
    dot_general x18, matrix products, block_output(): jnp.einsum('cijh,cjhp->cihp', weights, x_blocks, precision=highest)  187 us
    reduce_scatter x3, waiting for transfers between devices, mixer_output(): lax.psum_scatter(jnp.dot(normed_out, w_out, preferred_element_type=jnp.fl...  144 us
    unnamed x1231, local copies, waits for them, and re-layouts  98.7 us
    psum x1, waiting for transfers between devices, reduce_grads(): lax.psum((shared_part[0], shared_part[1], shared_part[2], shared_part[3])...  80.7 us
    dot_general x21, matrix products, block_output(): jnp.einsum('cin,chpn->cihp', c_blocks, incoming, precision=highest)  78.3 us
    psum x1, blocking collectives, reduce_grads(): lax.psum((shared_part[0], shared_part[1], shared_part[2], shared_part[3])...  75.9 us
  transfers between devices with their start and end apart: 45, of which 18 were waited for; matrix products, arithmetic and copies ran while one was open for 24% of the time, Pallas kernels for 0%

commit v1 on v0

--- a/solution.py
+++ b/solution.py
@@ -26,18 +26,16 @@
 def entering(value, axis, combine, identity):
     count, mine = (lax.axis_size(axis), lax.axis_index(axis))
     everything = jax.tree.map(lambda part: lax.all_gather(part, axis), value)
-    start = jax.tree.map(
+    before = jax.tree.map(
         lambda part, zero: jnp.broadcast_to(jnp.asarray(zero, part.dtype), part.shape),
         value,
         identity,
     )
-
-    def lap(k, before):
+    for k in range(count - 1):
         reached = k < mine
         new = combine(before, jax.tree.map(lambda part: part[k], everything))
-        return jax.tree.map(lambda a, b: jnp.where(reached, a, b), new, before)
-
-    return lax.fori_loop(0, count, lap, start)
+        before = jax.tree.map(lambda a, b: jnp.where(reached, a, b), new, before)
+    return before
 
 
 def entering_2(value, axis, join, neutral):
@@ -50,19 +48,15 @@
         jax.tree.map(lambda a: jnp.bfloat16 if a.dtype == jnp.float32 else a.dtype, value),
     )
     state = jax.tree.map(lambda a, e: jnp.zeros_like(a) + jnp.asarray(e, a.dtype), value, neutral)
-
-    def one(lap, state):
+    for lap in range(count - 1):
         source = count - 1 - lap
-        return join(
+        new = join(
             state,
-            jax.tree.map(
-                lambda a, own: lax.dynamic_index_in_dim(a, source, 0, False).astype(own.dtype),
-                gathered,
-                value,
-            ),
+            jax.tree.map(lambda a, own: a[source].astype(own.dtype), gathered, value),
         )
-
-    return lax.fori_loop(0, ahead, one, state)
+        active = lap < ahead
+        state = jax.tree.map(lambda a, b: jnp.where(active, a, b), new, state)
+    return state
 
 
 def rms_scale(values):
@@ -121,12 +115,14 @@
 
 
 def compose_blocks(block_decay, block_states, start_state):
-
-    def advance(chain_state, block_item):
-        factor, fresh_state = block_item
-        return (factor[:, None, None] * chain_state + fresh_state, chain_state)
-
-    return lax.scan(advance, start_state, (block_decay, block_states))
+    chain_state = start_state
+    incoming = []
+    for block_index in range(block_decay.shape[0]):
+        incoming.append(chain_state)
+        chain_state = (
+            block_decay[block_index][:, None, None] * chain_state + block_states[block_index]
+        )
+    return (chain_state, jnp.stack(incoming))
 
 
 def block_output(block_parts, b_mat, c_mat, skip, incoming):
@@ -197,7 +193,7 @@
     return (extended, marks_ext)
 
 
-def mixer_state(stream, start_marks, alive_mask, layer_weights):
+def mixer_forward(stream, start_marks, alive_mask, layer_weights):
     (
         norm_gain,
         w_main,
@@ -215,39 +211,51 @@
     normed = (stream * rms_scale(stream) * norm_gain).astype(jnp.bfloat16)
     gathered = lax.all_gather(normed, "head", axis=0, tiled=True)
     projected = jnp.dot(gathered, w_main, preferred_element_type=jnp.float32)
+    gate_pre = projected[:, :inner_width]
     pre_conv = projected[:, inner_width : 2 * inner_width + 2 * N]
     dt_pre = projected[:, 2 * inner_width + 2 * N :]
     marks_float = start_marks.astype(jnp.float32)
     tail_from = pre_conv.shape[0] - KW + 1
     edge_parts = shifted((pre_conv[tail_from:], marks_float[tail_from:]), "seq", 1)
     extended, marks_ext = extend(pre_conv, start_marks, edge_parts[0], edge_parts[1])
-    block_parts, b_mat, c_mat, total_decay, total_state = local_front(
-        marks_ext, alive_mask, extended, dt_pre, conv_weight, conv_bias, dt_bias, a_log
-    )
+    front_fn = partial(local_front, marks_ext, alive_mask)
+    front_out, front_pull = jax.vjp(
+        front_fn, extended, dt_pre, conv_weight, conv_bias, dt_bias, a_log
+    )
+    block_parts, b_mat, c_mat, total_decay, total_state = front_out
     neutral = (jnp.ones_like(total_decay), jnp.zeros_like(total_state))
     prefix = entering((total_decay, total_state), "seq", chain_combine, neutral)
     start_state = prefix[1]
-    mixed_out = local_rear(block_parts, b_mat, c_mat, skip, start_state)
-    gated_mix = mixed_out * jax.nn.silu(projected[:, :inner_width])
+    mixed_out, rear_pull = jax.vjp(local_rear, block_parts, b_mat, c_mat, skip, start_state)
+    silu_gate = jax.nn.silu(gate_pre)
+    gated_mix = mixed_out * silu_gate
     square_total = lax.psum(jnp.sum(gated_mix * gated_mix, axis=-1), "head")
-    return (
-        (gathered, projected, edge_parts[0], edge_parts[1], start_state, square_total),
-        gated_mix,
-    )
-
-
-def mixer_output(gated_mix, square_total, gate_gain, w_out):
     scale_out = lax.rsqrt(square_total / DI + norm_eps)
     normed_out = (gated_mix * scale_out[:, None] * gate_gain).astype(jnp.bfloat16)
-    return lax.psum_scatter(
+    branch = lax.psum_scatter(
         jnp.dot(normed_out, w_out, preferred_element_type=jnp.float32),
         "head",
         scatter_dimension=0,
         tiled=True,
     )
-
-
-def mixer_backward(stream, grad_next, start_marks, alive_mask, layer_weights, saved_parts):
+    saved = (
+        stream,
+        gathered,
+        gate_pre,
+        mixed_out,
+        silu_gate,
+        gated_mix,
+        scale_out,
+        normed_out,
+        total_decay,
+        start_state,
+        front_pull,
+        rear_pull,
+    )
+    return stream + branch, saved
+
+
+def mixer_backward(grad_next, layer_weights, saved):
     (
         norm_gain,
         w_main,
@@ -261,31 +269,29 @@
         gate_gain,
         w_out,
     ) = layer_weights
-    gathered, projected, edge_rows, edge_marks, start_state, square_total = saved_parts
+    (
+        stream,
+        gathered,
+        gate_pre,
+        mixed_out,
+        silu_gate,
+        gated_mix,
+        scale_out,
+        normed_out,
+        total_decay,
+        start_state,
+        front_pull,
+        rear_pull,
+    ) = saved
     inner_width = w_out.shape[0]
-    gate_pre = projected[:, :inner_width]
-    pre_conv = projected[:, inner_width : 2 * inner_width + 2 * N]
-    dt_pre = projected[:, 2 * inner_width + 2 * N :]
-    extended, marks_ext = extend(pre_conv, start_marks, edge_rows, edge_marks)
-    local_fn = partial(local_pass, marks_ext, alive_mask)
-    primal, pull_back = jax.vjp(
-        local_fn, extended, dt_pre, conv_weight, conv_bias, dt_bias, a_log, skip, start_state
-    )
-    mixed_out, total_decay, total_state = primal
-    silu_gate = jax.nn.silu(gate_pre)
-    gated_mix = mixed_out * silu_gate
-    scale_out = lax.rsqrt(square_total / DI + norm_eps)
-    normed_out = (gated_mix * scale_out[:, None] * gate_gain).astype(jnp.bfloat16)
     grad_branch = grad_next.astype(jnp.bfloat16)
     shard_rows = lax.all_gather(grad_branch, "head", axis=0, tiled=True)
-    out_grad = lax.dot_general(
+    g_w_out = lax.dot_general(
         normed_out, shard_rows, (((0,), (0,)), ((), ())), preferred_element_type=jnp.float32
     )
-    back_rows = lax.dot_general(
+    grad_normed = lax.dot_general(
         shard_rows, w_out, (((1,), (1,)), ((), ())), preferred_element_type=jnp.float32
     )
-    grad_normed = back_rows
-    g_w_out, grad_normed = (out_grad, grad_normed)
     weighted = grad_normed * gate_gain
     g_gate_gain = jnp.sum(grad_normed * gated_mix * scale_out[:, None], axis=0)
     cross_sum = lax.psum(jnp.sum(weighted * gated_mix, axis=-1), "head")
@@ -294,16 +300,14 @@
     )
     grad_mixed = grad_gated * silu_gate
     grad_gate = (grad_gated * mixed_out * silu_slope(gate_pre)).astype(jnp.bfloat16)
-    zero_decay = jnp.zeros_like(total_decay)
-    zero_state = jnp.zeros_like(total_state)
-    first_pull = pull_back((grad_mixed, zero_decay, zero_state))
-    neutral = (jnp.ones_like(total_decay), zero_state)
-    suffix = entering_2((total_decay, first_pull[7]), "seq", chain_combine, neutral)
+    g_parts, g_b_mat, g_c_mat, g_skip, g_start = rear_pull(grad_mixed)
+    neutral = (jnp.ones_like(total_decay), jnp.zeros_like(g_start))
+    suffix = entering_2((total_decay, g_start), "seq", chain_combine, neutral)
     after_state = suffix[1]
     grad_decay = jnp.sum(after_state * start_state, axis=(1, 2))
-    second = pull_back((jnp.zeros_like(mixed_out), grad_decay, after_state))
-    summed = tuple((former + latter for former, latter in zip(first_pull[:7], second[:7])))
-    grad_ext, grad_dt_pre, g_conv_w, g_conv_b, g_dt_bias, g_a_log, g_skip = summed
+    grad_ext, grad_dt_pre, g_conv_w, g_conv_b, g_dt_bias, g_a_log = front_pull(
+        (g_parts, g_b_mat, g_c_mat, grad_decay, after_state)
+    )
     returned = shifted(grad_ext[: KW - 1], "seq", -1)
     grad_pre = grad_ext[KW - 1 :]
     tail_from = grad_pre.shape[0] - KW + 1
@@ -312,6 +316,16 @@
     grad_bc = grad_pre[:, inner_width:]
     grad_low = jnp.concatenate([grad_gate, grad_inner, grad_dt_pre.astype(jnp.bfloat16)], axis=1)
     w_bc_float = w_bc.astype(jnp.float32)
+    g_low = lax.dot_general(
+        gathered, grad_low, (((0,), (0,)), ((), ())), preferred_element_type=jnp.float32
+    )
+    g_w_bc = lax.dot_general(
+        gathered.astype(jnp.float32),
+        grad_bc,
+        (((0,), (0,)), ((), ())),
+        precision=highest,
+        preferred_element_type=jnp.float32,
+    )
     main_term = lax.dot_general(
         grad_low, w_low, (((1,), (1,)), ((), ())), preferred_element_type=jnp.float32
     )
@@ -325,16 +339,6 @@
     grad_normed_in = lax.psum_scatter(
         (main_term + side_term).astype(jnp.bfloat16), "head", scatter_dimension=0, tiled=True
     ).astype(jnp.float32)
-    g_low = lax.dot_general(
-        gathered, grad_low, (((0,), (0,)), ((), ())), preferred_element_type=jnp.float32
-    )
-    g_w_bc = lax.dot_general(
-        gathered.astype(jnp.float32),
-        grad_bc,
-        (((0,), (0,)), ((), ())),
-        precision=highest,
-        preferred_element_type=jnp.float32,
-    )
     scale_in = rms_scale(stream)
     g_norm_gain = jnp.sum(grad_normed_in * stream * scale_in, axis=0)
     weighted_in = grad_normed_in * norm_gain
@@ -360,22 +364,11 @@
 
 
 def reduce_grads(head_part, shared_part):
-    head_sum = (
-        lax.psum(head_part[0].astype(jnp.bfloat16), "seq").astype(jnp.float32),
-        lax.psum(head_part[1].astype(jnp.bfloat16), "seq").astype(jnp.float32),
-        lax.psum(head_part[2].astype(jnp.bfloat16), "seq").astype(jnp.float32),
-        lax.psum(head_part[3].astype(jnp.bfloat16), "seq").astype(jnp.float32),
-        lax.psum(head_part[4].astype(jnp.bfloat16), "seq").astype(jnp.float32),
-        lax.psum(head_part[5].astype(jnp.bfloat16), "seq").astype(jnp.float32),
-        lax.psum(head_part[6].astype(jnp.bfloat16), "seq").astype(jnp.float32),
-        lax.psum(head_part[7].astype(jnp.bfloat16), "seq").astype(jnp.float32),
-        lax.psum(head_part[8].astype(jnp.bfloat16), "seq").astype(jnp.float32),
-        lax.psum(head_part[9].astype(jnp.bfloat16), "seq").astype(jnp.float32),
-    )
-    shared_sum = lax.psum(
-        (shared_part[0], shared_part[1], shared_part[2], shared_part[3]), ("seq", "head")
-    )
-    return (tuple(head_sum), tuple(shared_sum))
+    head_sum = tuple(
+        lax.psum(member.astype(jnp.bfloat16), "seq").astype(jnp.float32) for member in head_part
+    )
+    shared_sum = lax.psum(tuple(shared_part), ("seq", "head"))
+    return (head_sum, tuple(shared_sum))
 
 
 def store_slot(buffer, value, slot_index, is_valid):
@@ -427,9 +420,9 @@
         w_out[0],
     )
     row_shape = inputs.shape[1:]
-    kept_inputs = jnp.zeros((micro_count,) + row_shape, jnp.float32)
     outputs_all = jnp.zeros((micro_count,) + row_shape, jnp.float32)
     arrived = jnp.zeros(row_shape, jnp.float32)
+    ticks = []
     for tick_index in range(tick_count):
         slot_index = tick_index - section_index
         is_valid = (slot_index >= 0) & (slot_index < micro_count)
@@ -438,12 +431,9 @@
         stream = jnp.where(section_index == 0, fresh_rows, arrived)
         start_marks = lax.dynamic_index_in_dim(starts, clipped, 0, False)
         alive_mask = lax.dynamic_index_in_dim(live, clipped, 0, False).astype(jnp.float32)
-        saved_parts, gated_mix = mixer_state(stream, start_marks, alive_mask, layer_weights)
-        result = stream + mixer_output(
-            gated_mix, saved_parts[5], layer_weights[9], layer_weights[10]
-        )
-        kept_inputs = store_slot(kept_inputs, stream, clipped, is_valid)
+        result, saved = mixer_forward(stream, start_marks, alive_mask, layer_weights)
         outputs_all = store_slot(outputs_all, result, clipped, is_valid)
+        ticks.append((clipped, is_valid, saved))
         if tick_index + 1 < tick_count:
             arrived = shifted(result, "section", 1)
     back_arrived = jnp.zeros(row_shape, jnp.float32)
@@ -451,22 +441,13 @@
     head_total = ()
     shared_total = ()
     for tick_index in range(tick_count):
-        slot_index = tick_index - (section_count - 1 - section_index)
-        is_valid = (slot_index >= 0) & (slot_index < micro_count)
-        clipped = jnp.clip(slot_index, 0, micro_count - 1)
+        clipped, is_valid, saved = ticks[tick_count - 1 - tick_index]
         outer_grad = lax.dynamic_index_in_dim(cotangent, clipped, 0, False).astype(jnp.float32)
         grad_next = jnp.where(section_index == section_count - 1, outer_grad, back_arrived)
-        stream = lax.dynamic_index_in_dim(kept_inputs, clipped, 0, False)
-        start_marks = lax.dynamic_index_in_dim(starts, clipped, 0, False)
-        alive_mask = lax.dynamic_index_in_dim(live, clipped, 0, False).astype(jnp.float32)
-        saved_parts = mixer_state(stream, start_marks, alive_mask, layer_weights)[0]
-        grad_stream, head_part, shared_part = mixer_backward(
-            stream, grad_next, start_marks, alive_mask, layer_weights, saved_parts
-        )
+        grad_stream, head_part, shared_part = mixer_backward(grad_next, layer_weights, saved)
         mask_value = is_valid.astype(jnp.float32)
         head_part = tuple((member * mask_value for member in head_part))
         shared_part = tuple((member * mask_value for member in shared_part))
-        head_part, shared_part = reduce_grads(head_part, shared_part)
         if tick_index == 0:
             head_total = head_part
             shared_total = shared_part
@@ -480,6 +461,7 @@
             back_arrived = shifted(grad_stream.astype(jnp.bfloat16), "section", -1).astype(
                 grad_stream.dtype
             )
+    head_total, shared_total = reduce_grads(head_total, shared_total)
     return (
         outputs_all[None],
         input_grads[None],

time: 2900 us -> 1790 us (0.62)
  waiting for transfers between devices: 1180 us -> 739 us
  other arithmetic: 494 us -> 262 us
  matrix products: 543 us -> 353 us
  local copies, waits for them, and re-layouts: 349 us -> 165 us
  starting transfers between devices: 67.9 us -> 35.4 us
    psum x2, waiting for transfers between devices: 696 us -> 232 us  [the longest x1 120 us: reduce_grads(): lax.psum(member.astype(jnp.bfloat16), 'seq').astype(jnp.float32)]
    all_gather x6 -> x3, waiting for transfers between devices: 208 us -> 119 us  [mixer_forward(): gathered = lax.all_gather(normed, 'head', axis=0, tiled=True)]
    dot_general x18 -> x9, matrix products: 187 us -> 99.5 us  [block_output(): jnp.einsum('cijh,cjhp->cihp', weights, x_blocks, precision=highest)]
    all_gather x3, waiting for transfers between devices: 22.5 us -> 95 us  [mixer_backward(): shard_rows = lax.all_gather(grad_branch, 'head', axis=0, tiled=True)]
    add x54 -> x6, other arithmetic: 61.5 us -> 8.64 us  [compose_blocks(): block_decay[block_index][:, None, None] * chain_state]
    dot_general x21 -> x9, matrix products: 78.3 us -> 27.9 us  [block_output(): jnp.einsum('cin,chpn->cihp', c_blocks, incoming, precision=highest)]
    reduce_sum x36 -> x6, other arithmetic: 57.8 us -> 13.2 us  [the longest x3 11 us: mixer_forward(): square_total = lax.psum(jnp.sum(gated_mix * gated_mix, axis=-1), 'head')]
    another operation x130 -> x30, local copies, waits for them, and re-layouts: 42.2 us -> 2.4 us
  transfers between devices with their start and end apart: 45 -> 33, of which waited for: 18 -> 22; matrix products, arithmetic and copies ran while one was open for 24% -> 21% of each run, Pallas kernels for 0% -> 0%
where the time goes in v1:
time: 1790 us; the launch traced here: 1780 us
  waiting for transfers between devices  739 us (41%)
  matrix products  353 us (20%)
  other arithmetic  262 us (15%)
  blocking collectives  205 us (11%)
  local copies, waits for them, and re-layouts  165 us (9%)
  starting transfers between devices  35.4 us (2%)
  between operations  20.2 us (1%)
    reduce_scatter x3, waiting for transfers between devices, mixer_forward(): lax.psum_scatter(jnp.dot(normed_out, w_out, preferred_element_type=jnp.fl...  146 us
    psum x1, waiting for transfers between devices, reduce_grads(): lax.psum(member.astype(jnp.bfloat16), 'seq').astype(jnp.float32)  120 us
    all_gather x3, waiting for transfers between devices, mixer_forward(): gathered = lax.all_gather(normed, 'head', axis=0, tiled=True)  119 us
    psum x1, waiting for transfers between devices, reduce_grads(): shared_sum = lax.psum(tuple(shared_part), ('seq', 'head'))  111 us
    dot_general x9, matrix products, block_output(): jnp.einsum('cijh,cjhp->cihp', weights, x_blocks, precision=highest)  99.5 us
    all_gather x3, waiting for transfers between devices, mixer_backward(): shard_rows = lax.all_gather(grad_branch, 'head', axis=0, tiled=True)  95 us
    reduce_scatter x3, waiting for transfers between devices, mixer_backward(): lax.psum_scatter((main_term + side_term).astype(jnp.bfloat16), 'head', sc...  92.1 us
    psum x1, blocking collectives, reduce_grads(): shared_sum = lax.psum(tuple(shared_part), ('seq', 'head'))  73.5 us
  transfers between devices with their start and end apart: 33, of which 22 were waited for; matrix products, arithmetic and copies ran while one was open for 21% of the time, Pallas kernels for 0%

profile of v1, /device:TPU:0, one launch (start us, length us, event | category | flops | bytes accessed | tf_op | source)
XLA Modules:
  0.0 1780.1 jit_solution(17399478728924148988)
XLA Ops:
  27.1 32.8 %all-gather.19.cloned.1.call-done = bf16[512,2048]{1,0:T(8,128)(2,1)} async-done(((bf16[128,2048]{1,0:T(8,128)(2,1)}), bf16[512,2048]{1,0:T(8,128)(2,1)}) %all-gather.19.cloned.1.call-update) | async-done | bytes 2097168 | tf_op jit(solution)/shard_map/all_gather | solution.py:212
  59.9 12.5 fusion.438
  103.7 7.7 all-gather
  120.0 14.2 all-gather.21.cloned.1.call-done
  138.8 9.4 fusion.134
  153.2 11.7 psum.140
  165.0 6.7 fusion.45
  171.8 74.1 %reduce-scatter.7.cloned.1.call-done = f32[128,2048]{1,0:T(8,128)} async-done(((f32[512,2048]{1,0:T(8,128)}), f32[128,2048]{1,0:T(8,128)}) %reduce-scatter.7.cloned.1.call-update) | async-done | bytes 1048592 | tf_op jit(solution)/shard_map/reduce_scatter | solution.py:235
  255.0 45.0 %all-gather.23.cloned.1.call-done = bf16[512,2048]{1,0:T(8,128)(2,1)} async-done(((bf16[128,2048]{1,0:T(8,128)(2,1)}), bf16[512,2048]{1,0:T(8,128)(2,1)}) %all-gather.23.cloned.1.call-update) | async-done | bytes 2097168 | tf_op jit(solution)/shard_map/all_gather | solution.py:212
  300.1 12.8 fusion.437
  328.6 9.4 fusion.112
  349.2 8.3 all-gather.1
  365.5 16.9 all-gather.25.cloned.1.call-done
  387.1 9.4 fusion.133
  401.6 11.7 psum.141
  413.3 6.7 fusion.43
  422.3 71.8 %reduce-scatter.9.cloned.1.call-done = f32[128,2048]{1,0:T(8,128)} async-done(((f32[512,2048]{1,0:T(8,128)}), f32[128,2048]{1,0:T(8,128)}) %reduce-scatter.9.cloned.1.call-update) | async-done | bytes 1048592 | tf_op jit(solution)/shard_map/reduce_scatter | solution.py:235
  508.6 41.0 %all-gather.27.cloned.1.call-done = bf16[512,2048]{1,0:T(8,128)(2,1)} async-done(((bf16[128,2048]{1,0:T(8,128)(2,1)}), bf16[512,2048]{1,0:T(8,128)(2,1)}) %all-gather.27.cloned.1.call-update) | async-done | bytes 2097168 | tf_op jit(solution)/shard_map/all_gather | solution.py:212
  549.6 13.5 fusion.436
  579.2 9.9 fusion.111
  604.7 7.9 all-gather.3
  612.6 7.4 all-gather.2
  640.8 9.4 fusion.132
  657.1 12.8 psum.142
  671.1 12.6 all-gather.31.cloned.1.call-done
  683.7 7.9 multiply_reduce_fusion.20
  691.6 10.1 psum.143
  702.4 6.6 multiply_reduce_fusion.23
  721.7 16.4 fusion.28
  754.1 7.3 fusion.128
  771.8 11.0 multiply_reduce_fusion.13
  824.2 46.0 %reduce-scatter.13.cloned.1.call-done = bf16[128,2048]{1,0:T(8,128)(2,1)} async-done(((bf16[512,2048]{1,0:T(8,128)(2,1)}), bf16[128,2048]{1,0:T(8,128)(2,1)}) %reduce-scatter.13.cloned.1.call-update) | async-done | bytes 524304 | tf_op jit(solution)/shard_map/reduce_scatter | solution.py:339
  878.8 8.0 all-gather.4
  886.9 37.2 %all-gather.35.cloned.1.call-done = bf16[512,2048]{1,0:T(8,128)(2,1)} async-done(((bf16[128,2048]{1,0:T(8,128)(2,1)}), bf16[512,2048]{1,0:T(8,128)(2,1)}) %all-gather.35.cloned.1.call-update) | async-done | bytes 2097168 | tf_op jit(solution)/shard_map/all_gather | solution.py:288
  924.1 7.3 multiply_reduce_fusion.19
  931.4 9.5 psum.144
  940.9 6.0 multiply_reduce_fusion.22
  959.4 15.5 fusion.30
  990.4 7.4 fusion.124
  1008.8 8.2 multiply_reduce_fusion.9
  1055.9 46.0 %reduce-scatter.15.cloned.1.call-done = bf16[128,2048]{1,0:T(8,128)(2,1)} async-done(((bf16[512,2048]{1,0:T(8,128)(2,1)}), bf16[128,2048]{1,0:T(8,128)(2,1)}) %reduce-scatter.15.cloned.1.call-update) | async-done | bytes 524304 | tf_op jit(solution)/shard_map/reduce_scatter | solution.py:339
  1113.1 45.2 %all-gather.39.cloned.1.call-done = bf16[512,2048]{1,0:T(8,128)(2,1)} async-done(((bf16[128,2048]{1,0:T(8,128)(2,1)}), bf16[512,2048]{1,0:T(8,128)(2,1)}) %all-gather.39.cloned.1.call-update) | async-done | bytes 2097168 | tf_op jit(solution)/shard_map/all_gather | solution.py:288
  1158.3 7.3 multiply_reduce_fusion.18
  1165.5 9.5 psum.145
  1175.0 6.0 multiply_reduce_fusion.21
  1189.2 7.9 all-gather.5
  1197.2 7.3 fusion.41
  1204.6 8.3 fusion.434
  1213.0 11.5 fusion.271
  1230.3 10.9 fusion.269
  1241.3 14.4 fusion.32
  1280.0 10.4 fusion.120
  1303.7 6.8 multiply_reduce_fusion.5
  1317.7 6.7 pad_add_fusion
  1344.5 10.5 fusion.83
  1367.1 21.7 %fusion.34 = (bf16[1,2048,1024]{1,2,0:T(8,128)(2,1)}, bf16[1,2048,1024]{1,2,0:T(8,128)(2,1)}) fusion(f32[2048,2064]{0,1:T(8,128)} %copy-done.48, f32[2048,2064]{0,1:T(8,128)} %fusion.269, f32[2048,2064]{0,1:T(8,128)} %fusion.271, f32[]{:T(128)S(6)} %convert_element_type.614, f32[]{:T(128)S(6)} %convert_element_type.613, f32[]{:T(128)S(6)} %convert_element_type.612), kind=kLoop, calls=%fused_computation.58 | loop fusion | flops 25165824 | bytes 58720268 | tf_op jit(solution)/shard_map/broadcast_in_dim | solution.py:470
  1402.4 6.3 fusion.86
  1416.9 19.1 %all-reduce.64 = (bf16[1,4,1024]{2,1,0:T(4,128)(2,1)S(1)}, bf16[1,1024]{1,0:T(2,128)(2,1)S(1)}, bf16[1,16]{1,0:T(2,128)(2,1)S(1)}, bf16[1,16]{1,0:T(2,128)(2,1)S...) all-reduce(bf16[1,4,1024]{2,1,0:T(4,128)(2,1)S(1)} %fusion.355, ...), channel_id=1, replica_groups=mesh['section'=2,'seq'=4,'head'=4] {'seq'}, use_global_device_ids=true, to_apply=%region_98.100 | all-reduce | flops 6192 | bytes 24768 | tf_op jit(solution)/shard_map/psum | solution.py:368
  1441.0 73.5 %all-reduce.63 = (f32[1,2048]{1,0:T(1,128)}, f32[1,4,256]{2,1,0:T(4,128)}, f32[1,256]{1,0:T(1,128)}) all-reduce(f32[1,2048]{1,0:T(1,128)S(1)} %bitcast.1042, f32[1,4,256]{2,1,0:T(4,128)S(1)} %fusion.357, f32[1,256]{1,0:T(1,128)S(1)} %bitcast.1060), channel_id=1, replica_groups=mesh['section'=2,'seq'=4,'head'=4] {'seq','head'}, use_global_device_ids=true, to_apply=%region_81.83 | all-reduce | flops 3328 | bytes 26624 | tf_op jit(solution)/shard_map/psum | solution.py:370
  1517.4 120.0 %all-reduce.71.cloned.1.call-done = (bf16[1,2048,1024]{1,2,0:T(8,128)(2,1)}, bf16[1,2048,1024]{1,2,0:T(8,128)(2,1)}, bf16[1,2048,16]{1,2,0:T(8,128)(2,1)}, bf16[1,1024,2048]{2,1,0:T(8,128)(2,1)}) async-done(((bf16[1,2048,1024]{1,2,0:T(8,128)(2,1)}, bf16[1,2048,1024]{1,2,0:T(8,128)(2,1)}, bf16[1,2048,16]{1,2,0:T(8,128)(2,1)}, bf16[1,1024,2048]{2,1,0:T(8,128)(2,1)}), (bf16[1,2048,1024]{1,2,0:T(8,128)(2,1)}, ...) | async-done | bytes 12648464 | tf_op jit(solution)/shard_map/psum | solution.py:368
  1637.4 6.9 copy.601
  1644.3 6.9 copy.602
  1651.9 6.7 broadcast_in_dim.334
  1658.5 111.5 %all-reduce.69.cloned.1.call-done = f32[1,2048,256]{2,1,0:T(8,128)} async-done(((f32[1,2048,256]{2,1,0:T(8,128)}), f32[1,2048,256]{2,1,0:T(8,128)}) %all-reduce.69.cloned.1.call-update) | async-done | bytes 2097168 | tf_op jit(solution)/shard_map/psum | solution.py:370
  (1345 shorter events, 498.5 us)
Async XLA Ops:
  7.3 52.7 %all-gather.19.cloned.1.call-start = ((), (), s32[]{:S(2)}) async-start(), calls=%async_computation.6 | async-start | bytes 2621440 | tf_op jit(solution)/shard_map/all_gather | solution.py:212
  11.3 122.9 %all-gather.21.cloned.1.call-start = ((), (), s32[]{:S(2)}) async-start(), calls=%async_computation.7 | async-start | bytes 2621440 | tf_op jit(solution)/shard_map/all_gather | solution.py:28
  12.2 89.2 %copy-start.295 = (s32[1,512]{1,0:T(1,128)}, s32[1,512]{1,0:T(1,128)S(1)}, u32[]{:S(2)}) copy-start(s32[1,512]{1,0:T(1,128)S(1)} %get-tuple-element.284) | copy-start | bytes 6148
  12.3 13.4 collective-permute-start
  17.2 8.5 collective-permute-start.3
  24.8 67.0 %copy-start.213 = (f32[1,512]{1,0:T(1,128)}, f32[1,512]{1,0:T(1,128)S(1)}, u32[]{:S(2)}) copy-start(f32[1,512]{1,0:T(1,128)S(1)} %get-tuple-element.279) | copy-start | bytes 6148
  24.8 313.9 %copy-start.215 = (f32[1,512]{1,0:T(1,128)}, f32[1,512]{1,0:T(1,128)S(1)}, u32[]{:S(2)}) copy-start(f32[1,512]{1,0:T(1,128)S(1)} %get-tuple-element.280) | copy-start | bytes 6148
  25.0 303.5 %copy-start.170 = (f32[1280]{0:T(1024)}, f32[1280]{0:T(1024)S(1)}, u32[]{:S(2)}) copy-start(f32[1280]{0:T(1024)S(1)} %get-tuple-element.159) | copy-start | bytes 15364
  25.0 303.5 %copy-start.174 = (f32[1280]{0:T(1024)}, f32[1280]{0:T(1024)S(1)}, u32[]{:S(2)}) copy-start(f32[1280]{0:T(1024)S(1)} %get-tuple-element.160) | copy-start | bytes 15364
  25.0 303.5 %copy-start.178 = (f32[1280]{0:T(1024)}, f32[1280]{0:T(1024)S(1)}, u32[]{:S(2)}) copy-start(f32[1280]{0:T(1024)S(1)} %get-tuple-element.161) | copy-start | bytes 15364
  25.0 303.5 %copy-start.182 = (f32[1280]{0:T(1024)}, f32[1280]{0:T(1024)S(1)}, u32[]{:S(2)}) copy-start(f32[1280]{0:T(1024)S(1)} %get-tuple-element.162) | copy-start | bytes 15364
  75.1 10.2 collective-permute-start.1
  101.3 144.5 %reduce-scatter.7.cloned.1.call-start = ((), (), s32[]{:S(2)}) async-start(), calls=%async_computation.8 | async-start | bytes 5242880 | tf_op jit(solution)/shard_map/reduce_scatter | solution.py:235
  171.7 74.4 %copy-start.52 = (bf16[2,128,2048]{2,1,0:T(8,128)(2,1)S(1)}, bf16[2,128,2048]{2,1,0:T(8,128)(2,1)}, u32[]{:S(2)}) copy-start(bf16[2,128,2048]{2,1,0:T(8,128)(2,1)} %param.19) | copy-start | bytes 3145732
  171.7 128.4 %all-gather.23.cloned.1.call-start = ((), (), s32[]{:S(2)}) async-start(), calls=%async_computation.9 | async-start | bytes 2621440 | tf_op jit(solution)/shard_map/all_gather | solution.py:212
  247.3 4.2 collective-permute-start.2
  251.8 242.4 %copy-start.30 = (f32[128,2048]{1,0:T(8,128)}, f32[128,2048]{1,0:T(8,128)S(1)}, u32[]{:S(2)}) copy-start(f32[128,2048]{1,0:T(8,128)S(1)} %get-tuple-element.220) | copy-start | bytes 3145732
  253.4 129.0 %all-gather.25.cloned.1.call-start = ((), (), s32[]{:S(2)}) async-start(), calls=%async_computation.10 | async-start | bytes 2621440 | tf_op jit(solution)/shard_map/all_gather | solution.py:28
  254.2 69.8 %copy-start.284 = (f32[2,256]{1,0:T(2,128)}, f32[2,256]{1,0:T(2,128)S(1)}, u32[]{:S(2)}) copy-start(f32[2,256]{1,0:T(2,128)S(1)} %get-tuple-element.343) | copy-start | bytes 6148
  254.2 69.8 %copy-start.317 = (f32[2,256]{1,0:T(2,128)}, f32[2,256]{1,0:T(2,128)S(1)}, u32[]{:S(2)}) copy-start(f32[2,256]{1,0:T(2,128)S(1)} %get-tuple-element.344) | copy-start | bytes 6148
  255.0 73.6 %copy-start.257 = (f32[512]{0:T(512)}, f32[512]{0:T(512)S(1)}, u32[]{:S(2)}) copy-start(f32[512]{0:T(512)S(1)} %get-tuple-element.287) | copy-start | bytes 6148
  255.0 73.6 %copy-start.259 = (f32[512]{0:T(512)}, f32[512]{0:T(512)S(1)}, u32[]{:S(2)}) copy-start(f32[512]{0:T(512)S(1)} %get-tuple-element.288) | copy-start | bytes 6148
  255.0 73.6 %copy-start.261 = (f32[512]{0:T(512)}, f32[512]{0:T(512)S(1)}, u32[]{:S(2)}) copy-start(f32[512]{0:T(512)S(1)} %get-tuple-element.289) | copy-start | bytes 6148
  255.0 65.9 %copy-start.306 = (f32[1,16]{1,0:T(1,128)S(1)}, f32[1,16]{1,0:T(1,128)}, u32[]{:S(2)}) copy-start(f32[1,16]{1,0:T(1,128)} %param.32) | copy-start | bytes 196
  255.0 65.8 %copy-start.311 = (f32[16]{0:T(128)S(1)}, f32[16]{0:T(128)}, u32[]{:S(2)}) copy-start(f32[16]{0:T(128)} %copy-done.310) | copy-start | bytes 196
  255.0 68.3 %copy-start.371 = (f32[2]{0:T(128)S(1)}, f32[2]{0:T(128)}, u32[]{:S(2)}) copy-start(f32[2]{0:T(128)} %get-tuple-element.346) | copy-start | bytes 28
  317.5 10.8 collective-permute-start.4
  349.1 145.0 %reduce-scatter.9.cloned.1.call-start = ((), (), s32[]{:S(2)}) async-start(), calls=%async_computation.11 | async-start | bytes 5242880 | tf_op jit(solution)/shard_map/reduce_scatter | solution.py:235
  401.6 539.3 %copy-start.2 = (f32[512,1024]{0,1:T(8,128)}, f32[512,1024]{0,1:T(8,128)S(1)}, u32[]{:S(2)}) copy-start(f32[512,1024]{0,1:T(8,128)S(1)} %get-tuple-element.212) | copy-start | bytes 6291460
  420.0 129.6 %all-gather.27.cloned.1.call-start = ((), (), s32[]{:S(2)}) async-start(), calls=%async_computation.12 | async-start | bytes 2621440 | tf_op jit(solution)/shard_map/all_gather | solution.py:212
  496.9 4.2 collective-permute-start.5
  501.4 371.0 %copy-start.15 = (f32[128,2048]{1,0:T(8,128)}, f32[128,2048]{1,0:T(8,128)S(1)}, u32[]{:S(2)}) copy-start(f32[128,2048]{1,0:T(8,128)S(1)} %get-tuple-element.208) | copy-start | bytes 3145732
  503.0 133.0 %all-gather.29.cloned.1.call-start = ((), (), s32[]{:S(2)}) async-start(), calls=%async_computation.13 | async-start | bytes 2621440 | tf_op jit(solution)/shard_map/all_gather | solution.py:28
  503.1 4.7 collective-permute-start.6
  506.5 66.0 %copy-start.414 = (f32[2]{0:T(128)}, f32[2]{0:T(128)S(1)}, u32[]{:S(2)}) copy-start(f32[2]{0:T(128)S(1)} %fusion.387) | copy-start | bytes 28
  508.6 70.6 %copy-start.263 = (f32[512]{0:T(512)}, f32[512]{0:T(512)S(1)}, u32[]{:S(2)}) copy-start(f32[512]{0:T(512)S(1)} %get-tuple-element.281) | copy-start | bytes 6148
  508.6 70.6 %copy-start.265 = (f32[512]{0:T(512)}, f32[512]{0:T(512)S(1)}, u32[]{:S(2)}) copy-start(f32[512]{0:T(512)S(1)} %get-tuple-element.282) | copy-start | bytes 6148
  508.6 70.6 %copy-start.267 = (f32[512]{0:T(512)}, f32[512]{0:T(512)S(1)}, u32[]{:S(2)}) copy-start(f32[512]{0:T(512)S(1)} %get-tuple-element.283) | copy-start | bytes 6148
  566.6 11.5 collective-permute-start.7
  602.6 81.1 %all-gather.31.cloned.1.call-start = ((), (), s32[]{:S(2)}) async-start(), calls=%async_computation.15 | async-start | bytes 2621440 | tf_op jit(solution)/shard_map/all_gather | solution.py:288
  604.7 142.2 %all-gather.33.cloned.1.call-start = ((), (), s32[]{:S(2)}) async-start(), calls=%async_computation.16 | async-start | bytes 1310720 | tf_op jit(solution)/shard_map/all_gather | solution.py:46
  721.6 148.6 %reduce-scatter.13.cloned.1.call-start = ((), (), s32[]{:S(2)}) async-start(), calls=%async_computation.17 | async-start | bytes 2621440 | tf_op jit(solution)/shard_map/reduce_scatter | solution.py:339
  799.3 7.5 collective-permute-start.8
  824.2 99.9 %all-gather.35.cloned.1.call-start = ((), (), s32[]{:S(2)}) async-start(), calls=%async_computation.18 | async-start | bytes 2621440 | tf_op jit(solution)/shard_map/all_gather | solution.py:288
  873.9 3.8 collective-permute-start.9
  878.7 105.8 %all-gather.37.cloned.1.call-start = ((), (), s32[]{:S(2)}) async-start(), calls=%async_computation.19 | async-start | bytes 1310720 | tf_op jit(solution)/shard_map/all_gather | solution.py:46
  886.8 97.7 %copy-start.406 = (f32[16]{0:T(128)}, f32[16]{0:T(128)S(1)}, u32[]{:S(2)}) copy-start(f32[16]{0:T(128)S(1)} %fusion.393) | copy-start | bytes 196
  886.8 97.7 %copy-start.361 = (f32[16]{0:T(128)}, f32[16]{0:T(128)S(1)}, u32[]{:S(2)}) copy-start(f32[16]{0:T(128)S(1)} %get-tuple-element.295) | copy-start | bytes 196
  886.8 97.7 %copy-start.363 = (f32[16]{0:T(128)}, f32[16]{0:T(128)S(1)}, u32[]{:S(2)}) copy-start(f32[16]{0:T(128)S(1)} %get-tuple-element.296) | copy-start | bytes 196
  959.3 142.7 %reduce-scatter.15.cloned.1.call-start = ((), (), s32[]{:S(2)}) async-start(), calls=%async_computation.20 | async-start | bytes 2621440 | tf_op jit(solution)/shard_map/reduce_scatter | solution.py:339
  1032.3 7.4 collective-permute-start.10
  1055.9 102.4 %all-gather.39.cloned.1.call-start = ((), (), s32[]{:S(2)}) async-start(), calls=%async_computation.21 | async-start | bytes 2621440 | tf_op jit(solution)/shard_map/all_gather | solution.py:288
  1106.8 3.8 collective-permute-start.11
  1112.8 150.9 %all-gather.41.cloned.1.call-start = ((), (), s32[]{:S(2)}) async-start(), calls=%async_computation.22 | async-start | bytes 1310720 | tf_op jit(solution)/shard_map/all_gather | solution.py:46
  1189.2 210.2 %reduce-scatter.11.cloned.1.call-start = ((), (), s32[]{:S(2)}) async-start(), calls=%async_computation.14 | async-start | bytes 5242880 | tf_op jit(solution)/shard_map/reduce_scatter | solution.py:235
  1197.1 66.6 %copy-start.408 = (f32[16]{0:T(128)}, f32[16]{0:T(128)S(1)}, u32[]{:S(2)}) copy-start(f32[16]{0:T(128)S(1)} %fusion.389) | copy-start | bytes 196
  1197.1 66.6 %copy-start.365 = (f32[16]{0:T(128)}, f32[16]{0:T(128)S(1)}, u32[]{:S(2)}) copy-start(f32[16]{0:T(128)S(1)} %get-tuple-element.293) | copy-start | bytes 196
  1197.1 66.6 %copy-start.367 = (f32[16]{0:T(128)}, f32[16]{0:T(128)S(1)}, u32[]{:S(2)}) copy-start(f32[16]{0:T(128)S(1)} %get-tuple-element.294) | copy-start | bytes 196
  1204.5 234.9 %reduce-scatter.17.cloned.1.call-start = ((), (), s32[]{:S(2)}) async-start(), calls=%async_computation.23 | async-start | bytes 2621440 | tf_op jit(solution)/shard_map/reduce_scatter | solution.py:339
  1316.1 11.6 collective-permute-start.12
  1344.4 293.0 %all-reduce.71.cloned.1.call-start = ((), (), s32[]{:S(2)}) async-start(), calls=%async_computation.25 | async-start | bytes 25296896 | tf_op jit(solution)/shard_map/psum | solution.py:368
  1388.9 381.1 %all-reduce.69.cloned.1.call-start = ((), (), s32[]{:S(2)}) async-start(), calls=%async_computation.24 | async-start | bytes 4194304 | tf_op jit(solution)/shard_map/psum | solution.py:370
  1416.7 97.8 %copy-start.51 = (bf16[2,128,2048]{2,1,0:T(8,128)(2,1)S(1)}, bf16[2,128,2048]{2,1,0:T(8,128)(2,1)}, u32[]{:S(2)}) copy-start(bf16[2,128,2048]{2,1,0:T(8,128)(2,1)} %param.20) | copy-start | bytes 3145732
  1416.7 97.8 %copy-start.424 = (f32[128]{0:T(128)S(1)}, f32[128]{0:T(128)}, u32[]{:S(2)}) copy-start(f32[128]{0:T(128)} %get-tuple-element.332) | copy-start | bytes 1540
  (410 other events, 4039.5 us)
Sparse Core Ops, SparseCore 0:
  11.4 48.4 all-gather.18
  101.5 32.7 all-gather.20
  171.8 73.9 reduce-scatter.6
  253.5 46.5 all-gather.22
  349.2 33.1 all-gather.24
  420.1 73.9 reduce-scatter.8
  503.1 46.4 all-gather.26
  602.8 33.1 all-gather.28
  637.5 46.1 all-gather.30
  721.7 25.1 all-gather.32
  824.3 45.9 reduce-scatter.12
  878.8 45.2 all-gather.34
  959.4 25.0 all-gather.36
  1056.0 45.9 reduce-scatter.14
  1112.9 45.2 all-gather.38
  1189.3 25.0 all-gather.40
  1216.5 76.7 reduce-scatter.10
  1344.5 43.2 reduce-scatter.16
  1392.9 244.4 all-reduce.70
  1643.3 126.6 all-reduce.68

commit v2 on v1

--- a/solution.py
+++ b/solution.py
@@ -233,11 +233,11 @@
     scale_out = lax.rsqrt(square_total / DI + norm_eps)
     normed_out = (gated_mix * scale_out[:, None] * gate_gain).astype(jnp.bfloat16)
     branch = lax.psum_scatter(
-        jnp.dot(normed_out, w_out, preferred_element_type=jnp.float32),
+        jnp.dot(normed_out, w_out, preferred_element_type=jnp.float32).astype(jnp.bfloat16),
         "head",
         scatter_dimension=0,
         tiled=True,
-    )
+    ).astype(jnp.float32)
     saved = (
         stream,
         gathered,
@@ -255,7 +255,7 @@
     return stream + branch, saved
 
 
-def mixer_backward(grad_next, layer_weights, saved):
+def mixer_backward(grad_next, layer_weights, saved, mask_value):
     (
         norm_gain,
         w_main,
@@ -288,7 +288,7 @@
     shard_rows = lax.all_gather(grad_branch, "head", axis=0, tiled=True)
     g_w_out = lax.dot_general(
         normed_out, shard_rows, (((0,), (0,)), ((), ())), preferred_element_type=jnp.float32
-    )
+    ) * mask_value
     grad_normed = lax.dot_general(
         shard_rows, w_out, (((1,), (1,)), ((), ())), preferred_element_type=jnp.float32
     )
@@ -351,7 +351,6 @@
         g_low[:, :inner_width],
         g_low[:, inner_width : 2 * inner_width],
         g_low[:, 2 * inner_width :],
-        g_w_out,
         g_conv_w[:, :inner_width],
         g_conv_b[:inner_width],
         g_dt_bias,
@@ -360,7 +359,7 @@
         g_gate_gain,
     )
     shared_part = (g_norm_gain, g_w_bc, g_conv_w[:, inner_width:], g_conv_b[inner_width:])
-    return (grad_stream, head_part, shared_part)
+    return (grad_stream, head_part, shared_part, g_w_out)
 
 
 def reduce_grads(head_part, shared_part):
@@ -444,8 +443,16 @@
         clipped, is_valid, saved = ticks[tick_count - 1 - tick_index]
         outer_grad = lax.dynamic_index_in_dim(cotangent, clipped, 0, False).astype(jnp.float32)
         grad_next = jnp.where(section_index == section_count - 1, outer_grad, back_arrived)
-        grad_stream, head_part, shared_part = mixer_backward(grad_next, layer_weights, saved)
         mask_value = is_valid.astype(jnp.float32)
+        grad_stream, head_part, shared_part, out_part = mixer_backward(
+            grad_next, layer_weights, saved, mask_value
+        )
+        if tick_index == 0:
+            out_total = out_part
+        else:
+            out_total = out_total + out_part
+        if tick_index + 1 == tick_count:
+            out_total = lax.psum(out_total.astype(jnp.bfloat16), "seq")
         head_part = tuple((member * mask_value for member in head_part))
         shared_part = tuple((member * mask_value for member in shared_part))
         if tick_index == 0:
@@ -461,7 +468,10 @@
             back_arrived = shifted(grad_stream.astype(jnp.bfloat16), "section", -1).astype(
                 grad_stream.dtype
             )
+    anchor = out_total[0, 0].astype(jnp.float32) * 0.0
+    head_total = (head_total[0] + anchor,) + head_total[1:]
     head_total, shared_total = reduce_grads(head_total, shared_total)
+    head_total = head_total[:3] + (out_total.astype(jnp.float32),) + head_total[3:]
     return (
         outputs_all[None],
         input_grads[None],

time: 1790 us -> 1670 us (0.933)
  waiting for transfers between devices: 739 us -> 646 us
    reduce_scatter x3, waiting for transfers between devices: 146 us -> 79.9 us  [mixer_forward(): lax.psum_scatter(jnp.dot(normed_out, w_out, preferred_element_type=jnp.fl...]
    psum x1, waiting for transfers between devices: 120 us -> 91.5 us  [reduce_grads(): lax.psum(member.astype(jnp.bfloat16), 'seq').astype(jnp.float32)]
    unnamed x899 -> x869, local copies, waits for them, and re-layouts: 63.2 us -> 58.3 us
  transfers between devices with their start and end apart: 33 -> 34, of which waited for: 22 -> 22; matrix products, arithmetic and copies ran while one was open for 21% -> 21% of each run, Pallas kernels for 0% -> 0%
where the time goes in v2:
time: 1670 us; the launch traced here: 1660 us
  waiting for transfers between devices  646 us (39%)
  matrix products  343 us (21%)
  other arithmetic  252 us (15%)
  blocking collectives  204 us (12%)
  local copies, waits for them, and re-layouts  159 us (10%)
  starting transfers between devices  34.3 us (2%)
  between operations  20.8 us (1%)
    psum x1, waiting for transfers between devices, reduce_grads(): shared_sum = lax.psum(tuple(shared_part), ('seq', 'head'))  118 us
    all_gather x3, waiting for transfers between devices, mixer_forward(): gathered = lax.all_gather(normed, 'head', axis=0, tiled=True)  116 us
    dot_general x9, matrix products, block_output(): jnp.einsum('cijh,cjhp->cihp', weights, x_blocks, precision=highest)  97.1 us
    reduce_scatter x3, waiting for transfers between devices, mixer_backward(): lax.psum_scatter((main_term + side_term).astype(jnp.bfloat16), 'head', sc...  92.1 us
    psum x1, waiting for transfers between devices, reduce_grads(): lax.psum(member.astype(jnp.bfloat16), 'seq').astype(jnp.float32)  91.5 us
    all_gather x3, waiting for transfers between devices, mixer_backward(): shard_rows = lax.all_gather(grad_branch, 'head', axis=0, tiled=True)  89.9 us
    reduce_scatter x3, waiting for transfers between devices, mixer_forward(): lax.psum_scatter(jnp.dot(normed_out, w_out, preferred_element_type=jnp.fl...  79.9 us
    psum x1, blocking collectives, reduce_grads(): shared_sum = lax.psum(tuple(shared_part), ('seq', 'head'))  75.5 us
  transfers between devices with their start and end apart: 34, of which 22 were waited for; matrix products, arithmetic and copies ran while one was open for 21% of the time, Pallas kernels for 0%

profile of v2, /device:TPU:0, one launch (start us, length us, event | category | flops | bytes accessed | tf_op | source)
XLA Modules:
  0.0 1658.4 jit_solution(10944287971725481408)
XLA Ops:
  28.1 32.1 %all-gather.19.cloned.1.call-done = bf16[512,2048]{1,0:T(8,128)(2,1)} async-done(((bf16[128,2048]{1,0:T(8,128)(2,1)}), bf16[512,2048]{1,0:T(8,128)(2,1)}) %all-gather.19.cloned.1.call-update) | async-done | bytes 2097168 | tf_op jit(solution)/shard_map/all_gather | solution.py:212
  60.2 12.5 fusion.447
  103.3 8.1 all-gather
  119.8 14.3 all-gather.21.cloned.1.call-done
  138.7 9.4 fusion.143
  148.1 12.0 copy.498
  163.3 11.7 psum.140
  175.0 6.0 fusion.84
  181.2 41.2 %reduce-scatter.7.cloned.1.call-done = bf16[128,2048]{1,0:T(8,128)(2,1)} async-done(((bf16[512,2048]{1,0:T(8,128)(2,1)}), bf16[128,2048]{1,0:T(8,128)(2,1)}) %reduce-scatter.7.cloned.1.call-update) | async-done | bytes 524304 | tf_op jit(solution)/shard_map/reduce_scatter | solution.py:235
  231.4 44.0 %all-gather.23.cloned.1.call-done = bf16[512,2048]{1,0:T(8,128)(2,1)} async-done(((bf16[128,2048]{1,0:T(8,128)(2,1)}), bf16[512,2048]{1,0:T(8,128)(2,1)}) %all-gather.23.cloned.1.call-update) | async-done | bytes 2097168 | tf_op jit(solution)/shard_map/all_gather | solution.py:212
  275.4 12.8 fusion.446
  303.9 9.2 fusion.121
  324.2 8.3 all-gather.1
  341.2 16.3 all-gather.25.cloned.1.call-done
  362.2 9.4 fusion.142
  376.6 11.7 psum.141
  388.3 6.0 fusion.87
  397.0 38.6 %reduce-scatter.9.cloned.1.call-done = bf16[128,2048]{1,0:T(8,128)(2,1)} async-done(((bf16[512,2048]{1,0:T(8,128)(2,1)}), bf16[128,2048]{1,0:T(8,128)(2,1)}) %reduce-scatter.9.cloned.1.call-update) | async-done | bytes 524304 | tf_op jit(solution)/shard_map/reduce_scatter | solution.py:235
  449.3 40.2 %all-gather.27.cloned.1.call-done = bf16[512,2048]{1,0:T(8,128)(2,1)} async-done(((bf16[128,2048]{1,0:T(8,128)(2,1)}), bf16[512,2048]{1,0:T(8,128)(2,1)}) %all-gather.27.cloned.1.call-update) | async-done | bytes 2097168 | tf_op jit(solution)/shard_map/all_gather | solution.py:212
  489.6 12.5 fusion.445
  532.5 8.0 all-gather.3
  540.5 7.4 all-gather.2
  558.1 6.7 all-gather.29.cloned.1.call-done
  569.4 9.4 fusion.141
  585.1 12.1 psum.142
  597.2 16.0 all-gather.31.cloned.1.call-done
  613.2 7.9 multiply_reduce_fusion.20
  621.0 9.4 psum.143
  630.5 6.7 multiply_reduce_fusion.23
  649.6 15.6 fusion.29
  680.8 7.4 fusion.137
  698.8 8.0 multiply_reduce_fusion.13
  746.9 46.0 %reduce-scatter.13.cloned.1.call-done = bf16[128,2048]{1,0:T(8,128)(2,1)} async-done(((bf16[512,2048]{1,0:T(8,128)(2,1)}), bf16[128,2048]{1,0:T(8,128)(2,1)}) %reduce-scatter.13.cloned.1.call-update) | async-done | bytes 524304 | tf_op jit(solution)/shard_map/reduce_scatter | solution.py:339
  802.0 8.1 all-gather.4
  811.1 36.2 %all-gather.35.cloned.1.call-done = bf16[512,2048]{1,0:T(8,128)(2,1)} async-done(((bf16[128,2048]{1,0:T(8,128)(2,1)}), bf16[512,2048]{1,0:T(8,128)(2,1)}) %all-gather.35.cloned.1.call-update) | async-done | bytes 2097168 | tf_op jit(solution)/shard_map/all_gather | solution.py:288
  847.3 7.9 multiply_reduce_fusion.19
  855.2 9.5 psum.144
  864.7 6.1 multiply_reduce_fusion.22
  883.3 15.5 fusion.31
  914.3 7.3 fusion.133
  932.2 8.3 multiply_reduce_fusion.9
  980.5 46.0 %reduce-scatter.15.cloned.1.call-done = bf16[128,2048]{1,0:T(8,128)(2,1)} async-done(((bf16[512,2048]{1,0:T(8,128)(2,1)}), bf16[128,2048]{1,0:T(8,128)(2,1)}) %reduce-scatter.15.cloned.1.call-update) | async-done | bytes 524304 | tf_op jit(solution)/shard_map/reduce_scatter | solution.py:339
  1038.3 7.4 fusion.443
  1045.7 37.7 %all-gather.39.cloned.1.call-done = bf16[512,2048]{1,0:T(8,128)(2,1)} async-done(((bf16[128,2048]{1,0:T(8,128)(2,1)}), bf16[512,2048]{1,0:T(8,128)(2,1)}) %all-gather.39.cloned.1.call-update) | async-done | bytes 2097168 | tf_op jit(solution)/shard_map/all_gather | solution.py:288
  1083.4 7.9 multiply_reduce_fusion.18
  1091.3 9.5 psum.145
  1116.7 6.9 add_convert_fusion
  1124.3 7.8 all-gather.5
  1133.2 6.0 fusion.90
  1139.4 12.8 fusion.280
  1152.2 14.3 fusion.33
  1181.0 8.7 fusion.129
  1207.7 6.2 multiply_reduce_fusion.5
  1247.7 6.8 fusion.278
  1254.6 11.0 fusion.276
  1269.0 21.7 %fusion.34 = (bf16[1,2048,1024]{1,2,0:T(8,128)(2,1)}, bf16[1,2048,1024]{1,2,0:T(8,128)(2,1)}) fusion(f32[2048,2064]{0,1:T(8,128)} %fusion.276, f32[2048,2064]{0,1:T(8,128)} %copy-done.53, f32[2048,2064]{0,1:T(8,128)} %fusion.280, f32[]{:T(128)S(6)} %convert_element_type.642, f32[]{:T(128)S(6)} %convert_element_type.641, f32[]{:T(128)S(6)} %convert_element_type.640, ...), kind=kLoop, calls=%fused_computation.58 | loop fusion | flops 27262976 | bytes 58720272 | tf_op jit(solution)/shard_map/broadcast_in_dim | solution.py:480
  1303.1 6.2 fusion.95
  1311.4 17.4 %all-reduce.64 = (bf16[1,4,1024]{2,1,0:T(4,128)(2,1)S(1)}, bf16[1,1024]{1,0:T(2,128)(2,1)S(1)}, bf16[1,16]{1,0:T(2,128)(2,1)S(1)}, bf16[1,16]{1,0:T(2,128)(2,1)S...) all-reduce(bf16[1,4,1024]{2,1,0:T(4,128)(2,1)S(1)} %fusion.364, ...), channel_id=1, replica_groups=mesh['section'=2,'seq'=4,'head'=4] {'seq'}, use_global_device_ids=true, to_apply=%region_99.101 | all-reduce | flops 6192 | bytes 24768 | tf_op jit(solution)/shard_map/psum | solution.py:367
  1338.2 6.7 bitcast_convert_fusion
  1346.4 75.5 %all-reduce.63 = (f32[1,2048]{1,0:T(1,128)}, f32[1,4,256]{2,1,0:T(4,128)}, f32[1,256]{1,0:T(1,128)}) all-reduce(f32[1,2048]{1,0:T(1,128)S(1)} %bitcast.1045, f32[1,4,256]{2,1,0:T(4,128)S(1)} %fusion.366, f32[1,256]{1,0:T(1,128)S(1)} %bitcast.1063), channel_id=1, replica_groups=mesh['section'=2,'seq'=4,'head'=4] {'seq','head'}, use_global_device_ids=true, to_apply=%region_81.83 | all-reduce | flops 3328 | bytes 26624 | tf_op jit(solution)/shard_map/psum | solution.py:369
  1424.7 91.5 %all-reduce.74.cloned.1.call-done = (bf16[1,2048,1024]{1,2,0:T(8,128)(2,1)}, bf16[1,2048,1024]{1,2,0:T(8,128)(2,1)}, bf16[1,2048,16]{1,2,0:T(8,128)(2,1)}) async-done(((bf16[1,2048,1024]{1,2,0:T(8,128)(2,1)}, bf16[1,2048,1024]{1,2,0:T(8,128)(2,1)}, bf16[1,2048,16]{1,2,0:T(8,128)(2,1)}), (bf16[1,2048,1024]{1,2,0:T(8,128)(2,1)}, bf16[1,2048,1024]{1,2,0:T(8,128)(2,1)}, ...) | async-done | bytes 8454160 | tf_op jit(solution)/shard_map/psum | solution.py:367
  1516.2 6.9 copy.601
  1523.1 6.9 copy.602
  1530.6 117.7 %all-reduce.72.cloned.1.call-done = f32[1,2048,256]{2,1,0:T(8,128)} async-done(((f32[1,2048,256]{2,1,0:T(8,128)}), f32[1,2048,256]{2,1,0:T(8,128)}) %all-reduce.72.cloned.1.call-update) | async-done | bytes 2097168 | tf_op jit(solution)/shard_map/psum | solution.py:369
  (1319 shorter events, 482.4 us)
Async XLA Ops:
  7.3 52.9 %all-gather.19.cloned.1.call-start = ((), (), s32[]{:S(2)}) async-start(), calls=%async_computation.6 | async-start | bytes 2621440 | tf_op jit(solution)/shard_map/all_gather | solution.py:212
  11.3 122.9 %all-gather.21.cloned.1.call-start = ((), (), s32[]{:S(2)}) async-start(), calls=%async_computation.7 | async-start | bytes 2621440 | tf_op jit(solution)/shard_map/all_gather | solution.py:28
  12.8 13.9 collective-permute-start
  17.7 9.0 collective-permute-start.3
  25.4 66.0 %copy-start.208 = (f32[1,512]{1,0:T(1,128)}, f32[1,512]{1,0:T(1,128)S(1)}, u32[]{:S(2)}) copy-start(f32[1,512]{1,0:T(1,128)S(1)} %get-tuple-element.278) | copy-start | bytes 6148
  26.1 488.0 %copy-start.176 = (f32[1280]{0:T(1024)}, f32[1280]{0:T(1024)S(1)}, u32[]{:S(2)}) copy-start(f32[1280]{0:T(1024)S(1)} %get-tuple-element.159) | copy-start | bytes 15364
  26.1 488.1 %copy-start.180 = (f32[1280]{0:T(1024)}, f32[1280]{0:T(1024)S(1)}, u32[]{:S(2)}) copy-start(f32[1280]{0:T(1024)S(1)} %get-tuple-element.160) | copy-start | bytes 15364
  26.7 55.3 %copy-start.257 = (f32[2,256]{1,0:T(2,128)}, f32[2,256]{1,0:T(2,128)S(1)}, u32[]{:S(2)}) copy-start(f32[2,256]{1,0:T(2,128)S(1)} %get-tuple-element.309) | copy-start | bytes 6148
  26.7 55.3 %copy-start.300 = (f32[2,256]{1,0:T(2,128)}, f32[2,256]{1,0:T(2,128)S(1)}, u32[]{:S(2)}) copy-start(f32[2,256]{1,0:T(2,128)S(1)} %get-tuple-element.308) | copy-start | bytes 6148
  28.1 56.8 %copy-start.234 = (f32[512]{0:T(512)}, f32[512]{0:T(512)S(1)}, u32[]{:S(2)}) copy-start(f32[512]{0:T(512)S(1)} %get-tuple-element.289) | copy-start | bytes 6148
  28.1 56.9 %copy-start.236 = (f32[512]{0:T(512)}, f32[512]{0:T(512)S(1)}, u32[]{:S(2)}) copy-start(f32[512]{0:T(512)S(1)} %get-tuple-element.290) | copy-start | bytes 6148
  28.1 56.9 %copy-start.238 = (f32[512]{0:T(512)}, f32[512]{0:T(512)S(1)}, u32[]{:S(2)}) copy-start(f32[512]{0:T(512)S(1)} %get-tuple-element.291) | copy-start | bytes 6148
  75.4 9.3 collective-permute-start.1
  82.2 56.5 %copy-start.186 = (f32[2,256,16]{1,2,0:T(8,128)}, f32[2,256,16]{1,2,0:T(8,128)S(1)}, u32[]{:S(2)}) copy-start(f32[2,256,16]{1,2,0:T(8,128)S(1)} %get-tuple-element.275) | copy-start | bytes 98308
  101.0 121.3 %reduce-scatter.7.cloned.1.call-start = ((), (), s32[]{:S(2)}) async-start(), calls=%async_computation.8 | async-start | bytes 2621440 | tf_op jit(solution)/shard_map/reduce_scatter | solution.py:235
  181.1 94.3 %all-gather.23.cloned.1.call-start = ((), (), s32[]{:S(2)}) async-start(), calls=%async_computation.9 | async-start | bytes 2621440 | tf_op jit(solution)/shard_map/all_gather | solution.py:212
  224.0 4.0 collective-permute-start.2
  228.2 207.5 %copy-start.23 = (f32[128,2048]{1,0:T(8,128)}, f32[128,2048]{1,0:T(8,128)S(1)}, u32[]{:S(2)}) copy-start(f32[128,2048]{1,0:T(8,128)S(1)} %get-tuple-element.219) | copy-start | bytes 3145732
  229.7 127.8 %all-gather.25.cloned.1.call-start = ((), (), s32[]{:S(2)}) async-start(), calls=%async_computation.10 | async-start | bytes 2621440 | tf_op jit(solution)/shard_map/all_gather | solution.py:28
  230.6 68.7 %copy-start.267 = (f32[2,256]{1,0:T(2,128)}, f32[2,256]{1,0:T(2,128)S(1)}, u32[]{:S(2)}) copy-start(f32[2,256]{1,0:T(2,128)S(1)} %get-tuple-element.342) | copy-start | bytes 6148
  230.6 68.7 %copy-start.304 = (f32[2,256]{1,0:T(2,128)}, f32[2,256]{1,0:T(2,128)S(1)}, u32[]{:S(2)}) copy-start(f32[2,256]{1,0:T(2,128)S(1)} %get-tuple-element.343) | copy-start | bytes 6148
  231.3 72.5 %copy-start.240 = (f32[512]{0:T(512)}, f32[512]{0:T(512)S(1)}, u32[]{:S(2)}) copy-start(f32[512]{0:T(512)S(1)} %get-tuple-element.286) | copy-start | bytes 6148
  231.3 72.5 %copy-start.242 = (f32[512]{0:T(512)}, f32[512]{0:T(512)S(1)}, u32[]{:S(2)}) copy-start(f32[512]{0:T(512)S(1)} %get-tuple-element.287) | copy-start | bytes 6148
  231.3 72.5 %copy-start.244 = (f32[512]{0:T(512)}, f32[512]{0:T(512)S(1)}, u32[]{:S(2)}) copy-start(f32[512]{0:T(512)S(1)} %get-tuple-element.288) | copy-start | bytes 6148
  231.4 64.8 %copy-start.291 = (f32[1,16]{1,0:T(1,128)S(1)}, f32[1,16]{1,0:T(1,128)}, u32[]{:S(2)}) copy-start(f32[1,16]{1,0:T(1,128)} %param.32) | copy-start | bytes 196
  231.4 64.8 %copy-start.297 = (f32[16]{0:T(128)S(1)}, f32[16]{0:T(128)}, u32[]{:S(2)}) copy-start(f32[16]{0:T(128)} %copy-done.296) | copy-start | bytes 196
  231.4 67.3 %copy-start.355 = (f32[2]{0:T(128)S(1)}, f32[2]{0:T(128)}, u32[]{:S(2)}) copy-start(f32[2]{0:T(128)} %get-tuple-element.345) | copy-start | bytes 28
  292.8 10.8 collective-permute-start.4
  299.4 62.7 %copy-start.190 = (f32[2,256,16]{1,2,0:T(8,128)}, f32[2,256,16]{1,2,0:T(8,128)S(1)}, u32[]{:S(2)}) copy-start(f32[2,256,16]{1,2,0:T(8,128)S(1)} %get-tuple-element.273) | copy-start | bytes 98308
  324.2 111.5 %reduce-scatter.9.cloned.1.call-start = ((), (), s32[]{:S(2)}) async-start(), calls=%async_computation.11 | async-start | bytes 2621440 | tf_op jit(solution)/shard_map/reduce_scatter | solution.py:235
  394.4 95.2 %all-gather.27.cloned.1.call-start = ((), (), s32[]{:S(2)}) async-start(), calls=%async_computation.12 | async-start | bytes 2621440 | tf_op jit(solution)/shard_map/all_gather | solution.py:212
  437.4 4.1 collective-permute-start.5
  443.7 121.2 %all-gather.29.cloned.1.call-start = ((), (), s32[]{:S(2)}) async-start(), calls=%async_computation.13 | async-start | bytes 2621440 | tf_op jit(solution)/shard_map/all_gather | solution.py:28
  443.8 4.7 collective-permute-start.6
  447.2 63.3 %copy-start.400 = (f32[2]{0:T(128)}, f32[2]{0:T(128)S(1)}, u32[]{:S(2)}) copy-start(f32[2]{0:T(128)S(1)} %fusion.396) | copy-start | bytes 28
  449.3 64.9 %copy-start.246 = (f32[512]{0:T(512)}, f32[512]{0:T(512)S(1)}, u32[]{:S(2)}) copy-start(f32[512]{0:T(512)S(1)} %get-tuple-element.280) | copy-start | bytes 6148
  449.3 64.9 %copy-start.248 = (f32[512]{0:T(512)}, f32[512]{0:T(512)S(1)}, u32[]{:S(2)}) copy-start(f32[512]{0:T(512)S(1)} %get-tuple-element.281) | copy-start | bytes 6148
  449.3 64.9 %copy-start.250 = (f32[512]{0:T(512)}, f32[512]{0:T(512)S(1)}, u32[]{:S(2)}) copy-start(f32[512]{0:T(512)S(1)} %get-tuple-element.282) | copy-start | bytes 6148
  449.3 58.6 %copy-start.292 = (f32[1,16]{1,0:T(1,128)S(1)}, f32[1,16]{1,0:T(1,128)}, u32[]{:S(2)}) copy-start(f32[1,16]{1,0:T(1,128)} %param.32) | copy-start | bytes 196
  449.3 58.6 %copy-start.298 = (f32[16]{0:T(128)S(1)}, f32[16]{0:T(128)}, u32[]{:S(2)}) copy-start(f32[16]{0:T(128)} %copy-done.296) | copy-start | bytes 196
  449.3 61.8 %copy-start.269 = (f32[2,256]{1,0:T(2,128)S(1)}, f32[2,256]{1,0:T(2,128)}, u32[]{:S(2)}) copy-start(f32[2,256]{1,0:T(2,128)} %get-tuple-element.299) | copy-start | bytes 6148
  449.3 61.8 %copy-start.305 = (f32[2,256]{1,0:T(2,128)S(1)}, f32[2,256]{1,0:T(2,128)}, u32[]{:S(2)}) copy-start(f32[2,256]{1,0:T(2,128)} %get-tuple-element.298) | copy-start | bytes 6148
  504.8 9.1 collective-permute-start.7
  531.5 81.7 %all-gather.31.cloned.1.call-start = ((), (), s32[]{:S(2)}) async-start(), calls=%async_computation.15 | async-start | bytes 2621440 | tf_op jit(solution)/shard_map/all_gather | solution.py:288
  532.5 142.4 %all-gather.33.cloned.1.call-start = ((), (), s32[]{:S(2)}) async-start(), calls=%async_computation.16 | async-start | bytes 1310720 | tf_op jit(solution)/shard_map/all_gather | solution.py:46
  649.6 143.4 %reduce-scatter.13.cloned.1.call-start = ((), (), s32[]{:S(2)}) async-start(), calls=%async_computation.17 | async-start | bytes 2621440 | tf_op jit(solution)/shard_map/reduce_scatter | solution.py:339
  723.2 7.5 collective-permute-start.8
  746.9 100.5 %all-gather.35.cloned.1.call-start = ((), (), s32[]{:S(2)}) async-start(), calls=%async_computation.18 | async-start | bytes 2621440 | tf_op jit(solution)/shard_map/all_gather | solution.py:288
  794.9 60.3 %copy-start.387 = (f32[128]{0:T(128)}, f32[128]{0:T(128)S(1)}, u32[]{:S(2)}) copy-start(f32[128]{0:T(128)S(1)} %broadcast_multiply_fusion.14) | copy-start | bytes 1540
  796.3 3.8 collective-permute-start.9
  801.9 106.5 %all-gather.37.cloned.1.call-start = ((), (), s32[]{:S(2)}) async-start(), calls=%async_computation.19 | async-start | bytes 1310720 | tf_op jit(solution)/shard_map/all_gather | solution.py:46
  883.2 143.4 %reduce-scatter.15.cloned.1.call-start = ((), (), s32[]{:S(2)}) async-start(), calls=%async_computation.20 | async-start | bytes 2621440 | tf_op jit(solution)/shard_map/reduce_scatter | solution.py:339
  956.9 7.4 collective-permute-start.10
  980.5 102.9 %all-gather.39.cloned.1.call-start = ((), (), s32[]{:S(2)}) async-start(), calls=%async_computation.21 | async-start | bytes 2621440 | tf_op jit(solution)/shard_map/all_gather | solution.py:288
  1031.4 3.8 collective-permute-start.11
  1038.0 136.6 %all-gather.41.cloned.1.call-start = ((), (), s32[]{:S(2)}) async-start(), calls=%async_computation.22 | async-start | bytes 1310720 | tf_op jit(solution)/shard_map/all_gather | solution.py:46
  1045.7 55.1 %copy-start.209 = (f32[1,512]{1,0:T(1,128)S(1)}, f32[1,512]{1,0:T(1,128)}, u32[]{:S(2)}) copy-start(f32[1,512]{1,0:T(1,128)} %copy-done.208) | copy-start | bytes 6148
  1111.9 155.4 %all-reduce.70.cloned.1.call-start = ((), (), s32[]{:S(2)}) async-start(), calls=%async_computation.24 | async-start | bytes 8388608 | tf_op jit(solution)/shard_map/psum | solution.py:455
  1123.7 175.8 %reduce-scatter.11.cloned.1.call-start = ((), (), s32[]{:S(2)}) async-start(), calls=%async_computation.14 | async-start | bytes 2621440 | tf_op jit(solution)/shard_map/reduce_scatter | solution.py:235
  1139.3 205.7 %reduce-scatter.17.cloned.1.call-start = ((), (), s32[]{:S(2)}) async-start(), calls=%async_computation.23 | async-start | bytes 2621440 | tf_op jit(solution)/shard_map/reduce_scatter | solution.py:339
  1220.0 11.1 collective-permute-start.12
  1247.6 268.6 %all-reduce.74.cloned.1.call-start = ((), (), s32[]{:S(2)}) async-start(), calls=%async_computation.26 | async-start | bytes 16908288 | tf_op jit(solution)/shard_map/psum | solution.py:367
  1290.9 357.4 %all-reduce.72.cloned.1.call-start = ((), (), s32[]{:S(2)}) async-start(), calls=%async_computation.25 | async-start | bytes 4194304 | tf_op jit(solution)/shard_map/psum | solution.py:369
  1338.2 83.7 %copy-start.409 = (f32[128]{0:T(128)S(1)}, f32[128]{0:T(128)}, u32[]{:S(2)}) copy-start(f32[128]{0:T(128)} %get-tuple-element.331) | copy-start | bytes 1540
  (396 other events, 3516.7 us)
Sparse Core Ops, SparseCore 0:
  11.4 48.7 all-gather.18
  101.2 32.9 all-gather.20
  181.2 41.0 reduce-scatter.6
  229.8 45.4 all-gather.22
  324.3 33.1 all-gather.24
  394.5 41.0 reduce-scatter.8
  443.8 45.7 all-gather.26
  531.6 33.1 all-gather.28
  567.0 46.1 all-gather.30
  649.7 25.1 all-gather.32
  747.0 45.9 reduce-scatter.12
  802.0 45.2 all-gather.34
  883.3 25.0 all-gather.36
  980.6 45.9 reduce-scatter.14
  1038.1 45.2 all-gather.38
  1112.0 25.0 all-gather.40
  1140.8 103.9 all-reduce.69
  1247.6 43.9 reduce-scatter.10
  1293.9 43.0 reduce-scatter.16
  1341.9 174.2 all-reduce.73
  1522.3 125.9 all-reduce.71

commit v3 on v2

--- a/solution.py
+++ b/solution.py
@@ -1,8 +1,12 @@
 from functools import partial
+
+import functools
 
 import jax
 import jax.numpy as jnp
 from jax import lax
+from jax.experimental import pallas as pl
+from jax.experimental.pallas import tpu as pltpu
 from jax.sharding import PartitionSpec as P
 
 DI = 4096
@@ -10,6 +14,214 @@
 N = 128
 KW = 4
 SCAN_BLOCK = 256
+
+
+MESH = pl.DeviceIdType.MESH
+
+
+def _tick_valid(offset, sign, count):
+    slot = offset + sign * lax.axis_index("section")
+    return jnp.logical_and(slot >= 0, slot < count)
+
+
+def _enter(barrier, h, n):
+    @pl.when(h > 0)
+    def _():
+        pl.semaphore_signal(barrier, 1, device_id={"head": h - 1}, device_id_type=MESH)
+
+    @pl.when(h < n - 1)
+    def _():
+        pl.semaphore_signal(barrier, 1, device_id={"head": h + 1}, device_id_type=MESH)
+
+    @pl.when(jnp.logical_and(h > 0, h < n - 1))
+    def _():
+        pl.semaphore_wait(barrier, 2)
+
+    @pl.when(jnp.logical_or(h == 0, h == n - 1))
+    def _():
+        pl.semaphore_wait(barrier, 1)
+
+
+def gather_body(n, tick, x_ref, o_ref, land, send_r, send_l, recv):
+    h = lax.axis_index("head")
+    valid = _tick_valid(*tick)
+
+    @pl.when(valid)
+    def _():
+        _enter(pltpu.get_barrier_semaphore(), h, n)
+
+        def copy_right(s, k):
+            src = x_ref if s == 0 else land.at[k]
+            return pltpu.make_async_remote_copy(
+                src_ref=src, dst_ref=land.at[k], send_sem=send_r.at[s], recv_sem=recv.at[k],
+                device_id={"head": h + 1}, device_id_type=MESH)
+
+        def copy_left(s, k):
+            src = x_ref if s == 0 else land.at[k]
+            return pltpu.make_async_remote_copy(
+                src_ref=src, dst_ref=land.at[k], send_sem=send_l.at[s], recv_sem=recv.at[k],
+                device_id={"head": h - 1}, device_id_type=MESH)
+
+        for s in range(n):
+            k_r = h - s
+            k_l = h + s
+            if s >= 1:
+                @pl.when(k_r >= 0)
+                def _():
+                    pltpu.make_async_remote_copy(
+                        src_ref=land.at[k_r], dst_ref=land.at[k_r], send_sem=send_r.at[0],
+                        recv_sem=recv.at[k_r], device_id={"head": h}, device_id_type=MESH
+                    ).wait_recv()
+
+                @pl.when(k_l <= n - 1)
+                def _():
+                    pltpu.make_async_remote_copy(
+                        src_ref=land.at[k_l], dst_ref=land.at[k_l], send_sem=send_l.at[0],
+                        recv_sem=recv.at[k_l], device_id={"head": h}, device_id_type=MESH
+                    ).wait_recv()
+            if s <= n - 2:
+                @pl.when(jnp.logical_and(k_r >= 0, h < n - 1))
+                def _():
+                    copy_right(s, k_r).start()
+
+                @pl.when(jnp.logical_and(k_l <= n - 1, h > 0))
+                def _():
+                    copy_left(s, k_l).start()
+        land[h] = x_ref[...]
+        for s in range(n - 1):
+            k_r = h - s
+            k_l = h + s
+
+            @pl.when(jnp.logical_and(k_r >= 0, h < n - 1))
+            def _():
+                copy_right(s, k_r).wait_send()
+
+            @pl.when(jnp.logical_and(k_l <= n - 1, h > 0))
+            def _():
+                copy_left(s, k_l).wait_send()
+        o_ref[...] = land[...]
+
+    @pl.when(jnp.logical_not(valid))
+    def _():
+        o_ref[...] = jnp.zeros(o_ref.shape, o_ref.dtype)
+
+
+def head_gather(x, tick, cid):
+    n = lax.axis_size("head")
+    rows, cols = x.shape
+    return pl.pallas_call(
+        functools.partial(gather_body, n, tick),
+        out_shape=jax.ShapeDtypeStruct((n, rows, cols), x.dtype),
+        in_specs=[pl.BlockSpec(memory_space=pltpu.VMEM)],
+        out_specs=pl.BlockSpec(memory_space=pltpu.VMEM),
+        scratch_shapes=[
+            pltpu.VMEM((n, rows, cols), x.dtype),
+            pltpu.SemaphoreType.DMA((n,)),
+            pltpu.SemaphoreType.DMA((n,)),
+            pltpu.SemaphoreType.DMA((n,)),
+        ],
+        compiler_params=pltpu.CompilerParams(collective_id=cid, has_side_effects=True),
+    )(x)
+
+
+def scatter_body(n, tick, p_ref, o_ref, recv_l, recv_r, send_l, send_r, ssem_l, ssem_r, rsem_l, rsem_r):
+    h = lax.axis_index("head")
+    valid = _tick_valid(*tick)
+    link = send_r.dtype
+
+    @pl.when(valid)
+    def _():
+        _enter(pltpu.get_barrier_semaphore(), h, n)
+
+        def to_right(k):
+            return pltpu.make_async_remote_copy(
+                src_ref=send_r.at[k], dst_ref=recv_l.at[k], send_sem=ssem_r.at[k],
+                recv_sem=rsem_l.at[k], device_id={"head": h + 1}, device_id_type=MESH)
+
+        def to_left(k):
+            return pltpu.make_async_remote_copy(
+                src_ref=send_l.at[k], dst_ref=recv_r.at[k], send_sem=ssem_l.at[k],
+                recv_sem=rsem_r.at[k], device_id={"head": h - 1}, device_id_type=MESH)
+
+        for s in range(n - 1):
+            k_r = n - 1 - s
+            k_l = s
+
+            @pl.when(k_r > h)
+            def _():
+                @pl.when(h > 0)
+                def _():
+                    to_right(k_r).wait_recv()
+                    send_r[k_r] = (p_ref[k_r] + recv_l[k_r].astype(jnp.float32)).astype(link)
+
+                @pl.when(h == 0)
+                def _():
+                    send_r[k_r] = p_ref[k_r].astype(link)
+
+                to_right(k_r).start()
+
+            @pl.when(k_l < h)
+            def _():
+                @pl.when(h < n - 1)
+                def _():
+                    to_left(k_l).wait_recv()
+                    send_l[k_l] = (p_ref[k_l] + recv_r[k_l].astype(jnp.float32)).astype(link)
+
+                @pl.when(h == n - 1)
+                def _():
+                    send_l[k_l] = p_ref[k_l].astype(link)
+
+                to_left(k_l).start()
+        total = p_ref[h]
+
+        @pl.when(h > 0)
+        def _():
+            to_right(h).wait_recv()
+
+        @pl.when(h < n - 1)
+        def _():
+            to_left(h).wait_recv()
+
+        left_part = jnp.where(h > 0, recv_l[h].astype(jnp.float32), 0.0)
+        right_part = jnp.where(h < n - 1, recv_r[h].astype(jnp.float32), 0.0)
+        o_ref[...] = (total + left_part + right_part).astype(o_ref.dtype)
+        for s in range(n - 1):
+            k_r = n - 1 - s
+            k_l = s
+
+            @pl.when(k_r > h)
+            def _():
+                to_right(k_r).wait_send()
+
+            @pl.when(k_l < h)
+            def _():
+                to_left(k_l).wait_send()
+
+    @pl.when(jnp.logical_not(valid))
+    def _():
+        o_ref[...] = jnp.zeros(o_ref.shape, o_ref.dtype)
+
+
+def head_scatter(parts, tick, cid, link=jnp.bfloat16):
+    n = lax.axis_size("head")
+    _, rows, cols = parts.shape
+    return pl.pallas_call(
+        functools.partial(scatter_body, n, tick),
+        out_shape=jax.ShapeDtypeStruct((rows, cols), jnp.float32),
+        in_specs=[pl.BlockSpec(memory_space=pltpu.VMEM)],
+        out_specs=pl.BlockSpec(memory_space=pltpu.VMEM),
+        scratch_shapes=[
+            pltpu.VMEM((n, rows, cols), link),
+            pltpu.VMEM((n, rows, cols), link),
+            pltpu.VMEM((n, rows, cols), link),
+            pltpu.VMEM((n, rows, cols), link),
+            pltpu.SemaphoreType.DMA((n,)),
+            pltpu.SemaphoreType.DMA((n,)),
+            pltpu.SemaphoreType.DMA((n,)),
+            pltpu.SemaphoreType.DMA((n,)),
+        ],
+        compiler_params=pltpu.CompilerParams(collective_id=cid, has_side_effects=True),
+    )(parts)
 
 
 norm_eps = 1e-05
@@ -193,7 +405,7 @@
     return (extended, marks_ext)
 
 
-def mixer_forward(stream, start_marks, alive_mask, layer_weights):
+def mixer_forward(stream, start_marks, alive_mask, layer_weights, tick, ids):
     (
         norm_gain,
         w_main,
@@ -209,7 +421,8 @@
     ) = layer_weights
     inner_width = w_out.shape[0]
     normed = (stream * rms_scale(stream) * norm_gain).astype(jnp.bfloat16)
-    gathered = lax.all_gather(normed, "head", axis=0, tiled=True)
+    gathered = head_gather(normed, tick, ids[0])
+    gathered = gathered.reshape(-1, gathered.shape[-1])
     projected = jnp.dot(gathered, w_main, preferred_element_type=jnp.float32)
     gate_pre = projected[:, :inner_width]
     pre_conv = projected[:, inner_width : 2 * inner_width + 2 * N]
@@ -232,12 +445,14 @@
     square_total = lax.psum(jnp.sum(gated_mix * gated_mix, axis=-1), "head")
     scale_out = lax.rsqrt(square_total / DI + norm_eps)
     normed_out = (gated_mix * scale_out[:, None] * gate_gain).astype(jnp.bfloat16)
-    branch = lax.psum_scatter(
-        jnp.dot(normed_out, w_out, preferred_element_type=jnp.float32).astype(jnp.bfloat16),
-        "head",
-        scatter_dimension=0,
-        tiled=True,
-    ).astype(jnp.float32)
+    head_count = lax.axis_size("head")
+    branch = head_scatter(
+        jnp.dot(normed_out, w_out, preferred_element_type=jnp.float32).reshape(
+            head_count, -1, w_out.shape[1]
+        ),
+        tick,
+        ids[1],
+    )
     saved = (
         stream,
         gathered,
@@ -255,7 +470,7 @@
     return stream + branch, saved
 
 
-def mixer_backward(grad_next, layer_weights, saved, mask_value):
+def mixer_backward(grad_next, layer_weights, saved, mask_value, tick, ids):
     (
         norm_gain,
         w_main,
@@ -285,7 +500,8 @@
     ) = saved
     inner_width = w_out.shape[0]
     grad_branch = grad_next.astype(jnp.bfloat16)
-    shard_rows = lax.all_gather(grad_branch, "head", axis=0, tiled=True)
+    shard_rows = head_gather(grad_branch, tick, ids[0])
+    shard_rows = shard_rows.reshape(-1, shard_rows.shape[-1])
     g_w_out = lax.dot_general(
         normed_out, shard_rows, (((0,), (0,)), ((), ())), preferred_element_type=jnp.float32
     ) * mask_value
@@ -336,9 +552,10 @@
         precision=highest,
         preferred_element_type=jnp.float32,
     )
-    grad_normed_in = lax.psum_scatter(
-        (main_term + side_term).astype(jnp.bfloat16), "head", scatter_dimension=0, tiled=True
-    ).astype(jnp.float32)
+    head_count = lax.axis_size("head")
+    grad_normed_in = head_scatter(
+        (main_term + side_term).reshape(head_count, -1, main_term.shape[1]), tick, ids[1]
+    )
     scale_in = rms_scale(stream)
     g_norm_gain = jnp.sum(grad_normed_in * stream * scale_in, axis=0)
     weighted_in = grad_normed_in * norm_gain
@@ -430,7 +647,14 @@
         stream = jnp.where(section_index == 0, fresh_rows, arrived)
         start_marks = lax.dynamic_index_in_dim(starts, clipped, 0, False)
         alive_mask = lax.dynamic_index_in_dim(live, clipped, 0, False).astype(jnp.float32)
-        result, saved = mixer_forward(stream, start_marks, alive_mask, layer_weights)
+        result, saved = mixer_forward(
+            stream,
+            start_marks,
+            alive_mask,
+            layer_weights,
+            (tick_index, -1, micro_count),
+            (tick_index, tick_count + tick_index),
+        )
         outputs_all = store_slot(outputs_all, result, clipped, is_valid)
         ticks.append((clipped, is_valid, saved))
         if tick_index + 1 < tick_count:
@@ -445,7 +669,12 @@
         grad_next = jnp.where(section_index == section_count - 1, outer_grad, back_arrived)
         mask_value = is_valid.astype(jnp.float32)
         grad_stream, head_part, shared_part, out_part = mixer_backward(
-            grad_next, layer_weights, saved, mask_value
+            grad_next,
+            layer_weights,
+            saved,
+            mask_value,
+            (tick_count - 1 - tick_index, -1, micro_count),
+            (2 * tick_count + tick_index, 3 * tick_count + tick_index),
         )
         if tick_index == 0:
             out_total = out_part

time: 1670 us -> 1580 us (0.946)
  waiting for transfers between devices: 646 us -> 222 us
  Pallas kernels: 0 us -> 326 us
    pallas_call x0 -> x12, Pallas kernels: none -> 326 us  [the longest x6 180 us: head_scatter(): pl.pallas_call(functools.partial(scatter_body, n, tick), out_shape=jax.Sh...]
    all_gather x6 -> x0, waiting for transfers between devices: 206 us -> none  [the longest x3 116 us: mixer_forward(): gathered = lax.all_gather(normed, 'head', axis=0, tiled=True)]
    reduce_scatter x6 -> x0, waiting for transfers between devices: 172 us -> none  [the longest x3 92.1 us: mixer_backward(): lax.psum_scatter((main_term + side_term).astype(jnp.bfloat16), 'head', sc...]
    psum x1, waiting for transfers between devices: 91.5 us -> 0.01 us  [reduce_grads(): lax.psum(member.astype(jnp.bfloat16), 'seq').astype(jnp.float32)]
    psum x1, waiting for transfers between devices: 0.01 us -> 37.3 us  [on_device(): out_total = lax.psum(out_total.astype(jnp.bfloat16), 'seq')]
    psum x1, waiting for transfers between devices: 118 us -> 92.8 us  [reduce_grads(): shared_sum = lax.psum(tuple(shared_part), ('seq', 'head'))]
    all_gather x3, waiting for transfers between devices: 10.1 us -> 33 us  [entering_2(): lax.all_gather(a.astype(kind), axis)]
    unnamed x869 -> x833, local copies, waits for them, and re-layouts: 58.3 us -> 75 us
  transfers between devices with their start and end apart: 34 -> 22, of which waited for: 22 -> 10; matrix products, arithmetic and copies ran while one was open for 21% -> 24% of each run, Pallas kernels for 0% -> 8%
where the time goes in v3:
time: 1580 us; the launch traced here: 1570 us
  matrix products  350 us (22%)
  Pallas kernels  326 us (21%)
  other arithmetic  249 us (16%)
  waiting for transfers between devices  222 us (14%)
  blocking collectives  196 us (12%)
  local copies, waits for them, and re-layouts  173 us (11%)
  starting transfers between devices  34.6 us (2%)
  between operations  20.1 us (1%)
    pallas_call x6, Pallas kernels, head_scatter(): pl.pallas_call(functools.partial(scatter_body, n, tick), out_shape=jax.Sh...  180 us
    pallas_call x6, Pallas kernels, head_gather(): pl.pallas_call(functools.partial(gather_body, n, tick), out_shape=jax.Sha...  146 us
    dot_general x9, matrix products, block_output(): jnp.einsum('cijh,cjhp->cihp', weights, x_blocks, precision=highest)  101 us
    psum x1, waiting for transfers between devices, reduce_grads(): shared_sum = lax.psum(tuple(shared_part), ('seq', 'head'))  92.8 us
    unnamed x833, local copies, waits for them, and re-layouts  75 us
    psum x1, blocking collectives, reduce_grads(): shared_sum = lax.psum(tuple(shared_part), ('seq', 'head'))  73.3 us
    dot_general x3, matrix products, mixer_forward(): projected = jnp.dot(gathered, w_main, preferred_element_type=jnp.float32)  38.1 us
    psum x1, waiting for transfers between devices, on_device(): out_total = lax.psum(out_total.astype(jnp.bfloat16), 'seq')  37.3 us
  transfers between devices with their start and end apart: 22, of which 10 were waited for; matrix products, arithmetic and copies ran while one was open for 24% of the time, Pallas kernels for 8%

profile of v3, /device:TPU:0, one launch (start us, length us, event | category | flops | bytes accessed | tf_op | source)
XLA Modules:
  0.0 1570.8 jit_solution(1779284654549648704)
XLA Ops:
  20.9 29.3 %shard_map.297 = bf16[4,128,2048]{2,1,0:T(8,128)(2,1)} custom-call(bf16[128,2048]{1,0:T(8,128)(2,1)} %fusion.225.x_ref), custom_call_target="tpu_custom_call" | custom-call | tf_op jit(solution)/shard_map/pallas_call | solution.py:112
  50.6 12.7 fusion.416
  96.6 6.7 all-gather
  117.3 13.0 all-gather.13.cloned.1.call-done
  134.9 9.4 fusion.134
  149.3 11.7 psum.140
  162.7 6.9 fusion.39.p_ref
  169.5 36.7 %shard_map.298 = f32[128,2048]{1,0:T(8,128)} custom-call(f32[4,128,2048]{2,1,0:T(8,128)} %fusion.39.p_ref), custom_call_target="tpu_custom_call" | custom-call | tf_op jit(solution)/shard_map/pallas_call | solution.py:208
  214.7 43.4 %shard_map.299 = bf16[4,128,2048]{2,1,0:T(8,128)(2,1)} custom-call(bf16[128,2048]{1,0:T(8,128)(2,1)} %multiply_convert_fusion.7.x_ref), custom_call_target="tpu_custom_call" | custom-call | tf_op jit(solution)/shard_map/pallas_call | solution.py:112
  258.1 12.9 fusion.415
  286.8 9.6 fusion.112
  315.1 6.8 all-gather.1
  330.5 10.4 all-gather.15.cloned.1.call-done
  345.6 9.4 fusion.133
  360.1 11.7 psum.141
  375.3 6.9 fusion.37.p_ref
  382.2 46.7 %shard_map.300 = f32[128,2048]{1,0:T(8,128)} custom-call(f32[4,128,2048]{2,1,0:T(8,128)} %fusion.37.p_ref), custom_call_target="tpu_custom_call" | custom-call | tf_op jit(solution)/shard_map/pallas_call | solution.py:208
  440.4 12.5 fusion.414
  480.7 7.9 all-gather.5
  494.2 7.0 all-gather.4
  502.4 7.8 all-gather.3
  510.1 7.4 all-gather.2
  527.7 8.7 all-gather.17.cloned.1.call-done
  541.1 9.4 fusion.132
  556.8 11.7 psum.142
  568.5 7.9 multiply_reduce_fusion.20
  576.4 8.3 psum.143
  584.8 6.9 multiply_reduce_fusion.23
  600.7 15.7 %fusion.29 = (f32[2,256,16]{1,2,0:T(8,128)}, f32[2,256,16]{1,2,0:T(8,128)}, f32[2,256,16]{1,2,0:T(8,128)}, f32[2,256,256]{2,1,0:T(8,128)S(1)}) fusion(f32[2,256,16]{1,2,0:T(8,128)} %bitcast.1076, f32[2,256,256]{2,1,0:T(8,128)} %fusion.452, f32[2,256,16]{1,2,0:T(8,128)} %copy-done.215, pred[2,256,256]{2,1,0:T(8,128)(4,1)} %get-tuple-element.268, ...), kind=kOutput, calls=%fused_computation.47 | convolution fusion | flops 1637720064 | bytes 5537792 | tf_op jit(solution)/shard_map/transpose(jvp(cijh,cjhp->cihp))/dot_general | solution.py:355
  629.8 20.0 %all-gather.19.cloned.1.call-done = bf16[4,16,64,128]{3,2,1,0:T(8,128)(2,1)} async-done(((bf16[1,16,64,128]{3,2,1,0:T(8,128)(2,1)}), bf16[4,16,64,128]{3,2,1,0:T(8,128)(2,1)}) %all-gather.19.cloned.1.call-update) | async-done | bytes 1048592 | tf_op jit(solution)/shard_map/all_gather | solution.py:258
  659.5 9.2 fusion.128
  673.0 6.4 multiply_reduce_fusion.13
  732.7 11.0 fusion.252
  743.7 26.0 %collective-permute-done.9 = bf16[128,2048]{1,0:T(8,128)(2,1)S(1)} collective-permute-done((bf16[128,2048]{1,0:T(8,128)(2,1)S(1)}, bf16[128,2048]{1,0:T(8,128)(2,1)S(1)}, u32[]{:S(2)}, u32[]{:S(2)}) %collective-permute-start.9) | collective-permute-done | bytes 524320 | tf_op jit(solution)/shard_map/ppermute | solution.py:235
  771.4 39.3 %shard_map.305 = bf16[4,128,2048]{2,1,0:T(8,128)(2,1)} custom-call(bf16[128,2048]{1,0:T(8,128)(2,1)} %fusion.243.x_ref), custom_call_target="tpu_custom_call" | custom-call | tf_op jit(solution)/shard_map/pallas_call | solution.py:112
  810.8 8.0 multiply_reduce_fusion.19
  818.8 8.3 psum.144
  827.1 6.0 multiply_reduce_fusion.22
  842.7 15.7 fusion.31
  881.7 9.0 fusion.124
  895.1 6.4 multiply_reduce_fusion.9
  946.3 50.6 %shard_map.306 = f32[128,2048]{1,0:T(8,128)} custom-call(f32[4,128,2048]{2,1,0:T(8,128)} %bitcast.967), custom_call_target="tpu_custom_call" | custom-call | tf_op jit(solution)/shard_map/pallas_call | solution.py:208
  1002.0 10.9 fusion.250
  1014.7 28.7 %shard_map.307 = bf16[4,128,2048]{2,1,0:T(8,128)(2,1)} custom-call(bf16[128,2048]{1,0:T(8,128)(2,1)} %fusion.244.x_ref), custom_call_target="tpu_custom_call" | custom-call | tf_op jit(solution)/shard_map/pallas_call | solution.py:112
  1043.5 8.0 multiply_reduce_fusion.18
  1051.5 11.4 psum.145
  1062.9 6.0 multiply_reduce_fusion.21
  1072.7 15.4 fusion.33
  1099.1 10.6 add_convert_fusion
  1110.2 12.7 all-gather.23.cloned.1.call-done
  1132.9 7.4 fusion.120
  1165.9 5.9 pad_add_fusion
  1185.5 5.9 copy-done.51
  1193.1 37.3 %all-reduce.70.cloned.1.call-done = bf16[1024,2048]{1,0:T(8,128)(2,1)} async-done(((bf16[1024,2048]{1,0:T(8,128)(2,1)}), bf16[1024,2048]{1,0:T(8,128)(2,1)}) %all-reduce.70.cloned.1.call-update) | async-done | bytes 4194320 | tf_op jit(solution)/shard_map/psum | solution.py:684
  1232.2 21.5 %fusion.34 = (bf16[1,2048,1024]{1,2,0:T(8,128)(2,1)}, bf16[1,2048,1024]{1,2,0:T(8,128)(2,1)}) fusion(f32[2048,2064]{0,1:T(8,128)} %copy-done.51, f32[2048,2064]{0,1:T(8,128)} %fusion.250, f32[2048,2064]{0,1:T(8,128)} %fusion.252, f32[]{:T(128)S(6)} %convert_element_type.594, f32[]{:T(128)S(6)} %convert_element_type.593, f32[]{:T(128)S(6)} %convert_element_type.592, ...), kind=kLoop, calls=%fused_computation.58 | loop fusion | flops 27262976 | bytes 58720272 | tf_op jit(solution)/shard_map/broadcast_in_dim | solution.py:709
  1258.0 7.5 fusion.35.p_ref
  1289.1 15.9 %all-reduce.64 = (bf16[1,4,1024]{2,1,0:T(4,128)(2,1)S(1)}, bf16[1,1024]{1,0:T(2,128)(2,1)S(1)}, bf16[1,16]{1,0:T(2,128)(2,1)S(1)}, bf16[1,16]{1,0:T(2,128)(2,1)S...) all-reduce(bf16[1,4,1024]{2,1,0:T(4,128)(2,1)S(1)} %fusion.336, ...), channel_id=1, replica_groups=mesh['section'=2,'seq'=4,'head'=4] {'seq'}, use_global_device_ids=true, to_apply=%region_93.95 | all-reduce | flops 6192 | bytes 24768 | tf_op jit(solution)/shard_map/psum | solution.py:584
  1314.8 9.0 fusion.249
  1325.0 7.8 convolution_add_fusion
  1332.9 38.3 %shard_map.308 = f32[128,2048]{1,0:T(8,128)} custom-call(f32[4,128,2048]{2,1,0:T(8,128)} %bitcast.965), custom_call_target="tpu_custom_call" | custom-call | tf_op jit(solution)/shard_map/pallas_call | solution.py:208
  1372.8 73.3 %all-reduce.63 = (f32[1,2048]{1,0:T(1,128)}, f32[1,4,256]{2,1,0:T(4,128)}, f32[1,256]{1,0:T(1,128)}) all-reduce(f32[1,2048]{1,0:T(1,128)S(1)} %bitcast.1085, f32[1,4,256]{2,1,0:T(4,128)S(1)} %fusion.338, f32[1,256]{1,0:T(1,128)S(1)} %bitcast.1103), channel_id=1, replica_groups=mesh['section'=2,'seq'=4,'head'=4] {'seq','head'}, use_global_device_ids=true, to_apply=%region_75.77 | all-reduce | flops 3328 | bytes 26624 | tf_op jit(solution)/shard_map/psum | solution.py:586
  1453.7 6.9 copy.616
  1460.6 6.9 copy.617
  1468.2 92.8 %all-reduce.72.cloned.1.call-done = f32[1,2048,256]{2,1,0:T(8,128)} async-done(((f32[1,2048,256]{2,1,0:T(8,128)}), f32[1,2048,256]{2,1,0:T(8,128)}) %all-reduce.72.cloned.1.call-update) | async-done | bytes 2097168 | tf_op jit(solution)/shard_map/psum | solution.py:586
  (1264 shorter events, 499.0 us)
Async XLA Ops:
  7.2 43.1 %copy-start.217 = (bf16[1,2048,16]{1,2,0:T(8,128)(2,1)S(1)}, bf16[1,2048,16]{1,2,0:T(8,128)(2,1)}, u32[]{:S(2)}) copy-start(bf16[1,2048,16]{1,2,0:T(8,128)(2,1)} %param.27) | copy-start | bytes 196612
  7.2 43.4 %copy-start.58 = (bf16[1,2048,256]{2,1,0:T(8,128)(2,1)S(1)}, bf16[1,2048,256]{2,1,0:T(8,128)(2,1)}, u32[]{:S(2)}) copy-start(bf16[1,2048,256]{2,1,0:T(8,128)(2,1)} %param.26) | copy-start | bytes 3145732
  7.2 123.1 %all-gather.13.cloned.1.call-start = ((), (), s32[]{:S(2)}) async-start(), calls=%async_computation | async-start | bytes 2621440 | tf_op jit(solution)/shard_map/all_gather | solution.py:240
  8.7 70.6 %collective-permute-start = (f32[3]{0:T(128)S(1)}, f32[3]{0:T(128)S(1)}, u32[]{:S(2)}, u32[]{:S(2)}) collective-permute-start(f32[3]{0:T(128)S(1)} %slice.578), channel_id=1, source_target_pairs={{0,4},{4,8},{8,12},{1,5},{5,9},{9,13},{2,6},{6,10},{10,14},{3,7},{... | collective-permute-start | bytes 44 | tf_op jit(solution)/shard_map/ppermute | solution.py:235
  13.7 65.7 %collective-permute-start.3 = (f32[3]{0:T(128)S(1)}, f32[3]{0:T(128)S(1)}, u32[]{:S(2)}, u32[]{:S(2)}) collective-permute-start(f32[3]{0:T(128)S(1)} %slice.617), channel_id=1, source_target_pairs={{0,4},{4,8},{8,12},{1,5},{5,9},{9,13},{2,6},{6,10},{10,14},{3,7},{... | collective-permute-start | bytes 44 | tf_op jit(solution)/shard_map/ppermute | solution.py:235
  18.9 31.3 %copy-start.333 = (f32[128]{0:T(128)}, f32[128]{0:T(128)S(1)}, u32[]{:S(2)}) copy-start(f32[128]{0:T(128)S(1)} %get-tuple-element.335) | copy-start | bytes 1540
  66.0 14.9 collective-permute-start.1
  73.1 30.3 %copy-start.151 = (f32[512,16]{0,1:T(8,128)}, f32[512,16]{0,1:T(8,128)S(1)}, u32[]{:S(2)}) copy-start(f32[512,16]{0,1:T(8,128)S(1)} %get-tuple-element.229) | copy-start | bytes 98308
  79.4 55.4 %copy-start.184 = (f32[2,256,16]{1,2,0:T(8,128)}, f32[2,256,16]{1,2,0:T(8,128)S(1)}, u32[]{:S(2)}) copy-start(f32[2,256,16]{1,2,0:T(8,128)S(1)} %get-tuple-element.278) | copy-start | bytes 98308
  91.0 43.9 %copy-start.9 = (f32[2,256,16,64]{1,0,3,2:T(2,128)}, f32[2,256,16,64]{1,0,3,2:T(2,128)S(1)}, u32[]{:S(2)}) copy-start(f32[2,256,16,64]{1,0,3,2:T(2,128)S(1)} %reshape.957) | copy-start | bytes 6291460
  94.9 35.4 %copy-start.63 = (f32[2,16,64,128]{3,2,1,0:T(8,128)}, f32[2,16,64,128]{3,2,1,0:T(8,128)S(1)}, u32[]{:S(2)}) copy-start(f32[2,16,64,128]{3,2,1,0:T(8,128)S(1)} %fusion.160) | copy-start | bytes 3145732
  96.6 244.3 %all-gather.15.cloned.1.call-start = ((), (), s32[]{:S(2)}) async-start(), calls=%async_computation.1 | async-start | bytes 2621440 | tf_op jit(solution)/shard_map/all_gather | solution.py:240
  169.5 38.4 %copy-start.52 = (bf16[2,128,2048]{2,1,0:T(8,128)(2,1)S(1)}, bf16[2,128,2048]{2,1,0:T(8,128)(2,1)}, u32[]{:S(2)}) copy-start(bf16[2,128,2048]{2,1,0:T(8,128)(2,1)} %param.19) | copy-start | bytes 3145732
  209.2 3.7 collective-permute-start.2
  212.1 70.1 %copy-start.261 = (f32[2,256]{1,0:T(2,128)}, f32[2,256]{1,0:T(2,128)S(1)}, u32[]{:S(2)}) copy-start(f32[2,256]{1,0:T(2,128)S(1)} %get-tuple-element.345) | copy-start | bytes 6148
  212.1 70.1 %copy-start.300 = (f32[2,256]{1,0:T(2,128)}, f32[2,256]{1,0:T(2,128)S(1)}, u32[]{:S(2)}) copy-start(f32[2,256]{1,0:T(2,128)S(1)} %get-tuple-element.346) | copy-start | bytes 6148
  212.9 73.9 %copy-start.239 = (f32[512]{0:T(512)}, f32[512]{0:T(512)S(1)}, u32[]{:S(2)}) copy-start(f32[512]{0:T(512)S(1)} %get-tuple-element.289) | copy-start | bytes 6148
  212.9 73.9 %copy-start.241 = (f32[512]{0:T(512)}, f32[512]{0:T(512)S(1)}, u32[]{:S(2)}) copy-start(f32[512]{0:T(512)S(1)} %get-tuple-element.290) | copy-start | bytes 6148
  212.9 73.9 %copy-start.243 = (f32[512]{0:T(512)}, f32[512]{0:T(512)S(1)}, u32[]{:S(2)}) copy-start(f32[512]{0:T(512)S(1)} %get-tuple-element.291) | copy-start | bytes 6148
  213.1 215.7 %copy-start.25 = (f32[128,2048]{1,0:T(8,128)}, f32[128,2048]{1,0:T(8,128)S(1)}, u32[]{:S(2)}) copy-start(f32[128,2048]{1,0:T(8,128)S(1)} %get-tuple-element.221) | copy-start | bytes 3145732
  213.8 57.2 %copy-start.347 = (f32[128]{0:T(128)}, f32[128]{0:T(128)S(1)}, u32[]{:S(2)}) copy-start(f32[128]{0:T(128)S(1)} %get-tuple-element.337) | copy-start | bytes 1540
  258.1 23.4 %copy-start.345 = (f32[2]{0:T(128)S(1)}, f32[2]{0:T(128)}, u32[]{:S(2)}) copy-start(f32[2]{0:T(128)} %get-tuple-element.348) | copy-start | bytes 28
  275.6 10.9 collective-permute-start.4
  279.9 42.0 %copy-start.153 = (f32[512,16]{0,1:T(8,128)}, f32[512,16]{0,1:T(8,128)S(1)}, u32[]{:S(2)}) copy-start(f32[512,16]{0,1:T(8,128)S(1)} %get-tuple-element.217) | copy-start | bytes 98308
  282.3 63.2 %copy-start.188 = (f32[2,256,16]{1,2,0:T(8,128)}, f32[2,256,16]{1,2,0:T(8,128)S(1)}, u32[]{:S(2)}) copy-start(f32[2,256,16]{1,2,0:T(8,128)S(1)} %get-tuple-element.276) | copy-start | bytes 98308
  301.6 44.0 %copy-start.11 = (f32[2,256,16,64]{1,0,3,2:T(2,128)}, f32[2,256,16,64]{1,0,3,2:T(2,128)S(1)}, u32[]{:S(2)}) copy-start(f32[2,256,16,64]{1,0,3,2:T(2,128)S(1)} %reshape.969) | copy-start | bytes 6291460
  307.5 229.0 %all-gather.17.cloned.1.call-start = ((), (), s32[]{:S(2)}) async-start(), calls=%async_computation.2 | async-start | bytes 2621440 | tf_op jit(solution)/shard_map/all_gather | solution.py:240
  308.8 124.3 %collective-permute-start.6 = (f32[3]{0:T(128)}, f32[3]{0:T(128)}, u32[]{:S(2)}, u32[]{:S(2)}) collective-permute-start(f32[3]{0:T(128)} %slice.652), channel_id=1, source_target_pairs={{0,4},{4,8},{8,12},{1,5},{5,9},{9,13},{2,6},{6,10},{10,14},{3,7},{... | collective-permute-start | bytes 44 | tf_op jit(solution)/shard_map/ppermute | solution.py:235
  321.9 23.6 %copy-start.281 = (f32[2,2,8,256]{3,2,0,1:T(8,128)}, f32[2,2,8,256]{3,2,0,1:T(8,128)S(1)}, u32[]{:S(2)}) copy-start(f32[2,2,8,256]{3,2,0,1:T(8,128)S(1)} %copy.946) | copy-start | bytes 98308
  382.2 46.7 %copy-start.119 = (f32[1,128,2048]{2,1,0:T(8,128)S(1)}, f32[1,128,2048]{2,1,0:T(8,128)}, u32[]{:S(2)}) copy-start(f32[1,128,2048]{2,1,0:T(8,128)} %constant_dynamic-slice_fusion.3) | copy-start | bytes 3145732
  431.7 3.8 collective-permute-start.5
  433.1 28.4 %copy-start.384 = (f32[2]{0:T(128)}, f32[2]{0:T(128)S(1)}, u32[]{:S(2)}) copy-start(f32[2]{0:T(128)S(1)} %fusion.368) | copy-start | bytes 28
  434.6 31.1 %copy-start.245 = (f32[512]{0:T(512)}, f32[512]{0:T(512)S(1)}, u32[]{:S(2)}) copy-start(f32[512]{0:T(512)S(1)} %get-tuple-element.283) | copy-start | bytes 6148
  434.6 31.1 %copy-start.247 = (f32[512]{0:T(512)}, f32[512]{0:T(512)S(1)}, u32[]{:S(2)}) copy-start(f32[512]{0:T(512)S(1)} %get-tuple-element.284) | copy-start | bytes 6148
  434.6 31.1 %copy-start.249 = (f32[512]{0:T(512)}, f32[512]{0:T(512)S(1)}, u32[]{:S(2)}) copy-start(f32[512]{0:T(512)S(1)} %get-tuple-element.285) | copy-start | bytes 6148
  440.4 21.8 %copy-start.263 = (f32[2,256]{1,0:T(2,128)S(1)}, f32[2,256]{1,0:T(2,128)}, u32[]{:S(2)}) copy-start(f32[2,256]{1,0:T(2,128)} %get-tuple-element.302) | copy-start | bytes 6148
  455.6 9.8 collective-permute-start.7
  475.5 175.9 %copy-start.14 = (f32[2,256,16,64]{1,0,3,2:T(2,128)}, f32[2,256,16,64]{1,0,3,2:T(2,128)S(1)}, u32[]{:S(2)}) copy-start(f32[2,256,16,64]{1,0,3,2:T(2,128)S(1)} %reshape.981) | copy-start | bytes 6291460
  479.5 57.0 %copy-start.66 = (f32[2,16,64,128]{3,2,1,0:T(8,128)}, f32[2,16,64,128]{3,2,1,0:T(8,128)S(1)}, u32[]{:S(2)}) copy-start(f32[2,16,64,128]{3,2,1,0:T(8,128)S(1)} %fusion.152) | copy-start | bytes 3145732
  480.6 169.3 %all-gather.19.cloned.1.call-start = ((), (), s32[]{:S(2)}) async-start(), calls=%async_computation.3 | async-start | bytes 1310720 | tf_op jit(solution)/shard_map/all_gather | solution.py:258
  600.6 271.4 %all-gather.21.cloned.1.call-start = ((), (), s32[]{:S(2)}) async-start(), calls=%async_computation.4 | async-start | bytes 1310720 | tf_op jit(solution)/shard_map/all_gather | solution.py:258
  690.8 16.0 %collective-permute-start.8 = (f32[3,1280]{1,0:T(4,128)}, f32[3,1280]{1,0:T(4,128)}, u32[]{:S(2)}, u32[]{:S(2)}) collective-permute-start(f32[3,1280]{1,0:T(4,128)} %copy.559), channel_id=1, source_target_pairs={{4,0},{8,4},{12,8},{5,1},{9,5},{13,9},{6,2},{10,6},{14,10},{7,3},{... | collective-permute-start | bytes 46088 | tf_op jit(solution)/shard_map/ppermute | solution.py:235
  731.4 38.3 %collective-permute-start.9 = (bf16[128,2048]{1,0:T(8,128)(2,1)S(1)}, bf16[128,2048]{1,0:T(8,128)(2,1)S(1)}, u32[]{:S(2)}, u32[]{:S(2)}) collective-permute-start(bf16[128,2048]{1,0:T(8,128)(2,1)S(1)} %get-tuple-element.196), channel_id=1, source_target_pairs={{16,0},{17,1},{18,2},{19,3},{20,4},{21,5},{22,6},{23,7},{24,8},{25... | collective-permute-start | bytes 1572872 | tf_op jit(solution)/shard_map/ppermute | solution.py:235
  743.7 67.0 %copy-start.315 = (f32[512]{0:T(512)S(1)}, f32[512]{0:T(512)}, u32[]{:S(2)}) copy-start(f32[512]{0:T(512)} %copy-done.314) | copy-start | bytes 6148
  842.4 280.5 %all-gather.23.cloned.1.call-start = ((), (), s32[]{:S(2)}) async-start(), calls=%async_computation.5 | async-start | bytes 1310720 | tf_op jit(solution)/shard_map/all_gather | solution.py:258
  912.8 15.9 %collective-permute-start.10 = (f32[3,1280]{1,0:T(4,128)}, f32[3,1280]{1,0:T(4,128)}, u32[]{:S(2)}, u32[]{:S(2)}) collective-permute-start(f32[3,1280]{1,0:T(4,128)} %copy.582), channel_id=1, source_target_pairs={{4,0},{8,4},{12,8},{5,1},{9,5},{13,9},{6,2},{10,6},{14,10},{7,3},{... | collective-permute-start | bytes 46088 | tf_op jit(solution)/shard_map/ppermute | solution.py:235
  946.3 50.6 %copy-start.26 = (f32[128,2048]{1,0:T(8,128)S(1)}, f32[128,2048]{1,0:T(8,128)}, u32[]{:S(2)}) copy-start(f32[128,2048]{1,0:T(8,128)} %copy-done.25) | copy-start | bytes 3145732
  946.3 50.6 %copy-start.348 = (f32[128]{0:T(128)S(1)}, f32[128]{0:T(128)}, u32[]{:S(2)}) copy-start(f32[128]{0:T(128)} %copy-done.347) | copy-start | bytes 1540
  946.3 52.8 %copy-start.68 = (bf16[2,128,2048]{2,1,0:T(8,128)(2,1)S(1)}, bf16[2,128,2048]{2,1,0:T(8,128)(2,1)}, u32[]{:S(2)}) copy-start(bf16[2,128,2048]{2,1,0:T(8,128)(2,1)} %param.20) | copy-start | bytes 3145732
  946.3 52.9 %copy-start.144 = (bf16[128,2048]{1,0:T(8,128)(2,1)S(1)}, bf16[128,2048]{1,0:T(8,128)(2,1)}, u32[]{:S(2)}) copy-start(bf16[128,2048]{1,0:T(8,128)(2,1)} %copy-done.143) | copy-start | bytes 1572868
  946.3 52.9 %copy-start.393 = (f32[128]{0:T(128)S(1)}, f32[128]{0:T(128)}, u32[]{:S(2)}) copy-start(f32[128]{0:T(128)} %get-tuple-element.336) | copy-start | bytes 1540
  1000.6 12.4 collective-permute-start.11
  1012.9 30.5 %copy-start.313 = (f32[512]{0:T(512)S(1)}, f32[512]{0:T(512)}, u32[]{:S(2)}) copy-start(f32[512]{0:T(512)} %copy-done.312) | copy-start | bytes 6148
  1094.6 135.8 %all-reduce.70.cloned.1.call-start = ((), (), s32[]{:S(2)}) async-start(), calls=%async_computation.6 | async-start | bytes 8388608 | tf_op jit(solution)/shard_map/psum | solution.py:684
  1109.7 344.0 %all-reduce.74.cloned.1.call-start = ((), (), s32[]{:S(2)}) async-start(), calls=%async_computation.8 | async-start | bytes 16908288 | tf_op jit(solution)/shard_map/psum | solution.py:584
  1164.3 10.9 collective-permute-start.12
  1253.7 307.3 %all-reduce.72.cloned.1.call-start = ((), (), s32[]{:S(2)}) async-start(), calls=%async_computation.7 | async-start | bytes 4194304 | tf_op jit(solution)/shard_map/psum | solution.py:586
  1284.7 23.6 %copy-start.33 = (f32[509,1280]{0,1:T(8,128)S(1)}, f32[509,1280]{0,1:T(8,128)}, u32[]{:S(2)}) copy-start(f32[509,1280]{0,1:T(8,128)} %slice.870) | copy-start | bytes 7818244
  1332.9 38.4 %copy-start.54 = (bf16[2,128,2048]{2,1,0:T(8,128)(2,1)S(1)}, bf16[2,128,2048]{2,1,0:T(8,128)(2,1)}, u32[]{:S(2)}) copy-start(bf16[2,128,2048]{2,1,0:T(8,128)(2,1)} %param.19) | copy-start | bytes 3145732
  1332.9 38.4 %copy-start.334 = (f32[128]{0:T(128)S(1)}, f32[128]{0:T(128)}, u32[]{:S(2)}) copy-start(f32[128]{0:T(128)} %copy-done.333) | copy-start | bytes 1540
  1332.9 39.9 %copy-start.265 = (f32[2048]{0:T(1024)S(1)}, f32[2048]{0:T(1024)}, u32[]{:S(2)}) copy-start(f32[2048]{0:T(1024)} %get-tuple-element.141) | copy-start | bytes 24580
  1332.9 39.9 %copy-start.266 = (f32[2048]{0:T(1024)S(1)}, f32[2048]{0:T(1024)}, u32[]{:S(2)}) copy-start(f32[2048]{0:T(1024)} %get-tuple-element.143) | copy-start | bytes 24580
  1332.9 113.2 %copy-start.45 = (f32[2,128,2048]{2,1,0:T(8,128)S(1)}, f32[2,128,2048]{2,1,0:T(8,128)}, u32[]{:S(2)}) copy-start(f32[2,128,2048]{2,1,0:T(8,128)} %copy-done.44) | copy-start | bytes 6291460
  1332.9 113.2 %copy-start.392 = (f32[128]{0:T(128)S(1)}, f32[128]{0:T(128)}, u32[]{:S(2)}) copy-start(f32[128]{0:T(128)} %get-tuple-element.334) | copy-start | bytes 1540
  (366 other events, 2145.2 us)
Sparse Core Ops, SparseCore 0:
  96.7 33.5 all-gather.12
  307.6 33.1 all-gather.14
  480.7 55.6 all-gather.16
  600.7 49.1 all-gather.18
  842.5 29.4 all-gather.20
  1094.7 28.1 all-gather.22
  1126.2 104.1 all-reduce.69
  1253.8 175.7 all-reduce.73
  1435.1 125.8 all-reduce.71

commit v4 on v3

--- a/solution.py
+++ b/solution.py
@@ -235,9 +235,26 @@
     return lax.ppermute(value, axis, pairs)
 
 
+def gather_flat(value, axis, kind):
+    leaves, tree = jax.tree.flatten(value)
+    slabs = []
+    for leaf in leaves:
+        flat = leaf.reshape(-1).astype(kind or leaf.dtype)
+        flat = jnp.pad(flat, (0, -flat.size % 1024))
+        slabs.append(flat.reshape(-1, 128))
+    everything = lax.all_gather(jnp.concatenate(slabs, axis=0), axis)
+    pieces = []
+    start = 0
+    for leaf, slab in zip(leaves, slabs):
+        rows = everything[:, start : start + slab.shape[0]].reshape(everything.shape[0], -1)
+        pieces.append(rows[:, : leaf.size].reshape((-1,) + leaf.shape))
+        start += slab.shape[0]
+    return jax.tree.unflatten(tree, pieces)
+
+
 def entering(value, axis, combine, identity):
     count, mine = (lax.axis_size(axis), lax.axis_index(axis))
-    everything = jax.tree.map(lambda part: lax.all_gather(part, axis), value)
+    everything = gather_flat(value, axis, None)
     before = jax.tree.map(
         lambda part, zero: jnp.broadcast_to(jnp.asarray(zero, part.dtype), part.shape),
         value,
@@ -254,11 +271,7 @@
     count = lax.axis_size(axis)
     place = lax.axis_index(axis)
     ahead = count - 1 - place
-    gathered = jax.tree.map(
-        lambda a, kind: lax.all_gather(a.astype(kind), axis),
-        value,
-        jax.tree.map(lambda a: jnp.bfloat16 if a.dtype == jnp.float32 else a.dtype, value),
-    )
+    gathered = gather_flat(value, axis, jnp.bfloat16)
     state = jax.tree.map(lambda a, e: jnp.zeros_like(a) + jnp.asarray(e, a.dtype), value, neutral)
     for lap in range(count - 1):
         source = count - 1 - lap
@@ -579,12 +592,21 @@
     return (grad_stream, head_part, shared_part, g_w_out)
 
 
+def psum_flat(members, axes, kind):
+    flat = jnp.concatenate([member.reshape(-1).astype(kind) for member in members])
+    total = lax.psum(flat, axes).astype(jnp.float32)
+    pieces = []
+    start = 0
+    for member in members:
+        pieces.append(total[start : start + member.size].reshape(member.shape))
+        start += member.size
+    return tuple(pieces)
+
+
 def reduce_grads(head_part, shared_part):
-    head_sum = tuple(
-        lax.psum(member.astype(jnp.bfloat16), "seq").astype(jnp.float32) for member in head_part
-    )
-    shared_sum = lax.psum(tuple(shared_part), ("seq", "head"))
-    return (head_sum, tuple(shared_sum))
+    head_sum = psum_flat(head_part, "seq", jnp.bfloat16)
+    shared_sum = psum_flat(shared_part, ("seq", "head"), jnp.float32)
+    return (head_sum, shared_sum)
 
 
 def store_slot(buffer, value, slot_index, is_valid):

time: 1580 us -> 1690 us (1.070); the launches traced: 1570 us -> 1660 us
  local copies, waits for them, and re-layouts: 173 us -> 392 us
  blocking collectives: 196 us -> 63.3 us
  waiting for transfers between devices: 222 us -> 245 us
  Pallas kernels: 326 us -> 307 us
    concatenate x0 -> x1, local copies, waits for them, and re-layouts: none -> 122 us  [psum_flat(): jnp.concatenate([member.reshape(-1).astype(kind) for member in members])]
    psum x2 -> x0, blocking collectives: 89.2 us -> none  [the longest x1 73.3 us: reduce_grads(): shared_sum = lax.psum(tuple(shared_part), ('seq', 'head'))]
    psum x2, waiting for transfers between devices: 92.8 us -> 138 us  [psum_flat(): total = lax.psum(flat, axes).astype(jnp.float32)]
    all_gather x6 -> x0, blocking collectives: 43.7 us -> none  [the longest x3 22.7 us: entering_2(): lax.all_gather(a.astype(kind), axis)]
    psum x1, waiting for transfers between devices: 37.3 us -> 0.02 us  [on_device(): out_total = lax.psum(out_total.astype(jnp.bfloat16), 'seq')]
    convert_element_type x2 -> x14, other arithmetic: 0.02 us -> 33.8 us  [the longest x7 26.2 us: psum_flat(): member.reshape(-1).astype(kind)]
    broadcast_in_dim x14 -> x0, other arithmetic: 27.2 us -> none  [the longest x1 21.5 us: on_device(): head_total[1][None]]
    mul x0 -> x54, local copies, waits for them, and re-layouts: none -> 25 us  [the longest x36 16.2 us: chain_combine(): later[0][:, None, None] * earlier[1] + later[1]]
  transfers between devices with their start and end apart: 22 -> 22, of which waited for: 10 -> 7; matrix products, arithmetic and copies ran while one was open for 24% -> 34% of each run, Pallas kernels for 8% -> 7%
where the time goes in v4:
time: 1690 us; the launch traced here: 1660 us
  local copies, waits for them, and re-layouts  392 us (23%)
  matrix products  344 us (20%)
  Pallas kernels  307 us (18%)
  other arithmetic  254 us (15%)
  waiting for transfers between devices  245 us (14%)
  blocking collectives  63.3 us (4%)
  starting transfers between devices  33.6 us (2%)
  between operations  20.9 us (1%)
    pallas_call x6, Pallas kernels, head_scatter(): pl.pallas_call(functools.partial(scatter_body, n, tick), out_shape=jax.Sh...  167 us
    pallas_call x6, Pallas kernels, head_gather(): pl.pallas_call(functools.partial(gather_body, n, tick), out_shape=jax.Sha...  140 us
    psum x2, waiting for transfers between devices, psum_flat(): total = lax.psum(flat, axes).astype(jnp.float32)  138 us
    concatenate x1, local copies, waits for them, and re-layouts, psum_flat(): jnp.concatenate([member.reshape(-1).astype(kind) for member in members])  122 us
    dot_general x9, matrix products, block_output(): jnp.einsum('cijh,cjhp->cihp', weights, x_blocks, precision=highest)  100 us
    all_gather x6, waiting for transfers between devices, gather_flat(): everything = lax.all_gather(jnp.concatenate(slabs, axis=0), axis)  76.5 us
    unnamed x942, local copies, waits for them, and re-layouts  73.8 us
    dot_general x3, matrix products, mixer_forward(): projected = jnp.dot(gathered, w_main, preferred_element_type=jnp.float32)  38.1 us
  transfers between devices with their start and end apart: 22, of which 7 were waited for; matrix products, arithmetic and copies ran while one was open for 34% of the time, Pallas kernels for 7%

profile of v4, /device:TPU:0, one launch (start us, length us, event | category | flops | bytes accessed | tf_op | source)
XLA Modules:
  0.0 1660.5 jit_solution(3773205417791501386)
XLA Ops:
  20.8 29.3 %shard_map.297 = bf16[4,128,2048]{2,1,0:T(8,128)(2,1)} custom-call(bf16[128,2048]{1,0:T(8,128)(2,1)} %fusion.223.x_ref), custom_call_target="tpu_custom_call" | custom-call | tf_op jit(solution)/shard_map/pallas_call | solution.py:112
  50.5 12.7 fusion.377
  111.8 21.1 %all-gather.13.cloned.1.call-done = f32[4128,128]{1,0:T(8,128)} async-done(((f32[1032,128]{1,0:T(8,128)}), f32[4128,128]{1,0:T(8,128)}) %all-gather.13.cloned.1.call-update) | async-done | bytes 2113552 | tf_op jit(solution)/shard_map/all_gather | solution.py:245
  138.3 9.4 fusion.131
  152.8 11.7 psum.63
  166.1 6.9 fusion.38.p_ref
  173.0 36.8 %shard_map.298 = f32[128,2048]{1,0:T(8,128)} custom-call(f32[4,128,2048]{2,1,0:T(8,128)} %fusion.38.p_ref), custom_call_target="tpu_custom_call" | custom-call | tf_op jit(solution)/shard_map/pallas_call | solution.py:208
  218.2 43.4 %shard_map.299 = bf16[4,128,2048]{2,1,0:T(8,128)(2,1)} custom-call(bf16[128,2048]{1,0:T(8,128)(2,1)} %multiply_convert_fusion.7.x_ref), custom_call_target="tpu_custom_call" | custom-call | tf_op jit(solution)/shard_map/pallas_call | solution.py:112
  261.6 12.9 fusion.376
  290.1 9.9 fusion.109
  327.0 18.6 %all-gather.15.cloned.1.call-done = f32[4128,128]{1,0:T(8,128)} async-done(((f32[1032,128]{1,0:T(8,128)}), f32[4128,128]{1,0:T(8,128)}) %all-gather.15.cloned.1.call-update) | async-done | bytes 2113552 | tf_op jit(solution)/shard_map/all_gather | solution.py:245
  350.5 9.4 fusion.130
  365.0 11.7 psum.64
  380.2 6.9 fusion.36.p_ref
  387.1 46.6 %shard_map.300 = f32[128,2048]{1,0:T(8,128)} custom-call(f32[4,128,2048]{2,1,0:T(8,128)} %fusion.36.p_ref), custom_call_target="tpu_custom_call" | custom-call | tf_op jit(solution)/shard_map/pallas_call | solution.py:208
  445.2 12.5 fusion.375
  513.6 29.5 %all-gather.17.cloned.1.call-done = f32[4128,128]{1,0:T(8,128)} async-done(((f32[1032,128]{1,0:T(8,128)}), f32[4128,128]{1,0:T(8,128)}) %all-gather.17.cloned.1.call-update) | async-done | bytes 2113552 | tf_op jit(solution)/shard_map/all_gather | solution.py:245
  547.9 9.4 fusion.129
  563.6 11.7 psum.65
  575.3 7.9 multiply_reduce_fusion.20
  583.2 8.3 psum.66
  591.6 6.8 multiply_reduce_fusion.23
  607.7 15.6 fusion.29
  645.8 5.7 fusion.422
  662.9 9.2 fusion.125
  676.4 5.8 multiply_reduce_fusion.14
  727.5 5.7 convolution_add_fusion.2
  742.2 11.0 fusion.250
  757.0 28.7 %collective-permute-done.9 = bf16[128,2048]{1,0:T(8,128)(2,1)S(1)} collective-permute-done((bf16[128,2048]{1,0:T(8,128)(2,1)S(1)}, bf16[128,2048]{1,0:T(8,128)(2,1)S(1)}, u32[]{:S(2)}, u32[]{:S(2)}) %collective-permute-start.9) | collective-permute-done | bytes 524320 | tf_op jit(solution)/shard_map/ppermute | solution.py:235
  787.4 33.2 %shard_map.305 = bf16[4,128,2048]{2,1,0:T(8,128)(2,1)} custom-call(bf16[128,2048]{1,0:T(8,128)(2,1)} %fusion.241.x_ref), custom_call_target="tpu_custom_call" | custom-call | tf_op jit(solution)/shard_map/pallas_call | solution.py:112
  820.6 8.0 multiply_reduce_fusion.19
  828.6 10.5 psum.67
  839.2 5.4 multiply_reduce_fusion.22
  853.3 15.4 fusion.31
  880.4 5.7 fusion.423
  896.8 8.9 fusion.121
  910.1 5.7 multiply_reduce_fusion.10
  960.6 5.7 convolution_add_fusion.1
  966.3 37.8 %shard_map.306 = f32[128,2048]{1,0:T(8,128)} custom-call(f32[4,128,2048]{2,1,0:T(8,128)} %bitcast.942), custom_call_target="tpu_custom_call" | custom-call | tf_op jit(solution)/shard_map/pallas_call | solution.py:208
  1009.4 11.0 fusion.248
  1026.0 28.4 %shard_map.307 = bf16[4,128,2048]{2,1,0:T(8,128)(2,1)} custom-call(bf16[128,2048]{1,0:T(8,128)(2,1)} %fusion.242.x_ref), custom_call_target="tpu_custom_call" | custom-call | tf_op jit(solution)/shard_map/pallas_call | solution.py:112
  1054.5 7.4 multiply_reduce_fusion.18
  1061.9 9.4 psum.68
  1071.3 5.4 multiply_reduce_fusion.21
  1080.5 15.5 fusion.33
  1110.8 10.6 add_convert_fusion
  1125.6 7.2 all-gather.23.cloned.1.call-done
  1142.9 7.3 fusion.117
  1155.9 6.5 multiply_reduce_fusion.6
  1205.2 5.7 convolution_add_fusion
  1210.9 38.6 %shard_map.308 = f32[128,2048]{1,0:T(8,128)} custom-call(f32[4,128,2048]{2,1,0:T(8,128)} %bitcast.943), custom_call_target="tpu_custom_call" | custom-call | tf_op jit(solution)/shard_map/pallas_call | solution.py:208
  1258.5 6.4 fusion.246
  1264.9 5.9 copy-done.51
  1274.3 22.1 %fusion.1 = (bf16[2048,1024]{0,1:T(8,128)(2,1)}, bf16[2048,1024]{0,1:T(8,128)(2,1)}) fusion(f32[2048,2064]{0,1:T(8,128)} %copy-done.51, f32[2048,2064]{0,1:T(8,128)} %fusion.248, f32[2048,2064]{0,1:T(8,128)} %fusion.250, f32[]{:T(128)S(6)} %convert_element_type.710, f32[]{:T(128)S(6)} %convert_element_type.709, f32[]{:T(128)S(6)} %convert_element_type.708, ...), kind=kLoop, calls=%fused_computation.4 | loop fusion | flops 27262976 | bytes 58720272 | tf_op jit(solution)/shard_map/convert_element_type | solution.py:596
  1296.3 6.4 copy.617
  1308.1 6.4 copy.618
  1314.5 5.3 copy.741
  1319.8 122.1 %concatenate.95 = bf16[4233264]{0:T(1024)(128)(2,1)} concatenate(bf16[2097152]{0:T(1024)(128)(2,1)} %bitcast.946, bf16[2097152]{0:T(1024)(128)(2,1)} %bitcast.947, bf16[32768]{0:T(1024)(128)(2,1)S(1)} %convert_element_type.718, bf16[4096]{0:T(1024)(128)(2,1)S(1)} %bitcast.1093, bf16[1024]{0:T(1024)(128)(2,1)S(1)} %copy-done.369, bf16[16]{0:T(256)(128)(2,1)S(1)} %add_convert_fusion.4, ...), dimensions={0} | concatenate | bytes 16933056 | tf_op jit(solution)/shard_map/concatenate | solution.py:596
  1445.8 6.9 fusion.34.p_ref
  1471.1 6.7 bitcast_convert_fusion
  1477.8 138.2 %all-reduce.77.cloned.1.call-done = bf16[4233264]{0:T(1024)(128)(2,1)} async-done(((bf16[4233264]{0:T(1024)(128)(2,1)}), bf16[4233264]{0:T(1024)(128)(2,1)}) %all-reduce.77.cloned.1.call-update) | async-done | bytes 8466544 | tf_op jit(solution)/shard_map/psum | solution.py:597
  1616.0 8.7 fusion.406
  1624.7 9.2 broadcast_in_dim_reshape.18
  1633.9 9.2 broadcast_in_dim_reshape.19
  (1477 shorter events, 541.6 us)
Async XLA Ops:
  7.2 43.0 %copy-start.232 = (bf16[1,2048,16]{1,2,0:T(8,128)(2,1)S(1)}, bf16[1,2048,16]{1,2,0:T(8,128)(2,1)}, u32[]{:S(2)}) copy-start(bf16[1,2048,16]{1,2,0:T(8,128)(2,1)} %param.27) | copy-start | bytes 196612
  7.2 43.3 %copy-start.58 = (bf16[1,2048,256]{2,1,0:T(8,128)(2,1)S(1)}, bf16[1,2048,256]{2,1,0:T(8,128)(2,1)}, u32[]{:S(2)}) copy-start(bf16[1,2048,256]{2,1,0:T(8,128)(2,1)} %param.26) | copy-start | bytes 3145732
  7.2 125.6 %all-gather.13.cloned.1.call-start = ((), (), s32[]{:S(2)}) async-start(), calls=%async_computation.3 | async-start | bytes 2641920 | tf_op jit(solution)/shard_map/all_gather | solution.py:245
  8.7 72.5 %collective-permute-start = (f32[3]{0:T(128)S(1)}, f32[3]{0:T(128)S(1)}, u32[]{:S(2)}, u32[]{:S(2)}) collective-permute-start(f32[3]{0:T(128)S(1)} %slice.701), channel_id=1, source_target_pairs={{0,4},{4,8},{8,12},{1,5},{5,9},{9,13},{2,6},{6,10},{10,14},{3,7},{... | collective-permute-start | bytes 44 | tf_op jit(solution)/shard_map/ppermute | solution.py:235
  13.6 67.6 %collective-permute-start.3 = (f32[3]{0:T(128)S(1)}, f32[3]{0:T(128)S(1)}, u32[]{:S(2)}, u32[]{:S(2)}) collective-permute-start(f32[3]{0:T(128)S(1)} %slice.741), channel_id=1, source_target_pairs={{0,4},{4,8},{8,12},{1,5},{5,9},{9,13},{2,6},{6,10},{10,14},{3,7},{... | collective-permute-start | bytes 44 | tf_op jit(solution)/shard_map/ppermute | solution.py:235
  18.8 31.4 %copy-start.388 = (f32[128]{0:T(128)}, f32[128]{0:T(128)S(1)}, u32[]{:S(2)}) copy-start(f32[128]{0:T(128)S(1)} %get-tuple-element.344) | copy-start | bytes 1540
  65.9 16.8 %collective-permute-start.1 = (f32[3,1280]{1,0:T(4,128)S(1)}, f32[3,1280]{1,0:T(4,128)S(1)}, u32[]{:S(2)}, u32[]{:S(2)}) collective-permute-start(f32[3,1280]{1,0:T(4,128)S(1)} %copy.499), channel_id=1, source_target_pairs={{0,4},{4,8},{8,12},{1,5},{5,9},{9,13},{2,6},{6,10},{10,14},{3,7},{... | collective-permute-start | bytes 46088 | tf_op jit(solution)/shard_map/ppermute | solution.py:235
  73.0 26.0 %copy-start.161 = (f32[512,16]{0,1:T(8,128)}, f32[512,16]{0,1:T(8,128)S(1)}, u32[]{:S(2)}) copy-start(f32[512,16]{0,1:T(8,128)S(1)} %get-tuple-element.213) | copy-start | bytes 98308
  81.2 57.0 %copy-start.196 = (f32[2,256,16]{1,2,0:T(8,128)}, f32[2,256,16]{1,2,0:T(8,128)S(1)}, u32[]{:S(2)}) copy-start(f32[2,256,16]{1,2,0:T(8,128)S(1)} %get-tuple-element.293) | copy-start | bytes 98308
  92.9 45.4 %copy-start.9 = (f32[2,256,16,64]{1,0,3,2:T(2,128)}, f32[2,256,16,64]{1,0,3,2:T(2,128)S(1)}, u32[]{:S(2)}) copy-start(f32[2,256,16,64]{1,0,3,2:T(2,128)S(1)} %reshape.1621) | copy-start | bytes 6291460
  99.0 246.7 %all-gather.15.cloned.1.call-start = ((), (), s32[]{:S(2)}) async-start(), calls=%async_computation.4 | async-start | bytes 2641920 | tf_op jit(solution)/shard_map/all_gather | solution.py:245
  101.2 33.1 %copy-start.336 = (s32[1,2,2,128]{3,2,1,0:T(2,128)}, s32[1,2,2,128]{3,2,1,0:T(2,128)S(1)}, u32[]{:S(2)}) copy-start(s32[1,2,2,128]{3,2,1,0:T(2,128)S(1)} %add_bitcast_fusion.12) | copy-start | bytes 6148
  107.5 28.8 %copy-start.133 = (f32[2,256,128]{2,1,0:T(8,128)}, f32[2,256,128]{2,1,0:T(8,128)S(1)}, u32[]{:S(2)}) copy-start(f32[2,256,128]{2,1,0:T(8,128)S(1)} %copy.504) | copy-start | bytes 786436
  173.0 38.4 %copy-start.52 = (bf16[2,128,2048]{2,1,0:T(8,128)(2,1)S(1)}, bf16[2,128,2048]{2,1,0:T(8,128)(2,1)}, u32[]{:S(2)}) copy-start(bf16[2,128,2048]{2,1,0:T(8,128)(2,1)} %param.19) | copy-start | bytes 3145732
  212.7 3.7 collective-permute-start.2
  215.7 68.4 %copy-start.293 = (f32[2,256]{1,0:T(2,128)}, f32[2,256]{1,0:T(2,128)S(1)}, u32[]{:S(2)}) copy-start(f32[2,256]{1,0:T(2,128)S(1)} %get-tuple-element.354) | copy-start | bytes 6148
  215.7 68.4 %copy-start.327 = (f32[2,256]{1,0:T(2,128)}, f32[2,256]{1,0:T(2,128)S(1)}, u32[]{:S(2)}) copy-start(f32[2,256]{1,0:T(2,128)S(1)} %get-tuple-element.355) | copy-start | bytes 6148
  216.4 73.7 %copy-start.275 = (f32[512]{0:T(512)}, f32[512]{0:T(512)S(1)}, u32[]{:S(2)}) copy-start(f32[512]{0:T(512)S(1)} %get-tuple-element.319) | copy-start | bytes 6148
  216.4 73.7 %copy-start.277 = (f32[512]{0:T(512)}, f32[512]{0:T(512)S(1)}, u32[]{:S(2)}) copy-start(f32[512]{0:T(512)S(1)} %get-tuple-element.320) | copy-start | bytes 6148
  216.4 73.7 %copy-start.279 = (f32[512]{0:T(512)}, f32[512]{0:T(512)S(1)}, u32[]{:S(2)}) copy-start(f32[512]{0:T(512)S(1)} %get-tuple-element.321) | copy-start | bytes 6148
  216.6 217.1 %copy-start.28 = (f32[128,2048]{1,0:T(8,128)}, f32[128,2048]{1,0:T(8,128)S(1)}, u32[]{:S(2)}) copy-start(f32[128,2048]{1,0:T(8,128)S(1)} %get-tuple-element.205) | copy-start | bytes 3145732
  217.3 57.3 %copy-start.411 = (f32[128]{0:T(128)}, f32[128]{0:T(128)S(1)}, u32[]{:S(2)}) copy-start(f32[128]{0:T(128)S(1)} %get-tuple-element.346) | copy-start | bytes 1540
  277.0 41.4 %copy-start.163 = (f32[512,16]{0,1:T(8,128)}, f32[512,16]{0,1:T(8,128)S(1)}, u32[]{:S(2)}) copy-start(f32[512,16]{0,1:T(8,128)S(1)} %get-tuple-element.201) | copy-start | bytes 98308
  280.7 9.2 collective-permute-start.4
  284.2 22.0 %copy-start.198 = (f32[2,256,16]{1,2,0:T(8,128)}, f32[2,256,16]{1,2,0:T(8,128)S(1)}, u32[]{:S(2)}) copy-start(f32[2,256,16]{1,2,0:T(8,128)S(1)} %get-tuple-element.292) | copy-start | bytes 98308
  284.2 66.3 %copy-start.200 = (f32[2,256,16]{1,2,0:T(8,128)}, f32[2,256,16]{1,2,0:T(8,128)S(1)}, u32[]{:S(2)}) copy-start(f32[2,256,16]{1,2,0:T(8,128)S(1)} %get-tuple-element.291) | copy-start | bytes 98308
  305.1 45.3 %copy-start.11 = (f32[2,256,16,64]{1,0,3,2:T(2,128)}, f32[2,256,16,64]{1,0,3,2:T(2,128)S(1)}, u32[]{:S(2)}) copy-start(f32[2,256,16,64]{1,0,3,2:T(2,128)S(1)} %reshape.1635) | copy-start | bytes 6291460
  312.2 230.9 %all-gather.17.cloned.1.call-start = ((), (), s32[]{:S(2)}) async-start(), calls=%async_computation.5 | async-start | bytes 2641920 | tf_op jit(solution)/shard_map/all_gather | solution.py:245
  312.3 125.7 %collective-permute-start.6 = (f32[3]{0:T(128)S(1)}, f32[3]{0:T(128)S(1)}, u32[]{:S(2)}, u32[]{:S(2)}) collective-permute-start(f32[3]{0:T(128)S(1)} %slice.777), channel_id=1, source_target_pairs={{0,4},{4,8},{8,12},{1,5},{5,9},{9,13},{2,6},{6,10},{10,14},{3,7},{... | collective-permute-start | bytes 44 | tf_op jit(solution)/shard_map/ppermute | solution.py:235
  321.7 26.4 %copy-start.415 = (f32[16]{0:T(128)S(1)}, f32[16]{0:T(128)}, u32[]{:S(2)}) copy-start(f32[16]{0:T(128)} %get-tuple-element.340) | copy-start | bytes 196
  322.8 25.7 %copy-start.136 = (f32[2,256,128]{2,1,0:T(8,128)}, f32[2,256,128]{2,1,0:T(8,128)S(1)}, u32[]{:S(2)}) copy-start(f32[2,256,128]{2,1,0:T(8,128)S(1)} %copy.521) | copy-start | bytes 786436
  387.1 46.7 %copy-start.128 = (f32[1,128,2048]{2,1,0:T(8,128)S(1)}, f32[1,128,2048]{2,1,0:T(8,128)}, u32[]{:S(2)}) copy-start(f32[1,128,2048]{2,1,0:T(8,128)} %constant_dynamic-slice_fusion.3) | copy-start | bytes 3145732
  436.6 3.8 collective-permute-start.5
  438.0 23.7 %copy-start.431 = (f32[2]{0:T(128)}, f32[2]{0:T(128)S(1)}, u32[]{:S(2)}) copy-start(f32[2]{0:T(128)S(1)} %fusion.332) | copy-start | bytes 28
  438.8 32.4 %copy-start.281 = (f32[512]{0:T(512)}, f32[512]{0:T(512)S(1)}, u32[]{:S(2)}) copy-start(f32[512]{0:T(512)S(1)} %get-tuple-element.313) | copy-start | bytes 6148
  438.8 32.4 %copy-start.283 = (f32[512]{0:T(512)}, f32[512]{0:T(512)S(1)}, u32[]{:S(2)}) copy-start(f32[512]{0:T(512)S(1)} %get-tuple-element.314) | copy-start | bytes 6148
  438.8 32.4 %copy-start.285 = (f32[512]{0:T(512)}, f32[512]{0:T(512)S(1)}, u32[]{:S(2)}) copy-start(f32[512]{0:T(512)S(1)} %get-tuple-element.315) | copy-start | bytes 6148
  445.2 20.8 %copy-start.295 = (f32[2,256]{1,0:T(2,128)S(1)}, f32[2,256]{1,0:T(2,128)}, u32[]{:S(2)}) copy-start(f32[2,256]{1,0:T(2,128)} %get-tuple-element.326) | copy-start | bytes 6148
  462.6 8.4 collective-permute-start.7
  481.0 173.5 %copy-start.14 = (f32[2,256,16,64]{1,0,3,2:T(2,128)}, f32[2,256,16,64]{1,0,3,2:T(2,128)S(1)}, u32[]{:S(2)}) copy-start(f32[2,256,16,64]{1,0,3,2:T(2,128)S(1)} %reshape.1649) | copy-start | bytes 6291460
  487.1 164.4 %all-gather.19.cloned.1.call-start = ((), (), s32[]{:S(2)}) async-start(), calls=%async_computation.6 | async-start | bytes 1320960 | tf_op jit(solution)/shard_map/all_gather | solution.py:245
  508.3 37.1 %copy-start.88 = (f32[2,16,64,128]{3,2,1,0:T(8,128)S(1)}, f32[2,16,64,128]{3,2,1,0:T(8,128)}, u32[]{:S(2)}) copy-start(f32[2,16,64,128]{3,2,1,0:T(8,128)} %copy-done.87) | copy-start | bytes 3145732
  508.3 37.1 %copy-start.416 = (f32[16]{0:T(128)S(1)}, f32[16]{0:T(128)}, u32[]{:S(2)}) copy-start(f32[16]{0:T(128)} %get-tuple-element.338) | copy-start | bytes 196
  607.6 278.5 %all-gather.21.cloned.1.call-start = ((), (), s32[]{:S(2)}) async-start(), calls=%async_computation.7 | async-start | bytes 1320960 | tf_op jit(solution)/shard_map/all_gather | solution.py:245
  682.2 33.0 %copy-start.239 = (f32[1280]{0:T(1024)}, f32[1280]{0:T(1024)S(1)}, u32[]{:S(2)}) copy-start(f32[1280]{0:T(1024)S(1)} %get-tuple-element.120) | copy-start | bytes 15364
  695.1 20.7 %collective-permute-start.8 = (f32[3,1280]{1,0:T(4,128)}, f32[3,1280]{1,0:T(4,128)}, u32[]{:S(2)}, u32[]{:S(2)}) collective-permute-start(f32[3,1280]{1,0:T(4,128)} %copy.563), channel_id=1, source_target_pairs={{4,0},{8,4},{12,8},{5,1},{9,5},{13,9},{6,2},{10,6},{14,10},{7,3},{... | collective-permute-start | bytes 46088 | tf_op jit(solution)/shard_map/ppermute | solution.py:235
  740.7 44.9 %collective-permute-start.9 = (bf16[128,2048]{1,0:T(8,128)(2,1)S(1)}, bf16[128,2048]{1,0:T(8,128)(2,1)S(1)}, u32[]{:S(2)}, u32[]{:S(2)}) collective-permute-start(bf16[128,2048]{1,0:T(8,128)(2,1)S(1)} %get-tuple-element.178), channel_id=1, source_target_pairs={{16,0},{17,1},{18,2},{19,3},{20,4},{21,5},{22,6},{23,7},{24,8},{25... | collective-permute-start | bytes 1572872 | tf_op jit(solution)/shard_map/ppermute | solution.py:235
  757.0 63.6 %copy-start.341 = (f32[512]{0:T(512)S(1)}, f32[512]{0:T(512)}, u32[]{:S(2)}) copy-start(f32[512]{0:T(512)} %copy-done.340) | copy-start | bytes 6148
  852.6 280.2 %all-gather.23.cloned.1.call-start = ((), (), s32[]{:S(2)}) async-start(), calls=%async_computation.8 | async-start | bytes 1320960 | tf_op jit(solution)/shard_map/all_gather | solution.py:245
  915.9 32.5 %copy-start.241 = (f32[1280]{0:T(1024)}, f32[1280]{0:T(1024)S(1)}, u32[]{:S(2)}) copy-start(f32[1280]{0:T(1024)S(1)} %get-tuple-element.125) | copy-start | bytes 15364
  928.2 20.8 %collective-permute-start.10 = (f32[3,1280]{1,0:T(4,128)S(1)}, f32[3,1280]{1,0:T(4,128)}, u32[]{:S(2)}, u32[]{:S(2)}) collective-permute-start(f32[3,1280]{1,0:T(4,128)S(1)} %copy.586), channel_id=1, source_target_pairs={{4,0},{8,4},{12,8},{5,1},{9,5},{13,9},{6,2},{10,6},{14,10},{7,3},{... | collective-permute-start | bytes 46088 | tf_op jit(solution)/shard_map/ppermute | solution.py:235
  966.3 37.9 %copy-start.29 = (f32[128,2048]{1,0:T(8,128)S(1)}, f32[128,2048]{1,0:T(8,128)}, u32[]{:S(2)}) copy-start(f32[128,2048]{1,0:T(8,128)} %copy-done.28) | copy-start | bytes 3145732
  966.3 37.9 %copy-start.412 = (f32[128]{0:T(128)S(1)}, f32[128]{0:T(128)}, u32[]{:S(2)}) copy-start(f32[128]{0:T(128)} %copy-done.411) | copy-start | bytes 1540
  966.3 40.1 %copy-start.66 = (bf16[2,128,2048]{2,1,0:T(8,128)(2,1)S(1)}, bf16[2,128,2048]{2,1,0:T(8,128)(2,1)}, u32[]{:S(2)}) copy-start(bf16[2,128,2048]{2,1,0:T(8,128)(2,1)} %param.20) | copy-start | bytes 3145732
  966.3 40.1 %copy-start.155 = (bf16[128,2048]{1,0:T(8,128)(2,1)S(1)}, bf16[128,2048]{1,0:T(8,128)(2,1)}, u32[]{:S(2)}) copy-start(bf16[128,2048]{1,0:T(8,128)(2,1)} %copy-done.154) | copy-start | bytes 1572868
  966.3 40.1 %copy-start.439 = (f32[128]{0:T(128)S(1)}, f32[128]{0:T(128)}, u32[]{:S(2)}) copy-start(f32[128]{0:T(128)} %get-tuple-element.345) | copy-start | bytes 1540
  1007.9 16.4 collective-permute-start.11
  1024.3 30.2 %copy-start.339 = (f32[512]{0:T(512)S(1)}, f32[512]{0:T(512)}, u32[]{:S(2)}) copy-start(f32[512]{0:T(512)} %copy-done.338) | copy-start | bytes 6148
  1104.2 168.2 %all-reduce.75.cloned.1.call-start = ((), (), s32[]{:S(2)}) async-start(), calls=%async_computation.1 | async-start | bytes 8388608 | tf_op jit(solution)/shard_map/psum | solution.py:706
  1121.5 343.0 %all-reduce.73.cloned.1.call-start = ((), (), s32[]{:S(2)}) async-start(), calls=%async_computation | async-start | bytes 4227072 | tf_op jit(solution)/shard_map/psum | solution.py:597
  1184.7 8.9 collective-permute-start.12
  1210.9 38.6 %copy-start.54 = (bf16[2,128,2048]{2,1,0:T(8,128)(2,1)S(1)}, bf16[2,128,2048]{2,1,0:T(8,128)(2,1)}, u32[]{:S(2)}) copy-start(bf16[2,128,2048]{2,1,0:T(8,128)(2,1)} %param.19) | copy-start | bytes 3145732
  1210.9 38.6 %copy-start.389 = (f32[128]{0:T(128)S(1)}, f32[128]{0:T(128)}, u32[]{:S(2)}) copy-start(f32[128]{0:T(128)} %copy-done.388) | copy-start | bytes 1540
  1258.4 357.6 %all-reduce.77.cloned.1.call-start = ((), (), s32[]{:S(2)}) async-start(), calls=%async_computation.2 | async-start | bytes 16936960 | tf_op jit(solution)/shard_map/psum | solution.py:597
  (415 other events, 2338.5 us)
Sparse Core Ops, SparseCore 0:
  99.1 33.6 all-gather.12
  312.3 33.3 all-gather.14
  487.2 55.8 all-gather.16
  607.7 35.6 all-gather.18
  852.7 32.4 all-gather.20
  1104.3 28.4 all-gather.22
  1136.1 103.8 all-reduce.74
  1258.5 127.6 all-reduce.72
  1442.1 173.8 all-reduce.76

commit v5 on v4

--- a/solution.py
+++ b/solution.py
@@ -592,20 +592,30 @@
     return (grad_stream, head_part, shared_part, g_w_out)
 
 
-def psum_flat(members, axes, kind):
-    flat = jnp.concatenate([member.reshape(-1).astype(kind) for member in members])
-    total = lax.psum(flat, axes).astype(jnp.float32)
-    pieces = []
+def psum_packed(big, small, axes, kind):
+    host = big[0]
+    width = host.shape[-1]
+    flat = jnp.concatenate([member.reshape(-1).astype(kind) for member in small])
+    flat = jnp.pad(flat, (0, -flat.size % (16 * width)))
+    joined = jnp.concatenate([host.reshape(-1, width).astype(kind), flat.reshape(-1, width)])
+    summed = lax.psum((joined,) + tuple(member.astype(kind) for member in big[1:]), axes)
+    joined = summed[0].astype(jnp.float32)
+    pieces = [joined[: host.size // width].reshape(host.shape)]
+    pieces += [member.astype(jnp.float32) for member in summed[1:]]
+    packed = joined[host.size // width :].reshape(-1)
     start = 0
-    for member in members:
-        pieces.append(total[start : start + member.size].reshape(member.shape))
+    for member in small:
+        pieces.append(packed[start : start + member.size].reshape(member.shape))
         start += member.size
     return tuple(pieces)
 
 
 def reduce_grads(head_part, shared_part):
-    head_sum = psum_flat(head_part, "seq", jnp.bfloat16)
-    shared_sum = psum_flat(shared_part, ("seq", "head"), jnp.float32)
+    head_sum = psum_packed(head_part[:3], head_part[3:], "seq", jnp.bfloat16)
+    shared = psum_packed(
+        (shared_part[1],), (shared_part[0],) + shared_part[2:], ("seq", "head"), jnp.float32
+    )
+    shared_sum = (shared[1], shared[0]) + shared[2:]
     return (head_sum, shared_sum)
 
 

time: 1690 us -> 1660 us (0.982)
  local copies, waits for them, and re-layouts: 392 us -> 247 us
  waiting for transfers between devices: 245 us -> 363 us
    concatenate x1, local copies, waits for them, and re-layouts: 122 us -> 0.09 us  [psum_packed(): jnp.concatenate([member.reshape(-1).astype(kind) for member in small])]
    psum x2, waiting for transfers between devices: 138 us -> 258 us  [psum_packed(): lax.psum((joined,) + tuple((member.astype(kind) for member in big[1:])),...]
    another operation x34 -> x30, local copies, waits for them, and re-layouts: 24.4 us -> 3.77 us  [the longest x1 9.25 us: on_device(): head_total[0][None]]
    unnamed x942 -> x953, local copies, waits for them, and re-layouts: 73.8 us -> 74.7 us
  transfers between devices with their start and end apart: 22 -> 22, of which waited for: 7 -> 8; matrix products, arithmetic and copies ran while one was open for 34% -> 26% of each run, Pallas kernels for 7% -> 7%
where the time goes in v5:
time: 1660 us; the launch traced here: 1640 us
  waiting for transfers between devices  363 us (22%)
  matrix products  354 us (21%)
  Pallas kernels  308 us (19%)
  other arithmetic  256 us (15%)
  local copies, waits for them, and re-layouts  247 us (15%)
  blocking collectives  63.3 us (4%)
  starting transfers between devices  32.9 us (2%)
  between operations  20.9 us (1%)
    psum x2, waiting for transfers between devices, psum_packed(): lax.psum((joined,) + tuple((member.astype(kind) for member in big[1:])),...  258 us
    pallas_call x6, Pallas kernels, head_scatter(): pl.pallas_call(functools.partial(scatter_body, n, tick), out_shape=jax.Sh...  168 us
    pallas_call x6, Pallas kernels, head_gather(): pl.pallas_call(functools.partial(gather_body, n, tick), out_shape=jax.Sha...  140 us
    dot_general x9, matrix products, block_output(): jnp.einsum('cijh,cjhp->cihp', weights, x_blocks, precision=highest)  102 us
    all_gather x6, waiting for transfers between devices, gather_flat(): everything = lax.all_gather(jnp.concatenate(slabs, axis=0), axis)  75 us
    unnamed x953, local copies, waits for them, and re-layouts  74.7 us
    dot_general x3, matrix products, mixer_forward(): projected = jnp.dot(gathered, w_main, preferred_element_type=jnp.float32)  38.1 us
    psum x3, blocking collectives, mixer_forward(): square_total = lax.psum(jnp.sum(gated_mix * gated_mix, axis=-1), 'head')  35 us
  transfers between devices with their start and end apart: 22, of which 8 were waited for; matrix products, arithmetic and copies ran while one was open for 26% of the time, Pallas kernels for 7%

profile of v5, /device:TPU:0, one launch (start us, length us, event | category | flops | bytes accessed | tf_op | source)
XLA Modules:
  0.0 1644.6 jit_solution(3596844521175508970)
XLA Ops:
  20.9 29.3 %shard_map.297 = bf16[4,128,2048]{2,1,0:T(8,128)(2,1)} custom-call(bf16[128,2048]{1,0:T(8,128)(2,1)} %fusion.223.x_ref), custom_call_target="tpu_custom_call" | custom-call | tf_op jit(solution)/shard_map/pallas_call | solution.py:112
  50.5 12.7 fusion.378
  111.2 21.2 %all-gather.13.cloned.1.call-done = f32[4128,128]{1,0:T(8,128)} async-done(((f32[1032,128]{1,0:T(8,128)}), f32[4128,128]{1,0:T(8,128)}) %all-gather.13.cloned.1.call-update) | async-done | bytes 2113552 | tf_op jit(solution)/shard_map/all_gather | solution.py:245
  137.9 9.4 fusion.132
  147.3 13.7 copy.524
  164.2 11.7 psum.77
  177.5 6.9 fusion.39.p_ref
  184.4 36.8 %shard_map.298 = f32[128,2048]{1,0:T(8,128)} custom-call(f32[4,128,2048]{2,1,0:T(8,128)} %fusion.39.p_ref), custom_call_target="tpu_custom_call" | custom-call | tf_op jit(solution)/shard_map/pallas_call | solution.py:208
  229.6 43.4 %shard_map.299 = bf16[4,128,2048]{2,1,0:T(8,128)(2,1)} custom-call(bf16[128,2048]{1,0:T(8,128)(2,1)} %multiply_convert_fusion.7.x_ref), custom_call_target="tpu_custom_call" | custom-call | tf_op jit(solution)/shard_map/pallas_call | solution.py:112
  273.1 12.9 fusion.377
  301.6 9.9 fusion.110
  338.4 18.6 %all-gather.15.cloned.1.call-done = f32[4128,128]{1,0:T(8,128)} async-done(((f32[1032,128]{1,0:T(8,128)}), f32[4128,128]{1,0:T(8,128)}) %all-gather.15.cloned.1.call-update) | async-done | bytes 2113552 | tf_op jit(solution)/shard_map/all_gather | solution.py:245
  361.8 9.4 fusion.131
  376.3 11.7 psum.78
  391.5 6.9 fusion.37.p_ref
  398.4 46.7 %shard_map.300 = f32[128,2048]{1,0:T(8,128)} custom-call(f32[4,128,2048]{2,1,0:T(8,128)} %fusion.37.p_ref), custom_call_target="tpu_custom_call" | custom-call | tf_op jit(solution)/shard_map/pallas_call | solution.py:208
  456.5 12.5 fusion.376
  524.9 29.5 %all-gather.17.cloned.1.call-done = f32[4128,128]{1,0:T(8,128)} async-done(((f32[1032,128]{1,0:T(8,128)}), f32[4128,128]{1,0:T(8,128)}) %all-gather.17.cloned.1.call-update) | async-done | bytes 2113552 | tf_op jit(solution)/shard_map/all_gather | solution.py:245
  559.2 9.4 fusion.130
  575.0 11.7 psum.79
  586.6 7.9 multiply_reduce_fusion.20
  594.5 8.3 psum.80
  602.9 6.9 multiply_reduce_fusion.23
  619.1 15.5 fusion.29
  657.3 5.7 fusion.421
  674.3 9.2 fusion.126
  687.9 5.7 multiply_reduce_fusion.14
  713.2 5.2 reduce-window.115
  739.0 5.7 convolution_add_fusion.2
  753.6 11.0 fusion.250
  768.4 28.8 %collective-permute-done.9 = bf16[128,2048]{1,0:T(8,128)(2,1)S(1)} collective-permute-done((bf16[128,2048]{1,0:T(8,128)(2,1)S(1)}, bf16[128,2048]{1,0:T(8,128)(2,1)S(1)}, u32[]{:S(2)}, u32[]{:S(2)}) %collective-permute-start.9) | collective-permute-done | bytes 524320 | tf_op jit(solution)/shard_map/ppermute | solution.py:235
  798.9 33.2 %shard_map.305 = bf16[4,128,2048]{2,1,0:T(8,128)(2,1)} custom-call(bf16[128,2048]{1,0:T(8,128)(2,1)} %fusion.241.x_ref), custom_call_target="tpu_custom_call" | custom-call | tf_op jit(solution)/shard_map/pallas_call | solution.py:112
  832.1 8.0 multiply_reduce_fusion.19
  840.2 10.5 psum.81
  850.7 5.4 multiply_reduce_fusion.22
  864.9 15.4 fusion.31
  891.9 5.7 fusion.422
  908.6 8.9 fusion.122
  921.9 6.5 multiply_reduce_fusion.10
  946.5 5.2 reduce-window.119
  972.5 5.7 convolution_add_fusion.1
  978.2 37.8 %shard_map.306 = f32[128,2048]{1,0:T(8,128)} custom-call(f32[4,128,2048]{2,1,0:T(8,128)} %bitcast.950), custom_call_target="tpu_custom_call" | custom-call | tf_op jit(solution)/shard_map/pallas_call | solution.py:208
  1021.2 11.0 fusion.248
  1037.8 28.3 %shard_map.307 = bf16[4,128,2048]{2,1,0:T(8,128)(2,1)} custom-call(bf16[128,2048]{1,0:T(8,128)(2,1)} %fusion.242.x_ref), custom_call_target="tpu_custom_call" | custom-call | tf_op jit(solution)/shard_map/pallas_call | solution.py:112
  1066.2 8.0 multiply_reduce_fusion.18
  1074.2 9.4 psum.82
  1083.7 6.0 multiply_reduce_fusion.21
  1093.4 5.2 fusion.217
  1098.7 15.4 fusion.33
  1124.1 10.6 add_convert_fusion
  1140.8 5.8 all-gather.23.cloned.1.call-done
  1157.5 9.3 fusion.118
  1171.5 6.4 multiply_reduce_fusion.6
  1198.7 5.2 reduce-window.145
  1219.5 5.2 fusion.247
  1224.7 5.7 convolution_add_fusion
  1230.4 38.9 %shard_map.308 = f32[128,2048]{1,0:T(8,128)} custom-call(f32[4,128,2048]{2,1,0:T(8,128)} %bitcast.951), custom_call_target="tpu_custom_call" | custom-call | tf_op jit(solution)/shard_map/pallas_call | solution.py:208
  1277.4 12.5 fusion.246
  1293.5 20.8 %fusion.5 = (bf16[2048,1024]{0,1:T(8,128)(2,1)S(1)}, bf16[1,2048,1024]{1,2,0:T(8,128)(2,1)}) fusion(f32[2048,2064]{0,1:T(8,128)} %fusion.246, f32[2048,2064]{0,1:T(8,128)} %fusion.248, f32[2048,2064]{0,1:T(8,128)} %fusion.250, f32[]{:T(128)} %bitcast.229, f32[]{:T(128)S(6)} %convert_element_type.707, f32[]{:T(128)S(6)} %convert_element_type.706, ...), kind=kLoop, calls=%fused_computation.12 | loop fusion | flops 27262976 | bytes 58720272 | tf_op jit(solution)/shard_map/convert_element_type | solution.py:600
  1320.6 6.5 fusion.35.p_ref
  1339.1 87.4 %all-reduce.76.cloned.1.call-done = f32[2064,256]{1,0:T(8,128)} async-done(((f32[2064,256]{1,0:T(8,128)}), f32[2064,256]{1,0:T(8,128)}) %all-reduce.76.cloned.1.call-update) | async-done | bytes 2113552 | tf_op jit(solution)/shard_map/psum | solution.py:601
  1438.4 170.2 %all-reduce.80.cloned.1.call-done = (bf16[1,2048,1024]{1,2,0:T(8,128)(2,1)}, bf16[2064,1024]{0,1:T(8,128)(2,1)}, bf16[1,2048,16]{1,2,0:T(8,128)(2,1)}) async-done(((bf16[1,2048,1024]{1,2,0:T(8,128)(2,1)}, bf16[2064,1024]{0,1:T(8,128)(2,1)}, bf16[1,2048,16]{1,2,0:T(8,128)(2,1)}), (bf16[1,2048,1024]{1,2,0:T(8,128)(2,1)}, bf16[2064,1024]{0,1:T(8,128)(2,1)}, ...) | async-done | bytes 8486928 | tf_op jit(solution)/shard_map/psum | solution.py:601
  1619.5 9.2 copy.632
  1629.6 6.9 copy.633
  (1484 shorter events, 523.7 us)
Async XLA Ops:
  7.2 43.0 %copy-start.232 = (bf16[1,2048,16]{1,2,0:T(8,128)(2,1)S(1)}, bf16[1,2048,16]{1,2,0:T(8,128)(2,1)}, u32[]{:S(2)}) copy-start(bf16[1,2048,16]{1,2,0:T(8,128)(2,1)} %param.27) | copy-start | bytes 196612
  7.2 43.3 %copy-start.58 = (bf16[1,2048,256]{2,1,0:T(8,128)(2,1)S(1)}, bf16[1,2048,256]{2,1,0:T(8,128)(2,1)}, u32[]{:S(2)}) copy-start(bf16[1,2048,256]{2,1,0:T(8,128)(2,1)} %param.26) | copy-start | bytes 3145732
  7.2 125.2 %all-gather.13.cloned.1.call-start = ((), (), s32[]{:S(2)}) async-start(), calls=%async_computation.2 | async-start | bytes 2641920 | tf_op jit(solution)/shard_map/all_gather | solution.py:245
  8.7 72.1 %collective-permute-start = (f32[3]{0:T(128)S(1)}, f32[3]{0:T(128)S(1)}, u32[]{:S(2)}, u32[]{:S(2)}) collective-permute-start(f32[3]{0:T(128)S(1)} %slice.709), channel_id=1, source_target_pairs={{0,4},{4,8},{8,12},{1,5},{5,9},{9,13},{2,6},{6,10},{10,14},{3,7},{... | collective-permute-start | bytes 44 | tf_op jit(solution)/shard_map/ppermute | solution.py:235
  13.7 67.2 %collective-permute-start.3 = (f32[3]{0:T(128)S(1)}, f32[3]{0:T(128)S(1)}, u32[]{:S(2)}, u32[]{:S(2)}) collective-permute-start(f32[3]{0:T(128)S(1)} %slice.749), channel_id=1, source_target_pairs={{0,4},{4,8},{8,12},{1,5},{5,9},{9,13},{2,6},{6,10},{10,14},{3,7},{... | collective-permute-start | bytes 44 | tf_op jit(solution)/shard_map/ppermute | solution.py:235
  18.8 31.3 %copy-start.397 = (f32[128]{0:T(128)}, f32[128]{0:T(128)S(1)}, u32[]{:S(2)}) copy-start(f32[128]{0:T(128)S(1)} %get-tuple-element.359) | copy-start | bytes 1540
  65.9 16.4 collective-permute-start.1
  73.0 25.6 %copy-start.164 = (f32[512,16]{0,1:T(8,128)}, f32[512,16]{0,1:T(8,128)S(1)}, u32[]{:S(2)}) copy-start(f32[512,16]{0,1:T(8,128)S(1)} %get-tuple-element.232) | copy-start | bytes 98308
  80.8 57.0 %copy-start.198 = (f32[2,256,16]{1,2,0:T(8,128)}, f32[2,256,16]{1,2,0:T(8,128)S(1)}, u32[]{:S(2)}) copy-start(f32[2,256,16]{1,2,0:T(8,128)S(1)} %get-tuple-element.308) | copy-start | bytes 98308
  92.4 45.4 %copy-start.9 = (f32[2,256,16,64]{1,0,3,2:T(2,128)}, f32[2,256,16,64]{1,0,3,2:T(2,128)S(1)}, u32[]{:S(2)}) copy-start(f32[2,256,16,64]{1,0,3,2:T(2,128)S(1)} %reshape.1632) | copy-start | bytes 6291460
  98.5 258.4 %all-gather.15.cloned.1.call-start = ((), (), s32[]{:S(2)}) async-start(), calls=%async_computation.3 | async-start | bytes 2641920 | tf_op jit(solution)/shard_map/all_gather | solution.py:245
  100.7 33.2 %copy-start.343 = (s32[1,2,2,128]{3,2,1,0:T(2,128)}, s32[1,2,2,128]{3,2,1,0:T(2,128)S(1)}, u32[]{:S(2)}) copy-start(s32[1,2,2,128]{3,2,1,0:T(2,128)S(1)} %add_bitcast_fusion.12) | copy-start | bytes 6148
  106.9 28.9 %copy-start.135 = (f32[2,256,128]{2,1,0:T(8,128)}, f32[2,256,128]{2,1,0:T(8,128)S(1)}, u32[]{:S(2)}) copy-start(f32[2,256,128]{2,1,0:T(8,128)S(1)} %copy.514) | copy-start | bytes 786436
  184.4 38.4 %copy-start.52 = (bf16[2,128,2048]{2,1,0:T(8,128)(2,1)S(1)}, bf16[2,128,2048]{2,1,0:T(8,128)(2,1)}, u32[]{:S(2)}) copy-start(bf16[2,128,2048]{2,1,0:T(8,128)(2,1)} %param.19) | copy-start | bytes 3145732
  224.1 3.7 collective-permute-start.2
  227.0 68.4 %copy-start.298 = (f32[2,256]{1,0:T(2,128)}, f32[2,256]{1,0:T(2,128)S(1)}, u32[]{:S(2)}) copy-start(f32[2,256]{1,0:T(2,128)S(1)} %get-tuple-element.369) | copy-start | bytes 6148
  227.0 68.4 %copy-start.333 = (f32[2,256]{1,0:T(2,128)}, f32[2,256]{1,0:T(2,128)S(1)}, u32[]{:S(2)}) copy-start(f32[2,256]{1,0:T(2,128)S(1)} %get-tuple-element.370) | copy-start | bytes 6148
  227.8 73.8 %copy-start.276 = (f32[512]{0:T(512)}, f32[512]{0:T(512)S(1)}, u32[]{:S(2)}) copy-start(f32[512]{0:T(512)S(1)} %get-tuple-element.334) | copy-start | bytes 6148
  227.8 73.8 %copy-start.278 = (f32[512]{0:T(512)}, f32[512]{0:T(512)S(1)}, u32[]{:S(2)}) copy-start(f32[512]{0:T(512)S(1)} %get-tuple-element.335) | copy-start | bytes 6148
  227.8 73.8 %copy-start.280 = (f32[512]{0:T(512)}, f32[512]{0:T(512)S(1)}, u32[]{:S(2)}) copy-start(f32[512]{0:T(512)S(1)} %get-tuple-element.336) | copy-start | bytes 6148
  228.0 217.0 %copy-start.29 = (f32[128,2048]{1,0:T(8,128)}, f32[128,2048]{1,0:T(8,128)S(1)}, u32[]{:S(2)}) copy-start(f32[128,2048]{1,0:T(8,128)S(1)} %get-tuple-element.224) | copy-start | bytes 3145732
  228.6 57.3 %copy-start.419 = (f32[128]{0:T(128)}, f32[128]{0:T(128)S(1)}, u32[]{:S(2)}) copy-start(f32[128]{0:T(128)S(1)} %get-tuple-element.361) | copy-start | bytes 1540
  288.4 41.4 %copy-start.166 = (f32[512,16]{0,1:T(8,128)}, f32[512,16]{0,1:T(8,128)S(1)}, u32[]{:S(2)}) copy-start(f32[512,16]{0,1:T(8,128)S(1)} %get-tuple-element.220) | copy-start | bytes 98308
  292.1 9.2 collective-permute-start.4
  295.6 22.0 %copy-start.200 = (f32[2,256,16]{1,2,0:T(8,128)}, f32[2,256,16]{1,2,0:T(8,128)S(1)}, u32[]{:S(2)}) copy-start(f32[2,256,16]{1,2,0:T(8,128)S(1)} %get-tuple-element.307) | copy-start | bytes 98308
  295.6 66.2 %copy-start.202 = (f32[2,256,16]{1,2,0:T(8,128)}, f32[2,256,16]{1,2,0:T(8,128)S(1)}, u32[]{:S(2)}) copy-start(f32[2,256,16]{1,2,0:T(8,128)S(1)} %get-tuple-element.306) | copy-start | bytes 98308
  316.5 45.2 %copy-start.12 = (f32[2,256,16,64]{1,0,3,2:T(2,128)}, f32[2,256,16,64]{1,0,3,2:T(2,128)S(1)}, u32[]{:S(2)}) copy-start(f32[2,256,16,64]{1,0,3,2:T(2,128)S(1)} %reshape.1646) | copy-start | bytes 6291460
  323.6 230.9 %all-gather.17.cloned.1.call-start = ((), (), s32[]{:S(2)}) async-start(), calls=%async_computation.4 | async-start | bytes 2641920 | tf_op jit(solution)/shard_map/all_gather | solution.py:245
  323.7 125.6 %collective-permute-start.6 = (f32[3]{0:T(128)S(1)}, f32[3]{0:T(128)S(1)}, u32[]{:S(2)}, u32[]{:S(2)}) collective-permute-start(f32[3]{0:T(128)S(1)} %slice.785), channel_id=1, source_target_pairs={{0,4},{4,8},{8,12},{1,5},{5,9},{9,13},{2,6},{6,10},{10,14},{3,7},{... | collective-permute-start | bytes 44 | tf_op jit(solution)/shard_map/ppermute | solution.py:235
  333.1 26.3 %copy-start.423 = (f32[16]{0:T(128)S(1)}, f32[16]{0:T(128)}, u32[]{:S(2)}) copy-start(f32[16]{0:T(128)} %get-tuple-element.355) | copy-start | bytes 196
  334.2 25.6 %copy-start.138 = (f32[2,256,128]{2,1,0:T(8,128)}, f32[2,256,128]{2,1,0:T(8,128)S(1)}, u32[]{:S(2)}) copy-start(f32[2,256,128]{2,1,0:T(8,128)S(1)} %copy.531) | copy-start | bytes 786436
  398.4 46.7 %copy-start.130 = (f32[1,128,2048]{2,1,0:T(8,128)S(1)}, f32[1,128,2048]{2,1,0:T(8,128)}, u32[]{:S(2)}) copy-start(f32[1,128,2048]{2,1,0:T(8,128)} %constant_dynamic-slice_fusion.3) | copy-start | bytes 3145732
  447.9 3.8 collective-permute-start.5
  449.3 23.7 %copy-start.436 = (f32[2]{0:T(128)}, f32[2]{0:T(128)S(1)}, u32[]{:S(2)}) copy-start(f32[2]{0:T(128)S(1)} %fusion.333) | copy-start | bytes 28
  450.2 32.5 %copy-start.282 = (f32[512]{0:T(512)}, f32[512]{0:T(512)S(1)}, u32[]{:S(2)}) copy-start(f32[512]{0:T(512)S(1)} %get-tuple-element.328) | copy-start | bytes 6148
  450.2 32.5 %copy-start.284 = (f32[512]{0:T(512)}, f32[512]{0:T(512)S(1)}, u32[]{:S(2)}) copy-start(f32[512]{0:T(512)S(1)} %get-tuple-element.329) | copy-start | bytes 6148
  450.2 32.5 %copy-start.286 = (f32[512]{0:T(512)}, f32[512]{0:T(512)S(1)}, u32[]{:S(2)}) copy-start(f32[512]{0:T(512)S(1)} %get-tuple-element.330) | copy-start | bytes 6148
  473.9 8.4 collective-permute-start.7
  492.4 173.6 %copy-start.15 = (f32[2,256,16,64]{1,0,3,2:T(2,128)}, f32[2,256,16,64]{1,0,3,2:T(2,128)S(1)}, u32[]{:S(2)}) copy-start(f32[2,256,16,64]{1,0,3,2:T(2,128)S(1)} %reshape.1660) | copy-start | bytes 6291460
  498.5 164.5 %all-gather.19.cloned.1.call-start = ((), (), s32[]{:S(2)}) async-start(), calls=%async_computation.5 | async-start | bytes 1320960 | tf_op jit(solution)/shard_map/all_gather | solution.py:245
  519.7 37.1 %copy-start.89 = (f32[2,16,64,128]{3,2,1,0:T(8,128)S(1)}, f32[2,16,64,128]{3,2,1,0:T(8,128)}, u32[]{:S(2)}) copy-start(f32[2,16,64,128]{3,2,1,0:T(8,128)} %copy-done.88) | copy-start | bytes 3145732
  519.7 37.1 %copy-start.424 = (f32[16]{0:T(128)S(1)}, f32[16]{0:T(128)}, u32[]{:S(2)}) copy-start(f32[16]{0:T(128)} %get-tuple-element.353) | copy-start | bytes 196
  619.0 278.7 %all-gather.21.cloned.1.call-start = ((), (), s32[]{:S(2)}) async-start(), calls=%async_computation.6 | async-start | bytes 1320960 | tf_op jit(solution)/shard_map/all_gather | solution.py:245
  693.6 33.1 %copy-start.240 = (f32[1280]{0:T(1024)}, f32[1280]{0:T(1024)S(1)}, u32[]{:S(2)}) copy-start(f32[1280]{0:T(1024)S(1)} %get-tuple-element.136) | copy-start | bytes 15364
  706.6 20.7 %collective-permute-start.8 = (f32[3,1280]{1,0:T(4,128)}, f32[3,1280]{1,0:T(4,128)}, u32[]{:S(2)}, u32[]{:S(2)}) collective-permute-start(f32[3,1280]{1,0:T(4,128)} %copy.573), channel_id=1, source_target_pairs={{4,0},{8,4},{12,8},{5,1},{9,5},{13,9},{6,2},{10,6},{14,10},{7,3},{... | collective-permute-start | bytes 46088 | tf_op jit(solution)/shard_map/ppermute | solution.py:235
  752.2 45.0 %collective-permute-start.9 = (bf16[128,2048]{1,0:T(8,128)(2,1)S(1)}, bf16[128,2048]{1,0:T(8,128)(2,1)S(1)}, u32[]{:S(2)}, u32[]{:S(2)}) collective-permute-start(bf16[128,2048]{1,0:T(8,128)(2,1)S(1)} %get-tuple-element.197), channel_id=1, source_target_pairs={{16,0},{17,1},{18,2},{19,3},{20,4},{21,5},{22,6},{23,7},{24,8},{25... | collective-permute-start | bytes 1572872 | tf_op jit(solution)/shard_map/ppermute | solution.py:235
  768.4 63.7 %copy-start.348 = (f32[512]{0:T(512)S(1)}, f32[512]{0:T(512)}, u32[]{:S(2)}) copy-start(f32[512]{0:T(512)} %copy-done.347) | copy-start | bytes 6148
  864.2 282.4 %all-gather.23.cloned.1.call-start = ((), (), s32[]{:S(2)}) async-start(), calls=%async_computation.7 | async-start | bytes 1320960 | tf_op jit(solution)/shard_map/all_gather | solution.py:245
  940.7 20.2 %collective-permute-start.10 = (f32[3,1280]{1,0:T(4,128)S(1)}, f32[3,1280]{1,0:T(4,128)}, u32[]{:S(2)}, u32[]{:S(2)}) collective-permute-start(f32[3,1280]{1,0:T(4,128)S(1)} %copy.596), channel_id=1, source_target_pairs={{4,0},{8,4},{12,8},{5,1},{9,5},{13,9},{6,2},{10,6},{14,10},{7,3},{... | collective-permute-start | bytes 46088 | tf_op jit(solution)/shard_map/ppermute | solution.py:235
  978.2 37.8 %copy-start.30 = (f32[128,2048]{1,0:T(8,128)S(1)}, f32[128,2048]{1,0:T(8,128)}, u32[]{:S(2)}) copy-start(f32[128,2048]{1,0:T(8,128)} %copy-done.29) | copy-start | bytes 3145732
  978.2 37.8 %copy-start.420 = (f32[128]{0:T(128)S(1)}, f32[128]{0:T(128)}, u32[]{:S(2)}) copy-start(f32[128]{0:T(128)} %copy-done.419) | copy-start | bytes 1540
  978.2 40.0 %copy-start.66 = (bf16[2,128,2048]{2,1,0:T(8,128)(2,1)S(1)}, bf16[2,128,2048]{2,1,0:T(8,128)(2,1)}, u32[]{:S(2)}) copy-start(bf16[2,128,2048]{2,1,0:T(8,128)(2,1)} %param.20) | copy-start | bytes 3145732
  978.2 40.0 %copy-start.157 = (bf16[128,2048]{1,0:T(8,128)(2,1)S(1)}, bf16[128,2048]{1,0:T(8,128)(2,1)}, u32[]{:S(2)}) copy-start(bf16[128,2048]{1,0:T(8,128)(2,1)} %copy-done.156) | copy-start | bytes 1572868
  978.2 40.0 %copy-start.443 = (f32[128]{0:T(128)S(1)}, f32[128]{0:T(128)}, u32[]{:S(2)}) copy-start(f32[128]{0:T(128)} %get-tuple-element.360) | copy-start | bytes 1540
  1019.7 16.4 collective-permute-start.11
  1036.1 30.1 %copy-start.346 = (f32[512]{0:T(512)S(1)}, f32[512]{0:T(512)}, u32[]{:S(2)}) copy-start(f32[512]{0:T(512)} %copy-done.345) | copy-start | bytes 6148
  1118.0 173.7 %all-reduce.78.cloned.1.call-start = ((), (), s32[]{:S(2)}) async-start(), calls=%async_computation.1 | async-start | bytes 8388608 | tf_op jit(solution)/shard_map/psum | solution.py:716
  1134.7 291.8 %all-reduce.76.cloned.1.call-start = ((), (), s32[]{:S(2)}) async-start(), calls=%async_computation | async-start | bytes 4227072 | tf_op jit(solution)/shard_map/psum | solution.py:601
  1192.1 20.9 %collective-permute-start.12 = (f32[3,1280]{1,0:T(4,128)}, f32[3,1280]{1,0:T(4,128)}, u32[]{:S(2)}, u32[]{:S(2)}) collective-permute-start(f32[3,1280]{1,0:T(4,128)} %copy.618), channel_id=1, source_target_pairs={{4,0},{8,4},{12,8},{5,1},{9,5},{13,9},{6,2},{10,6},{14,10},{7,3},{... | collective-permute-start | bytes 46088 | tf_op jit(solution)/shard_map/ppermute | solution.py:235
  1230.4 38.9 %copy-start.54 = (bf16[2,128,2048]{2,1,0:T(8,128)(2,1)S(1)}, bf16[2,128,2048]{2,1,0:T(8,128)(2,1)}, u32[]{:S(2)}) copy-start(bf16[2,128,2048]{2,1,0:T(8,128)(2,1)} %param.19) | copy-start | bytes 3145732
  1230.4 38.9 %copy-start.398 = (f32[128]{0:T(128)S(1)}, f32[128]{0:T(128)}, u32[]{:S(2)}) copy-start(f32[128]{0:T(128)} %copy-done.397) | copy-start | bytes 1540
  1230.4 40.5 %copy-start.302 = (f32[2048]{0:T(1024)S(1)}, f32[2048]{0:T(1024)}, u32[]{:S(2)}) copy-start(f32[2048]{0:T(1024)} %get-tuple-element.150) | copy-start | bytes 24580
  1230.4 40.5 %copy-start.303 = (f32[2048]{0:T(1024)S(1)}, f32[2048]{0:T(1024)}, u32[]{:S(2)}) copy-start(f32[2048]{0:T(1024)} %get-tuple-element.152) | copy-start | bytes 24580
  1289.9 318.7 %all-reduce.80.cloned.1.call-start = ((), (), s32[]{:S(2)}) async-start(), calls=%async_computation.8 | async-start | bytes 17432576 | tf_op jit(solution)/shard_map/psum | solution.py:601
  (417 other events, 2435.3 us)
Sparse Core Ops, SparseCore 0:
  98.7 33.6 all-gather.12
  323.7 33.2 all-gather.14
  498.6 55.7 all-gather.16
  619.1 35.7 all-gather.18
  864.3 32.4 all-gather.20
  1118.1 28.4 all-gather.22
  1149.8 104.2 all-reduce.77
  1290.0 136.4 all-reduce.75
  1431.0 177.4 all-reduce.79

commit v6 on v3

--- a/solution.py
+++ b/solution.py
@@ -583,8 +583,12 @@
     head_sum = tuple(
         lax.psum(member.astype(jnp.bfloat16), "seq").astype(jnp.float32) for member in head_part
     )
-    shared_sum = lax.psum(tuple(shared_part), ("seq", "head"))
-    return (head_sum, tuple(shared_sum))
+    shared_sum = lax.psum(
+        (shared_part[0], shared_part[1].astype(jnp.bfloat16)) + tuple(shared_part[2:]),
+        ("seq", "head"),
+    )
+    shared_sum = (shared_sum[0], shared_sum[1].astype(jnp.float32)) + tuple(shared_sum[2:])
+    return (head_sum, shared_sum)
 
 
 def store_slot(buffer, value, slot_index, is_valid):

time: 1580 us -> 1570 us (level)
  waiting for transfers between devices: 222 us -> 202 us
    psum x1, waiting for transfers between devices: 92.8 us -> 0.01 us  [reduce_grads(): lax.psum((shared_part[0], shared_part[1].astype(jnp.bfloat16)) + tuple(sh...]
    psum x1, waiting for transfers between devices: 0.01 us -> 83.1 us  [reduce_grads(): lax.psum(member.astype(jnp.bfloat16), 'seq').astype(jnp.float32)]
    unnamed x833 -> x804, local copies, waits for them, and re-layouts: 75 us -> 65.7 us
where the time goes in v6:
time: 1570 us; the launch traced here: 1560 us
  matrix products  347 us (22%)
  Pallas kernels  332 us (21%)
  other arithmetic  254 us (16%)
  waiting for transfers between devices  202 us (13%)
  blocking collectives  197 us (13%)
  local copies, waits for them, and re-layouts  174 us (11%)
  starting transfers between devices  34.2 us (2%)
  between operations  20.1 us (1%)
    pallas_call x6, Pallas kernels, head_scatter(): pl.pallas_call(functools.partial(scatter_body, n, tick), out_shape=jax.Sh...  193 us
    pallas_call x6, Pallas kernels, head_gather(): pl.pallas_call(functools.partial(gather_body, n, tick), out_shape=jax.Sha...  139 us
    dot_general x9, matrix products, block_output(): jnp.einsum('cijh,cjhp->cihp', weights, x_blocks, precision=highest)  101 us
    psum x1, waiting for transfers between devices, reduce_grads(): lax.psum(member.astype(jnp.bfloat16), 'seq').astype(jnp.float32)  83.1 us
    psum x1, blocking collectives, reduce_grads(): lax.psum((shared_part[0], shared_part[1].astype(jnp.bfloat16)) + tuple(sh...  73.4 us
    unnamed x804, local copies, waits for them, and re-layouts  65.7 us
    dot_general x3, matrix products, mixer_forward(): projected = jnp.dot(gathered, w_main, preferred_element_type=jnp.float32)  38.1 us
    psum x3, blocking collectives, mixer_forward(): square_total = lax.psum(jnp.sum(gated_mix * gated_mix, axis=-1), 'head')  35.1 us
  transfers between devices with their start and end apart: 22, of which 10 were waited for; matrix products, arithmetic and copies ran while one was open for 24% of the time, Pallas kernels for 8%

profile of v6, /device:TPU:0, one launch (start us, length us, event | category | flops | bytes accessed | tf_op | source)
XLA Modules:
  0.0 1560.2 jit_solution(12255274290102451529)
XLA Ops:
  20.9 29.3 %shard_map.297 = bf16[4,128,2048]{2,1,0:T(8,128)(2,1)} custom-call(bf16[128,2048]{1,0:T(8,128)(2,1)} %fusion.226.x_ref), custom_call_target="tpu_custom_call" | custom-call | tf_op jit(solution)/shard_map/pallas_call | solution.py:112
  50.5 12.7 fusion.417
  96.5 7.1 all-gather
  117.3 12.9 all-gather.13.cloned.1.call-done
  134.8 9.4 fusion.135
  144.2 13.4 copy.510
  160.8 11.7 psum.140
  174.2 6.9 fusion.39.p_ref
  181.0 36.8 %shard_map.298 = f32[128,2048]{1,0:T(8,128)} custom-call(f32[4,128,2048]{2,1,0:T(8,128)} %fusion.39.p_ref), custom_call_target="tpu_custom_call" | custom-call | tf_op jit(solution)/shard_map/pallas_call | solution.py:208
  226.3 43.4 %shard_map.299 = bf16[4,128,2048]{2,1,0:T(8,128)(2,1)} custom-call(bf16[128,2048]{1,0:T(8,128)(2,1)} %multiply_convert_fusion.7.x_ref), custom_call_target="tpu_custom_call" | custom-call | tf_op jit(solution)/shard_map/pallas_call | solution.py:112
  269.7 12.9 fusion.416
  298.3 9.6 fusion.111
  326.4 6.9 all-gather.1
  342.0 10.2 all-gather.15.cloned.1.call-done
  356.9 9.4 fusion.134
  371.3 11.7 psum.141
  386.6 6.9 fusion.37.p_ref
  393.4 46.6 %shard_map.300 = f32[128,2048]{1,0:T(8,128)} custom-call(f32[4,128,2048]{2,1,0:T(8,128)} %fusion.37.p_ref), custom_call_target="tpu_custom_call" | custom-call | tf_op jit(solution)/shard_map/pallas_call | solution.py:208
  451.6 12.5 fusion.415
  491.7 7.9 all-gather.5
  505.2 7.0 all-gather.4
  513.4 7.8 all-gather.3
  521.2 7.4 all-gather.2
  538.9 8.6 all-gather.17.cloned.1.call-done
  552.0 9.4 fusion.133
  567.8 11.7 psum.142
  579.5 7.9 multiply_reduce_fusion.20
  587.4 8.3 psum.143
  595.7 6.9 multiply_reduce_fusion.23
  611.6 15.7 %fusion.29 = (f32[2,256,16]{1,2,0:T(8,128)}, f32[2,256,16]{1,2,0:T(8,128)}, f32[2,256,16]{1,2,0:T(8,128)}, f32[2,256,256]{2,1,0:T(8,128)S(1)}) fusion(f32[2,256,16]{1,2,0:T(8,128)} %bitcast.1076, f32[2,256,256]{2,1,0:T(8,128)} %fusion.453, f32[2,256,16]{1,2,0:T(8,128)} %copy-done.201, pred[2,256,256]{2,1,0:T(8,128)(4,1)} %get-tuple-element.268, ...), kind=kOutput, calls=%fused_computation.47 | convolution fusion | flops 1637720064 | bytes 5537792 | tf_op jit(solution)/shard_map/transpose(jvp(cijh,cjhp->cihp))/dot_general | solution.py:355
  640.8 19.8 %all-gather.19.cloned.1.call-done = bf16[4,16,64,128]{3,2,1,0:T(8,128)(2,1)} async-done(((bf16[1,16,64,128]{3,2,1,0:T(8,128)(2,1)}), bf16[4,16,64,128]{3,2,1,0:T(8,128)(2,1)}) %all-gather.19.cloned.1.call-update) | async-done | bytes 1048592 | tf_op jit(solution)/shard_map/all_gather | solution.py:258
  670.3 9.2 fusion.129
  683.8 6.4 multiply_reduce_fusion.13
  743.6 11.0 fusion.253
  758.3 22.3 %collective-permute-done.9 = bf16[128,2048]{1,0:T(8,128)(2,1)S(1)} collective-permute-done((bf16[128,2048]{1,0:T(8,128)(2,1)S(1)}, bf16[128,2048]{1,0:T(8,128)(2,1)S(1)}, u32[]{:S(2)}, u32[]{:S(2)}) %collective-permute-start.9) | collective-permute-done | bytes 524320 | tf_op jit(solution)/shard_map/ppermute | solution.py:235
  782.3 33.2 %shard_map.305 = bf16[4,128,2048]{2,1,0:T(8,128)(2,1)} custom-call(bf16[128,2048]{1,0:T(8,128)(2,1)} %fusion.244.x_ref), custom_call_target="tpu_custom_call" | custom-call | tf_op jit(solution)/shard_map/pallas_call | solution.py:112
  815.5 8.0 multiply_reduce_fusion.19
  823.5 10.6 psum.144
  834.2 6.0 multiply_reduce_fusion.22
  849.5 15.7 %fusion.31 = (f32[2,256,16]{1,2,0:T(8,128)}, f32[2,256,16]{1,2,0:T(8,128)}, f32[2,256,16]{1,2,0:T(8,128)}, f32[2,256,256]{2,1,0:T(8,128)S(1)}) fusion(f32[2,256,16]{1,2,0:T(8,128)S(1)} %bitcast.1075, f32[2,256,256]{2,1,0:T(8,128)} %fusion.452, f32[2,256,16]{1,2,0:T(8,128)S(1)} %copy-done.200, pred[2,256,256]{2,1,0:T(8,128)(4,1)S(1)} %copy-done.184, ...), kind=kOutput, calls=%fused_computation.49 | convolution fusion | flops 1637720064 | bytes 5537792 | tf_op jit(solution)/shard_map/transpose(jvp(cijh,cjhp->cihp))/dot_general | solution.py:355
  891.8 9.0 fusion.125
  905.2 6.4 multiply_reduce_fusion.9
  956.4 53.8 %shard_map.306 = f32[128,2048]{1,0:T(8,128)} custom-call(f32[4,128,2048]{2,1,0:T(8,128)} %bitcast.967), custom_call_target="tpu_custom_call" | custom-call | tf_op jit(solution)/shard_map/pallas_call | solution.py:208
  1015.3 10.9 fusion.251
  1031.9 28.3 %shard_map.307 = bf16[4,128,2048]{2,1,0:T(8,128)(2,1)} custom-call(bf16[128,2048]{1,0:T(8,128)(2,1)} %fusion.245.x_ref), custom_call_target="tpu_custom_call" | custom-call | tf_op jit(solution)/shard_map/pallas_call | solution.py:112
  1060.3 8.0 multiply_reduce_fusion.18
  1068.3 10.1 psum.145
  1078.5 6.0 multiply_reduce_fusion.21
  1088.3 15.6 fusion.33
  1115.0 10.3 add_convert_fusion
  1125.6 8.0 all-gather.23.cloned.1.call-done
  1143.7 7.4 fusion.121
  1195.0 6.6 fusion.249
  1209.1 32.0 %all-reduce.70.cloned.1.call-done = bf16[1024,2048]{1,0:T(8,128)(2,1)} async-done(((bf16[1024,2048]{1,0:T(8,128)(2,1)}), bf16[1024,2048]{1,0:T(8,128)(2,1)}) %all-reduce.70.cloned.1.call-update) | async-done | bytes 4194320 | tf_op jit(solution)/shard_map/psum | solution.py:688
  1243.0 21.6 %fusion.34 = (bf16[1,2048,1024]{1,2,0:T(8,128)(2,1)}, bf16[1,2048,1024]{1,2,0:T(8,128)(2,1)}) fusion(f32[2048,2064]{0,1:T(8,128)} %copy-done.48, f32[2048,2064]{0,1:T(8,128)} %fusion.251, f32[2048,2064]{0,1:T(8,128)} %fusion.253, f32[]{:T(128)S(6)} %convert_element_type.598, f32[]{:T(128)S(6)} %convert_element_type.597, f32[]{:T(128)S(6)} %convert_element_type.596, ...), kind=kLoop, calls=%fused_computation.58 | loop fusion | flops 27262976 | bytes 58720272 | tf_op jit(solution)/shard_map/broadcast_in_dim | solution.py:713
  1268.4 6.5 fusion.35.p_ref
  1286.9 15.8 %all-reduce.64 = (bf16[1,4,1024]{2,1,0:T(4,128)(2,1)S(1)}, bf16[1,1024]{1,0:T(2,128)(2,1)S(1)}, bf16[1,16]{1,0:T(2,128)(2,1)S(1)}, bf16[1,16]{1,0:T(2,128)(2,1)S...) all-reduce(bf16[1,4,1024]{2,1,0:T(4,128)(2,1)S(1)} %fusion.337, ...), channel_id=1, replica_groups=mesh['section'=2,'seq'=4,'head'=4] {'seq'}, use_global_device_ids=true, to_apply=%region_93.95 | all-reduce | flops 6192 | bytes 24768 | tf_op jit(solution)/shard_map/psum | solution.py:584
  1306.1 8.3 fusion.250
  1320.1 48.3 %shard_map.308 = f32[128,2048]{1,0:T(8,128)} custom-call(f32[4,128,2048]{2,1,0:T(8,128)} %bitcast.965), custom_call_target="tpu_custom_call" | custom-call | tf_op jit(solution)/shard_map/pallas_call | solution.py:208
  1370.2 73.4 %all-reduce.63 = (f32[1,2048]{1,0:T(1,128)}, f32[1,4,256]{2,1,0:T(4,128)}, f32[1,256]{1,0:T(1,128)}) all-reduce(f32[1,2048]{1,0:T(1,128)S(1)} %bitcast.1085, f32[1,4,256]{2,1,0:T(4,128)S(1)} %fusion.339, f32[1,256]{1,0:T(1,128)S(1)} %bitcast.1103), channel_id=1, replica_groups=mesh['section'=2,'seq'=4,'head'=4] {'seq','head'}, use_global_device_ids=true, to_apply=%region_75.77 | all-reduce | flops 3328 | bytes 26624 | tf_op jit(solution)/shard_map/psum | solution.py:586
  1449.3 6.7 bitcast_convert_fusion
  1455.9 83.1 %all-reduce.74.cloned.1.call-done = (bf16[1,2048,1024]{1,2,0:T(8,128)(2,1)}, bf16[1,2048,1024]{1,2,0:T(8,128)(2,1)}, bf16[1,2048,16]{1,2,0:T(8,128)(2,1)}) async-done(((bf16[1,2048,1024]{1,2,0:T(8,128)(2,1)}, bf16[1,2048,1024]{1,2,0:T(8,128)(2,1)}, bf16[1,2048,16]{1,2,0:T(8,128)(2,1)}), (bf16[1,2048,1024]{1,2,0:T(8,128)(2,1)}, bf16[1,2048,1024]{1,2,0:T(8,128)(2,1)}, ...) | async-done | bytes 8454160 | tf_op jit(solution)/shard_map/psum | solution.py:584
  1539.0 6.9 copy.616
  1545.9 6.9 copy.617
  (1236 shorter events, 499.2 us)
Async XLA Ops:
  7.2 43.0 %copy-start.203 = (bf16[1,2048,16]{1,2,0:T(8,128)(2,1)S(1)}, bf16[1,2048,16]{1,2,0:T(8,128)(2,1)}, u32[]{:S(2)}) copy-start(bf16[1,2048,16]{1,2,0:T(8,128)(2,1)} %param.27) | copy-start | bytes 196612
  7.2 43.3 %copy-start.55 = (bf16[1,2048,256]{2,1,0:T(8,128)(2,1)S(1)}, bf16[1,2048,256]{2,1,0:T(8,128)(2,1)}, u32[]{:S(2)}) copy-start(bf16[1,2048,256]{2,1,0:T(8,128)(2,1)} %param.26) | copy-start | bytes 3145732
  7.2 123.0 %all-gather.13.cloned.1.call-start = ((), (), s32[]{:S(2)}) async-start(), calls=%async_computation | async-start | bytes 2621440 | tf_op jit(solution)/shard_map/all_gather | solution.py:240
  8.7 70.5 %collective-permute-start = (f32[3]{0:T(128)S(1)}, f32[3]{0:T(128)S(1)}, u32[]{:S(2)}, u32[]{:S(2)}) collective-permute-start(f32[3]{0:T(128)S(1)} %slice.578), channel_id=1, source_target_pairs={{0,4},{4,8},{8,12},{1,5},{5,9},{9,13},{2,6},{6,10},{10,14},{3,7},{... | collective-permute-start | bytes 44 | tf_op jit(solution)/shard_map/ppermute | solution.py:235
  13.7 65.6 %collective-permute-start.3 = (f32[3]{0:T(128)S(1)}, f32[3]{0:T(128)S(1)}, u32[]{:S(2)}, u32[]{:S(2)}) collective-permute-start(f32[3]{0:T(128)S(1)} %slice.617), channel_id=1, source_target_pairs={{0,4},{4,8},{8,12},{1,5},{5,9},{9,13},{2,6},{6,10},{10,14},{3,7},{... | collective-permute-start | bytes 44 | tf_op jit(solution)/shard_map/ppermute | solution.py:235
  18.9 31.3 %copy-start.319 = (f32[128]{0:T(128)}, f32[128]{0:T(128)S(1)}, u32[]{:S(2)}) copy-start(f32[128]{0:T(128)S(1)} %get-tuple-element.335) | copy-start | bytes 1540
  66.0 14.8 collective-permute-start.1
  73.1 30.5 %copy-start.139 = (f32[512,16]{0,1:T(8,128)}, f32[512,16]{0,1:T(8,128)S(1)}, u32[]{:S(2)}) copy-start(f32[512,16]{0,1:T(8,128)S(1)} %get-tuple-element.229) | copy-start | bytes 98308
  79.2 55.5 %copy-start.170 = (f32[2,256,16]{1,2,0:T(8,128)}, f32[2,256,16]{1,2,0:T(8,128)S(1)}, u32[]{:S(2)}) copy-start(f32[2,256,16]{1,2,0:T(8,128)S(1)} %get-tuple-element.278) | copy-start | bytes 98308
  90.8 43.9 %copy-start.9 = (f32[2,256,16,64]{1,0,3,2:T(2,128)}, f32[2,256,16,64]{1,0,3,2:T(2,128)S(1)}, u32[]{:S(2)}) copy-start(f32[2,256,16,64]{1,0,3,2:T(2,128)S(1)} %reshape.957) | copy-start | bytes 6291460
  94.8 35.4 %copy-start.60 = (f32[2,16,64,128]{3,2,1,0:T(8,128)}, f32[2,16,64,128]{3,2,1,0:T(8,128)S(1)}, u32[]{:S(2)}) copy-start(f32[2,16,64,128]{3,2,1,0:T(8,128)S(1)} %fusion.161) | copy-start | bytes 3145732
  96.5 255.7 %all-gather.15.cloned.1.call-start = ((), (), s32[]{:S(2)}) async-start(), calls=%async_computation.1 | async-start | bytes 2621440 | tf_op jit(solution)/shard_map/all_gather | solution.py:240
  113.1 21.6 %copy-start.112 = (f32[2,256,128]{2,1,0:T(8,128)}, f32[2,256,128]{2,1,0:T(8,128)S(1)}, u32[]{:S(2)}) copy-start(f32[2,256,128]{2,1,0:T(8,128)S(1)} %copy.500) | copy-start | bytes 786436
  181.0 38.4 %copy-start.49 = (bf16[2,128,2048]{2,1,0:T(8,128)(2,1)S(1)}, bf16[2,128,2048]{2,1,0:T(8,128)(2,1)}, u32[]{:S(2)}) copy-start(bf16[2,128,2048]{2,1,0:T(8,128)(2,1)} %param.19) | copy-start | bytes 3145732
  220.7 3.7 collective-permute-start.2
  223.7 70.0 %copy-start.247 = (f32[2,256]{1,0:T(2,128)}, f32[2,256]{1,0:T(2,128)S(1)}, u32[]{:S(2)}) copy-start(f32[2,256]{1,0:T(2,128)S(1)} %get-tuple-element.345) | copy-start | bytes 6148
  223.7 70.0 %copy-start.286 = (f32[2,256]{1,0:T(2,128)}, f32[2,256]{1,0:T(2,128)S(1)}, u32[]{:S(2)}) copy-start(f32[2,256]{1,0:T(2,128)S(1)} %get-tuple-element.346) | copy-start | bytes 6148
  224.4 73.8 %copy-start.225 = (f32[512]{0:T(512)}, f32[512]{0:T(512)S(1)}, u32[]{:S(2)}) copy-start(f32[512]{0:T(512)S(1)} %get-tuple-element.289) | copy-start | bytes 6148
  224.4 73.9 %copy-start.227 = (f32[512]{0:T(512)}, f32[512]{0:T(512)S(1)}, u32[]{:S(2)}) copy-start(f32[512]{0:T(512)S(1)} %get-tuple-element.290) | copy-start | bytes 6148
  224.4 73.9 %copy-start.229 = (f32[512]{0:T(512)}, f32[512]{0:T(512)S(1)}, u32[]{:S(2)}) copy-start(f32[512]{0:T(512)S(1)} %get-tuple-element.291) | copy-start | bytes 6148
  224.7 215.4 %copy-start.25 = (f32[128,2048]{1,0:T(8,128)}, f32[128,2048]{1,0:T(8,128)S(1)}, u32[]{:S(2)}) copy-start(f32[128,2048]{1,0:T(8,128)S(1)} %get-tuple-element.221) | copy-start | bytes 3145732
  225.3 57.3 %copy-start.333 = (f32[128]{0:T(128)}, f32[128]{0:T(128)S(1)}, u32[]{:S(2)}) copy-start(f32[128]{0:T(128)S(1)} %get-tuple-element.337) | copy-start | bytes 1540
  269.7 23.4 %copy-start.331 = (f32[2]{0:T(128)S(1)}, f32[2]{0:T(128)}, u32[]{:S(2)}) copy-start(f32[2]{0:T(128)} %get-tuple-element.348) | copy-start | bytes 28
  287.2 10.8 collective-permute-start.4
  291.4 41.9 %copy-start.141 = (f32[512,16]{0,1:T(8,128)}, f32[512,16]{0,1:T(8,128)S(1)}, u32[]{:S(2)}) copy-start(f32[512,16]{0,1:T(8,128)S(1)} %get-tuple-element.217) | copy-start | bytes 98308
  293.8 63.0 %copy-start.174 = (f32[2,256,16]{1,2,0:T(8,128)}, f32[2,256,16]{1,2,0:T(8,128)S(1)}, u32[]{:S(2)}) copy-start(f32[2,256,16]{1,2,0:T(8,128)S(1)} %get-tuple-element.276) | copy-start | bytes 98308
  313.0 43.8 %copy-start.11 = (f32[2,256,16,64]{1,0,3,2:T(2,128)}, f32[2,256,16,64]{1,0,3,2:T(2,128)S(1)}, u32[]{:S(2)}) copy-start(f32[2,256,16,64]{1,0,3,2:T(2,128)S(1)} %reshape.969) | copy-start | bytes 6291460
  318.9 228.6 %all-gather.17.cloned.1.call-start = ((), (), s32[]{:S(2)}) async-start(), calls=%async_computation.2 | async-start | bytes 2621440 | tf_op jit(solution)/shard_map/all_gather | solution.py:240
  320.2 124.1 %collective-permute-start.6 = (f32[3]{0:T(128)}, f32[3]{0:T(128)}, u32[]{:S(2)}, u32[]{:S(2)}) collective-permute-start(f32[3]{0:T(128)} %slice.652), channel_id=1, source_target_pairs={{0,4},{4,8},{8,12},{1,5},{5,9},{9,13},{2,6},{6,10},{10,14},{3,7},{... | collective-permute-start | bytes 44 | tf_op jit(solution)/shard_map/ppermute | solution.py:235
  333.3 23.5 %copy-start.267 = (f32[2,2,8,256]{3,2,0,1:T(8,128)}, f32[2,2,8,256]{3,2,0,1:T(8,128)S(1)}, u32[]{:S(2)}) copy-start(f32[2,2,8,256]{3,2,0,1:T(8,128)S(1)} %copy.946) | copy-start | bytes 98308
  393.4 46.7 %copy-start.107 = (f32[1,128,2048]{2,1,0:T(8,128)S(1)}, f32[1,128,2048]{2,1,0:T(8,128)}, u32[]{:S(2)}) copy-start(f32[1,128,2048]{2,1,0:T(8,128)} %constant_dynamic-slice_fusion.3) | copy-start | bytes 3145732
  443.0 3.8 collective-permute-start.5
  444.3 28.3 %copy-start.370 = (f32[2]{0:T(128)}, f32[2]{0:T(128)S(1)}, u32[]{:S(2)}) copy-start(f32[2]{0:T(128)S(1)} %fusion.369) | copy-start | bytes 28
  445.8 31.0 %copy-start.231 = (f32[512]{0:T(512)}, f32[512]{0:T(512)S(1)}, u32[]{:S(2)}) copy-start(f32[512]{0:T(512)S(1)} %get-tuple-element.283) | copy-start | bytes 6148
  445.8 31.1 %copy-start.233 = (f32[512]{0:T(512)}, f32[512]{0:T(512)S(1)}, u32[]{:S(2)}) copy-start(f32[512]{0:T(512)S(1)} %get-tuple-element.284) | copy-start | bytes 6148
  445.8 31.1 %copy-start.235 = (f32[512]{0:T(512)}, f32[512]{0:T(512)S(1)}, u32[]{:S(2)}) copy-start(f32[512]{0:T(512)S(1)} %get-tuple-element.285) | copy-start | bytes 6148
  451.6 21.7 %copy-start.249 = (f32[2,256]{1,0:T(2,128)S(1)}, f32[2,256]{1,0:T(2,128)}, u32[]{:S(2)}) copy-start(f32[2,256]{1,0:T(2,128)} %get-tuple-element.302) | copy-start | bytes 6148
  451.6 21.7 %copy-start.288 = (f32[2,256]{1,0:T(2,128)S(1)}, f32[2,256]{1,0:T(2,128)}, u32[]{:S(2)}) copy-start(f32[2,256]{1,0:T(2,128)} %get-tuple-element.301) | copy-start | bytes 6148
  466.8 9.7 collective-permute-start.7
  486.6 175.6 %copy-start.14 = (f32[2,256,16,64]{1,0,3,2:T(2,128)}, f32[2,256,16,64]{1,0,3,2:T(2,128)S(1)}, u32[]{:S(2)}) copy-start(f32[2,256,16,64]{1,0,3,2:T(2,128)S(1)} %reshape.981) | copy-start | bytes 6291460
  490.5 57.0 %copy-start.63 = (f32[2,16,64,128]{3,2,1,0:T(8,128)}, f32[2,16,64,128]{3,2,1,0:T(8,128)S(1)}, u32[]{:S(2)}) copy-start(f32[2,16,64,128]{3,2,1,0:T(8,128)S(1)} %fusion.153) | copy-start | bytes 3145732
  491.6 169.0 %all-gather.19.cloned.1.call-start = ((), (), s32[]{:S(2)}) async-start(), calls=%async_computation.3 | async-start | bytes 1310720 | tf_op jit(solution)/shard_map/all_gather | solution.py:258
  611.6 270.6 %all-gather.21.cloned.1.call-start = ((), (), s32[]{:S(2)}) async-start(), calls=%async_computation.4 | async-start | bytes 1310720 | tf_op jit(solution)/shard_map/all_gather | solution.py:258
  701.5 16.0 %collective-permute-start.8 = (f32[3,1280]{1,0:T(4,128)}, f32[3,1280]{1,0:T(4,128)}, u32[]{:S(2)}, u32[]{:S(2)}) collective-permute-start(f32[3,1280]{1,0:T(4,128)} %copy.559), channel_id=1, source_target_pairs={{4,0},{8,4},{12,8},{5,1},{9,5},{13,9},{6,2},{10,6},{14,10},{7,3},{... | collective-permute-start | bytes 46088 | tf_op jit(solution)/shard_map/ppermute | solution.py:235
  742.1 38.5 %collective-permute-start.9 = (bf16[128,2048]{1,0:T(8,128)(2,1)S(1)}, bf16[128,2048]{1,0:T(8,128)(2,1)S(1)}, u32[]{:S(2)}, u32[]{:S(2)}) collective-permute-start(bf16[128,2048]{1,0:T(8,128)(2,1)S(1)} %get-tuple-element.196), channel_id=1, source_target_pairs={{16,0},{17,1},{18,2},{19,3},{20,4},{21,5},{22,6},{23,7},{24,8},{25... | collective-permute-start | bytes 1572872 | tf_op jit(solution)/shard_map/ppermute | solution.py:235
  758.3 57.2 %copy-start.301 = (f32[512]{0:T(512)S(1)}, f32[512]{0:T(512)}, u32[]{:S(2)}) copy-start(f32[512]{0:T(512)} %copy-done.300) | copy-start | bytes 6148
  849.4 284.3 %all-gather.23.cloned.1.call-start = ((), (), s32[]{:S(2)}) async-start(), calls=%async_computation.5 | async-start | bytes 1310720 | tf_op jit(solution)/shard_map/all_gather | solution.py:258
  922.9 16.1 %collective-permute-start.10 = (f32[3,1280]{1,0:T(4,128)}, f32[3,1280]{1,0:T(4,128)}, u32[]{:S(2)}, u32[]{:S(2)}) collective-permute-start(f32[3,1280]{1,0:T(4,128)} %copy.582), channel_id=1, source_target_pairs={{4,0},{8,4},{12,8},{5,1},{9,5},{13,9},{6,2},{10,6},{14,10},{7,3},{... | collective-permute-start | bytes 46088 | tf_op jit(solution)/shard_map/ppermute | solution.py:235
  956.4 53.8 %copy-start.26 = (f32[128,2048]{1,0:T(8,128)S(1)}, f32[128,2048]{1,0:T(8,128)}, u32[]{:S(2)}) copy-start(f32[128,2048]{1,0:T(8,128)} %copy-done.25) | copy-start | bytes 3145732
  956.4 53.8 %copy-start.334 = (f32[128]{0:T(128)S(1)}, f32[128]{0:T(128)}, u32[]{:S(2)}) copy-start(f32[128]{0:T(128)} %copy-done.333) | copy-start | bytes 1540
  956.4 56.0 %copy-start.65 = (bf16[2,128,2048]{2,1,0:T(8,128)(2,1)S(1)}, bf16[2,128,2048]{2,1,0:T(8,128)(2,1)}, u32[]{:S(2)}) copy-start(bf16[2,128,2048]{2,1,0:T(8,128)(2,1)} %param.20) | copy-start | bytes 3145732
  956.4 56.0 %copy-start.132 = (bf16[128,2048]{1,0:T(8,128)(2,1)S(1)}, bf16[128,2048]{1,0:T(8,128)(2,1)}, u32[]{:S(2)}) copy-start(bf16[128,2048]{1,0:T(8,128)(2,1)} %copy-done.131) | copy-start | bytes 1572868
  956.4 56.1 %copy-start.379 = (f32[128]{0:T(128)S(1)}, f32[128]{0:T(128)}, u32[]{:S(2)}) copy-start(f32[128]{0:T(128)} %get-tuple-element.336) | copy-start | bytes 1540
  1013.9 16.3 %collective-permute-start.11 = (bf16[128,2048]{1,0:T(8,128)(2,1)S(1)}, bf16[128,2048]{1,0:T(8,128)(2,1)S(1)}, u32[]{:S(2)}, u32[]{:S(2)}) collective-permute-start(bf16[128,2048]{1,0:T(8,128)(2,1)S(1)} %get-tuple-element.192), channel_id=1, source_target_pairs={{16,0},{17,1},{18,2},{19,3},{20,4},{21,5},{22,6},{23,7},{24,8},{25... | collective-permute-start | bytes 1572872 | tf_op jit(solution)/shard_map/ppermute | solution.py:235
  1030.2 30.1 %copy-start.299 = (f32[512]{0:T(512)S(1)}, f32[512]{0:T(512)}, u32[]{:S(2)}) copy-start(f32[512]{0:T(512)} %copy-done.298) | copy-start | bytes 6148
  1110.4 130.7 %all-reduce.70.cloned.1.call-start = ((), (), s32[]{:S(2)}) async-start(), calls=%async_computation.6 | async-start | bytes 8388608 | tf_op jit(solution)/shard_map/psum | solution.py:688
  1125.4 321.1 %all-reduce.72.cloned.1.call-start = ((), (), s32[]{:S(2)}) async-start(), calls=%async_computation.7 | async-start | bytes 2097152 | tf_op jit(solution)/shard_map/psum | solution.py:586
  1175.1 11.0 collective-permute-start.12
  1194.8 344.3 %all-reduce.74.cloned.1.call-start = ((), (), s32[]{:S(2)}) async-start(), calls=%async_computation.8 | async-start | bytes 16908288 | tf_op jit(solution)/shard_map/psum | solution.py:584
  1320.1 48.3 %copy-start.51 = (bf16[2,128,2048]{2,1,0:T(8,128)(2,1)S(1)}, bf16[2,128,2048]{2,1,0:T(8,128)(2,1)}, u32[]{:S(2)}) copy-start(bf16[2,128,2048]{2,1,0:T(8,128)(2,1)} %param.19) | copy-start | bytes 3145732
  1320.1 48.3 %copy-start.320 = (f32[128]{0:T(128)S(1)}, f32[128]{0:T(128)}, u32[]{:S(2)}) copy-start(f32[128]{0:T(128)} %copy-done.319) | copy-start | bytes 1540
  1320.1 50.1 %copy-start.251 = (f32[2048]{0:T(1024)S(1)}, f32[2048]{0:T(1024)}, u32[]{:S(2)}) copy-start(f32[2048]{0:T(1024)} %get-tuple-element.141) | copy-start | bytes 24580
  1320.1 50.1 %copy-start.252 = (f32[2048]{0:T(1024)S(1)}, f32[2048]{0:T(1024)}, u32[]{:S(2)}) copy-start(f32[2048]{0:T(1024)} %get-tuple-element.143) | copy-start | bytes 24580
  1320.1 123.5 %copy-start.378 = (f32[128]{0:T(128)S(1)}, f32[128]{0:T(128)}, u32[]{:S(2)}) copy-start(f32[128]{0:T(128)} %get-tuple-element.334) | copy-start | bytes 1540
  (352 other events, 2027.1 us)
Sparse Core Ops, SparseCore 0:
  96.6 33.5 all-gather.12
  319.0 33.1 all-gather.14
  491.8 55.6 all-gather.16
  611.7 48.9 all-gather.18
  849.5 32.5 all-gather.20
  1110.5 23.0 all-gather.22
  1136.9 104.1 all-reduce.69
  1247.3 112.3 all-reduce.71
  1364.7 174.3 all-reduce.73

commit v7 on v3

--- a/solution.py
+++ b/solution.py
@@ -1,6 +1,7 @@
 from functools import partial
 
 import functools
+import math
 
 import jax
 import jax.numpy as jnp
@@ -470,7 +471,7 @@
     return stream + branch, saved
 
 
-def mixer_backward(grad_next, layer_weights, saved, mask_value, tick, ids):
+def mixer_backward(grad_next, layer_weights, saved, mask_value, tick, ids, hook=None):
     (
         norm_gain,
         w_main,
@@ -553,8 +554,11 @@
         preferred_element_type=jnp.float32,
     )
     head_count = lax.axis_size("head")
+    lead = 0.0
+    if hook is not None:
+        lead = hook((g_w_bc, g_conv_w[:, inner_width:], g_conv_b[inner_width:]))
     grad_normed_in = head_scatter(
-        (main_term + side_term).reshape(head_count, -1, main_term.shape[1]), tick, ids[1]
+        (main_term + side_term + lead).reshape(head_count, -1, main_term.shape[1]), tick, ids[1]
     )
     scale_in = rms_scale(stream)
     g_norm_gain = jnp.sum(grad_normed_in * stream * scale_in, axis=0)
@@ -579,12 +583,35 @@
     return (grad_stream, head_part, shared_part, g_w_out)
 
 
-def reduce_grads(head_part, shared_part):
-    head_sum = tuple(
-        lax.psum(member.astype(jnp.bfloat16), "seq").astype(jnp.float32) for member in head_part
-    )
-    shared_sum = lax.psum(tuple(shared_part), ("seq", "head"))
-    return (head_sum, tuple(shared_sum))
+def pack_rows(members, width, multiple):
+    rows = jnp.concatenate([member.reshape(-1, width) for member in members], axis=0)
+    return jnp.pad(rows, ((0, -rows.shape[0] % multiple), (0, 0)))
+
+
+def unpack_rows(rows, shapes, width):
+    pieces = []
+    start = 0
+    for shape in shapes:
+        count = math.prod(shape) // width
+        pieces.append(rows[start : start + count].reshape(shape))
+        start += count
+    return tuple(pieces)
+
+
+def reduce_grads(head_part, norm_part, bc_part, tick_count):
+    head_count = lax.axis_size("head")
+    host = head_part[0]
+    width = host.shape[-1]
+    joined = jnp.concatenate([host, bc_part.reshape(-1, width)], axis=0)
+    summed = tuple(
+        lax.psum(member.astype(jnp.bfloat16), "seq").astype(jnp.float32)
+        for member in (joined,) + tuple(head_part[1:])
+    )
+    head_sum = (summed[0][: host.shape[0]],) + summed[1:]
+    bc_sum = summed[0][host.shape[0] :].reshape(bc_part.shape)
+    bc_rows = head_gather(bc_sum, (0, 0, 1), 4 * tick_count + 1)
+    norm_sum = lax.psum(norm_part, ("seq", "head"))
+    return (head_sum, norm_sum, bc_rows.reshape(-1, bc_rows.shape[-1]))
 
 
 def store_slot(buffer, value, slot_index, is_valid):
@@ -661,6 +688,8 @@
             arrived = shifted(result, "section", 1)
     back_arrived = jnp.zeros(row_shape, jnp.float32)
     input_grads = jnp.zeros((micro_count,) + row_shape, jnp.float32)
+    head_count = lax.axis_size("head")
+    bc_box = []
     head_total = ()
     shared_total = ()
     for tick_index in range(tick_count):
@@ -668,6 +697,21 @@
         outer_grad = lax.dynamic_index_in_dim(cotangent, clipped, 0, False).astype(jnp.float32)
         grad_next = jnp.where(section_index == section_count - 1, outer_grad, back_arrived)
         mask_value = is_valid.astype(jnp.float32)
+        hook = None
+        if tick_index + 1 == tick_count:
+
+            def hook(bc_local, mask_value=mask_value, earlier=shared_total):
+                totals = tuple(
+                    (prev + member * mask_value) if earlier else member * mask_value
+                    for prev, member in zip(earlier[1:] or bc_local, bc_local)
+                )
+                rows = pack_rows(totals, totals[0].shape[-1], 8 * head_count)
+                part = head_scatter(
+                    rows.reshape(head_count, -1, rows.shape[-1]), (0, 0, 1), 4 * tick_count
+                )
+                bc_box.append((part, [member.shape for member in totals]))
+                return part[0, 0] * 0.0
+
         grad_stream, head_part, shared_part, out_part = mixer_backward(
             grad_next,
             layer_weights,
@@ -675,6 +719,7 @@
             mask_value,
             (tick_count - 1 - tick_index, -1, micro_count),
             (2 * tick_count + tick_index, 3 * tick_count + tick_index),
+            hook,
         )
         if tick_index == 0:
             out_total = out_part
@@ -699,7 +744,9 @@
             )
     anchor = out_total[0, 0].astype(jnp.float32) * 0.0
     head_total = (head_total[0] + anchor,) + head_total[1:]
-    head_total, shared_total = reduce_grads(head_total, shared_total)
+    bc_part, bc_shapes = bc_box[0]
+    head_total, norm_sum, bc_rows = reduce_grads(head_total, shared_total[0], bc_part, tick_count)
+    shared_total = (norm_sum,) + unpack_rows(bc_rows, bc_shapes, bc_rows.shape[-1])
     head_total = head_total[:3] + (out_total.astype(jnp.float32),) + head_total[3:]
     return (
         outputs_all[None],

time: 1580 us -> 1560 us (0.987)
  waiting for transfers between devices: 222 us -> 126 us
  Pallas kernels: 326 us -> 394 us
  local copies, waits for them, and re-layouts: 173 us -> 209 us
  blocking collectives: 196 us -> 165 us
    psum x1 -> x0, waiting for transfers between devices: 92.8 us -> none  [reduce_grads(): shared_sum = lax.psum(tuple(shared_part), ('seq', 'head'))]
    psum x1, waiting for transfers between devices: 0.01 us -> 39.5 us  [reduce_grads(): lax.psum(member.astype(jnp.bfloat16), 'seq').astype(jnp.float32)]
    psum x1, waiting for transfers between devices: 37.3 us -> 0.01 us  [on_device(): out_total = lax.psum(out_total.astype(jnp.bfloat16), 'seq')]
    pallas_call x6 -> x7, Pallas kernels: 146 us -> 181 us  [head_gather(): pl.pallas_call(functools.partial(gather_body, n, tick), out_shape=jax.Sha...]
    psum x1, blocking collectives: 73.3 us -> 38.5 us  [reduce_grads(): norm_sum = lax.psum(norm_part, ('seq', 'head'))]
    pallas_call x6 -> x7, Pallas kernels: 180 us -> 213 us  [head_scatter(): pl.pallas_call(functools.partial(scatter_body, n, tick), out_shape=jax.Sh...]
    another operation x36 -> x38, other arithmetic: 24.3 us -> 46.1 us
    broadcast_in_dim x2 -> x0, other arithmetic: 21.5 us -> none  [the longest x1 21.5 us: on_device(): head_total[1][None]]
  transfers between devices with their start and end apart: 22 -> 21, of which waited for: 10 -> 9; matrix products, arithmetic and copies ran while one was open for 24% -> 23% of each run, Pallas kernels for 8% -> 10%
where the time goes in v7:
time: 1560 us; the launch traced here: 1550 us
  Pallas kernels  394 us (25%)
  matrix products  346 us (22%)
  other arithmetic  258 us (17%)
  local copies, waits for them, and re-layouts  209 us (13%)
  blocking collectives  165 us (11%)
  waiting for transfers between devices  126 us (8%)
  starting transfers between devices  33.8 us (2%)
  between operations  21.4 us (1%)
    pallas_call x7, Pallas kernels, head_scatter(): pl.pallas_call(functools.partial(scatter_body, n, tick), out_shape=jax.Sh...  213 us
    pallas_call x7, Pallas kernels, head_gather(): pl.pallas_call(functools.partial(gather_body, n, tick), out_shape=jax.Sha...  181 us
    dot_general x9, matrix products, block_output(): jnp.einsum('cijh,cjhp->cihp', weights, x_blocks, precision=highest)  101 us
    unnamed x892, local copies, waits for them, and re-layouts  71 us
    another operation x38, other arithmetic  46.1 us
    psum x1, waiting for transfers between devices, reduce_grads(): lax.psum(member.astype(jnp.bfloat16), 'seq').astype(jnp.float32)  39.5 us
    psum x1, blocking collectives, reduce_grads(): norm_sum = lax.psum(norm_part, ('seq', 'head'))  38.5 us
    dot_general x3, matrix products, mixer_forward(): projected = jnp.dot(gathered, w_main, preferred_element_type=jnp.float32)  38.1 us
  transfers between devices with their start and end apart: 21, of which 9 were waited for; matrix products, arithmetic and copies ran while one was open for 23% of the time, Pallas kernels for 10%

profile of v7, /device:TPU:0, one launch (start us, length us, event | category | flops | bytes accessed | tf_op | source)
XLA Modules:
  0.0 1553.6 jit_solution(17335964033709332156)
XLA Ops:
  20.8 29.3 %shard_map.297 = bf16[4,128,2048]{2,1,0:T(8,128)(2,1)} custom-call(bf16[128,2048]{1,0:T(8,128)(2,1)} %fusion.223.x_ref), custom_call_target="tpu_custom_call" | custom-call | tf_op jit(solution)/shard_map/pallas_call | solution.py:113
  50.4 12.7 fusion.416
  96.5 7.1 all-gather
  117.2 12.9 all-gather.13.cloned.1.call-done
  134.7 9.4 fusion.132
  144.1 13.4 copy.518
  160.8 11.7 psum.119
  174.1 6.9 fusion.39.p_ref
  180.9 36.7 %shard_map.298 = f32[128,2048]{1,0:T(8,128)} custom-call(f32[4,128,2048]{2,1,0:T(8,128)} %fusion.39.p_ref), custom_call_target="tpu_custom_call" | custom-call | tf_op jit(solution)/shard_map/pallas_call | solution.py:209
  226.1 43.4 %shard_map.299 = bf16[4,128,2048]{2,1,0:T(8,128)(2,1)} custom-call(bf16[128,2048]{1,0:T(8,128)(2,1)} %multiply_convert_fusion.7.x_ref), custom_call_target="tpu_custom_call" | custom-call | tf_op jit(solution)/shard_map/pallas_call | solution.py:113
  269.5 12.9 fusion.415
  298.1 9.5 fusion.110
  326.2 6.8 all-gather.1
  341.6 10.3 all-gather.15.cloned.1.call-done
  356.6 9.4 fusion.131
  371.1 11.7 psum.120
  386.3 6.9 fusion.37.p_ref
  393.2 46.6 %shard_map.300 = f32[128,2048]{1,0:T(8,128)} custom-call(f32[4,128,2048]{2,1,0:T(8,128)} %fusion.37.p_ref), custom_call_target="tpu_custom_call" | custom-call | tf_op jit(solution)/shard_map/pallas_call | solution.py:209
  451.3 12.5 fusion.414
  491.5 7.9 all-gather.5
  505.0 7.0 all-gather.4
  513.2 7.8 all-gather.3
  521.0 7.4 all-gather.2
  538.7 8.7 all-gather.17.cloned.1.call-done
  551.9 9.4 fusion.130
  567.6 11.7 psum.121
  579.3 7.9 multiply_reduce_fusion.20
  587.2 8.3 psum.122
  595.6 6.9 multiply_reduce_fusion.23
  611.5 15.7 %fusion.29 = (f32[2,256,16]{1,2,0:T(8,128)}, f32[2,256,16]{1,2,0:T(8,128)}, f32[2,256,16]{1,2,0:T(8,128)}, f32[2,256,256]{2,1,0:T(8,128)S(1)}) fusion(f32[2,256,16]{1,2,0:T(8,128)} %bitcast.1082, f32[2,256,256]{2,1,0:T(8,128)} %fusion.452, f32[2,256,16]{1,2,0:T(8,128)} %copy-done.211, pred[2,256,256]{2,1,0:T(8,128)(4,1)} %get-tuple-element.265, ...), kind=kOutput, calls=%fused_computation.48 | convolution fusion | flops 1637720064 | bytes 5537792 | tf_op jit(solution)/shard_map/transpose(jvp(cijh,cjhp->cihp))/dot_general | solution.py:356
  640.7 19.8 %all-gather.19.cloned.1.call-done = bf16[4,16,64,128]{3,2,1,0:T(8,128)(2,1)} async-done(((bf16[1,16,64,128]{3,2,1,0:T(8,128)(2,1)}), bf16[4,16,64,128]{3,2,1,0:T(8,128)(2,1)}) %all-gather.19.cloned.1.call-update) | async-done | bytes 1048592 | tf_op jit(solution)/shard_map/all_gather | solution.py:259
  670.1 9.2 fusion.126
  683.6 6.3 multiply_reduce_fusion.13
  746.5 11.0 fusion.250
  761.3 22.2 %collective-permute-done.9 = bf16[128,2048]{1,0:T(8,128)(2,1)S(1)} collective-permute-done((bf16[128,2048]{1,0:T(8,128)(2,1)S(1)}, bf16[128,2048]{1,0:T(8,128)(2,1)S(1)}, u32[]{:S(2)}, u32[]{:S(2)}) %collective-permute-start.9) | collective-permute-done | bytes 524320 | tf_op jit(solution)/shard_map/ppermute | solution.py:236
  785.3 33.2 %shard_map.305 = bf16[4,128,2048]{2,1,0:T(8,128)(2,1)} custom-call(bf16[128,2048]{1,0:T(8,128)(2,1)} %fusion.241.x_ref), custom_call_target="tpu_custom_call" | custom-call | tf_op jit(solution)/shard_map/pallas_call | solution.py:113
  818.5 8.0 multiply_reduce_fusion.19
  826.5 10.6 psum.123
  837.1 6.0 multiply_reduce_fusion.22
  852.4 15.7 %fusion.31 = (f32[2,256,16]{1,2,0:T(8,128)}, f32[2,256,16]{1,2,0:T(8,128)}, f32[2,256,16]{1,2,0:T(8,128)}, f32[2,256,256]{2,1,0:T(8,128)S(1)}) fusion(f32[2,256,16]{1,2,0:T(8,128)S(1)} %bitcast.1081, f32[2,256,256]{2,1,0:T(8,128)} %fusion.451, f32[2,256,16]{1,2,0:T(8,128)S(1)} %copy-done.210, pred[2,256,256]{2,1,0:T(8,128)(4,1)S(1)} %copy-done.194, ...), kind=kOutput, calls=%fused_computation.50 | convolution fusion | flops 1637720064 | bytes 5537792 | tf_op jit(solution)/shard_map/transpose(jvp(cijh,cjhp->cihp))/dot_general | solution.py:356
  894.7 9.0 fusion.122
  908.1 6.3 multiply_reduce_fusion.9
  961.1 53.8 %shard_map.306 = f32[128,2048]{1,0:T(8,128)} custom-call(f32[4,128,2048]{2,1,0:T(8,128)} %bitcast.969), custom_call_target="tpu_custom_call" | custom-call | tf_op jit(solution)/shard_map/pallas_call | solution.py:209
  1020.0 11.0 fusion.248
  1036.6 28.4 %shard_map.307 = bf16[4,128,2048]{2,1,0:T(8,128)(2,1)} custom-call(bf16[128,2048]{1,0:T(8,128)(2,1)} %fusion.242.x_ref), custom_call_target="tpu_custom_call" | custom-call | tf_op jit(solution)/shard_map/pallas_call | solution.py:113
  1065.1 8.0 multiply_reduce_fusion.18
  1073.1 10.2 psum.124
  1093.1 15.6 %fusion.33 = (f32[2,256,16]{1,2,0:T(8,128)}, f32[2,256,16]{1,2,0:T(8,128)}, f32[2,256,16]{1,2,0:T(8,128)}, f32[2,256,256]{2,1,0:T(8,128)S(1)}) fusion(f32[2,256,16]{1,2,0:T(8,128)S(1)} %bitcast.1077, f32[2,256,256]{2,1,0:T(8,128)S(1)} %copy-done.173, f32[2,256,16]{1,2,0:T(8,128)S(1)} %copy-done.207, pred[2,256,256]{2,1,0:T(8,128)(4,1)S(1)} %copy-done.191, ...), kind=kOutput, calls=%fused_computation.52 | convolution fusion | flops 1637720064 | bytes 5537792 | tf_op jit(solution)/shard_map/transpose(jvp(cijh,cjhp->cihp))/dot_general | solution.py:356
  1119.8 10.3 add_convert_fusion
  1130.4 8.0 all-gather.23.cloned.1.call-done
  1148.5 7.4 fusion.118
  1207.7 30.9 %shard_map.308 = f32[520,256]{1,0:T(8,128)} custom-call(f32[4,520,256]{2,1,0:T(8,128)} %bitcast.973), custom_call_target="tpu_custom_call" | custom-call | tf_op jit(solution)/shard_map/pallas_call | solution.py:209
  1258.6 20.1 %fusion.5 = (bf16[2048,1024]{0,1:T(8,128)(2,1)S(1)}, bf16[1,2048,1024]{1,2,0:T(8,128)(2,1)}) fusion(f32[2048,2064]{0,1:T(8,128)} %copy-done.49, f32[2048,2064]{0,1:T(8,128)} %fusion.248, f32[2048,2064]{0,1:T(8,128)} %fusion.250, f32[]{:T(128)} %bitcast.201, f32[]{:T(128)S(6)} %convert_element_type.593, f32[]{:T(128)S(6)} %convert_element_type.592, ...), kind=kLoop, calls=%fused_computation.12 | loop fusion | flops 27262976 | bytes 58720272 | tf_op jit(solution)/shard_map/convert.31
  1284.6 7.4 fusion.35.p_ref
  1303.6 18.7 %all-reduce.64 = (bf16[1,4,1024]{2,1,0:T(4,128)(2,1)S(1)}, bf16[1,1024]{1,0:T(2,128)(2,1)S(1)}, bf16[1,16]{1,0:T(2,128)(2,1)S(1)}, bf16[1,16]{1,0:T(2,128)(2,1)S...) all-reduce(bf16[1,4,1024]{2,1,0:T(4,128)(2,1)S(1)} %fusion.337, ...), channel_id=1, replica_groups=mesh['section'=2,'seq'=4,'head'=4] {'seq'}, use_global_device_ids=true, to_apply=%region_95.97 | all-reduce | flops 6192 | bytes 24768 | tf_op jit(solution)/shard_map/psum | solution.py:607
  1327.5 8.1 fusion.247
  1341.4 37.1 %shard_map.309 = f32[128,2048]{1,0:T(8,128)} custom-call(f32[4,128,2048]{2,1,0:T(8,128)} %bitcast.967), custom_call_target="tpu_custom_call" | custom-call | tf_op jit(solution)/shard_map/pallas_call | solution.py:209
  1380.2 38.5 %psum.125 = f32[1,2048]{1,0:T(1,128)} all-reduce(f32[1,2048]{1,0:T(1,128)S(1)} %bitcast.1091), channel_id=1, replica_groups=mesh['section'=2,'seq'=4,'head'=4] {'seq','head'}, use_global_device_ids=true, to_apply=%region_90.92 | all-reduce | flops 2048 | bytes 16384 | tf_op jit(solution)/shard_map/psum | solution.py:613
  1426.2 39.5 %all-reduce.71.cloned.1.call-done = (bf16[1,2048,1024]{1,2,0:T(8,128)(2,1)}, bf16[2178,1024]{0,1:T(8,128)(2,1)}, bf16[1,2048,16]{1,2,0:T(8,128)(2,1)}) async-done(((bf16[1,2048,1024]{1,2,0:T(8,128)(2,1)}, bf16[2178,1024]{0,1:T(8,128)(2,1)}, bf16[1,2048,16]{1,2,0:T(8,128)(2,1)}), (bf16[1,2048,1024]{1,2,0:T(8,128)(2,1)}, bf16[2178,1024]{0,1:T(8,128)(2,1)}, ...) | async-done | bytes 8720400 | tf_op jit(solution)/shard_map/psum | solution.py:607
  1465.7 6.7 convert_element_type.596
  1474.8 41.5 %shard_map.310 = f32[4,520,256]{2,1,0:T(8,128)} custom-call(f32[520,256]{1,0:T(8,128)} %reshape.1041.x_ref), custom_call_target="tpu_custom_call" | custom-call | tf_op jit(solution)/shard_map/pallas_call | solution.py:113
  1521.9 7.9 slice_bitcast_fusion
  1529.8 9.2 copy.626
  1539.0 6.9 copy.627
  (1335 shorter events, 541.2 us)
Async XLA Ops:
  7.2 43.0 %copy-start.213 = (bf16[1,2048,16]{1,2,0:T(8,128)(2,1)S(1)}, bf16[1,2048,16]{1,2,0:T(8,128)(2,1)}, u32[]{:S(2)}) copy-start(bf16[1,2048,16]{1,2,0:T(8,128)(2,1)} %param.27) | copy-start | bytes 196612
  7.2 43.2 %copy-start.56 = (bf16[1,2048,256]{2,1,0:T(8,128)(2,1)S(1)}, bf16[1,2048,256]{2,1,0:T(8,128)(2,1)}, u32[]{:S(2)}) copy-start(bf16[1,2048,256]{2,1,0:T(8,128)(2,1)} %param.26) | copy-start | bytes 3145732
  7.2 123.0 %all-gather.13.cloned.1.call-start = ((), (), s32[]{:S(2)}) async-start(), calls=%async_computation | async-start | bytes 2621440 | tf_op jit(solution)/shard_map/all_gather | solution.py:241
  8.7 70.5 %collective-permute-start = (f32[3]{0:T(128)S(1)}, f32[3]{0:T(128)S(1)}, u32[]{:S(2)}, u32[]{:S(2)}) collective-permute-start(f32[3]{0:T(128)S(1)} %slice.596), channel_id=1, source_target_pairs={{0,4},{4,8},{8,12},{1,5},{5,9},{9,13},{2,6},{6,10},{10,14},{3,7},{... | collective-permute-start | bytes 44 | tf_op jit(solution)/shard_map/ppermute | solution.py:236
  13.7 65.6 %collective-permute-start.3 = (f32[3]{0:T(128)S(1)}, f32[3]{0:T(128)S(1)}, u32[]{:S(2)}, u32[]{:S(2)}) collective-permute-start(f32[3]{0:T(128)S(1)} %slice.635), channel_id=1, source_target_pairs={{0,4},{4,8},{8,12},{1,5},{5,9},{9,13},{2,6},{6,10},{10,14},{3,7},{... | collective-permute-start | bytes 44 | tf_op jit(solution)/shard_map/ppermute | solution.py:236
  18.8 31.3 %copy-start.361 = (f32[128]{0:T(128)}, f32[128]{0:T(128)S(1)}, u32[]{:S(2)}) copy-start(f32[128]{0:T(128)S(1)} %get-tuple-element.332) | copy-start | bytes 1540
  65.9 14.9 collective-permute-start.1
  73.0 30.5 %copy-start.146 = (f32[512,16]{0,1:T(8,128)}, f32[512,16]{0,1:T(8,128)S(1)}, u32[]{:S(2)}) copy-start(f32[512,16]{0,1:T(8,128)S(1)} %get-tuple-element.226) | copy-start | bytes 98308
  79.2 55.4 %copy-start.180 = (f32[2,256,16]{1,2,0:T(8,128)}, f32[2,256,16]{1,2,0:T(8,128)S(1)}, u32[]{:S(2)}) copy-start(f32[2,256,16]{1,2,0:T(8,128)S(1)} %get-tuple-element.275) | copy-start | bytes 98308
  90.9 43.8 %copy-start.9 = (f32[2,256,16,64]{1,0,3,2:T(2,128)}, f32[2,256,16,64]{1,0,3,2:T(2,128)S(1)}, u32[]{:S(2)}) copy-start(f32[2,256,16,64]{1,0,3,2:T(2,128)S(1)} %reshape.964) | copy-start | bytes 6291460
  94.8 35.4 %copy-start.61 = (f32[2,16,64,128]{3,2,1,0:T(8,128)}, f32[2,16,64,128]{3,2,1,0:T(8,128)S(1)}, u32[]{:S(2)}) copy-start(f32[2,16,64,128]{3,2,1,0:T(8,128)S(1)} %fusion.158) | copy-start | bytes 3145732
  96.5 255.4 %all-gather.15.cloned.1.call-start = ((), (), s32[]{:S(2)}) async-start(), calls=%async_computation.1 | async-start | bytes 2621440 | tf_op jit(solution)/shard_map/all_gather | solution.py:241
  180.9 38.4 %copy-start.50 = (bf16[2,128,2048]{2,1,0:T(8,128)(2,1)S(1)}, bf16[2,128,2048]{2,1,0:T(8,128)(2,1)}, u32[]{:S(2)}) copy-start(bf16[2,128,2048]{2,1,0:T(8,128)(2,1)} %param.19) | copy-start | bytes 3145732
  220.6 3.7 collective-permute-start.2
  223.5 70.0 %copy-start.285 = (f32[2,256]{1,0:T(2,128)}, f32[2,256]{1,0:T(2,128)S(1)}, u32[]{:S(2)}) copy-start(f32[2,256]{1,0:T(2,128)S(1)} %get-tuple-element.342) | copy-start | bytes 6148
  223.5 70.0 %copy-start.327 = (f32[2,256]{1,0:T(2,128)}, f32[2,256]{1,0:T(2,128)S(1)}, u32[]{:S(2)}) copy-start(f32[2,256]{1,0:T(2,128)S(1)} %get-tuple-element.343) | copy-start | bytes 6148
  224.2 73.8 %copy-start.263 = (f32[512]{0:T(512)}, f32[512]{0:T(512)S(1)}, u32[]{:S(2)}) copy-start(f32[512]{0:T(512)S(1)} %get-tuple-element.286) | copy-start | bytes 6148
  224.2 73.8 %copy-start.265 = (f32[512]{0:T(512)}, f32[512]{0:T(512)S(1)}, u32[]{:S(2)}) copy-start(f32[512]{0:T(512)S(1)} %get-tuple-element.287) | copy-start | bytes 6148
  224.2 73.8 %copy-start.267 = (f32[512]{0:T(512)}, f32[512]{0:T(512)S(1)}, u32[]{:S(2)}) copy-start(f32[512]{0:T(512)S(1)} %get-tuple-element.288) | copy-start | bytes 6148
  224.5 215.3 %copy-start.25 = (f32[128,2048]{1,0:T(8,128)}, f32[128,2048]{1,0:T(8,128)S(1)}, u32[]{:S(2)}) copy-start(f32[128,2048]{1,0:T(8,128)S(1)} %get-tuple-element.218) | copy-start | bytes 3145732
  225.1 57.3 %copy-start.375 = (f32[128]{0:T(128)}, f32[128]{0:T(128)S(1)}, u32[]{:S(2)}) copy-start(f32[128]{0:T(128)S(1)} %get-tuple-element.334) | copy-start | bytes 1540
  287.0 10.8 collective-permute-start.4
  291.2 41.8 %copy-start.148 = (f32[512,16]{0,1:T(8,128)}, f32[512,16]{0,1:T(8,128)S(1)}, u32[]{:S(2)}) copy-start(f32[512,16]{0,1:T(8,128)S(1)} %get-tuple-element.214) | copy-start | bytes 98308
  293.6 62.9 %copy-start.184 = (f32[2,256,16]{1,2,0:T(8,128)}, f32[2,256,16]{1,2,0:T(8,128)S(1)}, u32[]{:S(2)}) copy-start(f32[2,256,16]{1,2,0:T(8,128)S(1)} %get-tuple-element.273) | copy-start | bytes 98308
  312.7 43.8 %copy-start.11 = (f32[2,256,16,64]{1,0,3,2:T(2,128)}, f32[2,256,16,64]{1,0,3,2:T(2,128)S(1)}, u32[]{:S(2)}) copy-start(f32[2,256,16,64]{1,0,3,2:T(2,128)S(1)} %reshape.976) | copy-start | bytes 6291460
  318.6 228.7 %all-gather.17.cloned.1.call-start = ((), (), s32[]{:S(2)}) async-start(), calls=%async_computation.2 | async-start | bytes 2621440 | tf_op jit(solution)/shard_map/all_gather | solution.py:241
  319.9 124.2 %collective-permute-start.6 = (f32[3]{0:T(128)}, f32[3]{0:T(128)}, u32[]{:S(2)}, u32[]{:S(2)}) collective-permute-start(f32[3]{0:T(128)} %slice.670), channel_id=1, source_target_pairs={{0,4},{4,8},{8,12},{1,5},{5,9},{9,13},{2,6},{6,10},{10,14},{3,7},{... | collective-permute-start | bytes 44 | tf_op jit(solution)/shard_map/ppermute | solution.py:236
  393.2 46.6 %copy-start.112 = (f32[1,128,2048]{2,1,0:T(8,128)S(1)}, f32[1,128,2048]{2,1,0:T(8,128)}, u32[]{:S(2)}) copy-start(f32[1,128,2048]{2,1,0:T(8,128)} %constant_dynamic-slice_fusion.3) | copy-start | bytes 3145732
  442.7 3.8 collective-permute-start.5
  444.0 28.3 %copy-start.414 = (f32[2]{0:T(128)}, f32[2]{0:T(128)S(1)}, u32[]{:S(2)}) copy-start(f32[2]{0:T(128)S(1)} %fusion.368) | copy-start | bytes 28
  445.5 31.1 %copy-start.269 = (f32[512]{0:T(512)}, f32[512]{0:T(512)S(1)}, u32[]{:S(2)}) copy-start(f32[512]{0:T(512)S(1)} %get-tuple-element.280) | copy-start | bytes 6148
  445.5 31.1 %copy-start.271 = (f32[512]{0:T(512)}, f32[512]{0:T(512)S(1)}, u32[]{:S(2)}) copy-start(f32[512]{0:T(512)S(1)} %get-tuple-element.281) | copy-start | bytes 6148
  445.5 31.1 %copy-start.273 = (f32[512]{0:T(512)}, f32[512]{0:T(512)S(1)}, u32[]{:S(2)}) copy-start(f32[512]{0:T(512)S(1)} %get-tuple-element.282) | copy-start | bytes 6148
  466.6 9.8 collective-permute-start.7
  486.4 175.7 %copy-start.14 = (f32[2,256,16,64]{1,0,3,2:T(2,128)}, f32[2,256,16,64]{1,0,3,2:T(2,128)S(1)}, u32[]{:S(2)}) copy-start(f32[2,256,16,64]{1,0,3,2:T(2,128)S(1)} %reshape.988) | copy-start | bytes 6291460
  490.3 57.0 %copy-start.64 = (f32[2,16,64,128]{3,2,1,0:T(8,128)}, f32[2,16,64,128]{3,2,1,0:T(8,128)S(1)}, u32[]{:S(2)}) copy-start(f32[2,16,64,128]{3,2,1,0:T(8,128)S(1)} %fusion.150) | copy-start | bytes 3145732
  491.5 169.0 %all-gather.19.cloned.1.call-start = ((), (), s32[]{:S(2)}) async-start(), calls=%async_computation.3 | async-start | bytes 1310720 | tf_op jit(solution)/shard_map/all_gather | solution.py:259
  611.4 273.6 %all-gather.21.cloned.1.call-start = ((), (), s32[]{:S(2)}) async-start(), calls=%async_computation.4 | async-start | bytes 1310720 | tf_op jit(solution)/shard_map/all_gather | solution.py:259
  689.9 29.9 %copy-start.221 = (f32[1280]{0:T(1024)}, f32[1280]{0:T(1024)S(1)}, u32[]{:S(2)}) copy-start(f32[1280]{0:T(1024)S(1)} %get-tuple-element.135) | copy-start | bytes 15364
  701.3 19.1 %collective-permute-start.8 = (f32[3,1280]{1,0:T(4,128)}, f32[3,1280]{1,0:T(4,128)}, u32[]{:S(2)}, u32[]{:S(2)}) collective-permute-start(f32[3,1280]{1,0:T(4,128)} %copy.567), channel_id=1, source_target_pairs={{4,0},{8,4},{12,8},{5,1},{9,5},{13,9},{6,2},{10,6},{14,10},{7,3},{... | collective-permute-start | bytes 46088 | tf_op jit(solution)/shard_map/ppermute | solution.py:236
  745.1 38.5 %collective-permute-start.9 = (bf16[128,2048]{1,0:T(8,128)(2,1)S(1)}, bf16[128,2048]{1,0:T(8,128)(2,1)S(1)}, u32[]{:S(2)}, u32[]{:S(2)}) collective-permute-start(bf16[128,2048]{1,0:T(8,128)(2,1)S(1)} %get-tuple-element.193), channel_id=1, source_target_pairs={{16,0},{17,1},{18,2},{19,3},{20,4},{21,5},{22,6},{23,7},{24,8},{25... | collective-permute-start | bytes 1572872 | tf_op jit(solution)/shard_map/ppermute | solution.py:236
  761.3 57.2 %copy-start.342 = (f32[512]{0:T(512)S(1)}, f32[512]{0:T(512)}, u32[]{:S(2)}) copy-start(f32[512]{0:T(512)} %copy-done.341) | copy-start | bytes 6148
  852.3 286.1 %all-gather.23.cloned.1.call-start = ((), (), s32[]{:S(2)}) async-start(), calls=%async_computation.5 | async-start | bytes 1310720 | tf_op jit(solution)/shard_map/all_gather | solution.py:259
  914.4 28.7 %copy-start.223 = (f32[1280]{0:T(1024)}, f32[1280]{0:T(1024)S(1)}, u32[]{:S(2)}) copy-start(f32[1280]{0:T(1024)S(1)} %get-tuple-element.136) | copy-start | bytes 15364
  925.8 18.0 %collective-permute-start.10 = (f32[3,1280]{1,0:T(4,128)}, f32[3,1280]{1,0:T(4,128)}, u32[]{:S(2)}, u32[]{:S(2)}) collective-permute-start(f32[3,1280]{1,0:T(4,128)} %copy.590), channel_id=1, source_target_pairs={{4,0},{8,4},{12,8},{5,1},{9,5},{13,9},{6,2},{10,6},{14,10},{7,3},{... | collective-permute-start | bytes 46088 | tf_op jit(solution)/shard_map/ppermute | solution.py:236
  941.9 248.6 %copy-start.235 = (f32[1,1280]{1,0:T(1,128)}, f32[1,1280]{1,0:T(1,128)S(1)}, u32[]{:S(2)}) copy-start(f32[1,1280]{1,0:T(1,128)S(1)} %reshape.1027) | copy-start | bytes 15364
  941.9 248.6 %copy-start.237 = (f32[1,1280]{1,0:T(1,128)}, f32[1,1280]{1,0:T(1,128)S(1)}, u32[]{:S(2)}) copy-start(f32[1,1280]{1,0:T(1,128)S(1)} %reshape.1028) | copy-start | bytes 15364
  961.1 53.8 %copy-start.26 = (f32[128,2048]{1,0:T(8,128)S(1)}, f32[128,2048]{1,0:T(8,128)}, u32[]{:S(2)}) copy-start(f32[128,2048]{1,0:T(8,128)} %copy-done.25) | copy-start | bytes 3145732
  961.1 53.8 %copy-start.376 = (f32[128]{0:T(128)S(1)}, f32[128]{0:T(128)}, u32[]{:S(2)}) copy-start(f32[128]{0:T(128)} %copy-done.375) | copy-start | bytes 1540
  961.1 56.0 %copy-start.66 = (bf16[2,128,2048]{2,1,0:T(8,128)(2,1)S(1)}, bf16[2,128,2048]{2,1,0:T(8,128)(2,1)}, u32[]{:S(2)}) copy-start(bf16[2,128,2048]{2,1,0:T(8,128)(2,1)} %param.20) | copy-start | bytes 3145732
  961.1 56.0 %copy-start.139 = (bf16[128,2048]{1,0:T(8,128)(2,1)S(1)}, bf16[128,2048]{1,0:T(8,128)(2,1)}, u32[]{:S(2)}) copy-start(bf16[128,2048]{1,0:T(8,128)(2,1)} %copy-done.138) | copy-start | bytes 1572868
  961.1 56.0 %copy-start.423 = (f32[128]{0:T(128)S(1)}, f32[128]{0:T(128)}, u32[]{:S(2)}) copy-start(f32[128]{0:T(128)} %get-tuple-element.333) | copy-start | bytes 1540
  1018.6 16.4 %collective-permute-start.11 = (bf16[128,2048]{1,0:T(8,128)(2,1)S(1)}, bf16[128,2048]{1,0:T(8,128)(2,1)S(1)}, u32[]{:S(2)}, u32[]{:S(2)}) collective-permute-start(bf16[128,2048]{1,0:T(8,128)(2,1)S(1)} %get-tuple-element.189), channel_id=1, source_target_pairs={{16,0},{17,1},{18,2},{19,3},{20,4},{21,5},{22,6},{23,7},{24,8},{25... | collective-permute-start | bytes 1572872 | tf_op jit(solution)/shard_map/ppermute | solution.py:236
  1034.9 30.1 %copy-start.340 = (f32[512]{0:T(512)S(1)}, f32[512]{0:T(512)}, u32[]{:S(2)}) copy-start(f32[512]{0:T(512)} %copy-done.339) | copy-start | bytes 6148
  1115.2 141.6 %all-reduce.69.cloned.1.call-start = ((), (), s32[]{:S(2)}) async-start(), calls=%async_computation.6 | async-start | bytes 8388608 | tf_op jit(solution)/shard_map/psum | solution.py:729
  1130.2 335.5 %all-reduce.71.cloned.1.call-start = ((), (), s32[]{:S(2)}) async-start(), calls=%async_computation.7 | async-start | bytes 17956864 | tf_op jit(solution)/shard_map/psum | solution.py:607
  1179.9 13.0 collective-permute-start.12
  1207.7 34.8 %copy-start.33 = (f32[509,1280]{0,1:T(8,128)S(1)}, f32[509,1280]{0,1:T(8,128)}, u32[]{:S(2)}) copy-start(f32[509,1280]{0,1:T(8,128)} %slice.894) | copy-start | bytes 7818244
  1341.3 37.2 %copy-start.52 = (bf16[2,128,2048]{2,1,0:T(8,128)(2,1)S(1)}, bf16[2,128,2048]{2,1,0:T(8,128)(2,1)}, u32[]{:S(2)}) copy-start(bf16[2,128,2048]{2,1,0:T(8,128)(2,1)} %param.19) | copy-start | bytes 3145732
  1341.3 37.2 %copy-start.167 = (f32[1,2048]{1,0:T(1,128)S(1)}, f32[1,2048]{1,0:T(1,128)}, u32[]{:S(2)}) copy-start(f32[1,2048]{1,0:T(1,128)} %param.23) | copy-start | bytes 24580
  1341.3 37.2 %copy-start.362 = (f32[128]{0:T(128)S(1)}, f32[128]{0:T(128)}, u32[]{:S(2)}) copy-start(f32[128]{0:T(128)} %copy-done.361) | copy-start | bytes 1540
  1341.3 38.8 %copy-start.291 = (f32[2048]{0:T(1024)S(1)}, f32[2048]{0:T(1024)}, u32[]{:S(2)}) copy-start(f32[2048]{0:T(1024)} %get-tuple-element.141) | copy-start | bytes 24580
  1341.3 38.8 %copy-start.292 = (f32[2048]{0:T(1024)S(1)}, f32[2048]{0:T(1024)}, u32[]{:S(2)}) copy-start(f32[2048]{0:T(1024)} %get-tuple-element.143) | copy-start | bytes 24580
  1341.3 77.3 %copy-start.422 = (f32[128]{0:T(128)S(1)}, f32[128]{0:T(128)}, u32[]{:S(2)}) copy-start(f32[128]{0:T(128)} %get-tuple-element.331) | copy-start | bytes 1540
  (395 other events, 2351.4 us)
Sparse Core Ops, SparseCore 0:
  96.6 33.5 all-gather.12
  318.7 33.1 all-gather.14
  491.6 55.6 all-gather.16
  611.6 48.9 all-gather.18
  852.4 32.5 all-gather.20
  1115.3 23.0 all-gather.22
  1141.7 104.1 all-reduce.68
  1281.5 184.2 all-reduce.70

commit v8 on v7

--- a/solution.py
+++ b/solution.py
@@ -599,17 +599,14 @@
 
 
 def reduce_grads(head_part, norm_part, bc_part, tick_count):
-    head_count = lax.axis_size("head")
-    host = head_part[0]
-    width = host.shape[-1]
-    joined = jnp.concatenate([host, bc_part.reshape(-1, width)], axis=0)
-    summed = tuple(
+    summed = lax.psum(
+        tuple(member.astype(jnp.bfloat16) for member in head_part[:3] + (bc_part,)), "seq"
+    )
+    head_sum = tuple(member.astype(jnp.float32) for member in summed[:3]) + tuple(
         lax.psum(member.astype(jnp.bfloat16), "seq").astype(jnp.float32)
-        for member in (joined,) + tuple(head_part[1:])
-    )
-    head_sum = (summed[0][: host.shape[0]],) + summed[1:]
-    bc_sum = summed[0][host.shape[0] :].reshape(bc_part.shape)
-    bc_rows = head_gather(bc_sum, (0, 0, 1), 4 * tick_count + 1)
+        for member in head_part[3:]
+    )
+    bc_rows = head_gather(summed[3], (0, 0, 1), 4 * tick_count + 1).astype(jnp.float32)
     norm_sum = lax.psum(norm_part, ("seq", "head"))
     return (head_sum, norm_sum, bc_rows.reshape(-1, bc_rows.shape[-1]))
 

time: 1560 us -> 1510 us (0.968)
  Pallas kernels: 394 us -> 374 us
  local copies, waits for them, and re-layouts: 209 us -> 191 us
    another operation x38 -> x36, other arithmetic: 46.1 us -> 24.2 us
    broadcast_in_dim x0 -> x1, other arithmetic: none -> 21.5 us  [on_device(): head_total[1][None]]
    pallas_call x7, Pallas kernels: 181 us -> 163 us  [head_gather(): pl.pallas_call(functools.partial(gather_body, n, tick), out_shape=jax.Sha...]
    unnamed x892 -> x844, local copies, waits for them, and re-layouts: 71 us -> 66.6 us
  transfers between devices with their start and end apart: 21 -> 21, of which waited for: 9 -> 9; matrix products, arithmetic and copies ran while one was open for 23% -> 24% of each run, Pallas kernels for 10% -> 10%
where the time goes in v8:
time: 1510 us; the launch traced here: 1500 us
  Pallas kernels  374 us (25%)
  matrix products  346 us (23%)
  other arithmetic  250 us (17%)
  local copies, waits for them, and re-layouts  191 us (13%)
  blocking collectives  166 us (11%)
  waiting for transfers between devices  123 us (8%)
  starting transfers between devices  33.8 us (2%)
  between operations  21.1 us (1%)
    pallas_call x7, Pallas kernels, head_scatter(): pl.pallas_call(functools.partial(scatter_body, n, tick), out_shape=jax.Sh...  210 us
    pallas_call x7, Pallas kernels, head_gather(): pl.pallas_call(functools.partial(gather_body, n, tick), out_shape=jax.Sha...  163 us
    dot_general x9, matrix products, block_output(): jnp.einsum('cijh,cjhp->cihp', weights, x_blocks, precision=highest)  101 us
    unnamed x844, local copies, waits for them, and re-layouts  66.6 us
    psum x1, blocking collectives, reduce_grads(): norm_sum = lax.psum(norm_part, ('seq', 'head'))  38.6 us
    dot_general x3, matrix products, mixer_forward(): projected = jnp.dot(gathered, w_main, preferred_element_type=jnp.float32)  38.1 us
    psum x1, waiting for transfers between devices, reduce_grads(): lax.psum(tuple((member.astype(jnp.bfloat16) for member in head_part[:3] +...  35.8 us
    psum x3, blocking collectives, mixer_forward(): square_total = lax.psum(jnp.sum(gated_mix * gated_mix, axis=-1), 'head')  35 us
  transfers between devices with their start and end apart: 21, of which 9 were waited for; matrix products, arithmetic and copies ran while one was open for 24% of the time, Pallas kernels for 10%

profile of v8, /device:TPU:0, one launch (start us, length us, event | category | flops | bytes accessed | tf_op | source)
XLA Modules:
  0.0 1504.6 jit_solution(488894429453921759)
XLA Ops:
  20.9 29.3 %shard_map.297 = bf16[4,128,2048]{2,1,0:T(8,128)(2,1)} custom-call(bf16[128,2048]{1,0:T(8,128)(2,1)} %fusion.224.x_ref), custom_call_target="tpu_custom_call" | custom-call | tf_op jit(solution)/shard_map/pallas_call | solution.py:113
  50.5 12.7 fusion.417
  96.4 7.1 all-gather
  117.3 12.8 all-gather.13.cloned.1.call-done
  134.7 9.4 fusion.133
  144.1 13.4 copy.510
  160.7 11.7 psum.126
  174.0 6.9 fusion.39.p_ref
  180.9 36.8 %shard_map.298 = f32[128,2048]{1,0:T(8,128)} custom-call(f32[4,128,2048]{2,1,0:T(8,128)} %fusion.39.p_ref), custom_call_target="tpu_custom_call" | custom-call | tf_op jit(solution)/shard_map/pallas_call | solution.py:209
  226.2 43.4 %shard_map.299 = bf16[4,128,2048]{2,1,0:T(8,128)(2,1)} custom-call(bf16[128,2048]{1,0:T(8,128)(2,1)} %multiply_convert_fusion.7.x_ref), custom_call_target="tpu_custom_call" | custom-call | tf_op jit(solution)/shard_map/pallas_call | solution.py:113
  269.6 12.9 fusion.416
  298.2 9.4 fusion.111
  326.2 6.9 all-gather.1
  341.7 10.2 all-gather.15.cloned.1.call-done
  356.6 9.4 fusion.132
  371.1 11.7 psum.127
  386.4 6.9 fusion.37.p_ref
  393.2 46.7 %shard_map.300 = f32[128,2048]{1,0:T(8,128)} custom-call(f32[4,128,2048]{2,1,0:T(8,128)} %fusion.37.p_ref), custom_call_target="tpu_custom_call" | custom-call | tf_op jit(solution)/shard_map/pallas_call | solution.py:209
  451.5 12.5 fusion.415
  491.6 7.9 all-gather.5
  505.1 7.0 all-gather.4
  513.3 7.8 all-gather.3
  521.1 7.4 all-gather.2
  538.7 8.7 all-gather.17.cloned.1.call-done
  552.0 9.4 fusion.131
  567.7 11.7 psum.128
  579.4 7.9 multiply_reduce_fusion.20
  587.3 8.3 psum.129
  595.7 6.9 multiply_reduce_fusion.23
  611.6 15.8 %fusion.29 = (f32[2,256,16]{1,2,0:T(8,128)}, f32[2,256,16]{1,2,0:T(8,128)}, f32[2,256,16]{1,2,0:T(8,128)}, f32[2,256,256]{2,1,0:T(8,128)S(1)}) fusion(f32[2,256,16]{1,2,0:T(8,128)} %bitcast.1081, f32[2,256,256]{2,1,0:T(8,128)} %fusion.453, f32[2,256,16]{1,2,0:T(8,128)} %copy-done.209, pred[2,256,256]{2,1,0:T(8,128)(4,1)} %get-tuple-element.266, ...), kind=kOutput, calls=%fused_computation.47 | convolution fusion | flops 1637720064 | bytes 5537792 | tf_op jit(solution)/shard_map/transpose(jvp(cijh,cjhp->cihp))/dot_general | solution.py:356
  640.7 20.1 %all-gather.19.cloned.1.call-done = bf16[4,16,64,128]{3,2,1,0:T(8,128)(2,1)} async-done(((bf16[1,16,64,128]{3,2,1,0:T(8,128)(2,1)}), bf16[4,16,64,128]{3,2,1,0:T(8,128)(2,1)}) %all-gather.19.cloned.1.call-update) | async-done | bytes 1048592 | tf_op jit(solution)/shard_map/all_gather | solution.py:259
  670.4 9.2 fusion.127
  683.9 6.3 multiply_reduce_fusion.13
  746.8 11.0 fusion.251
  761.5 22.2 %collective-permute-done.9 = bf16[128,2048]{1,0:T(8,128)(2,1)S(1)} collective-permute-done((bf16[128,2048]{1,0:T(8,128)(2,1)S(1)}, bf16[128,2048]{1,0:T(8,128)(2,1)S(1)}, u32[]{:S(2)}, u32[]{:S(2)}) %collective-permute-start.9) | collective-permute-done | bytes 524320 | tf_op jit(solution)/shard_map/ppermute | solution.py:236
  785.5 33.2 %shard_map.305 = bf16[4,128,2048]{2,1,0:T(8,128)(2,1)} custom-call(bf16[128,2048]{1,0:T(8,128)(2,1)} %fusion.242.x_ref), custom_call_target="tpu_custom_call" | custom-call | tf_op jit(solution)/shard_map/pallas_call | solution.py:113
  818.8 8.0 multiply_reduce_fusion.19
  826.8 10.6 psum.130
  837.4 6.0 multiply_reduce_fusion.22
  852.7 15.7 %fusion.31 = (f32[2,256,16]{1,2,0:T(8,128)}, f32[2,256,16]{1,2,0:T(8,128)}, f32[2,256,16]{1,2,0:T(8,128)}, f32[2,256,256]{2,1,0:T(8,128)S(1)}) fusion(f32[2,256,16]{1,2,0:T(8,128)S(1)} %bitcast.1080, f32[2,256,256]{2,1,0:T(8,128)} %fusion.452, f32[2,256,16]{1,2,0:T(8,128)S(1)} %copy-done.208, pred[2,256,256]{2,1,0:T(8,128)(4,1)S(1)} %copy-done.192, ...), kind=kOutput, calls=%fused_computation.49 | convolution fusion | flops 1637720064 | bytes 5537792 | tf_op jit(solution)/shard_map/transpose(jvp(cijh,cjhp->cihp))/dot_general | solution.py:356
  894.8 9.0 fusion.123
  908.2 6.3 multiply_reduce_fusion.9
  962.3 51.7 %shard_map.306 = f32[128,2048]{1,0:T(8,128)} custom-call(f32[4,128,2048]{2,1,0:T(8,128)} %bitcast.971), custom_call_target="tpu_custom_call" | custom-call | tf_op jit(solution)/shard_map/pallas_call | solution.py:209
  1019.1 10.9 fusion.249
  1035.8 28.3 %shard_map.307 = bf16[4,128,2048]{2,1,0:T(8,128)(2,1)} custom-call(bf16[128,2048]{1,0:T(8,128)(2,1)} %fusion.243.x_ref), custom_call_target="tpu_custom_call" | custom-call | tf_op jit(solution)/shard_map/pallas_call | solution.py:113
  1064.1 8.0 multiply_reduce_fusion.18
  1072.1 11.1 psum.131
  1092.5 15.6 %fusion.33 = (f32[2,256,16]{1,2,0:T(8,128)}, f32[2,256,16]{1,2,0:T(8,128)}, f32[2,256,16]{1,2,0:T(8,128)}, f32[2,256,256]{2,1,0:T(8,128)S(1)}) fusion(f32[2,256,16]{1,2,0:T(8,128)S(1)} %bitcast.1076, f32[2,256,256]{2,1,0:T(8,128)S(1)} %copy-done.171, f32[2,256,16]{1,2,0:T(8,128)S(1)} %copy-done.205, pred[2,256,256]{2,1,0:T(8,128)(4,1)S(1)} %copy-done.189, ...), kind=kOutput, calls=%fused_computation.51 | convolution fusion | flops 1637720064 | bytes 5537792 | tf_op jit(solution)/shard_map/transpose(jvp(cijh,cjhp->cihp))/dot_general | solution.py:356
  1119.3 10.3 add_convert_fusion
  1129.8 8.2 all-gather.23.cloned.1.call-done
  1148.0 7.4 fusion.119
  1183.0 6.0 pad_add_fusion
  1206.3 30.9 %shard_map.308 = f32[520,256]{1,0:T(8,128)} custom-call(f32[4,520,256]{2,1,0:T(8,128)} %bitcast.975), custom_call_target="tpu_custom_call" | custom-call | tf_op jit(solution)/shard_map/pallas_call | solution.py:209
  1244.0 5.9 copy-done.49
  1253.3 21.5 %fusion.34 = (bf16[1,2048,1024]{1,2,0:T(8,128)(2,1)}, bf16[1,2048,1024]{1,2,0:T(8,128)(2,1)}) fusion(f32[2048,2064]{0,1:T(8,128)} %copy-done.49, f32[2048,2064]{0,1:T(8,128)} %fusion.249, f32[2048,2064]{0,1:T(8,128)} %fusion.251, f32[]{:T(128)S(6)} %convert_element_type.597, f32[]{:T(128)S(6)} %convert_element_type.596, f32[]{:T(128)S(6)} %convert_element_type.595, ...), kind=kLoop, calls=%fused_computation.58 | loop fusion | flops 27262976 | bytes 58720272 | tf_op jit(solution)/shard_map/broadcast_in_dim | solution.py:753
  1278.1 7.5 fusion.35.p_ref
  1296.7 18.7 %all-reduce.64 = (bf16[1,4,1024]{2,1,0:T(4,128)(2,1)S(1)}, bf16[1,1024]{1,0:T(2,128)(2,1)S(1)}, bf16[1,16]{1,0:T(2,128)(2,1)S(1)}, bf16[1,16]{1,0:T(2,128)(2,1)S...) all-reduce(bf16[1,4,1024]{2,1,0:T(4,128)(2,1)S(1)} %fusion.338, ...), channel_id=1, replica_groups=mesh['section'=2,'seq'=4,'head'=4] {'seq'}, use_global_device_ids=true, to_apply=%region_96.98 | all-reduce | flops 6192 | bytes 24768 | tf_op jit(solution)/shard_map/psum | solution.py:606
  1320.6 8.1 fusion.248
  1334.4 37.1 %shard_map.309 = f32[128,2048]{1,0:T(8,128)} custom-call(f32[4,128,2048]{2,1,0:T(8,128)} %bitcast.969), custom_call_target="tpu_custom_call" | custom-call | tf_op jit(solution)/shard_map/pallas_call | solution.py:209
  1373.2 38.6 %psum.132 = f32[1,2048]{1,0:T(1,128)} all-reduce(f32[1,2048]{1,0:T(1,128)S(1)} %bitcast.1090), channel_id=1, replica_groups=mesh['section'=2,'seq'=4,'head'=4] {'seq','head'}, use_global_device_ids=true, to_apply=%region_90.92 | all-reduce | flops 2048 | bytes 16384 | tf_op jit(solution)/shard_map/psum | solution.py:610
  1419.5 35.8 %all-reduce.71.cloned.1.call-done = (bf16[1,2048,1024]{1,2,0:T(8,128)(2,1)}, bf16[1,2048,1024]{1,2,0:T(8,128)(2,1)}, bf16[520,256]{1,0:T(8,128)(2,1)}, bf16[1,2048,16]{1,2,0:T(8,128)(2,1)}) async-done(((bf16[1,2048,1024]{1,2,0:T(8,128)(2,1)}, bf16[1,2048,1024]{1,2,0:T(8,128)(2,1)}, bf16[520,256]{1,0:T(8,128)(2,1)}, bf16[1,2048,16]{1,2,0:T(8,128)(2,1)}), (bf16[1,2048,1024]{1,2,0:T(8,128)(2,1)}, ...) | async-done | bytes 8720400 | tf_op jit(solution)/shard_map/psum | solution.py:602
  1455.3 23.8 %shard_map.310 = bf16[4,520,256]{2,1,0:T(8,128)(2,1)} custom-call(bf16[520,256]{1,0:T(8,128)(2,1)} %get-tuple-element.171.x_ref), custom_call_target="tpu_custom_call" | custom-call | tf_op jit(solution)/shard_map/pallas_call | solution.py:113
  1483.1 6.9 copy.616
  1489.9 6.9 copy.617
  (1280 shorter events, 518.1 us)
Async XLA Ops:
  7.2 43.0 %copy-start.211 = (bf16[1,2048,16]{1,2,0:T(8,128)(2,1)S(1)}, bf16[1,2048,16]{1,2,0:T(8,128)(2,1)}, u32[]{:S(2)}) copy-start(bf16[1,2048,16]{1,2,0:T(8,128)(2,1)} %param.27) | copy-start | bytes 196612
  7.2 43.3 %copy-start.56 = (bf16[1,2048,256]{2,1,0:T(8,128)(2,1)S(1)}, bf16[1,2048,256]{2,1,0:T(8,128)(2,1)}, u32[]{:S(2)}) copy-start(bf16[1,2048,256]{2,1,0:T(8,128)(2,1)} %param.26) | copy-start | bytes 3145732
  7.2 122.9 %all-gather.13.cloned.1.call-start = ((), (), s32[]{:S(2)}) async-start(), calls=%async_computation | async-start | bytes 2621440 | tf_op jit(solution)/shard_map/all_gather | solution.py:241
  8.7 70.4 %collective-permute-start = (f32[3]{0:T(128)S(1)}, f32[3]{0:T(128)S(1)}, u32[]{:S(2)}, u32[]{:S(2)}) collective-permute-start(f32[3]{0:T(128)S(1)} %slice.590), channel_id=1, source_target_pairs={{0,4},{4,8},{8,12},{1,5},{5,9},{9,13},{2,6},{6,10},{10,14},{3,7},{... | collective-permute-start | bytes 44 | tf_op jit(solution)/shard_map/ppermute | solution.py:236
  13.7 65.5 %collective-permute-start.3 = (f32[3]{0:T(128)S(1)}, f32[3]{0:T(128)S(1)}, u32[]{:S(2)}, u32[]{:S(2)}) collective-permute-start(f32[3]{0:T(128)S(1)} %slice.629), channel_id=1, source_target_pairs={{0,4},{4,8},{8,12},{1,5},{5,9},{9,13},{2,6},{6,10},{10,14},{3,7},{... | collective-permute-start | bytes 44 | tf_op jit(solution)/shard_map/ppermute | solution.py:236
  18.9 31.3 %copy-start.339 = (f32[128]{0:T(128)}, f32[128]{0:T(128)S(1)}, u32[]{:S(2)}) copy-start(f32[128]{0:T(128)S(1)} %get-tuple-element.333) | copy-start | bytes 1540
  65.9 14.8 collective-permute-start.1
  73.0 30.5 %copy-start.145 = (f32[512,16]{0,1:T(8,128)}, f32[512,16]{0,1:T(8,128)S(1)}, u32[]{:S(2)}) copy-start(f32[512,16]{0,1:T(8,128)S(1)} %get-tuple-element.227) | copy-start | bytes 98308
  79.1 55.5 %copy-start.178 = (f32[2,256,16]{1,2,0:T(8,128)}, f32[2,256,16]{1,2,0:T(8,128)S(1)}, u32[]{:S(2)}) copy-start(f32[2,256,16]{1,2,0:T(8,128)S(1)} %get-tuple-element.276) | copy-start | bytes 98308
  90.7 43.9 %copy-start.9 = (f32[2,256,16,64]{1,0,3,2:T(2,128)}, f32[2,256,16,64]{1,0,3,2:T(2,128)S(1)}, u32[]{:S(2)}) copy-start(f32[2,256,16,64]{1,0,3,2:T(2,128)S(1)} %reshape.960) | copy-start | bytes 6291460
  94.7 35.4 %copy-start.61 = (f32[2,16,64,128]{3,2,1,0:T(8,128)}, f32[2,16,64,128]{3,2,1,0:T(8,128)S(1)}, u32[]{:S(2)}) copy-start(f32[2,16,64,128]{3,2,1,0:T(8,128)S(1)} %fusion.159) | copy-start | bytes 3145732
  96.4 255.5 %all-gather.15.cloned.1.call-start = ((), (), s32[]{:S(2)}) async-start(), calls=%async_computation.1 | async-start | bytes 2621440 | tf_op jit(solution)/shard_map/all_gather | solution.py:241
  180.9 38.4 %copy-start.50 = (bf16[2,128,2048]{2,1,0:T(8,128)(2,1)S(1)}, bf16[2,128,2048]{2,1,0:T(8,128)(2,1)}, u32[]{:S(2)}) copy-start(bf16[2,128,2048]{2,1,0:T(8,128)(2,1)} %param.19) | copy-start | bytes 3145732
  220.6 3.7 collective-permute-start.2
  223.6 70.1 %copy-start.265 = (f32[2,256]{1,0:T(2,128)}, f32[2,256]{1,0:T(2,128)S(1)}, u32[]{:S(2)}) copy-start(f32[2,256]{1,0:T(2,128)S(1)} %get-tuple-element.343) | copy-start | bytes 6148
  223.6 70.1 %copy-start.307 = (f32[2,256]{1,0:T(2,128)}, f32[2,256]{1,0:T(2,128)S(1)}, u32[]{:S(2)}) copy-start(f32[2,256]{1,0:T(2,128)S(1)} %get-tuple-element.344) | copy-start | bytes 6148
  224.3 73.8 %copy-start.243 = (f32[512]{0:T(512)}, f32[512]{0:T(512)S(1)}, u32[]{:S(2)}) copy-start(f32[512]{0:T(512)S(1)} %get-tuple-element.287) | copy-start | bytes 6148
  224.3 73.9 %copy-start.245 = (f32[512]{0:T(512)}, f32[512]{0:T(512)S(1)}, u32[]{:S(2)}) copy-start(f32[512]{0:T(512)S(1)} %get-tuple-element.288) | copy-start | bytes 6148
  224.3 73.9 %copy-start.247 = (f32[512]{0:T(512)}, f32[512]{0:T(512)S(1)}, u32[]{:S(2)}) copy-start(f32[512]{0:T(512)S(1)} %get-tuple-element.289) | copy-start | bytes 6148
  224.6 215.3 %copy-start.25 = (f32[128,2048]{1,0:T(8,128)}, f32[128,2048]{1,0:T(8,128)S(1)}, u32[]{:S(2)}) copy-start(f32[128,2048]{1,0:T(8,128)S(1)} %get-tuple-element.219) | copy-start | bytes 3145732
  225.2 57.3 %copy-start.353 = (f32[128]{0:T(128)}, f32[128]{0:T(128)S(1)}, u32[]{:S(2)}) copy-start(f32[128]{0:T(128)S(1)} %get-tuple-element.335) | copy-start | bytes 1540
  269.6 23.4 %copy-start.351 = (f32[2]{0:T(128)S(1)}, f32[2]{0:T(128)}, u32[]{:S(2)}) copy-start(f32[2]{0:T(128)} %get-tuple-element.346) | copy-start | bytes 28
  287.1 10.8 collective-permute-start.4
  291.4 41.7 %copy-start.147 = (f32[512,16]{0,1:T(8,128)}, f32[512,16]{0,1:T(8,128)S(1)}, u32[]{:S(2)}) copy-start(f32[512,16]{0,1:T(8,128)S(1)} %get-tuple-element.215) | copy-start | bytes 98308
  293.8 62.8 %copy-start.182 = (f32[2,256,16]{1,2,0:T(8,128)}, f32[2,256,16]{1,2,0:T(8,128)S(1)}, u32[]{:S(2)}) copy-start(f32[2,256,16]{1,2,0:T(8,128)S(1)} %get-tuple-element.274) | copy-start | bytes 98308
  312.7 43.8 %copy-start.11 = (f32[2,256,16,64]{1,0,3,2:T(2,128)}, f32[2,256,16,64]{1,0,3,2:T(2,128)S(1)}, u32[]{:S(2)}) copy-start(f32[2,256,16,64]{1,0,3,2:T(2,128)S(1)} %reshape.972) | copy-start | bytes 6291460
  318.7 228.7 %all-gather.17.cloned.1.call-start = ((), (), s32[]{:S(2)}) async-start(), calls=%async_computation.2 | async-start | bytes 2621440 | tf_op jit(solution)/shard_map/all_gather | solution.py:241
  320.0 124.2 %collective-permute-start.6 = (f32[3]{0:T(128)}, f32[3]{0:T(128)}, u32[]{:S(2)}, u32[]{:S(2)}) collective-permute-start(f32[3]{0:T(128)} %slice.664), channel_id=1, source_target_pairs={{0,4},{4,8},{8,12},{1,5},{5,9},{9,13},{2,6},{6,10},{10,14},{3,7},{... | collective-permute-start | bytes 44 | tf_op jit(solution)/shard_map/ppermute | solution.py:236
  333.1 23.5 %copy-start.287 = (f32[2,2,8,256]{3,2,0,1:T(8,128)}, f32[2,2,8,256]{3,2,0,1:T(8,128)S(1)}, u32[]{:S(2)}) copy-start(f32[2,2,8,256]{3,2,0,1:T(8,128)S(1)} %copy.946) | copy-start | bytes 98308
  393.2 46.7 %copy-start.112 = (f32[1,128,2048]{2,1,0:T(8,128)S(1)}, f32[1,128,2048]{2,1,0:T(8,128)}, u32[]{:S(2)}) copy-start(f32[1,128,2048]{2,1,0:T(8,128)} %constant_dynamic-slice_fusion.3) | copy-start | bytes 3145732
  442.8 3.8 collective-permute-start.5
  444.2 28.3 %copy-start.390 = (f32[2]{0:T(128)}, f32[2]{0:T(128)S(1)}, u32[]{:S(2)}) copy-start(f32[2]{0:T(128)S(1)} %fusion.369) | copy-start | bytes 28
  445.6 31.1 %copy-start.249 = (f32[512]{0:T(512)}, f32[512]{0:T(512)S(1)}, u32[]{:S(2)}) copy-start(f32[512]{0:T(512)S(1)} %get-tuple-element.281) | copy-start | bytes 6148
  445.6 31.1 %copy-start.251 = (f32[512]{0:T(512)}, f32[512]{0:T(512)S(1)}, u32[]{:S(2)}) copy-start(f32[512]{0:T(512)S(1)} %get-tuple-element.282) | copy-start | bytes 6148
  445.6 31.1 %copy-start.253 = (f32[512]{0:T(512)}, f32[512]{0:T(512)S(1)}, u32[]{:S(2)}) copy-start(f32[512]{0:T(512)S(1)} %get-tuple-element.283) | copy-start | bytes 6148
  466.7 9.7 collective-permute-start.7
  486.5 175.9 %copy-start.14 = (f32[2,256,16,64]{1,0,3,2:T(2,128)}, f32[2,256,16,64]{1,0,3,2:T(2,128)S(1)}, u32[]{:S(2)}) copy-start(f32[2,256,16,64]{1,0,3,2:T(2,128)S(1)} %reshape.984) | copy-start | bytes 6291460
  490.4 57.0 %copy-start.64 = (f32[2,16,64,128]{3,2,1,0:T(8,128)}, f32[2,16,64,128]{3,2,1,0:T(8,128)S(1)}, u32[]{:S(2)}) copy-start(f32[2,16,64,128]{3,2,1,0:T(8,128)S(1)} %fusion.151) | copy-start | bytes 3145732
  491.5 169.3 %all-gather.19.cloned.1.call-start = ((), (), s32[]{:S(2)}) async-start(), calls=%async_computation.3 | async-start | bytes 1310720 | tf_op jit(solution)/shard_map/all_gather | solution.py:259
  611.5 273.6 %all-gather.21.cloned.1.call-start = ((), (), s32[]{:S(2)}) async-start(), calls=%async_computation.4 | async-start | bytes 1310720 | tf_op jit(solution)/shard_map/all_gather | solution.py:259
  690.2 29.9 %copy-start.219 = (f32[1280]{0:T(1024)}, f32[1280]{0:T(1024)S(1)}, u32[]{:S(2)}) copy-start(f32[1280]{0:T(1024)S(1)} %get-tuple-element.135) | copy-start | bytes 15364
  701.6 19.1 %collective-permute-start.8 = (f32[3,1280]{1,0:T(4,128)}, f32[3,1280]{1,0:T(4,128)}, u32[]{:S(2)}, u32[]{:S(2)}) collective-permute-start(f32[3,1280]{1,0:T(4,128)} %copy.559), channel_id=1, source_target_pairs={{4,0},{8,4},{12,8},{5,1},{9,5},{13,9},{6,2},{10,6},{14,10},{7,3},{... | collective-permute-start | bytes 46088 | tf_op jit(solution)/shard_map/ppermute | solution.py:236
  745.3 38.5 %collective-permute-start.9 = (bf16[128,2048]{1,0:T(8,128)(2,1)S(1)}, bf16[128,2048]{1,0:T(8,128)(2,1)S(1)}, u32[]{:S(2)}, u32[]{:S(2)}) collective-permute-start(bf16[128,2048]{1,0:T(8,128)(2,1)S(1)} %get-tuple-element.194), channel_id=1, source_target_pairs={{16,0},{17,1},{18,2},{19,3},{20,4},{21,5},{22,6},{23,7},{24,8},{25... | collective-permute-start | bytes 1572872 | tf_op jit(solution)/shard_map/ppermute | solution.py:236
  761.5 57.2 %copy-start.322 = (f32[512]{0:T(512)S(1)}, f32[512]{0:T(512)}, u32[]{:S(2)}) copy-start(f32[512]{0:T(512)} %copy-done.321) | copy-start | bytes 6148
  852.6 285.4 %all-gather.23.cloned.1.call-start = ((), (), s32[]{:S(2)}) async-start(), calls=%async_computation.5 | async-start | bytes 1310720 | tf_op jit(solution)/shard_map/all_gather | solution.py:259
  914.5 29.8 %copy-start.221 = (f32[1280]{0:T(1024)}, f32[1280]{0:T(1024)S(1)}, u32[]{:S(2)}) copy-start(f32[1280]{0:T(1024)S(1)} %get-tuple-element.136) | copy-start | bytes 15364
  925.8 19.1 %collective-permute-start.10 = (f32[3,1280]{1,0:T(4,128)}, f32[3,1280]{1,0:T(4,128)}, u32[]{:S(2)}, u32[]{:S(2)}) collective-permute-start(f32[3,1280]{1,0:T(4,128)} %copy.582), channel_id=1, source_target_pairs={{4,0},{8,4},{12,8},{5,1},{9,5},{13,9},{6,2},{10,6},{14,10},{7,3},{... | collective-permute-start | bytes 46088 | tf_op jit(solution)/shard_map/ppermute | solution.py:236
  962.2 51.7 %copy-start.26 = (f32[128,2048]{1,0:T(8,128)S(1)}, f32[128,2048]{1,0:T(8,128)}, u32[]{:S(2)}) copy-start(f32[128,2048]{1,0:T(8,128)} %copy-done.25) | copy-start | bytes 3145732
  962.2 51.7 %copy-start.354 = (f32[128]{0:T(128)S(1)}, f32[128]{0:T(128)}, u32[]{:S(2)}) copy-start(f32[128]{0:T(128)} %copy-done.353) | copy-start | bytes 1540
  962.2 54.0 %copy-start.66 = (bf16[2,128,2048]{2,1,0:T(8,128)(2,1)S(1)}, bf16[2,128,2048]{2,1,0:T(8,128)(2,1)}, u32[]{:S(2)}) copy-start(bf16[2,128,2048]{2,1,0:T(8,128)(2,1)} %param.20) | copy-start | bytes 3145732
  962.2 54.0 %copy-start.138 = (bf16[128,2048]{1,0:T(8,128)(2,1)S(1)}, bf16[128,2048]{1,0:T(8,128)(2,1)}, u32[]{:S(2)}) copy-start(bf16[128,2048]{1,0:T(8,128)(2,1)} %copy-done.137) | copy-start | bytes 1572868
  962.2 54.0 %copy-start.399 = (f32[128]{0:T(128)S(1)}, f32[128]{0:T(128)}, u32[]{:S(2)}) copy-start(f32[128]{0:T(128)} %get-tuple-element.334) | copy-start | bytes 1540
  1017.7 16.3 %collective-permute-start.11 = (bf16[128,2048]{1,0:T(8,128)(2,1)S(1)}, bf16[128,2048]{1,0:T(8,128)(2,1)S(1)}, u32[]{:S(2)}, u32[]{:S(2)}) collective-permute-start(bf16[128,2048]{1,0:T(8,128)(2,1)S(1)} %get-tuple-element.190), channel_id=1, source_target_pairs={{16,0},{17,1},{18,2},{19,3},{20,4},{21,5},{22,6},{23,7},{24,8},{25... | collective-permute-start | bytes 1572872 | tf_op jit(solution)/shard_map/ppermute | solution.py:236
  1034.0 30.1 %copy-start.320 = (f32[512]{0:T(512)S(1)}, f32[512]{0:T(512)}, u32[]{:S(2)}) copy-start(f32[512]{0:T(512)} %copy-done.319) | copy-start | bytes 6148
  1114.6 136.9 %all-reduce.69.cloned.1.call-start = ((), (), s32[]{:S(2)}) async-start(), calls=%async_computation.6 | async-start | bytes 8388608 | tf_op jit(solution)/shard_map/psum | solution.py:726
  1129.6 325.7 %all-reduce.71.cloned.1.call-start = ((), (), s32[]{:S(2)}) async-start(), calls=%async_computation.7 | async-start | bytes 17440768 | tf_op jit(solution)/shard_map/psum | solution.py:602
  1179.5 11.9 collective-permute-start.12
  1206.3 32.9 %copy-start.33 = (f32[509,1280]{0,1:T(8,128)S(1)}, f32[509,1280]{0,1:T(8,128)}, u32[]{:S(2)}) copy-start(f32[509,1280]{0,1:T(8,128)} %slice.886) | copy-start | bytes 7818244
  1294.9 25.6 %copy-start.154 = (bf16[512,1024]{0,1:T(8,128)(2,1)S(1)}, bf16[512,1024]{0,1:T(8,128)(2,1)}, u32[]{:S(2)}) copy-start(bf16[512,1024]{0,1:T(8,128)(2,1)} %get-tuple-element.232) | copy-start | bytes 3145732
  1334.4 37.1 %copy-start.52 = (bf16[2,128,2048]{2,1,0:T(8,128)(2,1)S(1)}, bf16[2,128,2048]{2,1,0:T(8,128)(2,1)}, u32[]{:S(2)}) copy-start(bf16[2,128,2048]{2,1,0:T(8,128)(2,1)} %param.19) | copy-start | bytes 3145732
  1334.4 37.2 %copy-start.340 = (f32[128]{0:T(128)S(1)}, f32[128]{0:T(128)}, u32[]{:S(2)}) copy-start(f32[128]{0:T(128)} %copy-done.339) | copy-start | bytes 1540
  1334.4 38.8 %copy-start.271 = (f32[2048]{0:T(1024)S(1)}, f32[2048]{0:T(1024)}, u32[]{:S(2)}) copy-start(f32[2048]{0:T(1024)} %get-tuple-element.141) | copy-start | bytes 24580
  1334.4 38.8 %copy-start.272 = (f32[2048]{0:T(1024)S(1)}, f32[2048]{0:T(1024)}, u32[]{:S(2)}) copy-start(f32[2048]{0:T(1024)} %get-tuple-element.143) | copy-start | bytes 24580
  1334.4 77.4 %copy-start.398 = (f32[128]{0:T(128)S(1)}, f32[128]{0:T(128)}, u32[]{:S(2)}) copy-start(f32[128]{0:T(128)} %get-tuple-element.332) | copy-start | bytes 1540
  (371 other events, 2171.4 us)
Sparse Core Ops, SparseCore 0:
  96.5 33.5 all-gather.12
  318.8 33.1 all-gather.14
  491.7 55.6 all-gather.16
  611.6 49.1 all-gather.18
  852.7 32.3 all-gather.20
  1114.7 23.2 all-gather.22
  1141.3 104.1 all-reduce.68
  1275.0 180.3 all-reduce.70

commit v9 on v8

--- a/solution.py
+++ b/solution.py
@@ -201,6 +201,14 @@
     @pl.when(jnp.logical_not(valid))
     def _():
         o_ref[...] = jnp.zeros(o_ref.shape, o_ref.dtype)
+
+
+def head_sum_rows(values, tick, cid):
+    blocks = head_gather(values.reshape(-1, 128), tick, cid)
+    total = blocks[0]
+    for index in range(1, blocks.shape[0]):
+        total = total + blocks[index]
+    return total.reshape(values.shape)
 
 
 def head_scatter(parts, tick, cid, link=jnp.bfloat16):
@@ -443,7 +451,7 @@
     mixed_out, rear_pull = jax.vjp(local_rear, block_parts, b_mat, c_mat, skip, start_state)
     silu_gate = jax.nn.silu(gate_pre)
     gated_mix = mixed_out * silu_gate
-    square_total = lax.psum(jnp.sum(gated_mix * gated_mix, axis=-1), "head")
+    square_total = head_sum_rows(jnp.sum(gated_mix * gated_mix, axis=-1), tick, ids[2])
     scale_out = lax.rsqrt(square_total / DI + norm_eps)
     normed_out = (gated_mix * scale_out[:, None] * gate_gain).astype(jnp.bfloat16)
     head_count = lax.axis_size("head")
@@ -511,7 +519,7 @@
     )
     weighted = grad_normed * gate_gain
     g_gate_gain = jnp.sum(grad_normed * gated_mix * scale_out[:, None], axis=0)
-    cross_sum = lax.psum(jnp.sum(weighted * gated_mix, axis=-1), "head")
+    cross_sum = head_sum_rows(jnp.sum(weighted * gated_mix, axis=-1), tick, ids[2])
     grad_gated = (
         scale_out[:, None] * weighted - gated_mix * (scale_out**3 * cross_sum / DI)[:, None]
     )
@@ -677,7 +685,7 @@
             alive_mask,
             layer_weights,
             (tick_index, -1, micro_count),
-            (tick_index, tick_count + tick_index),
+            (tick_index, tick_count + tick_index, 4 * tick_count + 2 + tick_index),
         )
         outputs_all = store_slot(outputs_all, result, clipped, is_valid)
         ticks.append((clipped, is_valid, saved))
@@ -715,7 +723,11 @@
             saved,
             mask_value,
             (tick_count - 1 - tick_index, -1, micro_count),
-            (2 * tick_count + tick_index, 3 * tick_count + tick_index),
+            (
+                2 * tick_count + tick_index,
+                3 * tick_count + tick_index,
+                5 * tick_count + 2 + tick_index,
+            ),
             hook,
         )
         if tick_index == 0:

time: 1510 us -> 1520 us (level)
  blocking collectives: 166 us -> 101 us
  Pallas kernels: 374 us -> 419 us
  waiting for transfers between devices: 123 us -> 149 us
    psum x6 -> x0, blocking collectives: 65.1 us -> none  [the longest x3 35 us: mixer_forward(): square_total = lax.psum(jnp.sum(gated_mix * gated_mix, axis=-1), 'head')]
    pallas_call x7 -> x13, Pallas kernels: 163 us -> 209 us  [head_gather(): pl.pallas_call(functools.partial(gather_body, n, tick), out_shape=jax.Sha...]
    all_gather x3, waiting for transfers between devices: 31.7 us -> 59 us  [entering_2(): lax.all_gather(a.astype(kind), axis)]
    unnamed x844 -> x842, local copies, waits for them, and re-layouts: 66.6 us -> 66.6 us
  transfers between devices with their start and end apart: 21 -> 21, of which waited for: 9 -> 9; matrix products, arithmetic and copies ran while one was open for 24% -> 24% of each run, Pallas kernels for 10% -> 11%
where the time goes in v9:
time: 1520 us
  Pallas kernels  419 us (28%)
  matrix products  346 us (23%)
  other arithmetic  256 us (17%)
  local copies, waits for them, and re-layouts  191 us (13%)
  waiting for transfers between devices  149 us (10%)
  blocking collectives  101 us (7%)
  starting transfers between devices  33.9 us (2%)
  between operations  21.2 us (1%)
    pallas_call x7, Pallas kernels, head_scatter(): pl.pallas_call(functools.partial(scatter_body, n, tick), out_shape=jax.Sh...  210 us
    pallas_call x13, Pallas kernels, head_gather(): pl.pallas_call(functools.partial(gather_body, n, tick), out_shape=jax.Sha...  209 us
    dot_general x9, matrix products, block_output(): jnp.einsum('cijh,cjhp->cihp', weights, x_blocks, precision=highest)  101 us
    unnamed x842, local copies, waits for them, and re-layouts  66.6 us
    all_gather x3, waiting for transfers between devices, entering_2(): lax.all_gather(a.astype(kind), axis)  59 us
    psum x1, blocking collectives, reduce_grads(): norm_sum = lax.psum(norm_part, ('seq', 'head'))  38.6 us
    dot_general x3, matrix products, mixer_forward(): projected = jnp.dot(gathered, w_main, preferred_element_type=jnp.float32)  38.1 us
    psum x1, waiting for transfers between devices, reduce_grads(): lax.psum(tuple((member.astype(jnp.bfloat16) for member in head_part[:3] +...  35.8 us
  transfers between devices with their start and end apart: 21, of which 9 were waited for; matrix products, arithmetic and copies ran while one was open for 24% of the time, Pallas kernels for 11%

profile of v9, /device:TPU:0, one launch (start us, length us, event | category | flops | bytes accessed | tf_op | source)
XLA Modules:
  0.0 1517.3 jit_solution(5662425750307294428)
XLA Ops:
  20.9 29.3 %shard_map.297 = bf16[4,128,2048]{2,1,0:T(8,128)(2,1)} custom-call(bf16[128,2048]{1,0:T(8,128)(2,1)} %fusion.224.x_ref), custom_call_target="tpu_custom_call" | custom-call | tf_op jit(solution)/shard_map/pallas_call | solution.py:113
  50.5 12.7 fusion.417
  96.6 7.1 all-gather
  117.3 12.9 all-gather.13.cloned.1.call-done
  134.8 9.4 fusion.133
  144.2 13.4 copy.510
  161.4 11.1 shard_map.298
  174.8 6.9 fusion.39.p_ref
  181.7 36.8 %shard_map.299 = f32[128,2048]{1,0:T(8,128)} custom-call(f32[4,128,2048]{2,1,0:T(8,128)} %fusion.39.p_ref), custom_call_target="tpu_custom_call" | custom-call | tf_op jit(solution)/shard_map/pallas_call | solution.py:217
  226.8 43.5 %shard_map.300 = bf16[4,128,2048]{2,1,0:T(8,128)(2,1)} custom-call(bf16[128,2048]{1,0:T(8,128)(2,1)} %multiply_convert_fusion.7.x_ref), custom_call_target="tpu_custom_call" | custom-call | tf_op jit(solution)/shard_map/pallas_call | solution.py:113
  270.3 12.9 fusion.416
  298.8 9.2 fusion.111
  326.6 6.8 all-gather.1
  342.2 10.2 all-gather.15.cloned.1.call-done
  357.0 9.4 fusion.132
  372.1 11.1 shard_map.301
  387.4 6.9 fusion.37.p_ref
  394.2 45.3 %shard_map.302 = f32[128,2048]{1,0:T(8,128)} custom-call(f32[4,128,2048]{2,1,0:T(8,128)} %fusion.37.p_ref), custom_call_target="tpu_custom_call" | custom-call | tf_op jit(solution)/shard_map/pallas_call | solution.py:217
  451.1 12.5 fusion.415
  491.4 7.9 all-gather.5
  505.0 7.0 all-gather.4
  513.1 7.8 all-gather.3
  520.9 7.4 all-gather.2
  538.4 8.7 all-gather.17.cloned.1.call-done
  551.8 9.4 fusion.131
  570.2 7.9 multiply_reduce_fusion.20
  580.2 6.9 multiply_reduce_fusion.23
  596.2 15.7 %fusion.29 = (f32[2,256,16]{1,2,0:T(8,128)}, f32[2,256,16]{1,2,0:T(8,128)}, f32[2,256,16]{1,2,0:T(8,128)}, f32[2,256,256]{2,1,0:T(8,128)S(1)}) fusion(f32[2,256,16]{1,2,0:T(8,128)} %bitcast.1105, f32[2,256,256]{2,1,0:T(8,128)} %fusion.453, f32[2,256,16]{1,2,0:T(8,128)} %copy-done.212, pred[2,256,256]{2,1,0:T(8,128)(4,1)} %get-tuple-element.266, ...), kind=kOutput, calls=%fused_computation.47 | convolution fusion | flops 1637720064 | bytes 5537792 | tf_op jit(solution)/shard_map/transpose(jvp(cijh,cjhp->cihp))/dot_general | solution.py:364
  619.6 5.7 fusion.454
  625.3 36.8 %all-gather.19.cloned.1.call-done = bf16[4,16,64,128]{3,2,1,0:T(8,128)(2,1)} async-done(((bf16[1,16,64,128]{3,2,1,0:T(8,128)(2,1)}), bf16[4,16,64,128]{3,2,1,0:T(8,128)(2,1)}) %all-gather.19.cloned.1.call-update) | async-done | bytes 1048592 | tf_op jit(solution)/shard_map/all_gather | solution.py:267
  671.7 9.2 fusion.127
  685.2 6.3 multiply_reduce_fusion.13
  748.1 11.0 fusion.251
  762.9 21.4 %collective-permute-done.9 = bf16[128,2048]{1,0:T(8,128)(2,1)S(1)} collective-permute-done((bf16[128,2048]{1,0:T(8,128)(2,1)S(1)}, bf16[128,2048]{1,0:T(8,128)(2,1)S(1)}, u32[]{:S(2)}, u32[]{:S(2)}) %collective-permute-start.9) | collective-permute-done | bytes 524320 | tf_op jit(solution)/shard_map/ppermute | solution.py:244
  786.0 33.2 %shard_map.309 = bf16[4,128,2048]{2,1,0:T(8,128)(2,1)} custom-call(bf16[128,2048]{1,0:T(8,128)(2,1)} %fusion.242.x_ref), custom_call_target="tpu_custom_call" | custom-call | tf_op jit(solution)/shard_map/pallas_call | solution.py:113
  819.2 8.0 multiply_reduce_fusion.19
  827.3 10.3 shard_map.310
  838.3 6.0 multiply_reduce_fusion.22
  853.7 15.7 %fusion.31 = (f32[2,256,16]{1,2,0:T(8,128)}, f32[2,256,16]{1,2,0:T(8,128)}, f32[2,256,16]{1,2,0:T(8,128)}, f32[2,256,256]{2,1,0:T(8,128)S(1)}) fusion(f32[2,256,16]{1,2,0:T(8,128)S(1)} %bitcast.1104, f32[2,256,256]{2,1,0:T(8,128)} %fusion.452, f32[2,256,16]{1,2,0:T(8,128)S(1)} %copy-done.211, pred[2,256,256]{2,1,0:T(8,128)(4,1)S(1)} %copy-done.192, ...), kind=kOutput, calls=%fused_computation.49 | convolution fusion | flops 1637720064 | bytes 5537792 | tf_op jit(solution)/shard_map/transpose(jvp(cijh,cjhp->cihp))/dot_general | solution.py:364
  876.9 5.7 fusion.455
  896.6 9.0 fusion.123
  910.0 6.3 multiply_reduce_fusion.9
  964.1 53.1 %shard_map.311 = f32[128,2048]{1,0:T(8,128)} custom-call(f32[4,128,2048]{2,1,0:T(8,128)} %bitcast.995), custom_call_target="tpu_custom_call" | custom-call | tf_op jit(solution)/shard_map/pallas_call | solution.py:217
  1022.4 11.0 fusion.249
  1039.0 28.3 %shard_map.312 = bf16[4,128,2048]{2,1,0:T(8,128)(2,1)} custom-call(bf16[128,2048]{1,0:T(8,128)(2,1)} %fusion.243.x_ref), custom_call_target="tpu_custom_call" | custom-call | tf_op jit(solution)/shard_map/pallas_call | solution.py:113
  1067.4 8.0 multiply_reduce_fusion.18
  1075.4 10.3 shard_map.313
  1095.6 15.6 %fusion.33 = (f32[2,256,16]{1,2,0:T(8,128)}, f32[2,256,16]{1,2,0:T(8,128)}, f32[2,256,16]{1,2,0:T(8,128)}, f32[2,256,256]{2,1,0:T(8,128)S(1)}) fusion(f32[2,256,16]{1,2,0:T(8,128)S(1)} %bitcast.1100, f32[2,256,256]{2,1,0:T(8,128)S(1)} %copy-done.171, f32[2,256,16]{1,2,0:T(8,128)S(1)} %copy-done.208, pred[2,256,256]{2,1,0:T(8,128)(4,1)S(1)} %copy-done.189, ...), kind=kOutput, calls=%fused_computation.51 | convolution fusion | flops 1637720064 | bytes 5537792 | tf_op jit(solution)/shard_map/transpose(jvp(cijh,cjhp->cihp))/dot_general | solution.py:364
  1122.3 10.3 add_convert_fusion
  1132.9 17.9 %all-gather.23.cloned.1.call-done = bf16[4,16,64,128]{3,2,1,0:T(8,128)(2,1)} async-done(((bf16[1,16,64,128]{3,2,1,0:T(8,128)(2,1)}), bf16[4,16,64,128]{3,2,1,0:T(8,128)(2,1)}) %all-gather.23.cloned.1.call-update) | async-done | bytes 1048592 | tf_op jit(solution)/shard_map/all_gather | solution.py:267
  1160.8 7.4 fusion.119
  1195.7 6.0 pad_add_fusion
  1219.0 30.9 %shard_map.314 = f32[520,256]{1,0:T(8,128)} custom-call(f32[4,520,256]{2,1,0:T(8,128)} %bitcast.999), custom_call_target="tpu_custom_call" | custom-call | tf_op jit(solution)/shard_map/pallas_call | solution.py:217
  1256.8 5.9 copy-done.49
  1266.1 21.5 %fusion.34 = (bf16[1,2048,1024]{1,2,0:T(8,128)(2,1)}, bf16[1,2048,1024]{1,2,0:T(8,128)(2,1)}) fusion(f32[2048,2064]{0,1:T(8,128)} %copy-done.49, f32[2048,2064]{0,1:T(8,128)} %fusion.249, f32[2048,2064]{0,1:T(8,128)} %fusion.251, f32[]{:T(128)S(6)} %convert_element_type.597, f32[]{:T(128)S(6)} %convert_element_type.596, f32[]{:T(128)S(6)} %convert_element_type.595, ...), kind=kLoop, calls=%fused_computation.58 | loop fusion | flops 27262976 | bytes 58720272 | tf_op jit(solution)/shard_map/broadcast_in_dim | solution.py:765
  1290.9 7.5 fusion.35.p_ref
  1309.5 18.6 %all-reduce.64 = (bf16[1,4,1024]{2,1,0:T(4,128)(2,1)S(1)}, bf16[1,1024]{1,0:T(2,128)(2,1)S(1)}, bf16[1,16]{1,0:T(2,128)(2,1)S(1)}, bf16[1,16]{1,0:T(2,128)(2,1)S...) all-reduce(bf16[1,4,1024]{2,1,0:T(4,128)(2,1)S(1)} %fusion.338, ...), channel_id=1, replica_groups=mesh['section'=2,'seq'=4,'head'=4] {'seq'}, use_global_device_ids=true, to_apply=%region_90.92 | all-reduce | flops 6192 | bytes 24768 | tf_op jit(solution)/shard_map/psum | solution.py:614
  1333.4 8.1 fusion.248
  1347.2 37.1 %shard_map.315 = f32[128,2048]{1,0:T(8,128)} custom-call(f32[4,128,2048]{2,1,0:T(8,128)} %bitcast.993), custom_call_target="tpu_custom_call" | custom-call | tf_op jit(solution)/shard_map/pallas_call | solution.py:217
  1386.0 38.6 %psum.84 = f32[1,2048]{1,0:T(1,128)} all-reduce(f32[1,2048]{1,0:T(1,128)S(1)} %bitcast.1114), channel_id=1, replica_groups=mesh['section'=2,'seq'=4,'head'=4] {'seq','head'}, use_global_device_ids=true, to_apply=%region_84.86 | all-reduce | flops 2048 | bytes 16384 | tf_op jit(solution)/shard_map/psum | solution.py:618
  1432.3 35.8 %all-reduce.71.cloned.1.call-done = (bf16[1,2048,1024]{1,2,0:T(8,128)(2,1)}, bf16[1,2048,1024]{1,2,0:T(8,128)(2,1)}, bf16[520,256]{1,0:T(8,128)(2,1)}, bf16[1,2048,16]{1,2,0:T(8,128)(2,1)}) async-done(((bf16[1,2048,1024]{1,2,0:T(8,128)(2,1)}, bf16[1,2048,1024]{1,2,0:T(8,128)(2,1)}, bf16[520,256]{1,0:T(8,128)(2,1)}, bf16[1,2048,16]{1,2,0:T(8,128)(2,1)}), (bf16[1,2048,1024]{1,2,0:T(8,128)(2,1)}, ...) | async-done | bytes 8720400 | tf_op jit(solution)/shard_map/psum | solution.py:610
  1468.1 23.7 %shard_map.316 = bf16[4,520,256]{2,1,0:T(8,128)(2,1)} custom-call(bf16[520,256]{1,0:T(8,128)(2,1)} %get-tuple-element.171.x_ref), custom_call_target="tpu_custom_call" | custom-call | tf_op jit(solution)/shard_map/pallas_call | solution.py:113
  1495.9 6.9 copy.616
  1502.7 6.9 copy.617
  (1278 shorter events, 516.3 us)
Async XLA Ops:
  7.2 43.0 %copy-start.214 = (bf16[1,2048,16]{1,2,0:T(8,128)(2,1)S(1)}, bf16[1,2048,16]{1,2,0:T(8,128)(2,1)}, u32[]{:S(2)}) copy-start(bf16[1,2048,16]{1,2,0:T(8,128)(2,1)} %param.27) | copy-start | bytes 196612
  7.2 43.3 %copy-start.56 = (bf16[1,2048,256]{2,1,0:T(8,128)(2,1)S(1)}, bf16[1,2048,256]{2,1,0:T(8,128)(2,1)}, u32[]{:S(2)}) copy-start(bf16[1,2048,256]{2,1,0:T(8,128)(2,1)} %param.26) | copy-start | bytes 3145732
  7.2 123.0 %all-gather.13.cloned.1.call-start = ((), (), s32[]{:S(2)}) async-start(), calls=%async_computation | async-start | bytes 2621440 | tf_op jit(solution)/shard_map/all_gather | solution.py:249
  8.7 70.5 %collective-permute-start = (f32[3]{0:T(128)S(1)}, f32[3]{0:T(128)S(1)}, u32[]{:S(2)}, u32[]{:S(2)}) collective-permute-start(f32[3]{0:T(128)S(1)} %slice.662), channel_id=1, source_target_pairs={{0,4},{4,8},{8,12},{1,5},{5,9},{9,13},{2,6},{6,10},{10,14},{3,7},{... | collective-permute-start | bytes 44 | tf_op jit(solution)/shard_map/ppermute | solution.py:244
  13.7 65.6 %collective-permute-start.3 = (f32[3]{0:T(128)S(1)}, f32[3]{0:T(128)S(1)}, u32[]{:S(2)}, u32[]{:S(2)}) collective-permute-start(f32[3]{0:T(128)S(1)} %slice.705), channel_id=1, source_target_pairs={{0,4},{4,8},{8,12},{1,5},{5,9},{9,13},{2,6},{6,10},{10,14},{3,7},{... | collective-permute-start | bytes 44 | tf_op jit(solution)/shard_map/ppermute | solution.py:244
  18.9 31.3 %copy-start.338 = (f32[128]{0:T(128)}, f32[128]{0:T(128)S(1)}, u32[]{:S(2)}) copy-start(f32[128]{0:T(128)S(1)} %get-tuple-element.333) | copy-start | bytes 1540
  65.9 14.9 collective-permute-start.1
  73.0 30.6 %copy-start.145 = (f32[512,16]{0,1:T(8,128)}, f32[512,16]{0,1:T(8,128)S(1)}, u32[]{:S(2)}) copy-start(f32[512,16]{0,1:T(8,128)S(1)} %get-tuple-element.227) | copy-start | bytes 98308
  79.2 55.5 %copy-start.178 = (f32[2,256,16]{1,2,0:T(8,128)}, f32[2,256,16]{1,2,0:T(8,128)S(1)}, u32[]{:S(2)}) copy-start(f32[2,256,16]{1,2,0:T(8,128)S(1)} %get-tuple-element.276) | copy-start | bytes 98308
  90.9 43.9 %copy-start.9 = (f32[2,256,16,64]{1,0,3,2:T(2,128)}, f32[2,256,16,64]{1,0,3,2:T(2,128)S(1)}, u32[]{:S(2)}) copy-start(f32[2,256,16,64]{1,0,3,2:T(2,128)S(1)} %reshape.1197) | copy-start | bytes 6291460
  94.8 35.4 %copy-start.61 = (f32[2,16,64,128]{3,2,1,0:T(8,128)}, f32[2,16,64,128]{3,2,1,0:T(8,128)S(1)}, u32[]{:S(2)}) copy-start(f32[2,16,64,128]{3,2,1,0:T(8,128)S(1)} %fusion.159) | copy-start | bytes 3145732
  96.5 255.8 %all-gather.15.cloned.1.call-start = ((), (), s32[]{:S(2)}) async-start(), calls=%async_computation.1 | async-start | bytes 2621440 | tf_op jit(solution)/shard_map/all_gather | solution.py:249
  181.7 38.4 %copy-start.50 = (bf16[2,128,2048]{2,1,0:T(8,128)(2,1)S(1)}, bf16[2,128,2048]{2,1,0:T(8,128)(2,1)}, u32[]{:S(2)}) copy-start(bf16[2,128,2048]{2,1,0:T(8,128)(2,1)} %param.19) | copy-start | bytes 3145732
  221.3 3.7 collective-permute-start.2
  224.3 70.0 %copy-start.268 = (f32[2,256]{1,0:T(2,128)}, f32[2,256]{1,0:T(2,128)S(1)}, u32[]{:S(2)}) copy-start(f32[2,256]{1,0:T(2,128)S(1)} %get-tuple-element.343) | copy-start | bytes 6148
  224.3 70.0 %copy-start.310 = (f32[2,256]{1,0:T(2,128)}, f32[2,256]{1,0:T(2,128)S(1)}, u32[]{:S(2)}) copy-start(f32[2,256]{1,0:T(2,128)S(1)} %get-tuple-element.344) | copy-start | bytes 6148
  225.0 73.7 %copy-start.246 = (f32[512]{0:T(512)}, f32[512]{0:T(512)S(1)}, u32[]{:S(2)}) copy-start(f32[512]{0:T(512)S(1)} %get-tuple-element.287) | copy-start | bytes 6148
  225.0 73.7 %copy-start.248 = (f32[512]{0:T(512)}, f32[512]{0:T(512)S(1)}, u32[]{:S(2)}) copy-start(f32[512]{0:T(512)S(1)} %get-tuple-element.288) | copy-start | bytes 6148
  225.0 73.7 %copy-start.250 = (f32[512]{0:T(512)}, f32[512]{0:T(512)S(1)}, u32[]{:S(2)}) copy-start(f32[512]{0:T(512)S(1)} %get-tuple-element.289) | copy-start | bytes 6148
  225.3 214.3 %copy-start.25 = (f32[128,2048]{1,0:T(8,128)}, f32[128,2048]{1,0:T(8,128)S(1)}, u32[]{:S(2)}) copy-start(f32[128,2048]{1,0:T(8,128)S(1)} %get-tuple-element.219) | copy-start | bytes 3145732
  225.9 57.3 %copy-start.352 = (f32[128]{0:T(128)}, f32[128]{0:T(128)S(1)}, u32[]{:S(2)}) copy-start(f32[128]{0:T(128)S(1)} %get-tuple-element.335) | copy-start | bytes 1540
  270.3 23.3 %copy-start.350 = (f32[2]{0:T(128)S(1)}, f32[2]{0:T(128)}, u32[]{:S(2)}) copy-start(f32[2]{0:T(128)} %get-tuple-element.346) | copy-start | bytes 28
  287.8 10.7 collective-permute-start.4
  292.0 41.4 %copy-start.147 = (f32[512,16]{0,1:T(8,128)}, f32[512,16]{0,1:T(8,128)S(1)}, u32[]{:S(2)}) copy-start(f32[512,16]{0,1:T(8,128)S(1)} %get-tuple-element.215) | copy-start | bytes 98308
  294.4 62.6 %copy-start.182 = (f32[2,256,16]{1,2,0:T(8,128)}, f32[2,256,16]{1,2,0:T(8,128)S(1)}, u32[]{:S(2)}) copy-start(f32[2,256,16]{1,2,0:T(8,128)S(1)} %get-tuple-element.274) | copy-start | bytes 98308
  313.1 43.9 %copy-start.11 = (f32[2,256,16,64]{1,0,3,2:T(2,128)}, f32[2,256,16,64]{1,0,3,2:T(2,128)S(1)}, u32[]{:S(2)}) copy-start(f32[2,256,16,64]{1,0,3,2:T(2,128)S(1)} %reshape.1210) | copy-start | bytes 6291460
  319.0 228.1 %all-gather.17.cloned.1.call-start = ((), (), s32[]{:S(2)}) async-start(), calls=%async_computation.2 | async-start | bytes 2621440 | tf_op jit(solution)/shard_map/all_gather | solution.py:249
  320.4 123.5 %collective-permute-start.6 = (f32[3]{0:T(128)}, f32[3]{0:T(128)}, u32[]{:S(2)}, u32[]{:S(2)}) collective-permute-start(f32[3]{0:T(128)} %slice.744), channel_id=1, source_target_pairs={{0,4},{4,8},{8,12},{1,5},{5,9},{9,13},{2,6},{6,10},{10,14},{3,7},{... | collective-permute-start | bytes 44 | tf_op jit(solution)/shard_map/ppermute | solution.py:244
  333.5 23.5 %copy-start.290 = (f32[2,2,8,256]{3,2,0,1:T(8,128)}, f32[2,2,8,256]{3,2,0,1:T(8,128)S(1)}, u32[]{:S(2)}) copy-start(f32[2,2,8,256]{3,2,0,1:T(8,128)S(1)} %copy.946) | copy-start | bytes 98308
  394.2 45.3 %copy-start.112 = (f32[1,128,2048]{2,1,0:T(8,128)S(1)}, f32[1,128,2048]{2,1,0:T(8,128)}, u32[]{:S(2)}) copy-start(f32[1,128,2048]{2,1,0:T(8,128)} %constant_dynamic-slice_fusion.3) | copy-start | bytes 3145732
  442.4 3.8 collective-permute-start.5
  443.8 28.4 %copy-start.389 = (f32[2]{0:T(128)}, f32[2]{0:T(128)S(1)}, u32[]{:S(2)}) copy-start(f32[2]{0:T(128)S(1)} %fusion.369) | copy-start | bytes 28
  445.3 31.1 %copy-start.252 = (f32[512]{0:T(512)}, f32[512]{0:T(512)S(1)}, u32[]{:S(2)}) copy-start(f32[512]{0:T(512)S(1)} %get-tuple-element.281) | copy-start | bytes 6148
  445.3 31.1 %copy-start.254 = (f32[512]{0:T(512)}, f32[512]{0:T(512)S(1)}, u32[]{:S(2)}) copy-start(f32[512]{0:T(512)S(1)} %get-tuple-element.282) | copy-start | bytes 6148
  445.3 31.1 %copy-start.256 = (f32[512]{0:T(512)}, f32[512]{0:T(512)S(1)}, u32[]{:S(2)}) copy-start(f32[512]{0:T(512)S(1)} %get-tuple-element.283) | copy-start | bytes 6148
  466.4 9.8 collective-permute-start.7
  486.2 177.4 %copy-start.14 = (f32[2,256,16,64]{1,0,3,2:T(2,128)}, f32[2,256,16,64]{1,0,3,2:T(2,128)S(1)}, u32[]{:S(2)}) copy-start(f32[2,256,16,64]{1,0,3,2:T(2,128)S(1)} %reshape.1223) | copy-start | bytes 6291460
  490.2 57.0 %copy-start.64 = (f32[2,16,64,128]{3,2,1,0:T(8,128)}, f32[2,16,64,128]{3,2,1,0:T(8,128)S(1)}, u32[]{:S(2)}) copy-start(f32[2,16,64,128]{3,2,1,0:T(8,128)S(1)} %fusion.151) | copy-start | bytes 3145732
  491.3 170.8 %all-gather.19.cloned.1.call-start = ((), (), s32[]{:S(2)}) async-start(), calls=%async_computation.3 | async-start | bytes 1310720 | tf_op jit(solution)/shard_map/all_gather | solution.py:267
  596.1 290.8 %all-gather.21.cloned.1.call-start = ((), (), s32[]{:S(2)}) async-start(), calls=%async_computation.4 | async-start | bytes 1310720 | tf_op jit(solution)/shard_map/all_gather | solution.py:267
  691.5 29.9 %copy-start.222 = (f32[1280]{0:T(1024)}, f32[1280]{0:T(1024)S(1)}, u32[]{:S(2)}) copy-start(f32[1280]{0:T(1024)S(1)} %get-tuple-element.135) | copy-start | bytes 15364
  702.9 19.1 %collective-permute-start.8 = (f32[3,1280]{1,0:T(4,128)}, f32[3,1280]{1,0:T(4,128)}, u32[]{:S(2)}, u32[]{:S(2)}) collective-permute-start(f32[3,1280]{1,0:T(4,128)} %copy.559), channel_id=1, source_target_pairs={{4,0},{8,4},{12,8},{5,1},{9,5},{13,9},{6,2},{10,6},{14,10},{7,3},{... | collective-permute-start | bytes 46088 | tf_op jit(solution)/shard_map/ppermute | solution.py:244
  746.6 37.6 %collective-permute-start.9 = (bf16[128,2048]{1,0:T(8,128)(2,1)S(1)}, bf16[128,2048]{1,0:T(8,128)(2,1)S(1)}, u32[]{:S(2)}, u32[]{:S(2)}) collective-permute-start(bf16[128,2048]{1,0:T(8,128)(2,1)S(1)} %get-tuple-element.194), channel_id=1, source_target_pairs={{16,0},{17,1},{18,2},{19,3},{20,4},{21,5},{22,6},{23,7},{24,8},{25... | collective-permute-start | bytes 1572872 | tf_op jit(solution)/shard_map/ppermute | solution.py:244
  762.8 56.4 %copy-start.321 = (f32[512]{0:T(512)S(1)}, f32[512]{0:T(512)}, u32[]{:S(2)}) copy-start(f32[512]{0:T(512)} %copy-done.320) | copy-start | bytes 6148
  853.5 297.2 %all-gather.23.cloned.1.call-start = ((), (), s32[]{:S(2)}) async-start(), calls=%async_computation.5 | async-start | bytes 1310720 | tf_op jit(solution)/shard_map/all_gather | solution.py:267
  916.2 29.9 %copy-start.224 = (f32[1280]{0:T(1024)}, f32[1280]{0:T(1024)S(1)}, u32[]{:S(2)}) copy-start(f32[1280]{0:T(1024)S(1)} %get-tuple-element.136) | copy-start | bytes 15364
  927.6 19.2 %collective-permute-start.10 = (f32[3,1280]{1,0:T(4,128)}, f32[3,1280]{1,0:T(4,128)}, u32[]{:S(2)}, u32[]{:S(2)}) collective-permute-start(f32[3,1280]{1,0:T(4,128)} %copy.582), channel_id=1, source_target_pairs={{4,0},{8,4},{12,8},{5,1},{9,5},{13,9},{6,2},{10,6},{14,10},{7,3},{... | collective-permute-start | bytes 46088 | tf_op jit(solution)/shard_map/ppermute | solution.py:244
  964.1 53.1 %copy-start.26 = (f32[128,2048]{1,0:T(8,128)S(1)}, f32[128,2048]{1,0:T(8,128)}, u32[]{:S(2)}) copy-start(f32[128,2048]{1,0:T(8,128)} %copy-done.25) | copy-start | bytes 3145732
  964.1 53.1 %copy-start.353 = (f32[128]{0:T(128)S(1)}, f32[128]{0:T(128)}, u32[]{:S(2)}) copy-start(f32[128]{0:T(128)} %copy-done.352) | copy-start | bytes 1540
  964.1 55.3 %copy-start.66 = (bf16[2,128,2048]{2,1,0:T(8,128)(2,1)S(1)}, bf16[2,128,2048]{2,1,0:T(8,128)(2,1)}, u32[]{:S(2)}) copy-start(bf16[2,128,2048]{2,1,0:T(8,128)(2,1)} %param.20) | copy-start | bytes 3145732
  964.1 55.3 %copy-start.138 = (bf16[128,2048]{1,0:T(8,128)(2,1)S(1)}, bf16[128,2048]{1,0:T(8,128)(2,1)}, u32[]{:S(2)}) copy-start(bf16[128,2048]{1,0:T(8,128)(2,1)} %copy-done.137) | copy-start | bytes 1572868
  964.1 55.3 %copy-start.398 = (f32[128]{0:T(128)S(1)}, f32[128]{0:T(128)}, u32[]{:S(2)}) copy-start(f32[128]{0:T(128)} %get-tuple-element.334) | copy-start | bytes 1540
  1020.9 16.4 %collective-permute-start.11 = (bf16[128,2048]{1,0:T(8,128)(2,1)S(1)}, bf16[128,2048]{1,0:T(8,128)(2,1)S(1)}, u32[]{:S(2)}, u32[]{:S(2)}) collective-permute-start(bf16[128,2048]{1,0:T(8,128)(2,1)S(1)} %get-tuple-element.190), channel_id=1, source_target_pairs={{16,0},{17,1},{18,2},{19,3},{20,4},{21,5},{22,6},{23,7},{24,8},{25... | collective-permute-start | bytes 1572872 | tf_op jit(solution)/shard_map/ppermute | solution.py:244
  1037.3 30.1 %copy-start.319 = (f32[512]{0:T(512)S(1)}, f32[512]{0:T(512)}, u32[]{:S(2)}) copy-start(f32[512]{0:T(512)} %copy-done.318) | copy-start | bytes 6148
  1117.8 146.4 %all-reduce.69.cloned.1.call-start = ((), (), s32[]{:S(2)}) async-start(), calls=%async_computation.6 | async-start | bytes 8388608 | tf_op jit(solution)/shard_map/psum | solution.py:738
  1132.7 335.4 %all-reduce.71.cloned.1.call-start = ((), (), s32[]{:S(2)}) async-start(), calls=%async_computation.7 | async-start | bytes 17440768 | tf_op jit(solution)/shard_map/psum | solution.py:610
  1192.3 11.9 collective-permute-start.12
  1219.0 32.9 %copy-start.33 = (f32[509,1280]{0,1:T(8,128)S(1)}, f32[509,1280]{0,1:T(8,128)}, u32[]{:S(2)}) copy-start(f32[509,1280]{0,1:T(8,128)} %slice.982) | copy-start | bytes 7818244
  1307.8 25.6 %copy-start.154 = (bf16[512,1024]{0,1:T(8,128)(2,1)S(1)}, bf16[512,1024]{0,1:T(8,128)(2,1)}, u32[]{:S(2)}) copy-start(bf16[512,1024]{0,1:T(8,128)(2,1)} %get-tuple-element.232) | copy-start | bytes 3145732
  1347.2 37.1 %copy-start.52 = (bf16[2,128,2048]{2,1,0:T(8,128)(2,1)S(1)}, bf16[2,128,2048]{2,1,0:T(8,128)(2,1)}, u32[]{:S(2)}) copy-start(bf16[2,128,2048]{2,1,0:T(8,128)(2,1)} %param.19) | copy-start | bytes 3145732
  1347.2 37.1 %copy-start.339 = (f32[128]{0:T(128)S(1)}, f32[128]{0:T(128)}, u32[]{:S(2)}) copy-start(f32[128]{0:T(128)} %copy-done.338) | copy-start | bytes 1540
  1347.2 38.8 %copy-start.274 = (f32[2048]{0:T(1024)S(1)}, f32[2048]{0:T(1024)}, u32[]{:S(2)}) copy-start(f32[2048]{0:T(1024)} %get-tuple-element.141) | copy-start | bytes 24580
  1347.2 38.8 %copy-start.275 = (f32[2048]{0:T(1024)S(1)}, f32[2048]{0:T(1024)}, u32[]{:S(2)}) copy-start(f32[2048]{0:T(1024)} %get-tuple-element.143) | copy-start | bytes 24580
  1347.2 77.4 %copy-start.397 = (f32[128]{0:T(128)S(1)}, f32[128]{0:T(128)}, u32[]{:S(2)}) copy-start(f32[128]{0:T(128)} %get-tuple-element.332) | copy-start | bytes 1540
  (370 other events, 2227.2 us)
Sparse Core Ops, SparseCore 0:
  96.6 33.5 all-gather.12
  319.2 33.0 all-gather.14
  491.5 55.6 all-gather.16
  596.2 65.8 all-gather.18
  853.7 33.2 all-gather.20
  1118.0 32.7 all-gather.22
  1154.1 104.1 all-reduce.68
  1287.7 180.3 all-reduce.70

commit v10 on v8

--- a/solution.py
+++ b/solution.py
@@ -227,7 +227,7 @@
 
 norm_eps = 1e-05
 far_below = -1e30
-highest = lax.Precision.HIGHEST
+highest = lax.Precision.HIGH
 
 
 def shifted(value, axis, by):

time: 1510 us -> 1460 us (0.967)
  matrix products: 346 us -> 284 us
    dot_general x9, matrix products: 101 us -> 67.6 us  [block_output(): jnp.einsum('cijh,cjhp->cihp', weights, x_blocks, precision=highest)]
  transfers between devices with their start and end apart: 21 -> 21, of which waited for: 9 -> 9; matrix products, arithmetic and copies ran while one was open for 24% -> 23% of each run, Pallas kernels for 10% -> 10%
where the time goes in v10:
time: 1460 us; the launch traced here: 1450 us
  Pallas kernels  376 us (26%)
  matrix products  284 us (19%)
  other arithmetic  251 us (17%)
  local copies, waits for them, and re-layouts  179 us (12%)
  blocking collectives  165 us (11%)
  waiting for transfers between devices  136 us (9%)
  starting transfers between devices  33.8 us (2%)
  between operations  21.3 us (1%)
    pallas_call x7, Pallas kernels, head_scatter(): pl.pallas_call(functools.partial(scatter_body, n, tick), out_shape=jax.Sh...  212 us
    pallas_call x7, Pallas kernels, head_gather(): pl.pallas_call(functools.partial(gather_body, n, tick), out_shape=jax.Sha...  164 us
    dot_general x9, matrix products, block_output(): jnp.einsum('cijh,cjhp->cihp', weights, x_blocks, precision=highest)  67.6 us
    unnamed x844, local copies, waits for them, and re-layouts  66.6 us
    all_gather x3, waiting for transfers between devices, entering_2(): lax.all_gather(a.astype(kind), axis)  45.4 us
    psum x1, blocking collectives, reduce_grads(): norm_sum = lax.psum(norm_part, ('seq', 'head'))  38.7 us
    psum x1, waiting for transfers between devices, reduce_grads(): lax.psum(tuple((member.astype(jnp.bfloat16) for member in head_part[:3] +...  38.5 us
    dot_general x3, matrix products, mixer_forward(): projected = jnp.dot(gathered, w_main, preferred_element_type=jnp.float32)  38.1 us
  transfers between devices with their start and end apart: 21, of which 9 were waited for; matrix products, arithmetic and copies ran while one was open for 23% of the time, Pallas kernels for 10%

profile of v10, /device:TPU:0, one launch (start us, length us, event | category | flops | bytes accessed | tf_op | source)
XLA Modules:
  0.0 1446.1 jit_solution(10237053274272337754)
XLA Ops:
  20.9 29.3 %shard_map.297 = bf16[4,128,2048]{2,1,0:T(8,128)(2,1)} custom-call(bf16[128,2048]{1,0:T(8,128)(2,1)} %fusion.224.x_ref), custom_call_target="tpu_custom_call" | custom-call | tf_op jit(solution)/shard_map/pallas_call | solution.py:113
  50.5 12.7 fusion.417
  95.5 7.3 all-gather
  116.1 13.1 all-gather.13.cloned.1.call-done
  142.9 12.1 psum.126
  156.7 6.9 fusion.39.p_ref
  163.5 36.8 %shard_map.298 = f32[128,2048]{1,0:T(8,128)} custom-call(f32[4,128,2048]{2,1,0:T(8,128)} %fusion.39.p_ref), custom_call_target="tpu_custom_call" | custom-call | tf_op jit(solution)/shard_map/pallas_call | solution.py:209
  208.8 43.4 %shard_map.299 = bf16[4,128,2048]{2,1,0:T(8,128)(2,1)} custom-call(bf16[128,2048]{1,0:T(8,128)(2,1)} %multiply_convert_fusion.7.x_ref), custom_call_target="tpu_custom_call" | custom-call | tf_op jit(solution)/shard_map/pallas_call | solution.py:113
  252.2 12.9 fusion.416
  280.8 9.4 fusion.111
  307.8 6.7 all-gather.1
  322.9 10.7 all-gather.15.cloned.1.call-done
  347.5 11.9 psum.127
  362.9 6.9 fusion.37.p_ref
  369.8 46.7 %shard_map.300 = f32[128,2048]{1,0:T(8,128)} custom-call(f32[4,128,2048]{2,1,0:T(8,128)} %fusion.37.p_ref), custom_call_target="tpu_custom_call" | custom-call | tf_op jit(solution)/shard_map/pallas_call | solution.py:209
  428.1 12.5 fusion.415
  467.3 8.3 all-gather.5
  481.3 7.0 all-gather.4
  489.4 7.8 all-gather.3
  497.2 7.0 all-gather.2
  514.2 8.9 all-gather.17.cloned.1.call-done
  538.2 11.8 psum.128
  550.0 7.9 multiply_reduce_fusion.20
  557.9 8.3 psum.129
  566.3 6.9 multiply_reduce_fusion.23
  581.3 12.0 fusion.29
  599.1 5.7 fusion.454
  604.8 25.4 %all-gather.19.cloned.1.call-done = bf16[4,16,64,128]{3,2,1,0:T(8,128)(2,1)} async-done(((bf16[1,16,64,128]{3,2,1,0:T(8,128)(2,1)}), bf16[4,16,64,128]{3,2,1,0:T(8,128)(2,1)}) %all-gather.19.cloned.1.call-update) | async-done | bytes 1048592 | tf_op jit(solution)/shard_map/all_gather | solution.py:259
  636.9 6.3 fusion.127
  647.5 6.7 multiply_reduce_fusion.13
  709.5 11.0 fusion.251
  723.7 18.1 %collective-permute-done.9 = bf16[128,2048]{1,0:T(8,128)(2,1)S(1)} collective-permute-done((bf16[128,2048]{1,0:T(8,128)(2,1)S(1)}, bf16[128,2048]{1,0:T(8,128)(2,1)S(1)}, u32[]{:S(2)}, u32[]{:S(2)}) %collective-permute-start.9) | collective-permute-done | bytes 524320 | tf_op jit(solution)/shard_map/ppermute | solution.py:236
  743.4 34.3 %shard_map.305 = bf16[4,128,2048]{2,1,0:T(8,128)(2,1)} custom-call(bf16[128,2048]{1,0:T(8,128)(2,1)} %fusion.242.x_ref), custom_call_target="tpu_custom_call" | custom-call | tf_op jit(solution)/shard_map/pallas_call | solution.py:113
  777.8 8.0 multiply_reduce_fusion.19
  785.8 10.3 psum.130
  796.1 6.0 multiply_reduce_fusion.22
  810.5 11.9 fusion.31
  828.0 5.7 fusion.455
  833.8 9.1 all-gather.21.cloned.1.call-done
  849.5 6.2 fusion.123
  860.0 6.5 multiply_reduce_fusion.9
  913.2 52.5 %shard_map.306 = f32[128,2048]{1,0:T(8,128)} custom-call(f32[4,128,2048]{2,1,0:T(8,128)} %bitcast.971), custom_call_target="tpu_custom_call" | custom-call | tf_op jit(solution)/shard_map/pallas_call | solution.py:209
  971.0 10.9 fusion.249
  986.9 28.4 %shard_map.307 = bf16[4,128,2048]{2,1,0:T(8,128)(2,1)} custom-call(bf16[128,2048]{1,0:T(8,128)(2,1)} %fusion.243.x_ref), custom_call_target="tpu_custom_call" | custom-call | tf_op jit(solution)/shard_map/pallas_call | solution.py:113
  1015.3 8.0 multiply_reduce_fusion.18
  1023.3 9.8 psum.131
  1033.1 5.4 multiply_reduce_fusion.21
  1042.3 11.6 fusion.33
  1062.5 10.6 add_convert_fusion
  1073.7 10.9 all-gather.23.cloned.1.call-done
  1109.3 5.7 multiply_reduce_fusion.5
  1123.0 6.6 pad_add_fusion
  1146.3 31.6 %shard_map.308 = f32[520,256]{1,0:T(8,128)} custom-call(f32[4,520,256]{2,1,0:T(8,128)} %bitcast.975), custom_call_target="tpu_custom_call" | custom-call | tf_op jit(solution)/shard_map/pallas_call | solution.py:209
  1184.7 5.9 copy-done.49
  1194.1 21.5 %fusion.34 = (bf16[1,2048,1024]{1,2,0:T(8,128)(2,1)}, bf16[1,2048,1024]{1,2,0:T(8,128)(2,1)}) fusion(f32[2048,2064]{0,1:T(8,128)} %copy-done.49, f32[2048,2064]{0,1:T(8,128)} %fusion.249, f32[2048,2064]{0,1:T(8,128)} %fusion.251, f32[]{:T(128)S(6)} %convert_element_type.597, f32[]{:T(128)S(6)} %convert_element_type.596, f32[]{:T(128)S(6)} %convert_element_type.595, ...), kind=kLoop, calls=%fused_computation.58 | loop fusion | flops 27262976 | bytes 58720272 | tf_op jit(solution)/shard_map/broadcast_in_dim | solution.py:753
  1218.8 6.9 fusion.35.p_ref
  1236.9 18.5 %all-reduce.64 = (bf16[1,4,1024]{2,1,0:T(4,128)(2,1)S(1)}, bf16[1,1024]{1,0:T(2,128)(2,1)S(1)}, bf16[1,16]{1,0:T(2,128)(2,1)S(1)}, bf16[1,16]{1,0:T(2,128)(2,1)S...) all-reduce(bf16[1,4,1024]{2,1,0:T(4,128)(2,1)S(1)} %fusion.338, ...), channel_id=1, replica_groups=mesh['section'=2,'seq'=4,'head'=4] {'seq'}, use_global_device_ids=true, to_apply=%region_96.98 | all-reduce | flops 6192 | bytes 24768 | tf_op jit(solution)/shard_map/psum | solution.py:606
  1260.6 8.1 fusion.248
  1273.3 36.8 %shard_map.309 = f32[128,2048]{1,0:T(8,128)} custom-call(f32[4,128,2048]{2,1,0:T(8,128)} %bitcast.969), custom_call_target="tpu_custom_call" | custom-call | tf_op jit(solution)/shard_map/pallas_call | solution.py:209
  1311.8 38.7 %psum.132 = f32[1,2048]{1,0:T(1,128)} all-reduce(f32[1,2048]{1,0:T(1,128)S(1)} %bitcast.1090), channel_id=1, replica_groups=mesh['section'=2,'seq'=4,'head'=4] {'seq','head'}, use_global_device_ids=true, to_apply=%region_90.92 | all-reduce | flops 2048 | bytes 16384 | tf_op jit(solution)/shard_map/psum | solution.py:610
  1358.0 38.5 %all-reduce.71.cloned.1.call-done = (bf16[1,2048,1024]{1,2,0:T(8,128)(2,1)}, bf16[1,2048,1024]{1,2,0:T(8,128)(2,1)}, bf16[520,256]{1,0:T(8,128)(2,1)}, bf16[1,2048,16]{1,2,0:T(8,128)(2,1)}) async-done(((bf16[1,2048,1024]{1,2,0:T(8,128)(2,1)}, bf16[1,2048,1024]{1,2,0:T(8,128)(2,1)}, bf16[520,256]{1,0:T(8,128)(2,1)}, bf16[1,2048,16]{1,2,0:T(8,128)(2,1)}), (bf16[1,2048,1024]{1,2,0:T(8,128)(2,1)}, ...) | async-done | bytes 8720400 | tf_op jit(solution)/shard_map/psum | solution.py:602
  1396.5 23.8 %shard_map.310 = bf16[4,520,256]{2,1,0:T(8,128)(2,1)} custom-call(bf16[520,256]{1,0:T(8,128)(2,1)} %get-tuple-element.171.x_ref), custom_call_target="tpu_custom_call" | custom-call | tf_op jit(solution)/shard_map/pallas_call | solution.py:113
  1424.4 6.9 copy.616
  1431.2 6.9 copy.617
  (1280 shorter events, 483.9 us)
Async XLA Ops:
  7.2 43.0 %copy-start.211 = (bf16[1,2048,16]{1,2,0:T(8,128)(2,1)S(1)}, bf16[1,2048,16]{1,2,0:T(8,128)(2,1)}, u32[]{:S(2)}) copy-start(bf16[1,2048,16]{1,2,0:T(8,128)(2,1)} %param.27) | copy-start | bytes 196612
  7.2 43.3 %copy-start.56 = (bf16[1,2048,256]{2,1,0:T(8,128)(2,1)S(1)}, bf16[1,2048,256]{2,1,0:T(8,128)(2,1)}, u32[]{:S(2)}) copy-start(bf16[1,2048,256]{2,1,0:T(8,128)(2,1)} %param.26) | copy-start | bytes 3145732
  7.2 121.9 %all-gather.13.cloned.1.call-start = ((), (), s32[]{:S(2)}) async-start(), calls=%async_computation | async-start | bytes 2621440 | tf_op jit(solution)/shard_map/all_gather | solution.py:241
  8.7 70.4 %collective-permute-start = (f32[3]{0:T(128)S(1)}, f32[3]{0:T(128)S(1)}, u32[]{:S(2)}, u32[]{:S(2)}) collective-permute-start(f32[3]{0:T(128)S(1)} %slice.590), channel_id=1, source_target_pairs={{0,4},{4,8},{8,12},{1,5},{5,9},{9,13},{2,6},{6,10},{10,14},{3,7},{... | collective-permute-start | bytes 44 | tf_op jit(solution)/shard_map/ppermute | solution.py:236
  13.7 65.5 %collective-permute-start.3 = (f32[3]{0:T(128)S(1)}, f32[3]{0:T(128)S(1)}, u32[]{:S(2)}, u32[]{:S(2)}) collective-permute-start(f32[3]{0:T(128)S(1)} %slice.629), channel_id=1, source_target_pairs={{0,4},{4,8},{8,12},{1,5},{5,9},{9,13},{2,6},{6,10},{10,14},{3,7},{... | collective-permute-start | bytes 44 | tf_op jit(solution)/shard_map/ppermute | solution.py:236
  18.9 31.3 %copy-start.339 = (f32[128]{0:T(128)}, f32[128]{0:T(128)S(1)}, u32[]{:S(2)}) copy-start(f32[128]{0:T(128)S(1)} %get-tuple-element.333) | copy-start | bytes 1540
  65.9 14.8 %collective-permute-start.1 = (f32[3,1280]{1,0:T(4,128)S(1)}, f32[3,1280]{1,0:T(4,128)S(1)}, u32[]{:S(2)}, u32[]{:S(2)}) collective-permute-start(f32[3,1280]{1,0:T(4,128)S(1)} %copy.495), channel_id=1, source_target_pairs={{0,4},{4,8},{8,12},{1,5},{5,9},{9,13},{2,6},{6,10},{10,14},{3,7},{... | collective-permute-start | bytes 46088 | tf_op jit(solution)/shard_map/ppermute | solution.py:236
  73.0 29.7 %copy-start.145 = (f32[512,16]{0,1:T(8,128)}, f32[512,16]{0,1:T(8,128)S(1)}, u32[]{:S(2)}) copy-start(f32[512,16]{0,1:T(8,128)S(1)} %get-tuple-element.227) | copy-start | bytes 98308
  79.1 53.7 %copy-start.178 = (f32[2,256,16]{1,2,0:T(8,128)}, f32[2,256,16]{1,2,0:T(8,128)S(1)}, u32[]{:S(2)}) copy-start(f32[2,256,16]{1,2,0:T(8,128)S(1)} %get-tuple-element.276) | copy-start | bytes 98308
  90.7 42.1 %copy-start.9 = (f32[2,256,16,64]{1,0,3,2:T(2,128)}, f32[2,256,16,64]{1,0,3,2:T(2,128)S(1)}, u32[]{:S(2)}) copy-start(f32[2,256,16,64]{1,0,3,2:T(2,128)S(1)} %reshape.960) | copy-start | bytes 6291460
  93.7 35.4 %copy-start.61 = (f32[2,16,64,128]{3,2,1,0:T(8,128)}, f32[2,16,64,128]{3,2,1,0:T(8,128)S(1)}, u32[]{:S(2)}) copy-start(f32[2,16,64,128]{3,2,1,0:T(8,128)S(1)} %fusion.159) | copy-start | bytes 3145732
  95.4 238.1 %all-gather.15.cloned.1.call-start = ((), (), s32[]{:S(2)}) async-start(), calls=%async_computation.1 | async-start | bytes 2621440 | tf_op jit(solution)/shard_map/all_gather | solution.py:241
  163.5 38.4 %copy-start.50 = (bf16[2,128,2048]{2,1,0:T(8,128)(2,1)S(1)}, bf16[2,128,2048]{2,1,0:T(8,128)(2,1)}, u32[]{:S(2)}) copy-start(bf16[2,128,2048]{2,1,0:T(8,128)(2,1)} %param.19) | copy-start | bytes 3145732
  203.2 3.7 collective-permute-start.2
  206.2 70.1 %copy-start.265 = (f32[2,256]{1,0:T(2,128)}, f32[2,256]{1,0:T(2,128)S(1)}, u32[]{:S(2)}) copy-start(f32[2,256]{1,0:T(2,128)S(1)} %get-tuple-element.343) | copy-start | bytes 6148
  206.2 70.1 %copy-start.307 = (f32[2,256]{1,0:T(2,128)}, f32[2,256]{1,0:T(2,128)S(1)}, u32[]{:S(2)}) copy-start(f32[2,256]{1,0:T(2,128)S(1)} %get-tuple-element.344) | copy-start | bytes 6148
  206.9 73.8 %copy-start.243 = (f32[512]{0:T(512)}, f32[512]{0:T(512)S(1)}, u32[]{:S(2)}) copy-start(f32[512]{0:T(512)S(1)} %get-tuple-element.287) | copy-start | bytes 6148
  206.9 73.9 %copy-start.245 = (f32[512]{0:T(512)}, f32[512]{0:T(512)S(1)}, u32[]{:S(2)}) copy-start(f32[512]{0:T(512)S(1)} %get-tuple-element.288) | copy-start | bytes 6148
  206.9 73.9 %copy-start.247 = (f32[512]{0:T(512)}, f32[512]{0:T(512)S(1)}, u32[]{:S(2)}) copy-start(f32[512]{0:T(512)S(1)} %get-tuple-element.289) | copy-start | bytes 6148
  207.2 209.3 %copy-start.25 = (f32[128,2048]{1,0:T(8,128)}, f32[128,2048]{1,0:T(8,128)S(1)}, u32[]{:S(2)}) copy-start(f32[128,2048]{1,0:T(8,128)S(1)} %get-tuple-element.219) | copy-start | bytes 3145732
  207.8 57.3 %copy-start.353 = (f32[128]{0:T(128)}, f32[128]{0:T(128)S(1)}, u32[]{:S(2)}) copy-start(f32[128]{0:T(128)S(1)} %get-tuple-element.335) | copy-start | bytes 1540
  252.2 23.4 %copy-start.351 = (f32[2]{0:T(128)S(1)}, f32[2]{0:T(128)}, u32[]{:S(2)}) copy-start(f32[2]{0:T(128)} %get-tuple-element.346) | copy-start | bytes 28
  269.7 10.8 collective-permute-start.4
  274.0 40.5 %copy-start.147 = (f32[512,16]{0,1:T(8,128)}, f32[512,16]{0,1:T(8,128)S(1)}, u32[]{:S(2)}) copy-start(f32[512,16]{0,1:T(8,128)S(1)} %get-tuple-element.215) | copy-start | bytes 98308
  276.4 61.0 %copy-start.182 = (f32[2,256,16]{1,2,0:T(8,128)}, f32[2,256,16]{1,2,0:T(8,128)S(1)}, u32[]{:S(2)}) copy-start(f32[2,256,16]{1,2,0:T(8,128)S(1)} %get-tuple-element.274) | copy-start | bytes 98308
  295.4 42.0 %copy-start.11 = (f32[2,256,16,64]{1,0,3,2:T(2,128)}, f32[2,256,16,64]{1,0,3,2:T(2,128)S(1)}, u32[]{:S(2)}) copy-start(f32[2,256,16,64]{1,0,3,2:T(2,128)S(1)} %reshape.972) | copy-start | bytes 6291460
  300.3 222.8 %all-gather.17.cloned.1.call-start = ((), (), s32[]{:S(2)}) async-start(), calls=%async_computation.2 | async-start | bytes 2621440 | tf_op jit(solution)/shard_map/all_gather | solution.py:241
  301.6 119.2 %collective-permute-start.6 = (f32[3]{0:T(128)}, f32[3]{0:T(128)}, u32[]{:S(2)}, u32[]{:S(2)}) collective-permute-start(f32[3]{0:T(128)} %slice.664), channel_id=1, source_target_pairs={{0,4},{4,8},{8,12},{1,5},{5,9},{9,13},{2,6},{6,10},{10,14},{3,7},{... | collective-permute-start | bytes 44 | tf_op jit(solution)/shard_map/ppermute | solution.py:236
  314.5 22.9 %copy-start.287 = (f32[2,2,8,256]{3,2,0,1:T(8,128)}, f32[2,2,8,256]{3,2,0,1:T(8,128)S(1)}, u32[]{:S(2)}) copy-start(f32[2,2,8,256]{3,2,0,1:T(8,128)S(1)} %copy.946) | copy-start | bytes 98308
  369.8 46.7 %copy-start.112 = (f32[1,128,2048]{2,1,0:T(8,128)S(1)}, f32[1,128,2048]{2,1,0:T(8,128)}, u32[]{:S(2)}) copy-start(f32[1,128,2048]{2,1,0:T(8,128)} %constant_dynamic-slice_fusion.3) | copy-start | bytes 3145732
  419.4 3.8 collective-permute-start.5
  420.8 28.4 %copy-start.390 = (f32[2]{0:T(128)}, f32[2]{0:T(128)S(1)}, u32[]{:S(2)}) copy-start(f32[2]{0:T(128)S(1)} %fusion.369) | copy-start | bytes 28
  422.2 31.2 %copy-start.249 = (f32[512]{0:T(512)}, f32[512]{0:T(512)S(1)}, u32[]{:S(2)}) copy-start(f32[512]{0:T(512)S(1)} %get-tuple-element.281) | copy-start | bytes 6148
  422.2 31.2 %copy-start.251 = (f32[512]{0:T(512)}, f32[512]{0:T(512)S(1)}, u32[]{:S(2)}) copy-start(f32[512]{0:T(512)S(1)} %get-tuple-element.282) | copy-start | bytes 6148
  422.2 31.2 %copy-start.253 = (f32[512]{0:T(512)}, f32[512]{0:T(512)S(1)}, u32[]{:S(2)}) copy-start(f32[512]{0:T(512)S(1)} %get-tuple-element.283) | copy-start | bytes 6148
  443.3 9.8 collective-permute-start.7
  463.1 168.7 %copy-start.14 = (f32[2,256,16,64]{1,0,3,2:T(2,128)}, f32[2,256,16,64]{1,0,3,2:T(2,128)S(1)}, u32[]{:S(2)}) copy-start(f32[2,256,16,64]{1,0,3,2:T(2,128)S(1)} %reshape.984) | copy-start | bytes 6291460
  466.1 57.0 %copy-start.64 = (f32[2,16,64,128]{3,2,1,0:T(8,128)}, f32[2,16,64,128]{3,2,1,0:T(8,128)S(1)}, u32[]{:S(2)}) copy-start(f32[2,16,64,128]{3,2,1,0:T(8,128)S(1)} %fusion.151) | copy-start | bytes 3145732
  467.3 163.0 %all-gather.19.cloned.1.call-start = ((), (), s32[]{:S(2)}) async-start(), calls=%async_computation.3 | async-start | bytes 1310720 | tf_op jit(solution)/shard_map/all_gather | solution.py:259
  581.2 261.7 %all-gather.21.cloned.1.call-start = ((), (), s32[]{:S(2)}) async-start(), calls=%async_computation.4 | async-start | bytes 1310720 | tf_op jit(solution)/shard_map/all_gather | solution.py:259
  654.2 29.7 %copy-start.219 = (f32[1280]{0:T(1024)}, f32[1280]{0:T(1024)S(1)}, u32[]{:S(2)}) copy-start(f32[1280]{0:T(1024)S(1)} %get-tuple-element.135) | copy-start | bytes 15364
  665.6 18.8 %collective-permute-start.8 = (f32[3,1280]{1,0:T(4,128)}, f32[3,1280]{1,0:T(4,128)}, u32[]{:S(2)}, u32[]{:S(2)}) collective-permute-start(f32[3,1280]{1,0:T(4,128)} %copy.559), channel_id=1, source_target_pairs={{4,0},{8,4},{12,8},{5,1},{9,5},{13,9},{6,2},{10,6},{14,10},{7,3},{... | collective-permute-start | bytes 46088 | tf_op jit(solution)/shard_map/ppermute | solution.py:236
  708.1 33.6 %collective-permute-start.9 = (bf16[128,2048]{1,0:T(8,128)(2,1)S(1)}, bf16[128,2048]{1,0:T(8,128)(2,1)S(1)}, u32[]{:S(2)}, u32[]{:S(2)}) collective-permute-start(bf16[128,2048]{1,0:T(8,128)(2,1)S(1)} %get-tuple-element.194), channel_id=1, source_target_pairs={{16,0},{17,1},{18,2},{19,3},{20,4},{21,5},{22,6},{23,7},{24,8},{25... | collective-permute-start | bytes 1572872 | tf_op jit(solution)/shard_map/ppermute | solution.py:236
  723.7 54.1 %copy-start.322 = (f32[512]{0:T(512)S(1)}, f32[512]{0:T(512)}, u32[]{:S(2)}) copy-start(f32[512]{0:T(512)} %copy-done.321) | copy-start | bytes 6148
  810.4 274.1 %all-gather.23.cloned.1.call-start = ((), (), s32[]{:S(2)}) async-start(), calls=%async_computation.5 | async-start | bytes 1310720 | tf_op jit(solution)/shard_map/all_gather | solution.py:259
  866.5 29.8 %copy-start.221 = (f32[1280]{0:T(1024)}, f32[1280]{0:T(1024)S(1)}, u32[]{:S(2)}) copy-start(f32[1280]{0:T(1024)S(1)} %get-tuple-element.136) | copy-start | bytes 15364
  877.8 19.1 %collective-permute-start.10 = (f32[3,1280]{1,0:T(4,128)}, f32[3,1280]{1,0:T(4,128)}, u32[]{:S(2)}, u32[]{:S(2)}) collective-permute-start(f32[3,1280]{1,0:T(4,128)} %copy.582), channel_id=1, source_target_pairs={{4,0},{8,4},{12,8},{5,1},{9,5},{13,9},{6,2},{10,6},{14,10},{7,3},{... | collective-permute-start | bytes 46088 | tf_op jit(solution)/shard_map/ppermute | solution.py:236
  913.2 52.6 %copy-start.26 = (f32[128,2048]{1,0:T(8,128)S(1)}, f32[128,2048]{1,0:T(8,128)}, u32[]{:S(2)}) copy-start(f32[128,2048]{1,0:T(8,128)} %copy-done.25) | copy-start | bytes 3145732
  913.2 52.6 %copy-start.354 = (f32[128]{0:T(128)S(1)}, f32[128]{0:T(128)}, u32[]{:S(2)}) copy-start(f32[128]{0:T(128)} %copy-done.353) | copy-start | bytes 1540
  913.2 54.8 %copy-start.66 = (bf16[2,128,2048]{2,1,0:T(8,128)(2,1)S(1)}, bf16[2,128,2048]{2,1,0:T(8,128)(2,1)}, u32[]{:S(2)}) copy-start(bf16[2,128,2048]{2,1,0:T(8,128)(2,1)} %param.20) | copy-start | bytes 3145732
  913.2 54.8 %copy-start.138 = (bf16[128,2048]{1,0:T(8,128)(2,1)S(1)}, bf16[128,2048]{1,0:T(8,128)(2,1)}, u32[]{:S(2)}) copy-start(bf16[128,2048]{1,0:T(8,128)(2,1)} %copy-done.137) | copy-start | bytes 1572868
  913.2 54.8 %copy-start.399 = (f32[128]{0:T(128)S(1)}, f32[128]{0:T(128)}, u32[]{:S(2)}) copy-start(f32[128]{0:T(128)} %get-tuple-element.334) | copy-start | bytes 1540
  969.5 15.6 %collective-permute-start.11 = (bf16[128,2048]{1,0:T(8,128)(2,1)S(1)}, bf16[128,2048]{1,0:T(8,128)(2,1)S(1)}, u32[]{:S(2)}, u32[]{:S(2)}) collective-permute-start(bf16[128,2048]{1,0:T(8,128)(2,1)S(1)} %get-tuple-element.190), channel_id=1, source_target_pairs={{16,0},{17,1},{18,2},{19,3},{20,4},{21,5},{22,6},{23,7},{24,8},{25... | collective-permute-start | bytes 1572872 | tf_op jit(solution)/shard_map/ppermute | solution.py:236
  985.1 30.1 %copy-start.320 = (f32[512]{0:T(512)S(1)}, f32[512]{0:T(512)}, u32[]{:S(2)}) copy-start(f32[512]{0:T(512)} %copy-done.319) | copy-start | bytes 6148
  1058.3 134.0 %all-reduce.69.cloned.1.call-start = ((), (), s32[]{:S(2)}) async-start(), calls=%async_computation.6 | async-start | bytes 8388608 | tf_op jit(solution)/shard_map/psum | solution.py:726
  1073.2 323.4 %all-reduce.71.cloned.1.call-start = ((), (), s32[]{:S(2)}) async-start(), calls=%async_computation.7 | async-start | bytes 17440768 | tf_op jit(solution)/shard_map/psum | solution.py:602
  1120.0 12.1 collective-permute-start.12
  1146.3 33.7 %copy-start.33 = (f32[509,1280]{0,1:T(8,128)S(1)}, f32[509,1280]{0,1:T(8,128)}, u32[]{:S(2)}) copy-start(f32[509,1280]{0,1:T(8,128)} %slice.886) | copy-start | bytes 7818244
  1235.1 25.5 %copy-start.154 = (bf16[512,1024]{0,1:T(8,128)(2,1)S(1)}, bf16[512,1024]{0,1:T(8,128)(2,1)}, u32[]{:S(2)}) copy-start(bf16[512,1024]{0,1:T(8,128)(2,1)} %get-tuple-element.232) | copy-start | bytes 3145732
  1273.3 36.9 %copy-start.52 = (bf16[2,128,2048]{2,1,0:T(8,128)(2,1)S(1)}, bf16[2,128,2048]{2,1,0:T(8,128)(2,1)}, u32[]{:S(2)}) copy-start(bf16[2,128,2048]{2,1,0:T(8,128)(2,1)} %param.19) | copy-start | bytes 3145732
  1273.3 36.9 %copy-start.340 = (f32[128]{0:T(128)S(1)}, f32[128]{0:T(128)}, u32[]{:S(2)}) copy-start(f32[128]{0:T(128)} %copy-done.339) | copy-start | bytes 1540
  1273.3 38.5 %copy-start.271 = (f32[2048]{0:T(1024)S(1)}, f32[2048]{0:T(1024)}, u32[]{:S(2)}) copy-start(f32[2048]{0:T(1024)} %get-tuple-element.141) | copy-start | bytes 24580
  1273.3 38.5 %copy-start.272 = (f32[2048]{0:T(1024)S(1)}, f32[2048]{0:T(1024)}, u32[]{:S(2)}) copy-start(f32[2048]{0:T(1024)} %get-tuple-element.143) | copy-start | bytes 24580
  1273.3 77.2 %copy-start.398 = (f32[128]{0:T(128)S(1)}, f32[128]{0:T(128)}, u32[]{:S(2)}) copy-start(f32[128]{0:T(128)} %get-tuple-element.332) | copy-start | bytes 1540
  (371 other events, 2085.6 us)
Sparse Core Ops, SparseCore 0:
  95.5 33.5 all-gather.12
  300.4 33.1 all-gather.14
  467.4 55.6 all-gather.16
  581.3 48.9 all-gather.18
  810.5 32.2 all-gather.20
  1058.4 26.1 all-gather.22
  1087.8 103.8 all-reduce.68
  1215.7 180.7 all-reduce.70

commit v11 on v10

--- a/solution.py
+++ b/solution.py
@@ -144,9 +144,8 @@
                 src_ref=send_l.at[k], dst_ref=recv_r.at[k], send_sem=ssem_l.at[k],
                 recv_sem=rsem_r.at[k], device_id={"head": h - 1}, device_id_type=MESH)
 
-        for s in range(n - 1):
+        def rightward(s):
             k_r = n - 1 - s
-            k_l = s
 
             @pl.when(k_r > h)
             def _():
@@ -161,6 +160,9 @@
 
                 to_right(k_r).start()
 
+        def leftward(s):
+            k_l = s
+
             @pl.when(k_l < h)
             def _():
                 @pl.when(h < n - 1)
@@ -173,6 +175,19 @@
                     send_l[k_l] = p_ref[k_l].astype(link)
 
                 to_left(k_l).start()
+
+        for s in range(n - 1):
+
+            @pl.when(2 * h < n)
+            def _():
+                rightward(s)
+                leftward(s)
+
+            @pl.when(2 * h >= n)
+            def _():
+                leftward(s)
+                rightward(s)
+
         total = p_ref[h]
 
         @pl.when(h > 0)

time: 1460 us -> 1420 us (0.973)
  Pallas kernels: 376 us -> 331 us
    pallas_call x7, Pallas kernels: 212 us -> 166 us  [head_scatter(): pl.pallas_call(functools.partial(scatter_body, n, tick), out_shape=jax.Sh...]
  transfers between devices with their start and end apart: 21 -> 21, of which waited for: 9 -> 10; matrix products, arithmetic and copies ran while one was open for 23% -> 24% of each run, Pallas kernels for 10% -> 9%
where the time goes in v11:
time: 1420 us; the launch traced here: 1410 us
  Pallas kernels  331 us (23%)
  matrix products  284 us (20%)
  other arithmetic  251 us (18%)
  local copies, waits for them, and re-layouts  179 us (13%)
  blocking collectives  166 us (12%)
  waiting for transfers between devices  144 us (10%)
  starting transfers between devices  34.1 us (2%)
  between operations  21.1 us (1%)
    pallas_call x7, Pallas kernels, head_scatter(): pl.pallas_call(functools.partial(scatter_body, n, tick), out_shape=jax.Sh...  166 us
    pallas_call x7, Pallas kernels, head_gather(): pl.pallas_call(functools.partial(gather_body, n, tick), out_shape=jax.Sha...  165 us
    dot_general x9, matrix products, block_output(): jnp.einsum('cijh,cjhp->cihp', weights, x_blocks, precision=highest)  67.9 us
    unnamed x844, local copies, waits for them, and re-layouts  67 us
    psum x1, waiting for transfers between devices, reduce_grads(): lax.psum(tuple((member.astype(jnp.bfloat16) for member in head_part[:3] +...  44.9 us
    all_gather x3, waiting for transfers between devices, entering_2(): lax.all_gather(a.astype(kind), axis)  43.4 us
    psum x1, blocking collectives, reduce_grads(): norm_sum = lax.psum(norm_part, ('seq', 'head'))  40.3 us
    dot_general x3, matrix products, mixer_forward(): projected = jnp.dot(gathered, w_main, preferred_element_type=jnp.float32)  38.1 us
  transfers between devices with their start and end apart: 21, of which 10 were waited for; matrix products, arithmetic and copies ran while one was open for 24% of the time, Pallas kernels for 9%

profile of v11, /device:TPU:0, one launch (start us, length us, event | category | flops | bytes accessed | tf_op | source)
XLA Modules:
  0.0 1410.7 jit_solution(6420565074844289819)
XLA Ops:
  20.9 29.3 %shard_map.297 = bf16[4,128,2048]{2,1,0:T(8,128)(2,1)} custom-call(bf16[128,2048]{1,0:T(8,128)(2,1)} %fusion.224.x_ref), custom_call_target="tpu_custom_call" | custom-call | tf_op jit(solution)/shard_map/pallas_call | solution.py:113
  50.5 12.7 fusion.417
  95.5 7.3 all-gather
  116.1 13.1 all-gather.13.cloned.1.call-done
  142.9 12.1 psum.126
  156.7 6.9 fusion.39.p_ref
  163.5 27.6 %shard_map.298 = f32[128,2048]{1,0:T(8,128)} custom-call(f32[4,128,2048]{2,1,0:T(8,128)} %fusion.39.p_ref), custom_call_target="tpu_custom_call" | custom-call | tf_op jit(solution)/shard_map/pallas_call | solution.py:224
  199.6 43.4 %shard_map.299 = bf16[4,128,2048]{2,1,0:T(8,128)(2,1)} custom-call(bf16[128,2048]{1,0:T(8,128)(2,1)} %multiply_convert_fusion.7.x_ref), custom_call_target="tpu_custom_call" | custom-call | tf_op jit(solution)/shard_map/pallas_call | solution.py:113
  243.0 12.9 fusion.416
  271.8 9.4 fusion.111
  298.8 6.4 all-gather.1
  313.6 12.5 all-gather.15.cloned.1.call-done
  340.1 12.1 psum.127
  355.7 6.9 fusion.37.p_ref
  362.6 35.4 %shard_map.300 = f32[128,2048]{1,0:T(8,128)} custom-call(f32[4,128,2048]{2,1,0:T(8,128)} %fusion.37.p_ref), custom_call_target="tpu_custom_call" | custom-call | tf_op jit(solution)/shard_map/pallas_call | solution.py:224
  409.6 12.5 fusion.415
  448.8 7.9 all-gather.5
  462.4 7.0 all-gather.4
  470.5 7.8 all-gather.3
  478.3 7.2 all-gather.2
  495.4 11.5 all-gather.17.cloned.1.call-done
  522.0 11.9 psum.128
  533.9 7.9 multiply_reduce_fusion.20
  541.8 8.3 psum.129
  550.1 6.9 multiply_reduce_fusion.23
  565.1 12.2 fusion.29
  583.1 5.7 fusion.454
  588.9 24.4 %all-gather.19.cloned.1.call-done = bf16[4,16,64,128]{3,2,1,0:T(8,128)(2,1)} async-done(((bf16[1,16,64,128]{3,2,1,0:T(8,128)(2,1)}), bf16[4,16,64,128]{3,2,1,0:T(8,128)(2,1)}) %all-gather.19.cloned.1.call-update) | async-done | bytes 1048592 | tf_op jit(solution)/shard_map/all_gather | solution.py:274
  619.9 6.3 fusion.127
  630.5 6.5 multiply_reduce_fusion.13
  692.5 11.0 fusion.251
  706.7 11.1 collective-permute-done.9
  719.4 34.3 %shard_map.305 = bf16[4,128,2048]{2,1,0:T(8,128)(2,1)} custom-call(bf16[128,2048]{1,0:T(8,128)(2,1)} %fusion.242.x_ref), custom_call_target="tpu_custom_call" | custom-call | tf_op jit(solution)/shard_map/pallas_call | solution.py:113
  753.8 8.0 multiply_reduce_fusion.19
  761.8 11.0 psum.130
  772.9 6.0 multiply_reduce_fusion.22
  787.2 11.9 fusion.31
  804.8 5.7 fusion.455
  810.5 8.1 all-gather.21.cloned.1.call-done
  825.3 6.1 fusion.123
  835.8 6.7 multiply_reduce_fusion.9
  889.0 41.1 %shard_map.306 = f32[128,2048]{1,0:T(8,128)} custom-call(f32[4,128,2048]{2,1,0:T(8,128)} %bitcast.971), custom_call_target="tpu_custom_call" | custom-call | tf_op jit(solution)/shard_map/pallas_call | solution.py:224
  935.3 10.9 fusion.249
  951.2 28.6 %shard_map.307 = bf16[4,128,2048]{2,1,0:T(8,128)(2,1)} custom-call(bf16[128,2048]{1,0:T(8,128)(2,1)} %fusion.243.x_ref), custom_call_target="tpu_custom_call" | custom-call | tf_op jit(solution)/shard_map/pallas_call | solution.py:113
  979.9 8.0 multiply_reduce_fusion.18
  987.9 11.2 psum.131
  1008.3 11.6 fusion.33
  1028.5 10.6 add_convert_fusion
  1039.4 10.9 all-gather.23.cloned.1.call-done
  1075.0 5.7 multiply_reduce_fusion.5
  1089.2 6.6 pad_add_fusion
  1112.3 24.3 %shard_map.308 = f32[520,256]{1,0:T(8,128)} custom-call(f32[4,520,256]{2,1,0:T(8,128)} %bitcast.975), custom_call_target="tpu_custom_call" | custom-call | tf_op jit(solution)/shard_map/pallas_call | solution.py:224
  1143.4 6.0 copy-done.49
  1151.1 6.4 all-reduce.69.cloned.1.call-done
  1159.3 21.5 %fusion.34 = (bf16[1,2048,1024]{1,2,0:T(8,128)(2,1)}, bf16[1,2048,1024]{1,2,0:T(8,128)(2,1)}) fusion(f32[2048,2064]{0,1:T(8,128)} %copy-done.49, f32[2048,2064]{0,1:T(8,128)} %fusion.249, f32[2048,2064]{0,1:T(8,128)} %fusion.251, f32[]{:T(128)S(6)} %convert_element_type.597, f32[]{:T(128)S(6)} %convert_element_type.596, f32[]{:T(128)S(6)} %convert_element_type.595, ...), kind=kLoop, calls=%fused_computation.58 | loop fusion | flops 27262976 | bytes 58720272 | tf_op jit(solution)/shard_map/broadcast_in_dim | solution.py:768
  1184.0 7.1 fusion.35.p_ref
  1202.4 16.0 %all-reduce.64 = (bf16[1,4,1024]{2,1,0:T(4,128)(2,1)S(1)}, bf16[1,1024]{1,0:T(2,128)(2,1)S(1)}, bf16[1,16]{1,0:T(2,128)(2,1)S(1)}, bf16[1,16]{1,0:T(2,128)(2,1)S...) all-reduce(bf16[1,4,1024]{2,1,0:T(4,128)(2,1)S(1)} %fusion.338, ...), channel_id=1, replica_groups=mesh['section'=2,'seq'=4,'head'=4] {'seq'}, use_global_device_ids=true, to_apply=%region_96.98 | all-reduce | flops 6192 | bytes 24768 | tf_op jit(solution)/shard_map/psum | solution.py:621
  1223.6 8.1 fusion.248
  1236.3 30.4 %shard_map.309 = f32[128,2048]{1,0:T(8,128)} custom-call(f32[4,128,2048]{2,1,0:T(8,128)} %bitcast.969), custom_call_target="tpu_custom_call" | custom-call | tf_op jit(solution)/shard_map/pallas_call | solution.py:224
  1268.2 40.3 %psum.132 = f32[1,2048]{1,0:T(1,128)} all-reduce(f32[1,2048]{1,0:T(1,128)S(1)} %bitcast.1090), channel_id=1, replica_groups=mesh['section'=2,'seq'=4,'head'=4] {'seq','head'}, use_global_device_ids=true, to_apply=%region_90.92 | all-reduce | flops 2048 | bytes 16384 | tf_op jit(solution)/shard_map/psum | solution.py:625
  1316.4 44.9 %all-reduce.71.cloned.1.call-done = (bf16[1,2048,1024]{1,2,0:T(8,128)(2,1)}, bf16[1,2048,1024]{1,2,0:T(8,128)(2,1)}, bf16[520,256]{1,0:T(8,128)(2,1)}, bf16[1,2048,16]{1,2,0:T(8,128)(2,1)}) async-done(((bf16[1,2048,1024]{1,2,0:T(8,128)(2,1)}, bf16[1,2048,1024]{1,2,0:T(8,128)(2,1)}, bf16[520,256]{1,0:T(8,128)(2,1)}, bf16[1,2048,16]{1,2,0:T(8,128)(2,1)}), (bf16[1,2048,1024]{1,2,0:T(8,128)(2,1)}, ...) | async-done | bytes 8720400 | tf_op jit(solution)/shard_map/psum | solution.py:617
  1361.3 23.9 %shard_map.310 = bf16[4,520,256]{2,1,0:T(8,128)(2,1)} custom-call(bf16[520,256]{1,0:T(8,128)(2,1)} %get-tuple-element.171.x_ref), custom_call_target="tpu_custom_call" | custom-call | tf_op jit(solution)/shard_map/pallas_call | solution.py:113
  1389.3 6.9 copy.616
  1396.1 6.9 copy.617
  (1280 shorter events, 490.0 us)
Async XLA Ops:
  7.2 43.0 %copy-start.211 = (bf16[1,2048,16]{1,2,0:T(8,128)(2,1)S(1)}, bf16[1,2048,16]{1,2,0:T(8,128)(2,1)}, u32[]{:S(2)}) copy-start(bf16[1,2048,16]{1,2,0:T(8,128)(2,1)} %param.27) | copy-start | bytes 196612
  7.2 43.3 %copy-start.56 = (bf16[1,2048,256]{2,1,0:T(8,128)(2,1)S(1)}, bf16[1,2048,256]{2,1,0:T(8,128)(2,1)}, u32[]{:S(2)}) copy-start(bf16[1,2048,256]{2,1,0:T(8,128)(2,1)} %param.26) | copy-start | bytes 3145732
  7.2 121.9 %all-gather.13.cloned.1.call-start = ((), (), s32[]{:S(2)}) async-start(), calls=%async_computation | async-start | bytes 2621440 | tf_op jit(solution)/shard_map/all_gather | solution.py:256
  8.7 70.4 %collective-permute-start = (f32[3]{0:T(128)S(1)}, f32[3]{0:T(128)S(1)}, u32[]{:S(2)}, u32[]{:S(2)}) collective-permute-start(f32[3]{0:T(128)S(1)} %slice.590), channel_id=1, source_target_pairs={{0,4},{4,8},{8,12},{1,5},{5,9},{9,13},{2,6},{6,10},{10,14},{3,7},{... | collective-permute-start | bytes 44 | tf_op jit(solution)/shard_map/ppermute | solution.py:251
  13.7 65.5 %collective-permute-start.3 = (f32[3]{0:T(128)S(1)}, f32[3]{0:T(128)S(1)}, u32[]{:S(2)}, u32[]{:S(2)}) collective-permute-start(f32[3]{0:T(128)S(1)} %slice.629), channel_id=1, source_target_pairs={{0,4},{4,8},{8,12},{1,5},{5,9},{9,13},{2,6},{6,10},{10,14},{3,7},{... | collective-permute-start | bytes 44 | tf_op jit(solution)/shard_map/ppermute | solution.py:251
  18.9 31.3 %copy-start.339 = (f32[128]{0:T(128)}, f32[128]{0:T(128)S(1)}, u32[]{:S(2)}) copy-start(f32[128]{0:T(128)S(1)} %get-tuple-element.333) | copy-start | bytes 1540
  65.9 14.8 %collective-permute-start.1 = (f32[3,1280]{1,0:T(4,128)S(1)}, f32[3,1280]{1,0:T(4,128)S(1)}, u32[]{:S(2)}, u32[]{:S(2)}) collective-permute-start(f32[3,1280]{1,0:T(4,128)S(1)} %copy.495), channel_id=1, source_target_pairs={{0,4},{4,8},{8,12},{1,5},{5,9},{9,13},{2,6},{6,10},{10,14},{3,7},{... | collective-permute-start | bytes 46088 | tf_op jit(solution)/shard_map/ppermute | solution.py:251
  73.0 29.7 %copy-start.145 = (f32[512,16]{0,1:T(8,128)}, f32[512,16]{0,1:T(8,128)S(1)}, u32[]{:S(2)}) copy-start(f32[512,16]{0,1:T(8,128)S(1)} %get-tuple-element.227) | copy-start | bytes 98308
  79.1 53.7 %copy-start.178 = (f32[2,256,16]{1,2,0:T(8,128)}, f32[2,256,16]{1,2,0:T(8,128)S(1)}, u32[]{:S(2)}) copy-start(f32[2,256,16]{1,2,0:T(8,128)S(1)} %get-tuple-element.276) | copy-start | bytes 98308
  90.7 42.1 %copy-start.9 = (f32[2,256,16,64]{1,0,3,2:T(2,128)}, f32[2,256,16,64]{1,0,3,2:T(2,128)S(1)}, u32[]{:S(2)}) copy-start(f32[2,256,16,64]{1,0,3,2:T(2,128)S(1)} %reshape.960) | copy-start | bytes 6291460
  93.7 35.4 %copy-start.61 = (f32[2,16,64,128]{3,2,1,0:T(8,128)}, f32[2,16,64,128]{3,2,1,0:T(8,128)S(1)}, u32[]{:S(2)}) copy-start(f32[2,16,64,128]{3,2,1,0:T(8,128)S(1)} %fusion.159) | copy-start | bytes 3145732
  95.4 230.7 %all-gather.15.cloned.1.call-start = ((), (), s32[]{:S(2)}) async-start(), calls=%async_computation.1 | async-start | bytes 2621440 | tf_op jit(solution)/shard_map/all_gather | solution.py:256
  163.5 29.2 %copy-start.50 = (bf16[2,128,2048]{2,1,0:T(8,128)(2,1)S(1)}, bf16[2,128,2048]{2,1,0:T(8,128)(2,1)}, u32[]{:S(2)}) copy-start(bf16[2,128,2048]{2,1,0:T(8,128)(2,1)} %param.19) | copy-start | bytes 3145732
  194.0 3.7 collective-permute-start.2
  197.0 70.3 %copy-start.265 = (f32[2,256]{1,0:T(2,128)}, f32[2,256]{1,0:T(2,128)S(1)}, u32[]{:S(2)}) copy-start(f32[2,256]{1,0:T(2,128)S(1)} %get-tuple-element.343) | copy-start | bytes 6148
  197.0 70.3 %copy-start.307 = (f32[2,256]{1,0:T(2,128)}, f32[2,256]{1,0:T(2,128)S(1)}, u32[]{:S(2)}) copy-start(f32[2,256]{1,0:T(2,128)S(1)} %get-tuple-element.344) | copy-start | bytes 6148
  197.7 74.0 %copy-start.243 = (f32[512]{0:T(512)}, f32[512]{0:T(512)S(1)}, u32[]{:S(2)}) copy-start(f32[512]{0:T(512)S(1)} %get-tuple-element.287) | copy-start | bytes 6148
  197.7 74.0 %copy-start.245 = (f32[512]{0:T(512)}, f32[512]{0:T(512)S(1)}, u32[]{:S(2)}) copy-start(f32[512]{0:T(512)S(1)} %get-tuple-element.288) | copy-start | bytes 6148
  197.7 74.0 %copy-start.247 = (f32[512]{0:T(512)}, f32[512]{0:T(512)S(1)}, u32[]{:S(2)}) copy-start(f32[512]{0:T(512)S(1)} %get-tuple-element.289) | copy-start | bytes 6148
  198.0 200.0 %copy-start.25 = (f32[128,2048]{1,0:T(8,128)}, f32[128,2048]{1,0:T(8,128)S(1)}, u32[]{:S(2)}) copy-start(f32[128,2048]{1,0:T(8,128)S(1)} %get-tuple-element.219) | copy-start | bytes 3145732
  198.6 57.3 %copy-start.353 = (f32[128]{0:T(128)}, f32[128]{0:T(128)S(1)}, u32[]{:S(2)}) copy-start(f32[128]{0:T(128)S(1)} %get-tuple-element.335) | copy-start | bytes 1540
  243.0 23.6 %copy-start.351 = (f32[2]{0:T(128)S(1)}, f32[2]{0:T(128)}, u32[]{:S(2)}) copy-start(f32[2]{0:T(128)} %get-tuple-element.346) | copy-start | bytes 28
  260.5 11.0 collective-permute-start.4
  265.0 40.3 %copy-start.147 = (f32[512,16]{0,1:T(8,128)}, f32[512,16]{0,1:T(8,128)S(1)}, u32[]{:S(2)}) copy-start(f32[512,16]{0,1:T(8,128)S(1)} %get-tuple-element.215) | copy-start | bytes 98308
  267.4 62.6 %copy-start.182 = (f32[2,256,16]{1,2,0:T(8,128)}, f32[2,256,16]{1,2,0:T(8,128)S(1)}, u32[]{:S(2)}) copy-start(f32[2,256,16]{1,2,0:T(8,128)S(1)} %get-tuple-element.274) | copy-start | bytes 98308
  286.3 43.6 %copy-start.11 = (f32[2,256,16,64]{1,0,3,2:T(2,128)}, f32[2,256,16,64]{1,0,3,2:T(2,128)S(1)}, u32[]{:S(2)}) copy-start(f32[2,256,16,64]{1,0,3,2:T(2,128)S(1)} %reshape.972) | copy-start | bytes 6291460
  291.3 215.6 %all-gather.17.cloned.1.call-start = ((), (), s32[]{:S(2)}) async-start(), calls=%async_computation.2 | async-start | bytes 2621440 | tf_op jit(solution)/shard_map/all_gather | solution.py:256
  292.6 109.7 %collective-permute-start.6 = (f32[3]{0:T(128)}, f32[3]{0:T(128)}, u32[]{:S(2)}, u32[]{:S(2)}) collective-permute-start(f32[3]{0:T(128)} %slice.664), channel_id=1, source_target_pairs={{0,4},{4,8},{8,12},{1,5},{5,9},{9,13},{2,6},{6,10},{10,14},{3,7},{... | collective-permute-start | bytes 44 | tf_op jit(solution)/shard_map/ppermute | solution.py:251
  305.2 24.7 %copy-start.287 = (f32[2,2,8,256]{3,2,0,1:T(8,128)}, f32[2,2,8,256]{3,2,0,1:T(8,128)S(1)}, u32[]{:S(2)}) copy-start(f32[2,2,8,256]{3,2,0,1:T(8,128)S(1)} %copy.946) | copy-start | bytes 98308
  362.6 35.4 %copy-start.112 = (f32[1,128,2048]{2,1,0:T(8,128)S(1)}, f32[1,128,2048]{2,1,0:T(8,128)}, u32[]{:S(2)}) copy-start(f32[1,128,2048]{2,1,0:T(8,128)} %constant_dynamic-slice_fusion.3) | copy-start | bytes 3145732
  400.9 3.8 collective-permute-start.5
  402.3 28.4 %copy-start.390 = (f32[2]{0:T(128)}, f32[2]{0:T(128)S(1)}, u32[]{:S(2)}) copy-start(f32[2]{0:T(128)S(1)} %fusion.369) | copy-start | bytes 28
  403.7 31.2 %copy-start.249 = (f32[512]{0:T(512)}, f32[512]{0:T(512)S(1)}, u32[]{:S(2)}) copy-start(f32[512]{0:T(512)S(1)} %get-tuple-element.281) | copy-start | bytes 6148
  403.7 31.2 %copy-start.251 = (f32[512]{0:T(512)}, f32[512]{0:T(512)S(1)}, u32[]{:S(2)}) copy-start(f32[512]{0:T(512)S(1)} %get-tuple-element.282) | copy-start | bytes 6148
  403.7 31.2 %copy-start.253 = (f32[512]{0:T(512)}, f32[512]{0:T(512)S(1)}, u32[]{:S(2)}) copy-start(f32[512]{0:T(512)S(1)} %get-tuple-element.283) | copy-start | bytes 6148
  424.8 9.8 collective-permute-start.7
  444.7 170.2 %copy-start.14 = (f32[2,256,16,64]{1,0,3,2:T(2,128)}, f32[2,256,16,64]{1,0,3,2:T(2,128)S(1)}, u32[]{:S(2)}) copy-start(f32[2,256,16,64]{1,0,3,2:T(2,128)S(1)} %reshape.984) | copy-start | bytes 6291460
  447.6 59.3 %copy-start.64 = (f32[2,16,64,128]{3,2,1,0:T(8,128)}, f32[2,16,64,128]{3,2,1,0:T(8,128)S(1)}, u32[]{:S(2)}) copy-start(f32[2,16,64,128]{3,2,1,0:T(8,128)S(1)} %fusion.151) | copy-start | bytes 3145732
  448.8 164.5 %all-gather.19.cloned.1.call-start = ((), (), s32[]{:S(2)}) async-start(), calls=%async_computation.3 | async-start | bytes 1310720 | tf_op jit(solution)/shard_map/all_gather | solution.py:274
  565.0 253.6 %all-gather.21.cloned.1.call-start = ((), (), s32[]{:S(2)}) async-start(), calls=%async_computation.4 | async-start | bytes 1310720 | tf_op jit(solution)/shard_map/all_gather | solution.py:274
  637.0 29.7 %copy-start.219 = (f32[1280]{0:T(1024)}, f32[1280]{0:T(1024)S(1)}, u32[]{:S(2)}) copy-start(f32[1280]{0:T(1024)S(1)} %get-tuple-element.135) | copy-start | bytes 15364
  648.4 18.9 %collective-permute-start.8 = (f32[3,1280]{1,0:T(4,128)}, f32[3,1280]{1,0:T(4,128)}, u32[]{:S(2)}, u32[]{:S(2)}) collective-permute-start(f32[3,1280]{1,0:T(4,128)} %copy.559), channel_id=1, source_target_pairs={{4,0},{8,4},{12,8},{5,1},{9,5},{13,9},{6,2},{10,6},{14,10},{7,3},{... | collective-permute-start | bytes 46088 | tf_op jit(solution)/shard_map/ppermute | solution.py:251
  691.1 26.6 %collective-permute-start.9 = (bf16[128,2048]{1,0:T(8,128)(2,1)S(1)}, bf16[128,2048]{1,0:T(8,128)(2,1)S(1)}, u32[]{:S(2)}, u32[]{:S(2)}) collective-permute-start(bf16[128,2048]{1,0:T(8,128)(2,1)S(1)} %get-tuple-element.194), channel_id=1, source_target_pairs={{16,0},{17,1},{18,2},{19,3},{20,4},{21,5},{22,6},{23,7},{24,8},{25... | collective-permute-start | bytes 1572872 | tf_op jit(solution)/shard_map/ppermute | solution.py:251
  706.7 47.1 %copy-start.322 = (f32[512]{0:T(512)S(1)}, f32[512]{0:T(512)}, u32[]{:S(2)}) copy-start(f32[512]{0:T(512)} %copy-done.321) | copy-start | bytes 6148
  787.1 263.1 %all-gather.23.cloned.1.call-start = ((), (), s32[]{:S(2)}) async-start(), calls=%async_computation.5 | async-start | bytes 1310720 | tf_op jit(solution)/shard_map/all_gather | solution.py:274
  842.5 29.6 %copy-start.221 = (f32[1280]{0:T(1024)}, f32[1280]{0:T(1024)S(1)}, u32[]{:S(2)}) copy-start(f32[1280]{0:T(1024)S(1)} %get-tuple-element.136) | copy-start | bytes 15364
  853.8 18.9 %collective-permute-start.10 = (f32[3,1280]{1,0:T(4,128)}, f32[3,1280]{1,0:T(4,128)}, u32[]{:S(2)}, u32[]{:S(2)}) collective-permute-start(f32[3,1280]{1,0:T(4,128)} %copy.582), channel_id=1, source_target_pairs={{4,0},{8,4},{12,8},{5,1},{9,5},{13,9},{6,2},{10,6},{14,10},{7,3},{... | collective-permute-start | bytes 46088 | tf_op jit(solution)/shard_map/ppermute | solution.py:251
  888.9 41.1 %copy-start.26 = (f32[128,2048]{1,0:T(8,128)S(1)}, f32[128,2048]{1,0:T(8,128)}, u32[]{:S(2)}) copy-start(f32[128,2048]{1,0:T(8,128)} %copy-done.25) | copy-start | bytes 3145732
  888.9 41.1 %copy-start.354 = (f32[128]{0:T(128)S(1)}, f32[128]{0:T(128)}, u32[]{:S(2)}) copy-start(f32[128]{0:T(128)} %copy-done.353) | copy-start | bytes 1540
  888.9 43.4 %copy-start.66 = (bf16[2,128,2048]{2,1,0:T(8,128)(2,1)S(1)}, bf16[2,128,2048]{2,1,0:T(8,128)(2,1)}, u32[]{:S(2)}) copy-start(bf16[2,128,2048]{2,1,0:T(8,128)(2,1)} %param.20) | copy-start | bytes 3145732
  888.9 43.4 %copy-start.138 = (bf16[128,2048]{1,0:T(8,128)(2,1)S(1)}, bf16[128,2048]{1,0:T(8,128)(2,1)}, u32[]{:S(2)}) copy-start(bf16[128,2048]{1,0:T(8,128)(2,1)} %copy-done.137) | copy-start | bytes 1572868
  888.9 43.4 %copy-start.399 = (f32[128]{0:T(128)S(1)}, f32[128]{0:T(128)}, u32[]{:S(2)}) copy-start(f32[128]{0:T(128)} %get-tuple-element.334) | copy-start | bytes 1540
  933.8 15.6 %collective-permute-start.11 = (bf16[128,2048]{1,0:T(8,128)(2,1)S(1)}, bf16[128,2048]{1,0:T(8,128)(2,1)S(1)}, u32[]{:S(2)}, u32[]{:S(2)}) collective-permute-start(bf16[128,2048]{1,0:T(8,128)(2,1)S(1)} %get-tuple-element.190), channel_id=1, source_target_pairs={{16,0},{17,1},{18,2},{19,3},{20,4},{21,5},{22,6},{23,7},{24,8},{25... | collective-permute-start | bytes 1572872 | tf_op jit(solution)/shard_map/ppermute | solution.py:251
  949.4 30.4 %copy-start.320 = (f32[512]{0:T(512)S(1)}, f32[512]{0:T(512)}, u32[]{:S(2)}) copy-start(f32[512]{0:T(512)} %copy-done.319) | copy-start | bytes 6148
  1024.2 133.2 %all-reduce.69.cloned.1.call-start = ((), (), s32[]{:S(2)}) async-start(), calls=%async_computation.6 | async-start | bytes 8388608 | tf_op jit(solution)/shard_map/psum | solution.py:741
  1039.1 322.2 %all-reduce.71.cloned.1.call-start = ((), (), s32[]{:S(2)}) async-start(), calls=%async_computation.7 | async-start | bytes 17440768 | tf_op jit(solution)/shard_map/psum | solution.py:617
  1085.7 12.5 collective-permute-start.12
  1112.3 26.3 %copy-start.33 = (f32[509,1280]{0,1:T(8,128)S(1)}, f32[509,1280]{0,1:T(8,128)}, u32[]{:S(2)}) copy-start(f32[509,1280]{0,1:T(8,128)} %slice.886) | copy-start | bytes 7818244
  1200.7 22.9 %copy-start.154 = (bf16[512,1024]{0,1:T(8,128)(2,1)S(1)}, bf16[512,1024]{0,1:T(8,128)(2,1)}, u32[]{:S(2)}) copy-start(bf16[512,1024]{0,1:T(8,128)(2,1)} %get-tuple-element.232) | copy-start | bytes 3145732
  1236.2 30.4 %copy-start.52 = (bf16[2,128,2048]{2,1,0:T(8,128)(2,1)S(1)}, bf16[2,128,2048]{2,1,0:T(8,128)(2,1)}, u32[]{:S(2)}) copy-start(bf16[2,128,2048]{2,1,0:T(8,128)(2,1)} %param.19) | copy-start | bytes 3145732
  1236.3 30.4 %copy-start.340 = (f32[128]{0:T(128)S(1)}, f32[128]{0:T(128)}, u32[]{:S(2)}) copy-start(f32[128]{0:T(128)} %copy-done.339) | copy-start | bytes 1540
  1236.3 32.0 %copy-start.271 = (f32[2048]{0:T(1024)S(1)}, f32[2048]{0:T(1024)}, u32[]{:S(2)}) copy-start(f32[2048]{0:T(1024)} %get-tuple-element.141) | copy-start | bytes 24580
  1236.3 32.0 %copy-start.272 = (f32[2048]{0:T(1024)S(1)}, f32[2048]{0:T(1024)}, u32[]{:S(2)}) copy-start(f32[2048]{0:T(1024)} %get-tuple-element.143) | copy-start | bytes 24580
  1236.3 72.3 %copy-start.398 = (f32[128]{0:T(128)S(1)}, f32[128]{0:T(128)}, u32[]{:S(2)}) copy-start(f32[128]{0:T(128)} %get-tuple-element.332) | copy-start | bytes 1540
  (371 other events, 2095.4 us)
Sparse Core Ops, SparseCore 0:
  95.5 33.5 all-gather.12
  291.4 34.7 all-gather.14
  448.9 57.9 all-gather.16
  565.1 48.1 all-gather.18
  787.2 31.3 all-gather.20
  1024.3 25.8 all-gather.22
  1053.5 103.8 all-reduce.68
  1180.9 180.3 all-reduce.70

commit v12 on v11

--- a/solution.py
+++ b/solution.py
@@ -51,17 +51,37 @@
     def _():
         _enter(pltpu.get_barrier_semaphore(), h, n)
 
+        rows = x_ref.shape[0]
+        pieces = 2 if rows % 32 == 0 else 1
+        size = rows // pieces
+
+        def chunked(s, k, sems, peer):
+            copies = []
+            for c in range(pieces):
+                part = pl.ds(c * size, size)
+                src = x_ref.at[part] if s == 0 else land.at[k, part]
+                copies.append(pltpu.make_async_remote_copy(
+                    src_ref=src, dst_ref=land.at[k, part], send_sem=sems.at[s * pieces + c],
+                    recv_sem=recv.at[k], device_id={"head": peer}, device_id_type=MESH))
+            return copies
+
+        class Group:
+            def __init__(self, copies):
+                self.copies = copies
+
+            def start(self):
+                for copy in self.copies:
+                    copy.start()
+
+            def wait_send(self):
+                for copy in self.copies:
+                    copy.wait_send()
+
         def copy_right(s, k):
-            src = x_ref if s == 0 else land.at[k]
-            return pltpu.make_async_remote_copy(
-                src_ref=src, dst_ref=land.at[k], send_sem=send_r.at[s], recv_sem=recv.at[k],
-                device_id={"head": h + 1}, device_id_type=MESH)
+            return Group(chunked(s, k, send_r, h + 1))
 
         def copy_left(s, k):
-            src = x_ref if s == 0 else land.at[k]
-            return pltpu.make_async_remote_copy(
-                src_ref=src, dst_ref=land.at[k], send_sem=send_l.at[s], recv_sem=recv.at[k],
-                device_id={"head": h - 1}, device_id_type=MESH)
+            return Group(chunked(s, k, send_l, h - 1))
 
         for s in range(n):
             k_r = h - s
@@ -117,8 +137,8 @@
         out_specs=pl.BlockSpec(memory_space=pltpu.VMEM),
         scratch_shapes=[
             pltpu.VMEM((n, rows, cols), x.dtype),
-            pltpu.SemaphoreType.DMA((n,)),
-            pltpu.SemaphoreType.DMA((n,)),
+            pltpu.SemaphoreType.DMA((2 * n,)),
+            pltpu.SemaphoreType.DMA((2 * n,)),
             pltpu.SemaphoreType.DMA((n,)),
         ],
         compiler_params=pltpu.CompilerParams(collective_id=cid, has_side_effects=True),
@@ -134,15 +154,23 @@
     def _():
         _enter(pltpu.get_barrier_semaphore(), h, n)
 
-        def to_right(k):
+        rows = p_ref.shape[1]
+        pieces = 2 if rows % 32 == 0 else 1
+        size = rows // pieces
+
+        def to_right(k, c=None):
+            part = slice(None) if c is None else pl.ds(c * size, size)
             return pltpu.make_async_remote_copy(
-                src_ref=send_r.at[k], dst_ref=recv_l.at[k], send_sem=ssem_r.at[k],
-                recv_sem=rsem_l.at[k], device_id={"head": h + 1}, device_id_type=MESH)
-
-        def to_left(k):
+                src_ref=send_r.at[k, part], dst_ref=recv_l.at[k, part],
+                send_sem=ssem_r.at[k * pieces + (c or 0)], recv_sem=rsem_l.at[k],
+                device_id={"head": h + 1}, device_id_type=MESH)
+
+        def to_left(k, c=None):
+            part = slice(None) if c is None else pl.ds(c * size, size)
             return pltpu.make_async_remote_copy(
-                src_ref=send_l.at[k], dst_ref=recv_r.at[k], send_sem=ssem_l.at[k],
-                recv_sem=rsem_r.at[k], device_id={"head": h - 1}, device_id_type=MESH)
+                src_ref=send_l.at[k, part], dst_ref=recv_r.at[k, part],
+                send_sem=ssem_l.at[k * pieces + (c or 0)], recv_sem=rsem_r.at[k],
+                device_id={"head": h - 1}, device_id_type=MESH)
 
         def rightward(s):
             k_r = n - 1 - s
@@ -152,13 +180,21 @@
                 @pl.when(h > 0)
                 def _():
                     to_right(k_r).wait_recv()
-                    send_r[k_r] = (p_ref[k_r] + recv_l[k_r].astype(jnp.float32)).astype(link)
-
-                @pl.when(h == 0)
-                def _():
-                    send_r[k_r] = p_ref[k_r].astype(link)
-
-                to_right(k_r).start()
+
+                for c in range(pieces):
+                    part = pl.ds(c * size, size)
+
+                    @pl.when(h > 0)
+                    def _():
+                        send_r[k_r, part] = (
+                            p_ref[k_r, part] + recv_l[k_r, part].astype(jnp.float32)
+                        ).astype(link)
+
+                    @pl.when(h == 0)
+                    def _():
+                        send_r[k_r, part] = p_ref[k_r, part].astype(link)
+
+                    to_right(k_r, c).start()
 
         def leftward(s):
             k_l = s
@@ -168,13 +204,21 @@
                 @pl.when(h < n - 1)
                 def _():
                     to_left(k_l).wait_recv()
-                    send_l[k_l] = (p_ref[k_l] + recv_r[k_l].astype(jnp.float32)).astype(link)
-
-                @pl.when(h == n - 1)
-                def _():
-                    send_l[k_l] = p_ref[k_l].astype(link)
-
-                to_left(k_l).start()
+
+                for c in range(pieces):
+                    part = pl.ds(c * size, size)
+
+                    @pl.when(h < n - 1)
+                    def _():
+                        send_l[k_l, part] = (
+                            p_ref[k_l, part] + recv_r[k_l, part].astype(jnp.float32)
+                        ).astype(link)
+
+                    @pl.when(h == n - 1)
+                    def _():
+                        send_l[k_l, part] = p_ref[k_l, part].astype(link)
+
+                    to_left(k_l, c).start()
 
         for s in range(n - 1):
 
@@ -207,11 +251,13 @@
 
             @pl.when(k_r > h)
             def _():
-                to_right(k_r).wait_send()
+                for c in range(pieces):
+                    to_right(k_r, c).wait_send()
 
             @pl.when(k_l < h)
             def _():
-                to_left(k_l).wait_send()
+                for c in range(pieces):
+                    to_left(k_l, c).wait_send()
 
     @pl.when(jnp.logical_not(valid))
     def _():
@@ -231,8 +277,8 @@
             pltpu.VMEM((n, rows, cols), link),
             pltpu.VMEM((n, rows, cols), link),
             pltpu.VMEM((n, rows, cols), link),
-            pltpu.SemaphoreType.DMA((n,)),
-            pltpu.SemaphoreType.DMA((n,)),
+            pltpu.SemaphoreType.DMA((2 * n,)),
+            pltpu.SemaphoreType.DMA((2 * n,)),
             pltpu.SemaphoreType.DMA((n,)),
             pltpu.SemaphoreType.DMA((n,)),
         ],

time: 1420 us -> 1420 us (level)
  no operation moved by 1% of the time
where the time goes in v12:
time: 1420 us; the launch traced here: 1410 us
  Pallas kernels  332 us (23%)
  matrix products  284 us (20%)
  other arithmetic  251 us (18%)
  local copies, waits for them, and re-layouts  179 us (13%)
  blocking collectives  166 us (12%)
  waiting for transfers between devices  144 us (10%)
  starting transfers between devices  34.1 us (2%)
  between operations  21.1 us (1%)
    pallas_call x7, Pallas kernels, head_scatter(): pl.pallas_call(functools.partial(scatter_body, n, tick), out_shape=jax.Sh...  167 us
    pallas_call x7, Pallas kernels, head_gather(): pl.pallas_call(functools.partial(gather_body, n, tick), out_shape=jax.Sha...  165 us
    dot_general x9, matrix products, block_output(): jnp.einsum('cijh,cjhp->cihp', weights, x_blocks, precision=highest)  67.9 us
    unnamed x844, local copies, waits for them, and re-layouts  67 us
    psum x1, waiting for transfers between devices, reduce_grads(): lax.psum(tuple((member.astype(jnp.bfloat16) for member in head_part[:3] +...  44.8 us
    all_gather x3, waiting for transfers between devices, entering_2(): lax.all_gather(a.astype(kind), axis)  43.5 us
    psum x1, blocking collectives, reduce_grads(): norm_sum = lax.psum(norm_part, ('seq', 'head'))  40.3 us
    dot_general x3, matrix products, mixer_forward(): projected = jnp.dot(gathered, w_main, preferred_element_type=jnp.float32)  38.1 us
  transfers between devices with their start and end apart: 21, of which 10 were waited for; matrix products, arithmetic and copies ran while one was open for 24% of the time, Pallas kernels for 9%

profile of v12, /device:TPU:0, one launch (start us, length us, event | category | flops | bytes accessed | tf_op | source)
XLA Modules:
  0.0 1411.3 jit_solution(10919450760527956019)
XLA Ops:
  20.9 29.3 %shard_map.297 = bf16[4,128,2048]{2,1,0:T(8,128)(2,1)} custom-call(bf16[128,2048]{1,0:T(8,128)(2,1)} %fusion.224.x_ref), custom_call_target="tpu_custom_call" | custom-call | tf_op jit(solution)/shard_map/pallas_call | solution.py:133
  50.6 12.7 fusion.417
  95.6 7.3 all-gather
  116.1 13.1 all-gather.13.cloned.1.call-done
  143.0 12.1 psum.126
  156.7 6.9 fusion.39.p_ref
  163.6 27.6 %shard_map.298 = f32[128,2048]{1,0:T(8,128)} custom-call(f32[4,128,2048]{2,1,0:T(8,128)} %fusion.39.p_ref), custom_call_target="tpu_custom_call" | custom-call | tf_op jit(solution)/shard_map/pallas_call | solution.py:270
  199.6 43.5 %shard_map.299 = bf16[4,128,2048]{2,1,0:T(8,128)(2,1)} custom-call(bf16[128,2048]{1,0:T(8,128)(2,1)} %multiply_convert_fusion.7.x_ref), custom_call_target="tpu_custom_call" | custom-call | tf_op jit(solution)/shard_map/pallas_call | solution.py:133
  243.2 12.9 fusion.416
  271.9 9.4 fusion.111
  299.0 6.4 all-gather.1
  313.8 12.5 all-gather.15.cloned.1.call-done
  340.2 12.1 psum.127
  355.9 6.9 fusion.37.p_ref
  362.7 35.5 %shard_map.300 = f32[128,2048]{1,0:T(8,128)} custom-call(f32[4,128,2048]{2,1,0:T(8,128)} %fusion.37.p_ref), custom_call_target="tpu_custom_call" | custom-call | tf_op jit(solution)/shard_map/pallas_call | solution.py:270
  409.8 12.5 fusion.415
  449.1 7.9 all-gather.5
  462.7 7.0 all-gather.4
  470.8 7.8 all-gather.3
  478.6 7.2 all-gather.2
  495.7 11.5 all-gather.17.cloned.1.call-done
  522.3 11.9 psum.128
  534.1 7.9 multiply_reduce_fusion.20
  542.0 8.3 psum.129
  550.4 6.9 multiply_reduce_fusion.23
  565.4 12.2 fusion.29
  583.4 5.7 fusion.454
  589.2 24.5 %all-gather.19.cloned.1.call-done = bf16[4,16,64,128]{3,2,1,0:T(8,128)(2,1)} async-done(((bf16[1,16,64,128]{3,2,1,0:T(8,128)(2,1)}), bf16[4,16,64,128]{3,2,1,0:T(8,128)(2,1)}) %all-gather.19.cloned.1.call-update) | async-done | bytes 1048592 | tf_op jit(solution)/shard_map/all_gather | solution.py:320
  620.2 6.3 fusion.127
  630.9 6.5 multiply_reduce_fusion.13
  692.9 11.0 fusion.251
  707.1 11.0 collective-permute-done.9
  719.7 34.4 %shard_map.305 = bf16[4,128,2048]{2,1,0:T(8,128)(2,1)} custom-call(bf16[128,2048]{1,0:T(8,128)(2,1)} %fusion.242.x_ref), custom_call_target="tpu_custom_call" | custom-call | tf_op jit(solution)/shard_map/pallas_call | solution.py:133
  754.2 8.0 multiply_reduce_fusion.19
  762.2 11.0 psum.130
  773.2 6.0 multiply_reduce_fusion.22
  787.6 11.9 fusion.31
  805.2 5.7 fusion.455
  810.9 8.1 all-gather.21.cloned.1.call-done
  825.7 6.1 fusion.123
  836.2 6.7 multiply_reduce_fusion.9
  889.4 41.1 %shard_map.306 = f32[128,2048]{1,0:T(8,128)} custom-call(f32[4,128,2048]{2,1,0:T(8,128)} %bitcast.971), custom_call_target="tpu_custom_call" | custom-call | tf_op jit(solution)/shard_map/pallas_call | solution.py:270
  935.6 10.9 fusion.249
  951.5 28.8 %shard_map.307 = bf16[4,128,2048]{2,1,0:T(8,128)(2,1)} custom-call(bf16[128,2048]{1,0:T(8,128)(2,1)} %fusion.243.x_ref), custom_call_target="tpu_custom_call" | custom-call | tf_op jit(solution)/shard_map/pallas_call | solution.py:133
  980.4 8.0 multiply_reduce_fusion.18
  988.4 11.1 psum.131
  1008.8 11.6 fusion.33
  1029.0 10.6 add_convert_fusion
  1039.8 10.9 all-gather.23.cloned.1.call-done
  1075.5 5.7 multiply_reduce_fusion.5
  1089.7 6.6 pad_add_fusion
  1112.8 24.4 %shard_map.308 = f32[520,256]{1,0:T(8,128)} custom-call(f32[4,520,256]{2,1,0:T(8,128)} %bitcast.975), custom_call_target="tpu_custom_call" | custom-call | tf_op jit(solution)/shard_map/pallas_call | solution.py:270
  1144.0 6.0 copy-done.49
  1151.6 6.3 all-reduce.69.cloned.1.call-done
  1159.8 21.5 %fusion.34 = (bf16[1,2048,1024]{1,2,0:T(8,128)(2,1)}, bf16[1,2048,1024]{1,2,0:T(8,128)(2,1)}) fusion(f32[2048,2064]{0,1:T(8,128)} %copy-done.49, f32[2048,2064]{0,1:T(8,128)} %fusion.249, f32[2048,2064]{0,1:T(8,128)} %fusion.251, f32[]{:T(128)S(6)} %convert_element_type.597, f32[]{:T(128)S(6)} %convert_element_type.596, f32[]{:T(128)S(6)} %convert_element_type.595, ...), kind=kLoop, calls=%fused_computation.58 | loop fusion | flops 27262976 | bytes 58720272 | tf_op jit(solution)/shard_map/broadcast_in_dim | solution.py:814
  1184.5 7.1 fusion.35.p_ref
  1203.0 16.0 %all-reduce.64 = (bf16[1,4,1024]{2,1,0:T(4,128)(2,1)S(1)}, bf16[1,1024]{1,0:T(2,128)(2,1)S(1)}, bf16[1,16]{1,0:T(2,128)(2,1)S(1)}, bf16[1,16]{1,0:T(2,128)(2,1)S...) all-reduce(bf16[1,4,1024]{2,1,0:T(4,128)(2,1)S(1)} %fusion.338, ...), channel_id=1, replica_groups=mesh['section'=2,'seq'=4,'head'=4] {'seq'}, use_global_device_ids=true, to_apply=%region_96.98 | all-reduce | flops 6192 | bytes 24768 | tf_op jit(solution)/shard_map/psum | solution.py:667
  1224.2 8.1 fusion.248
  1236.9 30.4 %shard_map.309 = f32[128,2048]{1,0:T(8,128)} custom-call(f32[4,128,2048]{2,1,0:T(8,128)} %bitcast.969), custom_call_target="tpu_custom_call" | custom-call | tf_op jit(solution)/shard_map/pallas_call | solution.py:270
  1268.8 40.3 %psum.132 = f32[1,2048]{1,0:T(1,128)} all-reduce(f32[1,2048]{1,0:T(1,128)S(1)} %bitcast.1090), channel_id=1, replica_groups=mesh['section'=2,'seq'=4,'head'=4] {'seq','head'}, use_global_device_ids=true, to_apply=%region_90.92 | all-reduce | flops 2048 | bytes 16384 | tf_op jit(solution)/shard_map/psum | solution.py:671
  1317.0 44.8 %all-reduce.71.cloned.1.call-done = (bf16[1,2048,1024]{1,2,0:T(8,128)(2,1)}, bf16[1,2048,1024]{1,2,0:T(8,128)(2,1)}, bf16[520,256]{1,0:T(8,128)(2,1)}, bf16[1,2048,16]{1,2,0:T(8,128)(2,1)}) async-done(((bf16[1,2048,1024]{1,2,0:T(8,128)(2,1)}, bf16[1,2048,1024]{1,2,0:T(8,128)(2,1)}, bf16[520,256]{1,0:T(8,128)(2,1)}, bf16[1,2048,16]{1,2,0:T(8,128)(2,1)}), (bf16[1,2048,1024]{1,2,0:T(8,128)(2,1)}, ...) | async-done | bytes 8720400 | tf_op jit(solution)/shard_map/psum | solution.py:663
  1361.8 24.0 %shard_map.310 = bf16[4,520,256]{2,1,0:T(8,128)(2,1)} custom-call(bf16[520,256]{1,0:T(8,128)(2,1)} %get-tuple-element.171.x_ref), custom_call_target="tpu_custom_call" | custom-call | tf_op jit(solution)/shard_map/pallas_call | solution.py:133
  1389.8 6.9 copy.616
  1396.7 6.9 copy.617
  (1280 shorter events, 490.3 us)
Async XLA Ops:
  7.2 43.1 %copy-start.211 = (bf16[1,2048,16]{1,2,0:T(8,128)(2,1)S(1)}, bf16[1,2048,16]{1,2,0:T(8,128)(2,1)}, u32[]{:S(2)}) copy-start(bf16[1,2048,16]{1,2,0:T(8,128)(2,1)} %param.27) | copy-start | bytes 196612
  7.2 43.4 %copy-start.56 = (bf16[1,2048,256]{2,1,0:T(8,128)(2,1)S(1)}, bf16[1,2048,256]{2,1,0:T(8,128)(2,1)}, u32[]{:S(2)}) copy-start(bf16[1,2048,256]{2,1,0:T(8,128)(2,1)} %param.26) | copy-start | bytes 3145732
  7.2 122.0 %all-gather.13.cloned.1.call-start = ((), (), s32[]{:S(2)}) async-start(), calls=%async_computation | async-start | bytes 2621440 | tf_op jit(solution)/shard_map/all_gather | solution.py:302
  8.7 70.5 %collective-permute-start = (f32[3]{0:T(128)S(1)}, f32[3]{0:T(128)S(1)}, u32[]{:S(2)}, u32[]{:S(2)}) collective-permute-start(f32[3]{0:T(128)S(1)} %slice.590), channel_id=1, source_target_pairs={{0,4},{4,8},{8,12},{1,5},{5,9},{9,13},{2,6},{6,10},{10,14},{3,7},{... | collective-permute-start | bytes 44 | tf_op jit(solution)/shard_map/ppermute | solution.py:297
  13.7 65.6 %collective-permute-start.3 = (f32[3]{0:T(128)S(1)}, f32[3]{0:T(128)S(1)}, u32[]{:S(2)}, u32[]{:S(2)}) collective-permute-start(f32[3]{0:T(128)S(1)} %slice.629), channel_id=1, source_target_pairs={{0,4},{4,8},{8,12},{1,5},{5,9},{9,13},{2,6},{6,10},{10,14},{3,7},{... | collective-permute-start | bytes 44 | tf_op jit(solution)/shard_map/ppermute | solution.py:297
  18.9 31.4 %copy-start.339 = (f32[128]{0:T(128)}, f32[128]{0:T(128)S(1)}, u32[]{:S(2)}) copy-start(f32[128]{0:T(128)S(1)} %get-tuple-element.333) | copy-start | bytes 1540
  66.0 14.8 %collective-permute-start.1 = (f32[3,1280]{1,0:T(4,128)S(1)}, f32[3,1280]{1,0:T(4,128)S(1)}, u32[]{:S(2)}, u32[]{:S(2)}) collective-permute-start(f32[3,1280]{1,0:T(4,128)S(1)} %copy.495), channel_id=1, source_target_pairs={{0,4},{4,8},{8,12},{1,5},{5,9},{9,13},{2,6},{6,10},{10,14},{3,7},{... | collective-permute-start | bytes 46088 | tf_op jit(solution)/shard_map/ppermute | solution.py:297
  73.1 29.7 %copy-start.145 = (f32[512,16]{0,1:T(8,128)}, f32[512,16]{0,1:T(8,128)S(1)}, u32[]{:S(2)}) copy-start(f32[512,16]{0,1:T(8,128)S(1)} %get-tuple-element.227) | copy-start | bytes 98308
  79.2 53.7 %copy-start.178 = (f32[2,256,16]{1,2,0:T(8,128)}, f32[2,256,16]{1,2,0:T(8,128)S(1)}, u32[]{:S(2)}) copy-start(f32[2,256,16]{1,2,0:T(8,128)S(1)} %get-tuple-element.276) | copy-start | bytes 98308
  90.8 42.1 %copy-start.9 = (f32[2,256,16,64]{1,0,3,2:T(2,128)}, f32[2,256,16,64]{1,0,3,2:T(2,128)S(1)}, u32[]{:S(2)}) copy-start(f32[2,256,16,64]{1,0,3,2:T(2,128)S(1)} %reshape.960) | copy-start | bytes 6291460
  93.8 35.4 %copy-start.61 = (f32[2,16,64,128]{3,2,1,0:T(8,128)}, f32[2,16,64,128]{3,2,1,0:T(8,128)S(1)}, u32[]{:S(2)}) copy-start(f32[2,16,64,128]{3,2,1,0:T(8,128)S(1)} %fusion.159) | copy-start | bytes 3145732
  95.5 230.8 %all-gather.15.cloned.1.call-start = ((), (), s32[]{:S(2)}) async-start(), calls=%async_computation.1 | async-start | bytes 2621440 | tf_op jit(solution)/shard_map/all_gather | solution.py:302
  163.6 29.2 %copy-start.50 = (bf16[2,128,2048]{2,1,0:T(8,128)(2,1)S(1)}, bf16[2,128,2048]{2,1,0:T(8,128)(2,1)}, u32[]{:S(2)}) copy-start(bf16[2,128,2048]{2,1,0:T(8,128)(2,1)} %param.19) | copy-start | bytes 3145732
  194.1 3.7 collective-permute-start.2
  197.0 70.4 %copy-start.265 = (f32[2,256]{1,0:T(2,128)}, f32[2,256]{1,0:T(2,128)S(1)}, u32[]{:S(2)}) copy-start(f32[2,256]{1,0:T(2,128)S(1)} %get-tuple-element.343) | copy-start | bytes 6148
  197.0 70.4 %copy-start.307 = (f32[2,256]{1,0:T(2,128)}, f32[2,256]{1,0:T(2,128)S(1)}, u32[]{:S(2)}) copy-start(f32[2,256]{1,0:T(2,128)S(1)} %get-tuple-element.344) | copy-start | bytes 6148
  197.8 74.1 %copy-start.243 = (f32[512]{0:T(512)}, f32[512]{0:T(512)S(1)}, u32[]{:S(2)}) copy-start(f32[512]{0:T(512)S(1)} %get-tuple-element.287) | copy-start | bytes 6148
  197.8 74.1 %copy-start.245 = (f32[512]{0:T(512)}, f32[512]{0:T(512)S(1)}, u32[]{:S(2)}) copy-start(f32[512]{0:T(512)S(1)} %get-tuple-element.288) | copy-start | bytes 6148
  197.8 74.1 %copy-start.247 = (f32[512]{0:T(512)}, f32[512]{0:T(512)S(1)}, u32[]{:S(2)}) copy-start(f32[512]{0:T(512)S(1)} %get-tuple-element.289) | copy-start | bytes 6148
  198.0 200.2 %copy-start.25 = (f32[128,2048]{1,0:T(8,128)}, f32[128,2048]{1,0:T(8,128)S(1)}, u32[]{:S(2)}) copy-start(f32[128,2048]{1,0:T(8,128)S(1)} %get-tuple-element.219) | copy-start | bytes 3145732
  198.7 57.4 %copy-start.353 = (f32[128]{0:T(128)}, f32[128]{0:T(128)S(1)}, u32[]{:S(2)}) copy-start(f32[128]{0:T(128)S(1)} %get-tuple-element.335) | copy-start | bytes 1540
  243.2 23.6 %copy-start.351 = (f32[2]{0:T(128)S(1)}, f32[2]{0:T(128)}, u32[]{:S(2)}) copy-start(f32[2]{0:T(128)} %get-tuple-element.346) | copy-start | bytes 28
  260.6 11.0 collective-permute-start.4
  265.1 40.3 %copy-start.147 = (f32[512,16]{0,1:T(8,128)}, f32[512,16]{0,1:T(8,128)S(1)}, u32[]{:S(2)}) copy-start(f32[512,16]{0,1:T(8,128)S(1)} %get-tuple-element.215) | copy-start | bytes 98308
  267.5 62.6 %copy-start.182 = (f32[2,256,16]{1,2,0:T(8,128)}, f32[2,256,16]{1,2,0:T(8,128)S(1)}, u32[]{:S(2)}) copy-start(f32[2,256,16]{1,2,0:T(8,128)S(1)} %get-tuple-element.274) | copy-start | bytes 98308
  286.5 43.6 %copy-start.11 = (f32[2,256,16,64]{1,0,3,2:T(2,128)}, f32[2,256,16,64]{1,0,3,2:T(2,128)S(1)}, u32[]{:S(2)}) copy-start(f32[2,256,16,64]{1,0,3,2:T(2,128)S(1)} %reshape.972) | copy-start | bytes 6291460
  291.4 215.8 %all-gather.17.cloned.1.call-start = ((), (), s32[]{:S(2)}) async-start(), calls=%async_computation.2 | async-start | bytes 2621440 | tf_op jit(solution)/shard_map/all_gather | solution.py:302
  292.7 109.7 %collective-permute-start.6 = (f32[3]{0:T(128)}, f32[3]{0:T(128)}, u32[]{:S(2)}, u32[]{:S(2)}) collective-permute-start(f32[3]{0:T(128)} %slice.664), channel_id=1, source_target_pairs={{0,4},{4,8},{8,12},{1,5},{5,9},{9,13},{2,6},{6,10},{10,14},{3,7},{... | collective-permute-start | bytes 44 | tf_op jit(solution)/shard_map/ppermute | solution.py:297
  305.4 24.7 %copy-start.287 = (f32[2,2,8,256]{3,2,0,1:T(8,128)}, f32[2,2,8,256]{3,2,0,1:T(8,128)S(1)}, u32[]{:S(2)}) copy-start(f32[2,2,8,256]{3,2,0,1:T(8,128)S(1)} %copy.946) | copy-start | bytes 98308
  362.7 35.5 %copy-start.112 = (f32[1,128,2048]{2,1,0:T(8,128)S(1)}, f32[1,128,2048]{2,1,0:T(8,128)}, u32[]{:S(2)}) copy-start(f32[1,128,2048]{2,1,0:T(8,128)} %constant_dynamic-slice_fusion.3) | copy-start | bytes 3145732
  401.1 3.8 collective-permute-start.5
  402.5 28.5 %copy-start.390 = (f32[2]{0:T(128)}, f32[2]{0:T(128)S(1)}, u32[]{:S(2)}) copy-start(f32[2]{0:T(128)S(1)} %fusion.369) | copy-start | bytes 28
  403.9 31.2 %copy-start.249 = (f32[512]{0:T(512)}, f32[512]{0:T(512)S(1)}, u32[]{:S(2)}) copy-start(f32[512]{0:T(512)S(1)} %get-tuple-element.281) | copy-start | bytes 6148
  403.9 31.3 %copy-start.251 = (f32[512]{0:T(512)}, f32[512]{0:T(512)S(1)}, u32[]{:S(2)}) copy-start(f32[512]{0:T(512)S(1)} %get-tuple-element.282) | copy-start | bytes 6148
  403.9 31.3 %copy-start.253 = (f32[512]{0:T(512)}, f32[512]{0:T(512)S(1)}, u32[]{:S(2)}) copy-start(f32[512]{0:T(512)S(1)} %get-tuple-element.283) | copy-start | bytes 6148
  425.1 9.8 collective-permute-start.7
  444.9 170.3 %copy-start.14 = (f32[2,256,16,64]{1,0,3,2:T(2,128)}, f32[2,256,16,64]{1,0,3,2:T(2,128)S(1)}, u32[]{:S(2)}) copy-start(f32[2,256,16,64]{1,0,3,2:T(2,128)S(1)} %reshape.984) | copy-start | bytes 6291460
  447.9 59.3 %copy-start.64 = (f32[2,16,64,128]{3,2,1,0:T(8,128)}, f32[2,16,64,128]{3,2,1,0:T(8,128)S(1)}, u32[]{:S(2)}) copy-start(f32[2,16,64,128]{3,2,1,0:T(8,128)S(1)} %fusion.151) | copy-start | bytes 3145732
  449.0 164.6 %all-gather.19.cloned.1.call-start = ((), (), s32[]{:S(2)}) async-start(), calls=%async_computation.3 | async-start | bytes 1310720 | tf_op jit(solution)/shard_map/all_gather | solution.py:320
  565.3 253.7 %all-gather.21.cloned.1.call-start = ((), (), s32[]{:S(2)}) async-start(), calls=%async_computation.4 | async-start | bytes 1310720 | tf_op jit(solution)/shard_map/all_gather | solution.py:320
  637.3 29.7 %copy-start.219 = (f32[1280]{0:T(1024)}, f32[1280]{0:T(1024)S(1)}, u32[]{:S(2)}) copy-start(f32[1280]{0:T(1024)S(1)} %get-tuple-element.135) | copy-start | bytes 15364
  648.8 18.9 %collective-permute-start.8 = (f32[3,1280]{1,0:T(4,128)}, f32[3,1280]{1,0:T(4,128)}, u32[]{:S(2)}, u32[]{:S(2)}) collective-permute-start(f32[3,1280]{1,0:T(4,128)} %copy.559), channel_id=1, source_target_pairs={{4,0},{8,4},{12,8},{5,1},{9,5},{13,9},{6,2},{10,6},{14,10},{7,3},{... | collective-permute-start | bytes 46088 | tf_op jit(solution)/shard_map/ppermute | solution.py:297
  691.5 26.5 %collective-permute-start.9 = (bf16[128,2048]{1,0:T(8,128)(2,1)S(1)}, bf16[128,2048]{1,0:T(8,128)(2,1)S(1)}, u32[]{:S(2)}, u32[]{:S(2)}) collective-permute-start(bf16[128,2048]{1,0:T(8,128)(2,1)S(1)} %get-tuple-element.194), channel_id=1, source_target_pairs={{16,0},{17,1},{18,2},{19,3},{20,4},{21,5},{22,6},{23,7},{24,8},{25... | collective-permute-start | bytes 1572872 | tf_op jit(solution)/shard_map/ppermute | solution.py:297
  707.1 47.0 %copy-start.322 = (f32[512]{0:T(512)S(1)}, f32[512]{0:T(512)}, u32[]{:S(2)}) copy-start(f32[512]{0:T(512)} %copy-done.321) | copy-start | bytes 6148
  787.5 263.2 %all-gather.23.cloned.1.call-start = ((), (), s32[]{:S(2)}) async-start(), calls=%async_computation.5 | async-start | bytes 1310720 | tf_op jit(solution)/shard_map/all_gather | solution.py:320
  842.9 29.6 %copy-start.221 = (f32[1280]{0:T(1024)}, f32[1280]{0:T(1024)S(1)}, u32[]{:S(2)}) copy-start(f32[1280]{0:T(1024)S(1)} %get-tuple-element.136) | copy-start | bytes 15364
  854.2 18.9 %collective-permute-start.10 = (f32[3,1280]{1,0:T(4,128)}, f32[3,1280]{1,0:T(4,128)}, u32[]{:S(2)}, u32[]{:S(2)}) collective-permute-start(f32[3,1280]{1,0:T(4,128)} %copy.582), channel_id=1, source_target_pairs={{4,0},{8,4},{12,8},{5,1},{9,5},{13,9},{6,2},{10,6},{14,10},{7,3},{... | collective-permute-start | bytes 46088 | tf_op jit(solution)/shard_map/ppermute | solution.py:297
  889.3 41.1 %copy-start.26 = (f32[128,2048]{1,0:T(8,128)S(1)}, f32[128,2048]{1,0:T(8,128)}, u32[]{:S(2)}) copy-start(f32[128,2048]{1,0:T(8,128)} %copy-done.25) | copy-start | bytes 3145732
  889.3 41.1 %copy-start.354 = (f32[128]{0:T(128)S(1)}, f32[128]{0:T(128)}, u32[]{:S(2)}) copy-start(f32[128]{0:T(128)} %copy-done.353) | copy-start | bytes 1540
  889.3 43.3 %copy-start.66 = (bf16[2,128,2048]{2,1,0:T(8,128)(2,1)S(1)}, bf16[2,128,2048]{2,1,0:T(8,128)(2,1)}, u32[]{:S(2)}) copy-start(bf16[2,128,2048]{2,1,0:T(8,128)(2,1)} %param.20) | copy-start | bytes 3145732
  889.3 43.3 %copy-start.138 = (bf16[128,2048]{1,0:T(8,128)(2,1)S(1)}, bf16[128,2048]{1,0:T(8,128)(2,1)}, u32[]{:S(2)}) copy-start(bf16[128,2048]{1,0:T(8,128)(2,1)} %copy-done.137) | copy-start | bytes 1572868
  889.3 43.3 %copy-start.399 = (f32[128]{0:T(128)S(1)}, f32[128]{0:T(128)}, u32[]{:S(2)}) copy-start(f32[128]{0:T(128)} %get-tuple-element.334) | copy-start | bytes 1540
  934.2 15.6 %collective-permute-start.11 = (bf16[128,2048]{1,0:T(8,128)(2,1)S(1)}, bf16[128,2048]{1,0:T(8,128)(2,1)S(1)}, u32[]{:S(2)}, u32[]{:S(2)}) collective-permute-start(bf16[128,2048]{1,0:T(8,128)(2,1)S(1)} %get-tuple-element.190), channel_id=1, source_target_pairs={{16,0},{17,1},{18,2},{19,3},{20,4},{21,5},{22,6},{23,7},{24,8},{25... | collective-permute-start | bytes 1572872 | tf_op jit(solution)/shard_map/ppermute | solution.py:297
  949.8 30.5 %copy-start.320 = (f32[512]{0:T(512)S(1)}, f32[512]{0:T(512)}, u32[]{:S(2)}) copy-start(f32[512]{0:T(512)} %copy-done.319) | copy-start | bytes 6148
  1024.7 133.2 %all-reduce.69.cloned.1.call-start = ((), (), s32[]{:S(2)}) async-start(), calls=%async_computation.6 | async-start | bytes 8388608 | tf_op jit(solution)/shard_map/psum | solution.py:787
  1039.6 322.2 %all-reduce.71.cloned.1.call-start = ((), (), s32[]{:S(2)}) async-start(), calls=%async_computation.7 | async-start | bytes 17440768 | tf_op jit(solution)/shard_map/psum | solution.py:663
  1086.2 12.5 collective-permute-start.12
  1112.8 26.3 %copy-start.33 = (f32[509,1280]{0,1:T(8,128)S(1)}, f32[509,1280]{0,1:T(8,128)}, u32[]{:S(2)}) copy-start(f32[509,1280]{0,1:T(8,128)} %slice.886) | copy-start | bytes 7818244
  1201.2 22.9 %copy-start.154 = (bf16[512,1024]{0,1:T(8,128)(2,1)S(1)}, bf16[512,1024]{0,1:T(8,128)(2,1)}, u32[]{:S(2)}) copy-start(bf16[512,1024]{0,1:T(8,128)(2,1)} %get-tuple-element.232) | copy-start | bytes 3145732
  1236.8 30.4 %copy-start.52 = (bf16[2,128,2048]{2,1,0:T(8,128)(2,1)S(1)}, bf16[2,128,2048]{2,1,0:T(8,128)(2,1)}, u32[]{:S(2)}) copy-start(bf16[2,128,2048]{2,1,0:T(8,128)(2,1)} %param.19) | copy-start | bytes 3145732
  1236.8 30.4 %copy-start.340 = (f32[128]{0:T(128)S(1)}, f32[128]{0:T(128)}, u32[]{:S(2)}) copy-start(f32[128]{0:T(128)} %copy-done.339) | copy-start | bytes 1540
  1236.8 32.0 %copy-start.271 = (f32[2048]{0:T(1024)S(1)}, f32[2048]{0:T(1024)}, u32[]{:S(2)}) copy-start(f32[2048]{0:T(1024)} %get-tuple-element.141) | copy-start | bytes 24580
  1236.8 32.0 %copy-start.272 = (f32[2048]{0:T(1024)S(1)}, f32[2048]{0:T(1024)}, u32[]{:S(2)}) copy-start(f32[2048]{0:T(1024)} %get-tuple-element.143) | copy-start | bytes 24580
  1236.8 72.3 %copy-start.398 = (f32[128]{0:T(128)S(1)}, f32[128]{0:T(128)}, u32[]{:S(2)}) copy-start(f32[128]{0:T(128)} %get-tuple-element.332) | copy-start | bytes 1540
  (371 other events, 2096.1 us)
Sparse Core Ops, SparseCore 0:
  95.6 33.5 all-gather.12
  291.5 34.7 all-gather.14
  449.1 57.9 all-gather.16
  565.4 48.1 all-gather.18
  787.6 31.3 all-gather.20
  1024.8 25.8 all-gather.22
  1054.0 103.8 all-reduce.68
  1181.4 180.3 all-reduce.70

commit v13 on v11

--- a/solution.py
+++ b/solution.py
@@ -614,14 +614,20 @@
 
 
 def reduce_grads(head_part, norm_part, bc_part, tick_count):
+    bc_all = lax.all_gather(bc_part.astype(jnp.bfloat16), "seq")
+    bc_sum = bc_all[0].astype(jnp.float32)
+    for index in range(1, bc_all.shape[0]):
+        bc_sum = bc_sum + bc_all[index].astype(jnp.float32)
+    anchor = bc_all[0, 0, 0].astype(jnp.float32) * 0.0
     summed = lax.psum(
-        tuple(member.astype(jnp.bfloat16) for member in head_part[:3] + (bc_part,)), "seq"
-    )
-    head_sum = tuple(member.astype(jnp.float32) for member in summed[:3]) + tuple(
+        tuple(member.astype(jnp.bfloat16) for member in (head_part[0] + anchor,) + head_part[1:3]),
+        "seq",
+    )
+    head_sum = tuple(member.astype(jnp.float32) for member in summed) + tuple(
         lax.psum(member.astype(jnp.bfloat16), "seq").astype(jnp.float32)
         for member in head_part[3:]
     )
-    bc_rows = head_gather(summed[3], (0, 0, 1), 4 * tick_count + 1).astype(jnp.float32)
+    bc_rows = head_gather(bc_sum, (0, 0, 1), 4 * tick_count + 1)
     norm_sum = lax.psum(norm_part, ("seq", "head"))
     return (head_sum, norm_sum, bc_rows.reshape(-1, bc_rows.shape[-1]))
 

time: 1420 us -> 1480 us (1.042)
  waiting for transfers between devices: 144 us -> 186 us
    psum x1, waiting for transfers between devices: 6.35 us -> 82.8 us  [on_device(): out_total = lax.psum(out_total.astype(jnp.bfloat16), 'seq')]
    psum x1, waiting for transfers between devices: 44.9 us -> 4.22 us  [reduce_grads(): lax.psum(tuple((member.astype(jnp.bfloat16) for member in (head_part[0] +...]
    unnamed x844 -> x850, local copies, waits for them, and re-layouts: 67 us -> 71.4 us
  transfers between devices with their start and end apart: 21 -> 22, of which waited for: 10 -> 10; matrix products, arithmetic and copies ran while one was open for 24% -> 22% of each run, Pallas kernels for 9% -> 9%
where the time goes in v13:
time: 1480 us; the launch traced here: 1470 us
  Pallas kernels  336 us (23%)
  matrix products  289 us (20%)
  other arithmetic  249 us (17%)
  local copies, waits for them, and re-layouts  188 us (13%)
  waiting for transfers between devices  186 us (13%)
  blocking collectives  166 us (11%)
  starting transfers between devices  34 us (2%)
  between operations  21.4 us (1%)
    pallas_call x7, Pallas kernels, head_gather(): pl.pallas_call(functools.partial(gather_body, n, tick), out_shape=jax.Sha...  170 us
    pallas_call x7, Pallas kernels, head_scatter(): pl.pallas_call(functools.partial(scatter_body, n, tick), out_shape=jax.Sh...  166 us
    psum x1, waiting for transfers between devices, on_device(): out_total = lax.psum(out_total.astype(jnp.bfloat16), 'seq')  82.8 us
    unnamed x850, local copies, waits for them, and re-layouts  71.4 us
    dot_general x9, matrix products, block_output(): jnp.einsum('cijh,cjhp->cihp', weights, x_blocks, precision=highest)  69.6 us
    all_gather x3, waiting for transfers between devices, entering_2(): lax.all_gather(a.astype(kind), axis)  49.4 us
    psum x1, blocking collectives, reduce_grads(): norm_sum = lax.psum(norm_part, ('seq', 'head'))  40.4 us
    dot_general x3, matrix products, mixer_forward(): projected = jnp.dot(gathered, w_main, preferred_element_type=jnp.float32)  38.1 us
  transfers between devices with their start and end apart: 22, of which 10 were waited for; matrix products, arithmetic and copies ran while one was open for 22% of the time, Pallas kernels for 9%

profile of v13, /device:TPU:0, one launch (start us, length us, event | category | flops | bytes accessed | tf_op | source)
XLA Modules:
  0.0 1468.7 jit_solution(12277429100743378492)
XLA Ops:
  20.9 29.3 %shard_map.297 = bf16[4,128,2048]{2,1,0:T(8,128)(2,1)} custom-call(bf16[128,2048]{1,0:T(8,128)(2,1)} %fusion.225.x_ref), custom_call_target="tpu_custom_call" | custom-call | tf_op jit(solution)/shard_map/pallas_call | solution.py:113
  50.5 12.7 fusion.418
  95.6 6.9 all-gather.1
  115.7 13.5 all-gather.15.cloned.1.call-done
  143.0 11.9 psum.119
  156.5 6.9 fusion.40.p_ref
  163.4 27.6 %shard_map.298 = f32[128,2048]{1,0:T(8,128)} custom-call(f32[4,128,2048]{2,1,0:T(8,128)} %fusion.40.p_ref), custom_call_target="tpu_custom_call" | custom-call | tf_op jit(solution)/shard_map/pallas_call | solution.py:224
  199.4 43.4 %shard_map.299 = bf16[4,128,2048]{2,1,0:T(8,128)(2,1)} custom-call(bf16[128,2048]{1,0:T(8,128)(2,1)} %multiply_convert_fusion.7.x_ref), custom_call_target="tpu_custom_call" | custom-call | tf_op jit(solution)/shard_map/pallas_call | solution.py:113
  242.8 12.9 fusion.417
  271.9 9.3 fusion.112
  298.8 6.3 all-gather.2
  313.5 12.6 all-gather.17.cloned.1.call-done
  340.0 11.9 psum.120
  355.4 6.9 fusion.38.p_ref
  362.2 35.4 %shard_map.300 = f32[128,2048]{1,0:T(8,128)} custom-call(f32[4,128,2048]{2,1,0:T(8,128)} %fusion.38.p_ref), custom_call_target="tpu_custom_call" | custom-call | tf_op jit(solution)/shard_map/pallas_call | solution.py:224
  409.2 12.5 fusion.416
  448.6 7.9 all-gather.6
  462.1 7.0 all-gather.5
  470.3 7.8 all-gather.4
  478.0 7.3 all-gather.3
  495.2 11.4 all-gather.19.cloned.1.call-done
  521.7 12.1 psum.121
  533.8 7.9 multiply_reduce_fusion.20
  541.7 8.3 psum.122
  550.0 6.8 multiply_reduce_fusion.23
  565.0 12.0 fusion.30
  582.8 5.7 fusion.455
  588.5 24.7 %all-gather.21.cloned.1.call-done = bf16[4,16,64,128]{3,2,1,0:T(8,128)(2,1)} async-done(((bf16[1,16,64,128]{3,2,1,0:T(8,128)(2,1)}), bf16[4,16,64,128]{3,2,1,0:T(8,128)(2,1)}) %all-gather.21.cloned.1.call-update) | async-done | bytes 1048592 | tf_op jit(solution)/shard_map/all_gather | solution.py:274
  619.9 6.3 fusion.128
  630.5 6.5 multiply_reduce_fusion.13
  653.1 5.4 reduce-window.115
  692.6 11.0 fusion.252
  706.7 11.1 collective-permute-done.9
  719.5 34.3 %shard_map.305 = bf16[4,128,2048]{2,1,0:T(8,128)(2,1)} custom-call(bf16[128,2048]{1,0:T(8,128)(2,1)} %fusion.243.x_ref), custom_call_target="tpu_custom_call" | custom-call | tf_op jit(solution)/shard_map/pallas_call | solution.py:113
  753.8 8.0 multiply_reduce_fusion.19
  761.9 11.1 psum.123
  773.0 6.0 multiply_reduce_fusion.22
  790.3 11.6 fusion.32
  806.7 15.0 %all-gather.23.cloned.1.call-done = bf16[4,16,64,128]{3,2,1,0:T(8,128)(2,1)} async-done(((bf16[1,16,64,128]{3,2,1,0:T(8,128)(2,1)}), bf16[4,16,64,128]{3,2,1,0:T(8,128)(2,1)}) %all-gather.23.cloned.1.call-update) | async-done | bytes 1048592 | tf_op jit(solution)/shard_map/all_gather | solution.py:274
  828.4 6.7 fusion.124
  839.4 6.3 multiply_reduce_fusion.9
  889.2 41.4 %shard_map.306 = f32[128,2048]{1,0:T(8,128)} custom-call(f32[4,128,2048]{2,1,0:T(8,128)} %bitcast.973), custom_call_target="tpu_custom_call" | custom-call | tf_op jit(solution)/shard_map/pallas_call | solution.py:224
  935.9 5.7 fusion.456
  949.5 28.7 %shard_map.307 = bf16[4,128,2048]{2,1,0:T(8,128)(2,1)} custom-call(bf16[128,2048]{1,0:T(8,128)(2,1)} %fusion.244.x_ref), custom_call_target="tpu_custom_call" | custom-call | tf_op jit(solution)/shard_map/pallas_call | solution.py:113
  978.3 8.0 multiply_reduce_fusion.18
  986.3 10.8 psum.124
  997.1 6.0 multiply_reduce_fusion.21
  1013.8 10.3 fusion.34
  1026.3 9.7 all-gather.25.cloned.1.call-done
  1042.6 7.3 fusion.120
  1087.7 24.0 %shard_map.308 = f32[520,256]{1,0:T(8,128)} custom-call(f32[4,520,256]{2,1,0:T(8,128)} %bitcast.977), custom_call_target="tpu_custom_call" | custom-call | tf_op jit(solution)/shard_map/pallas_call | solution.py:224
  1113.6 10.5 fusion.250
  1124.1 10.3 add_convert_fusion
  1155.9 6.3 copy-done.50
  1165.7 82.8 %all-reduce.69.cloned.1.call-done = bf16[1024,2048]{1,0:T(8,128)(2,1)} async-done(((bf16[1024,2048]{1,0:T(8,128)(2,1)}), bf16[1024,2048]{1,0:T(8,128)(2,1)}) %all-reduce.69.cloned.1.call-update) | async-done | bytes 4194320 | tf_op jit(solution)/shard_map/psum | solution.py:747
  1250.3 21.5 %fusion.35 = (bf16[1,2048,1024]{1,2,0:T(8,128)(2,1)}, bf16[1,2048,1024]{1,2,0:T(8,128)(2,1)}) fusion(f32[2048,2064]{0,1:T(8,128)} %copy-done.50, f32[2048,2064]{0,1:T(8,128)} %fusion.250, f32[2048,2064]{0,1:T(8,128)} %fusion.252, f32[]{:T(128)S(6)} %convert_element_type.616, f32[]{:T(128)S(6)} %convert_element_type.615, f32[]{:T(128)S(6)} %convert_element_type.614, ...), kind=kLoop, calls=%fused_computation.59 | loop fusion | flops 29360128 | bytes 58720276 | tf_op jit(solution)/shard_map/broadcast_in_dim | solution.py:774
  1275.1 7.1 fusion.36.p_ref
  1293.5 16.0 %all-reduce.64 = (bf16[1,4,1024]{2,1,0:T(4,128)(2,1)S(1)}, bf16[1,1024]{1,0:T(2,128)(2,1)S(1)}, bf16[1,16]{1,0:T(2,128)(2,1)S(1)}, bf16[1,16]{1,0:T(2,128)(2,1)S...) all-reduce(bf16[1,4,1024]{2,1,0:T(4,128)(2,1)S(1)} %fusion.339, ...), channel_id=1, replica_groups=mesh['section'=2,'seq'=4,'head'=4] {'seq'}, use_global_device_ids=true, to_apply=%region_95.97 | all-reduce | flops 6192 | bytes 24768 | tf_op jit(solution)/shard_map/psum | solution.py:627
  1314.7 8.2 fusion.249
  1327.5 30.3 %shard_map.309 = f32[128,2048]{1,0:T(8,128)} custom-call(f32[4,128,2048]{2,1,0:T(8,128)} %bitcast.971), custom_call_target="tpu_custom_call" | custom-call | tf_op jit(solution)/shard_map/pallas_call | solution.py:224
  1359.4 40.4 %psum.125 = f32[1,2048]{1,0:T(1,128)} all-reduce(f32[1,2048]{1,0:T(1,128)S(1)} %bitcast.1096), channel_id=1, replica_groups=mesh['section'=2,'seq'=4,'head'=4] {'seq','head'}, use_global_device_ids=true, to_apply=%region_90.92 | all-reduce | flops 2048 | bytes 16384 | tf_op jit(solution)/shard_map/psum | solution.py:631
  1404.1 29.1 %shard_map.310 = f32[4,520,256]{2,1,0:T(8,128)} custom-call(f32[520,256]{1,0:T(8,128)} %add_add_fusion.4.x_ref), custom_call_target="tpu_custom_call" | custom-call | tf_op jit(solution)/shard_map/pallas_call | solution.py:113
  1447.6 6.9 copy.616
  1454.4 6.9 copy.617
  (1291 shorter events, 501.4 us)
Async XLA Ops:
  7.2 43.0 %copy-start.207 = (bf16[1,2048,16]{1,2,0:T(8,128)(2,1)S(1)}, bf16[1,2048,16]{1,2,0:T(8,128)(2,1)}, u32[]{:S(2)}) copy-start(bf16[1,2048,16]{1,2,0:T(8,128)(2,1)} %param.27) | copy-start | bytes 196612
  7.2 43.3 %copy-start.57 = (bf16[1,2048,256]{2,1,0:T(8,128)(2,1)S(1)}, bf16[1,2048,256]{2,1,0:T(8,128)(2,1)}, u32[]{:S(2)}) copy-start(bf16[1,2048,256]{2,1,0:T(8,128)(2,1)} %param.26) | copy-start | bytes 3145732
  7.2 122.0 %all-gather.15.cloned.1.call-start = ((), (), s32[]{:S(2)}) async-start(), calls=%async_computation | async-start | bytes 2621440 | tf_op jit(solution)/shard_map/all_gather | solution.py:256
  8.7 70.5 %collective-permute-start = (f32[3]{0:T(128)S(1)}, f32[3]{0:T(128)S(1)}, u32[]{:S(2)}, u32[]{:S(2)}) collective-permute-start(f32[3]{0:T(128)S(1)} %slice.605), channel_id=1, source_target_pairs={{0,4},{4,8},{8,12},{1,5},{5,9},{9,13},{2,6},{6,10},{10,14},{3,7},{... | collective-permute-start | bytes 44 | tf_op jit(solution)/shard_map/ppermute | solution.py:251
  13.7 65.6 %collective-permute-start.3 = (f32[3]{0:T(128)S(1)}, f32[3]{0:T(128)S(1)}, u32[]{:S(2)}, u32[]{:S(2)}) collective-permute-start(f32[3]{0:T(128)S(1)} %slice.644), channel_id=1, source_target_pairs={{0,4},{4,8},{8,12},{1,5},{5,9},{9,13},{2,6},{6,10},{10,14},{3,7},{... | collective-permute-start | bytes 44 | tf_op jit(solution)/shard_map/ppermute | solution.py:251
  18.9 31.3 %copy-start.338 = (f32[128]{0:T(128)}, f32[128]{0:T(128)S(1)}, u32[]{:S(2)}) copy-start(f32[128]{0:T(128)S(1)} %get-tuple-element.332) | copy-start | bytes 1540
  65.9 14.8 %collective-permute-start.1 = (f32[3,1280]{1,0:T(4,128)S(1)}, f32[3,1280]{1,0:T(4,128)S(1)}, u32[]{:S(2)}, u32[]{:S(2)}) collective-permute-start(f32[3,1280]{1,0:T(4,128)S(1)} %copy.495), channel_id=1, source_target_pairs={{0,4},{4,8},{8,12},{1,5},{5,9},{9,13},{2,6},{6,10},{10,14},{3,7},{... | collective-permute-start | bytes 46088 | tf_op jit(solution)/shard_map/ppermute | solution.py:251
  73.1 29.4 %copy-start.145 = (f32[512,16]{0,1:T(8,128)}, f32[512,16]{0,1:T(8,128)S(1)}, u32[]{:S(2)}) copy-start(f32[512,16]{0,1:T(8,128)S(1)} %get-tuple-element.226) | copy-start | bytes 98308
  79.2 53.7 %copy-start.176 = (f32[2,256,16]{1,2,0:T(8,128)}, f32[2,256,16]{1,2,0:T(8,128)S(1)}, u32[]{:S(2)}) copy-start(f32[2,256,16]{1,2,0:T(8,128)S(1)} %get-tuple-element.275) | copy-start | bytes 98308
  90.9 42.0 %copy-start.9 = (f32[2,256,16,64]{1,0,3,2:T(2,128)}, f32[2,256,16,64]{1,0,3,2:T(2,128)S(1)}, u32[]{:S(2)}) copy-start(f32[2,256,16,64]{1,0,3,2:T(2,128)S(1)} %reshape.967) | copy-start | bytes 6291460
  93.9 35.4 %copy-start.62 = (f32[2,16,64,128]{3,2,1,0:T(8,128)}, f32[2,16,64,128]{3,2,1,0:T(8,128)S(1)}, u32[]{:S(2)}) copy-start(f32[2,16,64,128]{3,2,1,0:T(8,128)S(1)} %fusion.160) | copy-start | bytes 3145732
  95.5 230.5 %all-gather.17.cloned.1.call-start = ((), (), s32[]{:S(2)}) async-start(), calls=%async_computation.1 | async-start | bytes 2621440 | tf_op jit(solution)/shard_map/all_gather | solution.py:256
  163.4 29.2 %copy-start.51 = (bf16[2,128,2048]{2,1,0:T(8,128)(2,1)S(1)}, bf16[2,128,2048]{2,1,0:T(8,128)(2,1)}, u32[]{:S(2)}) copy-start(bf16[2,128,2048]{2,1,0:T(8,128)(2,1)} %param.19) | copy-start | bytes 3145732
  193.9 3.7 collective-permute-start.2
  196.8 70.5 %copy-start.267 = (f32[2,256]{1,0:T(2,128)}, f32[2,256]{1,0:T(2,128)S(1)}, u32[]{:S(2)}) copy-start(f32[2,256]{1,0:T(2,128)S(1)} %get-tuple-element.342) | copy-start | bytes 6148
  196.8 70.5 %copy-start.302 = (f32[2,256]{1,0:T(2,128)}, f32[2,256]{1,0:T(2,128)S(1)}, u32[]{:S(2)}) copy-start(f32[2,256]{1,0:T(2,128)S(1)} %get-tuple-element.343) | copy-start | bytes 6148
  197.5 74.3 %copy-start.245 = (f32[512]{0:T(512)}, f32[512]{0:T(512)S(1)}, u32[]{:S(2)}) copy-start(f32[512]{0:T(512)S(1)} %get-tuple-element.286) | copy-start | bytes 6148
  197.5 74.3 %copy-start.247 = (f32[512]{0:T(512)}, f32[512]{0:T(512)S(1)}, u32[]{:S(2)}) copy-start(f32[512]{0:T(512)S(1)} %get-tuple-element.287) | copy-start | bytes 6148
  197.5 74.3 %copy-start.249 = (f32[512]{0:T(512)}, f32[512]{0:T(512)S(1)}, u32[]{:S(2)}) copy-start(f32[512]{0:T(512)S(1)} %get-tuple-element.288) | copy-start | bytes 6148
  197.8 199.8 %copy-start.26 = (f32[128,2048]{1,0:T(8,128)}, f32[128,2048]{1,0:T(8,128)S(1)}, u32[]{:S(2)}) copy-start(f32[128,2048]{1,0:T(8,128)S(1)} %get-tuple-element.218) | copy-start | bytes 3145732
  198.4 57.2 %copy-start.354 = (f32[128]{0:T(128)}, f32[128]{0:T(128)S(1)}, u32[]{:S(2)}) copy-start(f32[128]{0:T(128)S(1)} %get-tuple-element.334) | copy-start | bytes 1540
  260.3 11.3 collective-permute-start.4
  265.0 40.1 %copy-start.147 = (f32[512,16]{0,1:T(8,128)}, f32[512,16]{0,1:T(8,128)S(1)}, u32[]{:S(2)}) copy-start(f32[512,16]{0,1:T(8,128)S(1)} %get-tuple-element.214) | copy-start | bytes 98308
  267.5 62.4 %copy-start.180 = (f32[2,256,16]{1,2,0:T(8,128)}, f32[2,256,16]{1,2,0:T(8,128)S(1)}, u32[]{:S(2)}) copy-start(f32[2,256,16]{1,2,0:T(8,128)S(1)} %get-tuple-element.273) | copy-start | bytes 98308
  286.3 43.6 %copy-start.12 = (f32[2,256,16,64]{1,0,3,2:T(2,128)}, f32[2,256,16,64]{1,0,3,2:T(2,128)S(1)}, u32[]{:S(2)}) copy-start(f32[2,256,16,64]{1,0,3,2:T(2,128)S(1)} %reshape.979) | copy-start | bytes 6291460
  291.2 215.5 %all-gather.19.cloned.1.call-start = ((), (), s32[]{:S(2)}) async-start(), calls=%async_computation.2 | async-start | bytes 2621440 | tf_op jit(solution)/shard_map/all_gather | solution.py:256
  292.5 109.4 %collective-permute-start.6 = (f32[3]{0:T(128)}, f32[3]{0:T(128)}, u32[]{:S(2)}, u32[]{:S(2)}) collective-permute-start(f32[3]{0:T(128)} %slice.679), channel_id=1, source_target_pairs={{0,4},{4,8},{8,12},{1,5},{5,9},{9,13},{2,6},{6,10},{10,14},{3,7},{... | collective-permute-start | bytes 44 | tf_op jit(solution)/shard_map/ppermute | solution.py:251
  362.2 35.4 %copy-start.115 = (f32[1,128,2048]{2,1,0:T(8,128)S(1)}, f32[1,128,2048]{2,1,0:T(8,128)}, u32[]{:S(2)}) copy-start(f32[1,128,2048]{2,1,0:T(8,128)} %constant_dynamic-slice_fusion.3) | copy-start | bytes 3145732
  400.5 3.8 collective-permute-start.5
  401.9 28.4 %copy-start.391 = (f32[2]{0:T(128)}, f32[2]{0:T(128)S(1)}, u32[]{:S(2)}) copy-start(f32[2]{0:T(128)S(1)} %fusion.370) | copy-start | bytes 28
  403.4 31.2 %copy-start.251 = (f32[512]{0:T(512)}, f32[512]{0:T(512)S(1)}, u32[]{:S(2)}) copy-start(f32[512]{0:T(512)S(1)} %get-tuple-element.280) | copy-start | bytes 6148
  403.4 31.2 %copy-start.253 = (f32[512]{0:T(512)}, f32[512]{0:T(512)S(1)}, u32[]{:S(2)}) copy-start(f32[512]{0:T(512)S(1)} %get-tuple-element.281) | copy-start | bytes 6148
  403.4 31.2 %copy-start.255 = (f32[512]{0:T(512)}, f32[512]{0:T(512)S(1)}, u32[]{:S(2)}) copy-start(f32[512]{0:T(512)S(1)} %get-tuple-element.282) | copy-start | bytes 6148
  424.4 9.9 collective-permute-start.7
  444.4 170.5 %copy-start.15 = (f32[2,256,16,64]{1,0,3,2:T(2,128)}, f32[2,256,16,64]{1,0,3,2:T(2,128)S(1)}, u32[]{:S(2)}) copy-start(f32[2,256,16,64]{1,0,3,2:T(2,128)S(1)} %reshape.991) | copy-start | bytes 6291460
  447.4 59.3 %copy-start.65 = (f32[2,16,64,128]{3,2,1,0:T(8,128)}, f32[2,16,64,128]{3,2,1,0:T(8,128)S(1)}, u32[]{:S(2)}) copy-start(f32[2,16,64,128]{3,2,1,0:T(8,128)S(1)} %fusion.152) | copy-start | bytes 3145732
  448.5 164.8 %all-gather.21.cloned.1.call-start = ((), (), s32[]{:S(2)}) async-start(), calls=%async_computation.3 | async-start | bytes 1310720 | tf_op jit(solution)/shard_map/all_gather | solution.py:274
  564.9 256.8 %all-gather.23.cloned.1.call-start = ((), (), s32[]{:S(2)}) async-start(), calls=%async_computation.4 | async-start | bytes 1310720 | tf_op jit(solution)/shard_map/all_gather | solution.py:274
  637.0 29.9 %copy-start.215 = (f32[1280]{0:T(1024)}, f32[1280]{0:T(1024)S(1)}, u32[]{:S(2)}) copy-start(f32[1280]{0:T(1024)S(1)} %get-tuple-element.135) | copy-start | bytes 15364
  648.4 19.1 %collective-permute-start.8 = (f32[3,1280]{1,0:T(4,128)}, f32[3,1280]{1,0:T(4,128)}, u32[]{:S(2)}, u32[]{:S(2)}) collective-permute-start(f32[3,1280]{1,0:T(4,128)} %copy.559), channel_id=1, source_target_pairs={{4,0},{8,4},{12,8},{5,1},{9,5},{13,9},{6,2},{10,6},{14,10},{7,3},{... | collective-permute-start | bytes 46088 | tf_op jit(solution)/shard_map/ppermute | solution.py:251
  691.1 26.6 %collective-permute-start.9 = (bf16[128,2048]{1,0:T(8,128)(2,1)S(1)}, bf16[128,2048]{1,0:T(8,128)(2,1)S(1)}, u32[]{:S(2)}, u32[]{:S(2)}) collective-permute-start(bf16[128,2048]{1,0:T(8,128)(2,1)S(1)} %get-tuple-element.193), channel_id=1, source_target_pairs={{16,0},{17,1},{18,2},{19,3},{20,4},{21,5},{22,6},{23,7},{24,8},{25... | collective-permute-start | bytes 1572872 | tf_op jit(solution)/shard_map/ppermute | solution.py:251
  706.7 47.1 %copy-start.317 = (f32[512]{0:T(512)S(1)}, f32[512]{0:T(512)}, u32[]{:S(2)}) copy-start(f32[512]{0:T(512)} %copy-done.316) | copy-start | bytes 6148
  790.2 245.8 %all-gather.25.cloned.1.call-start = ((), (), s32[]{:S(2)}) async-start(), calls=%async_computation.5 | async-start | bytes 1310720 | tf_op jit(solution)/shard_map/all_gather | solution.py:274
  845.7 98.4 %copy-start.217 = (f32[1280]{0:T(1024)}, f32[1280]{0:T(1024)S(1)}, u32[]{:S(2)}) copy-start(f32[1280]{0:T(1024)S(1)} %get-tuple-element.136) | copy-start | bytes 15364
  857.1 15.9 %collective-permute-start.10 = (f32[3,1280]{1,0:T(4,128)}, f32[3,1280]{1,0:T(4,128)}, u32[]{:S(2)}, u32[]{:S(2)}) collective-permute-start(f32[3,1280]{1,0:T(4,128)} %copy.582), channel_id=1, source_target_pairs={{4,0},{8,4},{12,8},{5,1},{9,5},{13,9},{6,2},{10,6},{14,10},{7,3},{... | collective-permute-start | bytes 46088 | tf_op jit(solution)/shard_map/ppermute | solution.py:251
  889.2 41.4 %copy-start.27 = (f32[128,2048]{1,0:T(8,128)S(1)}, f32[128,2048]{1,0:T(8,128)}, u32[]{:S(2)}) copy-start(f32[128,2048]{1,0:T(8,128)} %copy-done.26) | copy-start | bytes 3145732
  889.2 41.4 %copy-start.355 = (f32[128]{0:T(128)S(1)}, f32[128]{0:T(128)}, u32[]{:S(2)}) copy-start(f32[128]{0:T(128)} %copy-done.354) | copy-start | bytes 1540
  889.2 43.6 %copy-start.67 = (bf16[2,128,2048]{2,1,0:T(8,128)(2,1)S(1)}, bf16[2,128,2048]{2,1,0:T(8,128)(2,1)}, u32[]{:S(2)}) copy-start(bf16[2,128,2048]{2,1,0:T(8,128)(2,1)} %param.20) | copy-start | bytes 3145732
  889.2 43.6 %copy-start.140 = (bf16[128,2048]{1,0:T(8,128)(2,1)S(1)}, bf16[128,2048]{1,0:T(8,128)(2,1)}, u32[]{:S(2)}) copy-start(bf16[128,2048]{1,0:T(8,128)(2,1)} %copy-done.139) | copy-start | bytes 1572868
  889.2 43.6 %copy-start.400 = (f32[128]{0:T(128)S(1)}, f32[128]{0:T(128)}, u32[]{:S(2)}) copy-start(f32[128]{0:T(128)} %get-tuple-element.333) | copy-start | bytes 1540
  934.3 13.5 collective-permute-start.11
  947.8 30.4 %copy-start.315 = (f32[512]{0:T(512)S(1)}, f32[512]{0:T(512)}, u32[]{:S(2)}) copy-start(f32[512]{0:T(512)} %copy-done.314) | copy-start | bytes 6148
  1010.0 153.9 %all-gather.27.cloned.1.call-start = ((), (), s32[]{:S(2)}) async-start(), calls=%async_computation.7 | async-start | bytes 1331200 | tf_op jit(solution)/shard_map/all_gather | solution.py:617
  1067.7 6.3 collective-permute-start.12
  1087.7 25.9 %copy-start.76 = (bf16[4,128,2048]{2,1,0:T(8,128)(2,1)S(1)}, bf16[4,128,2048]{2,1,0:T(8,128)(2,1)}, u32[]{:S(2)}) copy-start(bf16[4,128,2048]{2,1,0:T(8,128)(2,1)} %shard_map.299) | copy-start | bytes 6291460
  1087.7 25.9 %copy-start.321 = (bf16[512,16]{0,1:T(8,128)(2,1)S(1)}, bf16[512,16]{0,1:T(8,128)(2,1)}, u32[]{:S(2)}) copy-start(bf16[512,16]{0,1:T(8,128)(2,1)} %copy-done.320) | copy-start | bytes 49156
  1113.5 135.0 %all-reduce.69.cloned.1.call-start = ((), (), s32[]{:S(2)}) async-start(), calls=%async_computation.6 | async-start | bytes 8388608 | tf_op jit(solution)/shard_map/psum | solution.py:747
  1134.5 313.1 %all-reduce.71.cloned.1.call-start = ((), (), s32[]{:S(2)}) async-start(), calls=%async_computation.8 | async-start | bytes 16908288 | tf_op jit(solution)/shard_map/psum | solution.py:622
  1327.4 30.4 %copy-start.53 = (bf16[2,128,2048]{2,1,0:T(8,128)(2,1)S(1)}, bf16[2,128,2048]{2,1,0:T(8,128)(2,1)}, u32[]{:S(2)}) copy-start(bf16[2,128,2048]{2,1,0:T(8,128)(2,1)} %param.19) | copy-start | bytes 3145732
  1327.4 30.4 %copy-start.165 = (f32[1,2048]{1,0:T(1,128)S(1)}, f32[1,2048]{1,0:T(1,128)}, u32[]{:S(2)}) copy-start(f32[1,2048]{1,0:T(1,128)} %param.23) | copy-start | bytes 24580
  1327.4 30.4 %copy-start.339 = (f32[128]{0:T(128)S(1)}, f32[128]{0:T(128)}, u32[]{:S(2)}) copy-start(f32[128]{0:T(128)} %copy-done.338) | copy-start | bytes 1540
  1327.4 31.9 %copy-start.273 = (f32[2048]{0:T(1024)S(1)}, f32[2048]{0:T(1024)}, u32[]{:S(2)}) copy-start(f32[2048]{0:T(1024)} %get-tuple-element.141) | copy-start | bytes 24580
  1327.5 31.9 %copy-start.274 = (f32[2048]{0:T(1024)S(1)}, f32[2048]{0:T(1024)}, u32[]{:S(2)}) copy-start(f32[2048]{0:T(1024)} %get-tuple-element.143) | copy-start | bytes 24580
  1327.5 72.4 %copy-start.399 = (f32[128]{0:T(128)S(1)}, f32[128]{0:T(128)}, u32[]{:S(2)}) copy-start(f32[128]{0:T(128)} %get-tuple-element.331) | copy-start | bytes 1540
  (375 other events, 2265.4 us)
Sparse Core Ops, SparseCore 0:
  95.6 33.5 all-gather.14
  291.3 34.7 all-gather.16
  448.6 57.9 all-gather.18
  565.0 48.2 all-gather.20
  790.3 31.3 all-gather.22
  1010.1 25.8 all-gather.24
  1113.6 27.6 all-gather.26
  1144.6 103.8 all-reduce.68
  1271.9 175.5 all-reduce.70

commit v14 on v13

--- a/solution.py
+++ b/solution.py
@@ -763,6 +763,7 @@
     anchor = out_total[0, 0].astype(jnp.float32) * 0.0
     head_total = (head_total[0] + anchor,) + head_total[1:]
     bc_part, bc_shapes = bc_box[0]
+    bc_part = bc_part + anchor
     head_total, norm_sum, bc_rows = reduce_grads(head_total, shared_total[0], bc_part, tick_count)
     shared_total = (norm_sum,) + unpack_rows(bc_rows, bc_shapes, bc_rows.shape[-1])
     head_total = head_total[:3] + (out_total.astype(jnp.float32),) + head_total[3:]

time: 1480 us -> 1420 us (0.959)
  waiting for transfers between devices: 186 us -> 129 us
    psum x1, waiting for transfers between devices: 82.8 us -> 19.7 us  [on_device(): out_total = lax.psum(out_total.astype(jnp.bfloat16), 'seq')]
    unnamed x850 -> x840, local copies, waits for them, and re-layouts: 71.4 us -> 66.6 us
  transfers between devices with their start and end apart: 22 -> 22, of which waited for: 10 -> 11; matrix products, arithmetic and copies ran while one was open for 22% -> 24% of each run, Pallas kernels for 9% -> 11%
where the time goes in v14:
time: 1420 us; the launch traced here: 1410 us
  Pallas kernels  336 us (24%)
  matrix products  285 us (20%)
  other arithmetic  251 us (18%)
  local copies, waits for them, and re-layouts  185 us (13%)
  blocking collectives  167 us (12%)
  waiting for transfers between devices  129 us (9%)
  starting transfers between devices  34.4 us (2%)
  between operations  21.4 us (2%)
    pallas_call x7, Pallas kernels, head_gather(): pl.pallas_call(functools.partial(gather_body, n, tick), out_shape=jax.Sha...  170 us
    pallas_call x7, Pallas kernels, head_scatter(): pl.pallas_call(functools.partial(scatter_body, n, tick), out_shape=jax.Sh...  166 us
    dot_general x9, matrix products, block_output(): jnp.einsum('cijh,cjhp->cihp', weights, x_blocks, precision=highest)  67.9 us
    unnamed x840, local copies, waits for them, and re-layouts  66.6 us
    all_gather x3, waiting for transfers between devices, entering_2(): lax.all_gather(a.astype(kind), axis)  43.5 us
    psum x1, blocking collectives, reduce_grads(): norm_sum = lax.psum(norm_part, ('seq', 'head'))  40.4 us
    dot_general x3, matrix products, mixer_forward(): projected = jnp.dot(gathered, w_main, preferred_element_type=jnp.float32)  38.1 us
    all_gather x3, waiting for transfers between devices, entering(): everything = jax.tree.map(lambda part: lax.all_gather(part, axis), value)  37.5 us
  transfers between devices with their start and end apart: 22, of which 11 were waited for; matrix products, arithmetic and copies ran while one was open for 24% of the time, Pallas kernels for 11%

profile of v14, /device:TPU:0, one launch (start us, length us, event | category | flops | bytes accessed | tf_op | source)
XLA Modules:
  0.0 1408.6 jit_solution(11008396770007560002)
XLA Ops:
  20.9 29.3 %shard_map.297 = bf16[4,128,2048]{2,1,0:T(8,128)(2,1)} custom-call(bf16[128,2048]{1,0:T(8,128)(2,1)} %fusion.225.x_ref), custom_call_target="tpu_custom_call" | custom-call | tf_op jit(solution)/shard_map/pallas_call | solution.py:113
  50.6 12.7 fusion.418
  95.8 7.0 all-gather.1
  116.0 13.4 all-gather.15.cloned.1.call-done
  143.2 12.1 psum.119
  157.0 6.9 fusion.40.p_ref
  163.9 27.6 %shard_map.298 = f32[128,2048]{1,0:T(8,128)} custom-call(f32[4,128,2048]{2,1,0:T(8,128)} %fusion.40.p_ref), custom_call_target="tpu_custom_call" | custom-call | tf_op jit(solution)/shard_map/pallas_call | solution.py:224
  199.9 43.4 %shard_map.299 = bf16[4,128,2048]{2,1,0:T(8,128)(2,1)} custom-call(bf16[128,2048]{1,0:T(8,128)(2,1)} %multiply_convert_fusion.7.x_ref), custom_call_target="tpu_custom_call" | custom-call | tf_op jit(solution)/shard_map/pallas_call | solution.py:113
  243.3 12.9 fusion.417
  272.0 9.4 fusion.112
  299.0 6.3 all-gather.2
  313.8 12.6 all-gather.17.cloned.1.call-done
  340.2 12.1 psum.120
  355.9 6.9 fusion.38.p_ref
  362.8 35.4 %shard_map.300 = f32[128,2048]{1,0:T(8,128)} custom-call(f32[4,128,2048]{2,1,0:T(8,128)} %fusion.38.p_ref), custom_call_target="tpu_custom_call" | custom-call | tf_op jit(solution)/shard_map/pallas_call | solution.py:224
  409.7 12.5 fusion.416
  449.1 7.9 all-gather.6
  462.6 7.0 all-gather.5
  470.8 7.8 all-gather.4
  478.5 7.2 all-gather.3
  495.7 11.5 all-gather.19.cloned.1.call-done
  522.3 11.9 psum.121
  534.2 7.9 multiply_reduce_fusion.20
  542.1 8.3 psum.122
  550.4 6.9 multiply_reduce_fusion.23
  565.4 12.2 fusion.30
  583.4 5.7 fusion.455
  589.2 24.4 %all-gather.21.cloned.1.call-done = bf16[4,16,64,128]{3,2,1,0:T(8,128)(2,1)} async-done(((bf16[1,16,64,128]{3,2,1,0:T(8,128)(2,1)}), bf16[4,16,64,128]{3,2,1,0:T(8,128)(2,1)}) %all-gather.21.cloned.1.call-update) | async-done | bytes 1048592 | tf_op jit(solution)/shard_map/all_gather | solution.py:274
  620.2 6.3 fusion.128
  630.8 6.5 multiply_reduce_fusion.13
  692.9 11.0 fusion.252
  707.0 11.0 collective-permute-done.9
  719.8 34.3 %shard_map.305 = bf16[4,128,2048]{2,1,0:T(8,128)(2,1)} custom-call(bf16[128,2048]{1,0:T(8,128)(2,1)} %fusion.243.x_ref), custom_call_target="tpu_custom_call" | custom-call | tf_op jit(solution)/shard_map/pallas_call | solution.py:113
  754.1 8.0 multiply_reduce_fusion.19
  762.1 11.0 psum.123
  773.2 6.1 multiply_reduce_fusion.22
  787.6 11.9 fusion.32
  805.1 5.7 fusion.456
  810.9 8.1 all-gather.23.cloned.1.call-done
  825.7 6.2 fusion.124
  836.1 6.7 multiply_reduce_fusion.9
  889.4 41.1 %shard_map.306 = f32[128,2048]{1,0:T(8,128)} custom-call(f32[4,128,2048]{2,1,0:T(8,128)} %bitcast.971), custom_call_target="tpu_custom_call" | custom-call | tf_op jit(solution)/shard_map/pallas_call | solution.py:224
  935.7 10.9 fusion.250
  951.5 28.6 %shard_map.307 = bf16[4,128,2048]{2,1,0:T(8,128)(2,1)} custom-call(bf16[128,2048]{1,0:T(8,128)(2,1)} %fusion.244.x_ref), custom_call_target="tpu_custom_call" | custom-call | tf_op jit(solution)/shard_map/pallas_call | solution.py:113
  980.2 8.0 multiply_reduce_fusion.18
  988.2 11.2 psum.124
  1008.6 11.7 fusion.34
  1028.8 10.5 add_convert_fusion
  1039.6 11.0 all-gather.25.cloned.1.call-done
  1089.5 6.6 pad_add_fusion
  1112.6 24.2 %shard_map.308 = f32[520,256]{1,0:T(8,128)} custom-call(f32[4,520,256]{2,1,0:T(8,128)} %bitcast.975), custom_call_target="tpu_custom_call" | custom-call | tf_op jit(solution)/shard_map/pallas_call | solution.py:224
  1138.0 19.7 %all-reduce.69.cloned.1.call-done = bf16[1024,2048]{1,0:T(8,128)(2,1)} async-done(((bf16[1024,2048]{1,0:T(8,128)(2,1)}), bf16[1024,2048]{1,0:T(8,128)(2,1)}) %all-reduce.69.cloned.1.call-update) | async-done | bytes 4194320 | tf_op jit(solution)/shard_map/psum | solution.py:747
  1161.7 7.0 fusion.248
  1168.7 5.9 copy-done.49
  1176.2 12.2 all-gather.27.cloned.1.call-done
  1190.2 21.5 %fusion.35 = (bf16[1,2048,1024]{1,2,0:T(8,128)(2,1)}, bf16[1,2048,1024]{1,2,0:T(8,128)(2,1)}) fusion(f32[2048,2064]{0,1:T(8,128)} %copy-done.49, f32[2048,2064]{0,1:T(8,128)} %fusion.250, f32[2048,2064]{0,1:T(8,128)} %fusion.252, f32[]{:T(128)S(6)} %convert_element_type.616, f32[]{:T(128)S(6)} %convert_element_type.615, f32[]{:T(128)S(6)} %convert_element_type.614, ...), kind=kLoop, calls=%fused_computation.59 | loop fusion | flops 29360128 | bytes 58720276 | tf_op jit(solution)/shard_map/broadcast_in_dim | solution.py:775
  1215.0 7.1 fusion.36.p_ref
  1233.2 16.3 %all-reduce.64 = (bf16[1,4,1024]{2,1,0:T(4,128)(2,1)S(1)}, bf16[1,1024]{1,0:T(2,128)(2,1)S(1)}, bf16[1,16]{1,0:T(2,128)(2,1)S(1)}, bf16[1,16]{1,0:T(2,128)(2,1)S...) all-reduce(bf16[1,4,1024]{2,1,0:T(4,128)(2,1)S(1)} %fusion.339, ...), channel_id=1, replica_groups=mesh['section'=2,'seq'=4,'head'=4] {'seq'}, use_global_device_ids=true, to_apply=%region_95.97 | all-reduce | flops 6192 | bytes 24768 | tf_op jit(solution)/shard_map/psum | solution.py:627
  1254.7 8.2 fusion.249
  1267.5 30.3 %shard_map.309 = f32[128,2048]{1,0:T(8,128)} custom-call(f32[4,128,2048]{2,1,0:T(8,128)} %bitcast.969), custom_call_target="tpu_custom_call" | custom-call | tf_op jit(solution)/shard_map/pallas_call | solution.py:224
  1299.4 40.4 %psum.125 = f32[1,2048]{1,0:T(1,128)} all-reduce(f32[1,2048]{1,0:T(1,128)S(1)} %bitcast.1094), channel_id=1, replica_groups=mesh['section'=2,'seq'=4,'head'=4] {'seq','head'}, use_global_device_ids=true, to_apply=%region_90.92 | all-reduce | flops 2048 | bytes 16384 | tf_op jit(solution)/shard_map/psum | solution.py:631
  1348.6 29.1 %shard_map.310 = f32[4,520,256]{2,1,0:T(8,128)} custom-call(f32[520,256]{1,0:T(8,128)} %add_add_fusion.4.x_ref), custom_call_target="tpu_custom_call" | custom-call | tf_op jit(solution)/shard_map/pallas_call | solution.py:113
  1387.4 6.9 copy.616
  1394.3 6.9 copy.617
  (1280 shorter events, 500.0 us)
Async XLA Ops:
  7.2 43.1 %copy-start.209 = (bf16[1,2048,16]{1,2,0:T(8,128)(2,1)S(1)}, bf16[1,2048,16]{1,2,0:T(8,128)(2,1)}, u32[]{:S(2)}) copy-start(bf16[1,2048,16]{1,2,0:T(8,128)(2,1)} %param.27) | copy-start | bytes 196612
  7.2 43.4 %copy-start.56 = (bf16[1,2048,256]{2,1,0:T(8,128)(2,1)S(1)}, bf16[1,2048,256]{2,1,0:T(8,128)(2,1)}, u32[]{:S(2)}) copy-start(bf16[1,2048,256]{2,1,0:T(8,128)(2,1)} %param.26) | copy-start | bytes 3145732
  7.2 122.2 %all-gather.15.cloned.1.call-start = ((), (), s32[]{:S(2)}) async-start(), calls=%async_computation | async-start | bytes 2621440 | tf_op jit(solution)/shard_map/all_gather | solution.py:256
  8.7 70.7 %collective-permute-start = (f32[3]{0:T(128)S(1)}, f32[3]{0:T(128)S(1)}, u32[]{:S(2)}, u32[]{:S(2)}) collective-permute-start(f32[3]{0:T(128)S(1)} %slice.605), channel_id=1, source_target_pairs={{0,4},{4,8},{8,12},{1,5},{5,9},{9,13},{2,6},{6,10},{10,14},{3,7},{... | collective-permute-start | bytes 44 | tf_op jit(solution)/shard_map/ppermute | solution.py:251
  13.7 65.8 %collective-permute-start.3 = (f32[3]{0:T(128)S(1)}, f32[3]{0:T(128)S(1)}, u32[]{:S(2)}, u32[]{:S(2)}) collective-permute-start(f32[3]{0:T(128)S(1)} %slice.644), channel_id=1, source_target_pairs={{0,4},{4,8},{8,12},{1,5},{5,9},{9,13},{2,6},{6,10},{10,14},{3,7},{... | collective-permute-start | bytes 44 | tf_op jit(solution)/shard_map/ppermute | solution.py:251
  18.9 31.4 %copy-start.337 = (f32[128]{0:T(128)}, f32[128]{0:T(128)S(1)}, u32[]{:S(2)}) copy-start(f32[128]{0:T(128)S(1)} %get-tuple-element.332) | copy-start | bytes 1540
  66.0 14.9 %collective-permute-start.1 = (f32[3,1280]{1,0:T(4,128)S(1)}, f32[3,1280]{1,0:T(4,128)S(1)}, u32[]{:S(2)}, u32[]{:S(2)}) collective-permute-start(f32[3,1280]{1,0:T(4,128)S(1)} %copy.495), channel_id=1, source_target_pairs={{0,4},{4,8},{8,12},{1,5},{5,9},{9,13},{2,6},{6,10},{10,14},{3,7},{... | collective-permute-start | bytes 46088 | tf_op jit(solution)/shard_map/ppermute | solution.py:251
  73.2 29.5 %copy-start.144 = (f32[512,16]{0,1:T(8,128)}, f32[512,16]{0,1:T(8,128)S(1)}, u32[]{:S(2)}) copy-start(f32[512,16]{0,1:T(8,128)S(1)} %get-tuple-element.226) | copy-start | bytes 98308
  79.4 53.7 %copy-start.176 = (f32[2,256,16]{1,2,0:T(8,128)}, f32[2,256,16]{1,2,0:T(8,128)S(1)}, u32[]{:S(2)}) copy-start(f32[2,256,16]{1,2,0:T(8,128)S(1)} %get-tuple-element.275) | copy-start | bytes 98308
  91.0 42.1 %copy-start.9 = (f32[2,256,16,64]{1,0,3,2:T(2,128)}, f32[2,256,16,64]{1,0,3,2:T(2,128)S(1)}, u32[]{:S(2)}) copy-start(f32[2,256,16,64]{1,0,3,2:T(2,128)S(1)} %reshape.967) | copy-start | bytes 6291460
  94.0 35.4 %copy-start.61 = (f32[2,16,64,128]{3,2,1,0:T(8,128)}, f32[2,16,64,128]{3,2,1,0:T(8,128)S(1)}, u32[]{:S(2)}) copy-start(f32[2,16,64,128]{3,2,1,0:T(8,128)S(1)} %fusion.160) | copy-start | bytes 3145732
  95.7 230.6 %all-gather.17.cloned.1.call-start = ((), (), s32[]{:S(2)}) async-start(), calls=%async_computation.1 | async-start | bytes 2621440 | tf_op jit(solution)/shard_map/all_gather | solution.py:256
  163.9 29.2 %copy-start.50 = (bf16[2,128,2048]{2,1,0:T(8,128)(2,1)S(1)}, bf16[2,128,2048]{2,1,0:T(8,128)(2,1)}, u32[]{:S(2)}) copy-start(bf16[2,128,2048]{2,1,0:T(8,128)(2,1)} %param.19) | copy-start | bytes 3145732
  194.3 3.7 collective-permute-start.2
  197.3 70.2 %copy-start.263 = (f32[2,256]{1,0:T(2,128)}, f32[2,256]{1,0:T(2,128)S(1)}, u32[]{:S(2)}) copy-start(f32[2,256]{1,0:T(2,128)S(1)} %get-tuple-element.342) | copy-start | bytes 6148
  197.3 70.2 %copy-start.305 = (f32[2,256]{1,0:T(2,128)}, f32[2,256]{1,0:T(2,128)S(1)}, u32[]{:S(2)}) copy-start(f32[2,256]{1,0:T(2,128)S(1)} %get-tuple-element.343) | copy-start | bytes 6148
  198.0 73.9 %copy-start.241 = (f32[512]{0:T(512)}, f32[512]{0:T(512)S(1)}, u32[]{:S(2)}) copy-start(f32[512]{0:T(512)S(1)} %get-tuple-element.286) | copy-start | bytes 6148
  198.1 73.9 %copy-start.243 = (f32[512]{0:T(512)}, f32[512]{0:T(512)S(1)}, u32[]{:S(2)}) copy-start(f32[512]{0:T(512)S(1)} %get-tuple-element.287) | copy-start | bytes 6148
  198.1 73.9 %copy-start.245 = (f32[512]{0:T(512)}, f32[512]{0:T(512)S(1)}, u32[]{:S(2)}) copy-start(f32[512]{0:T(512)S(1)} %get-tuple-element.288) | copy-start | bytes 6148
  198.3 199.8 %copy-start.25 = (f32[128,2048]{1,0:T(8,128)}, f32[128,2048]{1,0:T(8,128)S(1)}, u32[]{:S(2)}) copy-start(f32[128,2048]{1,0:T(8,128)S(1)} %get-tuple-element.218) | copy-start | bytes 3145732
  198.9 57.2 %copy-start.351 = (f32[128]{0:T(128)}, f32[128]{0:T(128)S(1)}, u32[]{:S(2)}) copy-start(f32[128]{0:T(128)S(1)} %get-tuple-element.334) | copy-start | bytes 1540
  243.3 23.6 %copy-start.349 = (f32[2]{0:T(128)S(1)}, f32[2]{0:T(128)}, u32[]{:S(2)}) copy-start(f32[2]{0:T(128)} %get-tuple-element.345) | copy-start | bytes 28
  260.7 11.0 collective-permute-start.4
  265.3 40.1 %copy-start.146 = (f32[512,16]{0,1:T(8,128)}, f32[512,16]{0,1:T(8,128)S(1)}, u32[]{:S(2)}) copy-start(f32[512,16]{0,1:T(8,128)S(1)} %get-tuple-element.214) | copy-start | bytes 98308
  267.6 62.5 %copy-start.180 = (f32[2,256,16]{1,2,0:T(8,128)}, f32[2,256,16]{1,2,0:T(8,128)S(1)}, u32[]{:S(2)}) copy-start(f32[2,256,16]{1,2,0:T(8,128)S(1)} %get-tuple-element.273) | copy-start | bytes 98308
  286.6 43.6 %copy-start.11 = (f32[2,256,16,64]{1,0,3,2:T(2,128)}, f32[2,256,16,64]{1,0,3,2:T(2,128)S(1)}, u32[]{:S(2)}) copy-start(f32[2,256,16,64]{1,0,3,2:T(2,128)S(1)} %reshape.979) | copy-start | bytes 6291460
  291.5 215.7 %all-gather.19.cloned.1.call-start = ((), (), s32[]{:S(2)}) async-start(), calls=%async_computation.2 | async-start | bytes 2621440 | tf_op jit(solution)/shard_map/all_gather | solution.py:256
  292.8 109.6 %collective-permute-start.6 = (f32[3]{0:T(128)}, f32[3]{0:T(128)}, u32[]{:S(2)}, u32[]{:S(2)}) collective-permute-start(f32[3]{0:T(128)} %slice.679), channel_id=1, source_target_pairs={{0,4},{4,8},{8,12},{1,5},{5,9},{9,13},{2,6},{6,10},{10,14},{3,7},{... | collective-permute-start | bytes 44 | tf_op jit(solution)/shard_map/ppermute | solution.py:251
  305.4 24.8 %copy-start.285 = (f32[2,2,8,256]{3,2,0,1:T(8,128)}, f32[2,2,8,256]{3,2,0,1:T(8,128)S(1)}, u32[]{:S(2)}) copy-start(f32[2,2,8,256]{3,2,0,1:T(8,128)S(1)} %copy.946) | copy-start | bytes 98308
  362.8 35.4 %copy-start.111 = (f32[1,128,2048]{2,1,0:T(8,128)S(1)}, f32[1,128,2048]{2,1,0:T(8,128)}, u32[]{:S(2)}) copy-start(f32[1,128,2048]{2,1,0:T(8,128)} %constant_dynamic-slice_fusion.3) | copy-start | bytes 3145732
  401.0 3.8 collective-permute-start.5
  402.4 28.4 %copy-start.388 = (f32[2]{0:T(128)}, f32[2]{0:T(128)S(1)}, u32[]{:S(2)}) copy-start(f32[2]{0:T(128)S(1)} %fusion.370) | copy-start | bytes 28
  403.9 31.2 %copy-start.247 = (f32[512]{0:T(512)}, f32[512]{0:T(512)S(1)}, u32[]{:S(2)}) copy-start(f32[512]{0:T(512)S(1)} %get-tuple-element.280) | copy-start | bytes 6148
  403.9 31.2 %copy-start.249 = (f32[512]{0:T(512)}, f32[512]{0:T(512)S(1)}, u32[]{:S(2)}) copy-start(f32[512]{0:T(512)S(1)} %get-tuple-element.281) | copy-start | bytes 6148
  403.9 31.2 %copy-start.251 = (f32[512]{0:T(512)}, f32[512]{0:T(512)S(1)}, u32[]{:S(2)}) copy-start(f32[512]{0:T(512)S(1)} %get-tuple-element.282) | copy-start | bytes 6148
  424.9 9.9 collective-permute-start.7
  444.9 170.3 %copy-start.14 = (f32[2,256,16,64]{1,0,3,2:T(2,128)}, f32[2,256,16,64]{1,0,3,2:T(2,128)S(1)}, u32[]{:S(2)}) copy-start(f32[2,256,16,64]{1,0,3,2:T(2,128)S(1)} %reshape.991) | copy-start | bytes 6291460
  447.9 59.3 %copy-start.64 = (f32[2,16,64,128]{3,2,1,0:T(8,128)}, f32[2,16,64,128]{3,2,1,0:T(8,128)S(1)}, u32[]{:S(2)}) copy-start(f32[2,16,64,128]{3,2,1,0:T(8,128)S(1)} %fusion.152) | copy-start | bytes 3145732
  449.0 164.6 %all-gather.21.cloned.1.call-start = ((), (), s32[]{:S(2)}) async-start(), calls=%async_computation.3 | async-start | bytes 1310720 | tf_op jit(solution)/shard_map/all_gather | solution.py:274
  565.3 253.7 %all-gather.23.cloned.1.call-start = ((), (), s32[]{:S(2)}) async-start(), calls=%async_computation.4 | async-start | bytes 1310720 | tf_op jit(solution)/shard_map/all_gather | solution.py:274
  637.3 29.7 %copy-start.217 = (f32[1280]{0:T(1024)}, f32[1280]{0:T(1024)S(1)}, u32[]{:S(2)}) copy-start(f32[1280]{0:T(1024)S(1)} %get-tuple-element.135) | copy-start | bytes 15364
  648.7 18.9 %collective-permute-start.8 = (f32[3,1280]{1,0:T(4,128)}, f32[3,1280]{1,0:T(4,128)}, u32[]{:S(2)}, u32[]{:S(2)}) collective-permute-start(f32[3,1280]{1,0:T(4,128)} %copy.559), channel_id=1, source_target_pairs={{4,0},{8,4},{12,8},{5,1},{9,5},{13,9},{6,2},{10,6},{14,10},{7,3},{... | collective-permute-start | bytes 46088 | tf_op jit(solution)/shard_map/ppermute | solution.py:251
  691.4 26.6 %collective-permute-start.9 = (bf16[128,2048]{1,0:T(8,128)(2,1)S(1)}, bf16[128,2048]{1,0:T(8,128)(2,1)S(1)}, u32[]{:S(2)}, u32[]{:S(2)}) collective-permute-start(bf16[128,2048]{1,0:T(8,128)(2,1)S(1)} %get-tuple-element.193), channel_id=1, source_target_pairs={{16,0},{17,1},{18,2},{19,3},{20,4},{21,5},{22,6},{23,7},{24,8},{25... | collective-permute-start | bytes 1572872 | tf_op jit(solution)/shard_map/ppermute | solution.py:251
  707.0 47.0 %copy-start.320 = (f32[512]{0:T(512)S(1)}, f32[512]{0:T(512)}, u32[]{:S(2)}) copy-start(f32[512]{0:T(512)} %copy-done.319) | copy-start | bytes 6148
  787.5 263.1 %all-gather.25.cloned.1.call-start = ((), (), s32[]{:S(2)}) async-start(), calls=%async_computation.5 | async-start | bytes 1310720 | tf_op jit(solution)/shard_map/all_gather | solution.py:274
  842.8 29.7 %copy-start.219 = (f32[1280]{0:T(1024)}, f32[1280]{0:T(1024)S(1)}, u32[]{:S(2)}) copy-start(f32[1280]{0:T(1024)S(1)} %get-tuple-element.136) | copy-start | bytes 15364
  854.2 19.0 %collective-permute-start.10 = (f32[3,1280]{1,0:T(4,128)}, f32[3,1280]{1,0:T(4,128)}, u32[]{:S(2)}, u32[]{:S(2)}) collective-permute-start(f32[3,1280]{1,0:T(4,128)} %copy.582), channel_id=1, source_target_pairs={{4,0},{8,4},{12,8},{5,1},{9,5},{13,9},{6,2},{10,6},{14,10},{7,3},{... | collective-permute-start | bytes 46088 | tf_op jit(solution)/shard_map/ppermute | solution.py:251
  889.4 41.1 %copy-start.26 = (f32[128,2048]{1,0:T(8,128)S(1)}, f32[128,2048]{1,0:T(8,128)}, u32[]{:S(2)}) copy-start(f32[128,2048]{1,0:T(8,128)} %copy-done.25) | copy-start | bytes 3145732
  889.4 41.1 %copy-start.352 = (f32[128]{0:T(128)S(1)}, f32[128]{0:T(128)}, u32[]{:S(2)}) copy-start(f32[128]{0:T(128)} %copy-done.351) | copy-start | bytes 1540
  889.4 43.4 %copy-start.66 = (bf16[2,128,2048]{2,1,0:T(8,128)(2,1)S(1)}, bf16[2,128,2048]{2,1,0:T(8,128)(2,1)}, u32[]{:S(2)}) copy-start(bf16[2,128,2048]{2,1,0:T(8,128)(2,1)} %param.20) | copy-start | bytes 3145732
  889.4 43.4 %copy-start.137 = (bf16[128,2048]{1,0:T(8,128)(2,1)S(1)}, bf16[128,2048]{1,0:T(8,128)(2,1)}, u32[]{:S(2)}) copy-start(bf16[128,2048]{1,0:T(8,128)(2,1)} %copy-done.136) | copy-start | bytes 1572868
  889.4 43.4 %copy-start.397 = (f32[128]{0:T(128)S(1)}, f32[128]{0:T(128)}, u32[]{:S(2)}) copy-start(f32[128]{0:T(128)} %get-tuple-element.333) | copy-start | bytes 1540
  934.2 15.6 %collective-permute-start.11 = (bf16[128,2048]{1,0:T(8,128)(2,1)S(1)}, bf16[128,2048]{1,0:T(8,128)(2,1)S(1)}, u32[]{:S(2)}, u32[]{:S(2)}) collective-permute-start(bf16[128,2048]{1,0:T(8,128)(2,1)S(1)} %get-tuple-element.189), channel_id=1, source_target_pairs={{16,0},{17,1},{18,2},{19,3},{20,4},{21,5},{22,6},{23,7},{24,8},{25... | collective-permute-start | bytes 1572872 | tf_op jit(solution)/shard_map/ppermute | solution.py:251
  949.8 30.3 %copy-start.318 = (f32[512]{0:T(512)S(1)}, f32[512]{0:T(512)}, u32[]{:S(2)}) copy-start(f32[512]{0:T(512)} %copy-done.317) | copy-start | bytes 6148
  1024.6 133.2 %all-reduce.69.cloned.1.call-start = ((), (), s32[]{:S(2)}) async-start(), calls=%async_computation.6 | async-start | bytes 8388608 | tf_op jit(solution)/shard_map/psum | solution.py:747
  1039.4 149.0 %all-gather.27.cloned.1.call-start = ((), (), s32[]{:S(2)}) async-start(), calls=%async_computation.7 | async-start | bytes 1331200 | tf_op jit(solution)/shard_map/all_gather | solution.py:617
  1086.0 12.4 collective-permute-start.12
  1109.3 27.5 %copy-start.35 = (f32[509,1280]{0,1:T(8,128)S(1)}, f32[509,1280]{0,1:T(8,128)}, u32[]{:S(2)}) copy-start(f32[509,1280]{0,1:T(8,128)} %slice.910) | copy-start | bytes 7818244
  1161.4 226.0 %all-reduce.71.cloned.1.call-start = ((), (), s32[]{:S(2)}) async-start(), calls=%async_computation.8 | async-start | bytes 16908288 | tf_op jit(solution)/shard_map/psum | solution.py:622
  1267.5 30.4 %copy-start.52 = (bf16[2,128,2048]{2,1,0:T(8,128)(2,1)S(1)}, bf16[2,128,2048]{2,1,0:T(8,128)(2,1)}, u32[]{:S(2)}) copy-start(bf16[2,128,2048]{2,1,0:T(8,128)(2,1)} %param.19) | copy-start | bytes 3145732
  1267.5 30.4 %copy-start.338 = (f32[128]{0:T(128)S(1)}, f32[128]{0:T(128)}, u32[]{:S(2)}) copy-start(f32[128]{0:T(128)} %copy-done.337) | copy-start | bytes 1540
  1267.5 31.9 %copy-start.269 = (f32[2048]{0:T(1024)S(1)}, f32[2048]{0:T(1024)}, u32[]{:S(2)}) copy-start(f32[2048]{0:T(1024)} %get-tuple-element.141) | copy-start | bytes 24580
  1267.5 31.9 %copy-start.270 = (f32[2048]{0:T(1024)S(1)}, f32[2048]{0:T(1024)}, u32[]{:S(2)}) copy-start(f32[2048]{0:T(1024)} %get-tuple-element.143) | copy-start | bytes 24580
  1267.5 72.4 %copy-start.396 = (f32[128]{0:T(128)S(1)}, f32[128]{0:T(128)}, u32[]{:S(2)}) copy-start(f32[128]{0:T(128)} %get-tuple-element.331) | copy-start | bytes 1540
  (370 other events, 2117.9 us)
Sparse Core Ops, SparseCore 0:
  95.8 33.5 all-gather.14
  291.6 34.7 all-gather.16
  449.1 57.9 all-gather.18
  565.4 48.1 all-gather.20
  787.6 31.3 all-gather.22
  1024.7 25.8 all-gather.24
  1053.9 103.8 all-reduce.68
  1161.6 26.7 all-gather.26
  1211.8 175.5 all-reduce.70

commit v15 on v14

--- a/solution.py
+++ b/solution.py
@@ -368,7 +368,9 @@
         linked[..., None], cum_decay[:, :, None, :] - cum_decay[:, None, :, :], far_below
     )
     weights = jnp.exp(spread) * inner_prod[..., None] * dt_blocks[:, None, :, :]
-    y_intra = jnp.einsum("cijh,cjhp->cihp", weights, x_blocks, precision=highest)
+    y_intra = jnp.einsum(
+        "cijh,cjhp->cihp", weights, x_blocks, precision=lax.Precision.DEFAULT
+    )
     carry_in = jnp.exp(cum_decay) * (mark_count == 0).astype(jnp.float32)[:, :, None]
     y_inter = (
         jnp.einsum("cin,chpn->cihp", c_blocks, incoming, precision=highest) * carry_in[..., None]
@@ -552,20 +554,18 @@
         gathered, grad_low, (((0,), (0,)), ((), ())), preferred_element_type=jnp.float32
     )
     g_w_bc = lax.dot_general(
-        gathered.astype(jnp.float32),
-        grad_bc,
+        gathered,
+        grad_bc.astype(jnp.bfloat16),
         (((0,), (0,)), ((), ())),
-        precision=highest,
         preferred_element_type=jnp.float32,
     )
     main_term = lax.dot_general(
         grad_low, w_low, (((1,), (1,)), ((), ())), preferred_element_type=jnp.float32
     )
     side_term = lax.dot_general(
-        grad_bc,
-        w_bc_float,
+        grad_bc.astype(jnp.bfloat16),
+        w_bc,
         (((1,), (1,)), ((), ())),
-        precision=highest,
         preferred_element_type=jnp.float32,
     )
     head_count = lax.axis_size("head")

time: 1420 us -> 1390 us (0.979)
  matrix products: 285 us -> 254 us
    dot_general x15, matrix products: 89.8 us -> 59.2 us  [the longest x9 44.4 us: block_output(): jnp.einsum('cijh,cjhp->cihp', weights, x_blocks, precision=lax.Precision....]
    unnamed x840 -> x830, local copies, waits for them, and re-layouts: 66.6 us -> 63 us
where the time goes in v15:
time: 1390 us; the launch traced here: 1380 us
  Pallas kernels  338 us (24%)
  matrix products  254 us (18%)
  other arithmetic  253 us (18%)
  local copies, waits for them, and re-layouts  180 us (13%)
  blocking collectives  166 us (12%)
  waiting for transfers between devices  136 us (10%)
  starting transfers between devices  34.5 us (2%)
  between operations  21.4 us (2%)
    pallas_call x7, Pallas kernels, head_gather(): pl.pallas_call(functools.partial(gather_body, n, tick), out_shape=jax.Sha...  171 us
    pallas_call x7, Pallas kernels, head_scatter(): pl.pallas_call(functools.partial(scatter_body, n, tick), out_shape=jax.Sh...  166 us
    unnamed x830, local copies, waits for them, and re-layouts  63 us
    all_gather x3, waiting for transfers between devices, entering_2(): lax.all_gather(a.astype(kind), axis)  50.5 us
    dot_general x9, matrix products, block_output(): jnp.einsum('cijh,cjhp->cihp', weights, x_blocks, precision=lax.Precision....  44.4 us
    psum x1, blocking collectives, reduce_grads(): norm_sum = lax.psum(norm_part, ('seq', 'head'))  40.3 us
    dot_general x3, matrix products, mixer_forward(): projected = jnp.dot(gathered, w_main, preferred_element_type=jnp.float32)  38.1 us
    all_gather x3, waiting for transfers between devices, entering(): everything = jax.tree.map(lambda part: lax.all_gather(part, axis), value)  36.7 us
  transfers between devices with their start and end apart: 22, of which 11 were waited for; matrix products, arithmetic and copies ran while one was open for 24% of the time, Pallas kernels for 11%

profile of v15, /device:TPU:0, one launch (start us, length us, event | category | flops | bytes accessed | tf_op | source)
XLA Modules:
  0.0 1381.1 jit_solution(7323005939891004719)
XLA Ops:
  20.9 29.3 %shard_map.297 = bf16[4,128,2048]{2,1,0:T(8,128)(2,1)} custom-call(bf16[128,2048]{1,0:T(8,128)(2,1)} %fusion.219.x_ref), custom_call_target="tpu_custom_call" | custom-call | tf_op jit(solution)/shard_map/pallas_call | solution.py:113
  50.6 12.7 fusion.412
  95.6 7.3 all-gather.1
  116.2 13.1 all-gather.15.cloned.1.call-done
  140.5 11.7 psum.119
  153.9 6.9 fusion.40.p_ref
  160.7 28.0 %shard_map.298 = f32[128,2048]{1,0:T(8,128)} custom-call(f32[4,128,2048]{2,1,0:T(8,128)} %fusion.40.p_ref), custom_call_target="tpu_custom_call" | custom-call | tf_op jit(solution)/shard_map/pallas_call | solution.py:224
  197.3 43.4 %shard_map.299 = bf16[4,128,2048]{2,1,0:T(8,128)(2,1)} custom-call(bf16[128,2048]{1,0:T(8,128)(2,1)} %multiply_convert_fusion.7.x_ref), custom_call_target="tpu_custom_call" | custom-call | tf_op jit(solution)/shard_map/pallas_call | solution.py:113
  240.7 12.9 fusion.411
  269.3 9.6 fusion.112
  296.5 6.6 all-gather.2
  311.5 12.3 all-gather.17.cloned.1.call-done
  335.2 11.7 psum.120
  350.4 6.9 fusion.38.p_ref
  357.3 35.6 %shard_map.300 = f32[128,2048]{1,0:T(8,128)} custom-call(f32[4,128,2048]{2,1,0:T(8,128)} %fusion.38.p_ref), custom_call_target="tpu_custom_call" | custom-call | tf_op jit(solution)/shard_map/pallas_call | solution.py:224
  404.4 12.5 fusion.410
  443.7 7.9 all-gather.6
  457.4 7.0 all-gather.5
  465.5 7.8 all-gather.4
  473.3 7.4 all-gather.3
  490.6 11.3 all-gather.19.cloned.1.call-done
  514.4 11.7 psum.121
  526.0 7.9 multiply_reduce_fusion.20
  533.9 8.3 psum.122
  542.3 6.9 multiply_reduce_fusion.23
  557.5 8.1 fusion.30
  571.4 5.7 fusion.449
  577.1 28.7 %all-gather.21.cloned.1.call-done = bf16[4,16,64,128]{3,2,1,0:T(8,128)(2,1)} async-done(((bf16[1,16,64,128]{3,2,1,0:T(8,128)(2,1)}), bf16[4,16,64,128]{3,2,1,0:T(8,128)(2,1)}) %all-gather.21.cloned.1.call-update) | async-done | bytes 1048592 | tf_op jit(solution)/shard_map/all_gather | solution.py:274
  621.7 6.3 multiply_reduce_fusion.13
  678.2 11.2 fusion.246
  691.6 11.8 collective-permute-done.9
  705.1 35.3 %shard_map.305 = bf16[4,128,2048]{2,1,0:T(8,128)(2,1)} custom-call(bf16[128,2048]{1,0:T(8,128)(2,1)} %fusion.237.x_ref), custom_call_target="tpu_custom_call" | custom-call | tf_op jit(solution)/shard_map/pallas_call | solution.py:113
  740.5 8.0 multiply_reduce_fusion.19
  748.5 10.6 psum.123
  759.1 6.1 multiply_reduce_fusion.22
  773.5 8.2 fusion.32
  787.5 5.7 fusion.450
  793.2 10.9 all-gather.23.cloned.1.call-done
  820.1 6.3 multiply_reduce_fusion.9
  867.1 40.9 %shard_map.306 = f32[128,2048]{1,0:T(8,128)} custom-call(f32[4,128,2048]{2,1,0:T(8,128)} %bitcast.977), custom_call_target="tpu_custom_call" | custom-call | tf_op jit(solution)/shard_map/pallas_call | solution.py:224
  913.3 11.0 fusion.244
  928.1 28.6 %shard_map.307 = bf16[4,128,2048]{2,1,0:T(8,128)(2,1)} custom-call(bf16[128,2048]{1,0:T(8,128)(2,1)} %fusion.238.x_ref), custom_call_target="tpu_custom_call" | custom-call | tf_op jit(solution)/shard_map/pallas_call | solution.py:113
  956.7 8.0 multiply_reduce_fusion.18
  964.7 11.2 psum.124
  985.1 7.9 fusion.34
  1001.5 10.6 add_convert_fusion
  1012.4 11.0 all-gather.25.cloned.1.call-done
  1046.8 5.7 multiply_reduce_fusion.5
  1061.9 6.7 pad_add_fusion
  1077.4 6.2 concatenate.67
  1086.9 24.7 %shard_map.308 = f32[520,256]{1,0:T(8,128)} custom-call(f32[4,520,256]{2,1,0:T(8,128)} %bitcast.984), custom_call_target="tpu_custom_call" | custom-call | tf_op jit(solution)/shard_map/pallas_call | solution.py:224
  1111.6 19.0 %all-reduce.69.cloned.1.call-done = bf16[1024,2048]{1,0:T(8,128)(2,1)} async-done(((bf16[1024,2048]{1,0:T(8,128)(2,1)}), bf16[1024,2048]{1,0:T(8,128)(2,1)}) %all-reduce.69.cloned.1.call-update) | async-done | bytes 4194320 | tf_op jit(solution)/shard_map/psum | solution.py:747
  1134.7 6.0 fusion.242
  1140.7 5.8 copy-done.49
  1148.2 12.9 all-gather.27.cloned.1.call-done
  1162.9 21.5 %fusion.35 = (bf16[1,2048,1024]{1,2,0:T(8,128)(2,1)}, bf16[1,2048,1024]{1,2,0:T(8,128)(2,1)}) fusion(f32[2048,2064]{0,1:T(8,128)} %copy-done.49, f32[2048,2064]{0,1:T(8,128)} %fusion.244, f32[2048,2064]{0,1:T(8,128)} %fusion.246, f32[]{:T(128)S(6)} %convert_element_type.616, f32[]{:T(128)S(6)} %convert_element_type.615, f32[]{:T(128)S(6)} %convert_element_type.614, ...), kind=kLoop, calls=%fused_computation.59 | loop fusion | flops 29360128 | bytes 58720276 | tf_op jit(solution)/shard_map/broadcast_in_dim | solution.py:775
  1187.7 7.1 fusion.36.p_ref
  1208.3 16.3 %all-reduce.64 = (bf16[1,4,1024]{2,1,0:T(4,128)(2,1)S(1)}, bf16[1,1024]{1,0:T(2,128)(2,1)S(1)}, bf16[1,16]{1,0:T(2,128)(2,1)S(1)}, bf16[1,16]{1,0:T(2,128)(2,1)S...) all-reduce(bf16[1,4,1024]{2,1,0:T(4,128)(2,1)S(1)} %fusion.333, ...), channel_id=1, replica_groups=mesh['section'=2,'seq'=4,'head'=4] {'seq'}, use_global_device_ids=true, to_apply=%region_95.97 | all-reduce | flops 6192 | bytes 24768 | tf_op jit(solution)/shard_map/psum | solution.py:627
  1229.8 8.1 fusion.243
  1240.7 30.3 %shard_map.309 = f32[128,2048]{1,0:T(8,128)} custom-call(f32[4,128,2048]{2,1,0:T(8,128)} %bitcast.975), custom_call_target="tpu_custom_call" | custom-call | tf_op jit(solution)/shard_map/pallas_call | solution.py:224
  1272.7 40.3 %psum.125 = f32[1,2048]{1,0:T(1,128)} all-reduce(f32[1,2048]{1,0:T(1,128)S(1)} %bitcast.1094), channel_id=1, replica_groups=mesh['section'=2,'seq'=4,'head'=4] {'seq','head'}, use_global_device_ids=true, to_apply=%region_90.92 | all-reduce | flops 2048 | bytes 16384 | tf_op jit(solution)/shard_map/psum | solution.py:631
  1321.7 29.0 %shard_map.310 = f32[4,520,256]{2,1,0:T(8,128)} custom-call(f32[520,256]{1,0:T(8,128)} %add_add_fusion.4.x_ref), custom_call_target="tpu_custom_call" | custom-call | tf_op jit(solution)/shard_map/pallas_call | solution.py:113
  1360.0 6.9 copy.616
  1366.8 6.9 copy.617
  (1273 shorter events, 477.7 us)
Async XLA Ops:
  7.2 43.1 %copy-start.206 = (bf16[1,2048,16]{1,2,0:T(8,128)(2,1)S(1)}, bf16[1,2048,16]{1,2,0:T(8,128)(2,1)}, u32[]{:S(2)}) copy-start(bf16[1,2048,16]{1,2,0:T(8,128)(2,1)} %param.27) | copy-start | bytes 196612
  7.2 43.4 %copy-start.60 = (bf16[1,2048,256]{2,1,0:T(8,128)(2,1)S(1)}, bf16[1,2048,256]{2,1,0:T(8,128)(2,1)}, u32[]{:S(2)}) copy-start(bf16[1,2048,256]{2,1,0:T(8,128)(2,1)} %param.26) | copy-start | bytes 3145732
  7.2 122.1 %all-gather.15.cloned.1.call-start = ((), (), s32[]{:S(2)}) async-start(), calls=%async_computation | async-start | bytes 2621440 | tf_op jit(solution)/shard_map/all_gather | solution.py:256
  8.7 70.6 %collective-permute-start = (f32[3]{0:T(128)S(1)}, f32[3]{0:T(128)S(1)}, u32[]{:S(2)}, u32[]{:S(2)}) collective-permute-start(f32[3]{0:T(128)S(1)} %slice.608), channel_id=1, source_target_pairs={{0,4},{4,8},{8,12},{1,5},{5,9},{9,13},{2,6},{6,10},{10,14},{3,7},{... | collective-permute-start | bytes 44 | tf_op jit(solution)/shard_map/ppermute | solution.py:251
  13.7 65.7 %collective-permute-start.3 = (f32[3]{0:T(128)S(1)}, f32[3]{0:T(128)S(1)}, u32[]{:S(2)}, u32[]{:S(2)}) collective-permute-start(f32[3]{0:T(128)S(1)} %slice.647), channel_id=1, source_target_pairs={{0,4},{4,8},{8,12},{1,5},{5,9},{9,13},{2,6},{6,10},{10,14},{3,7},{... | collective-permute-start | bytes 44 | tf_op jit(solution)/shard_map/ppermute | solution.py:251
  18.9 31.4 %copy-start.337 = (f32[128]{0:T(128)}, f32[128]{0:T(128)S(1)}, u32[]{:S(2)}) copy-start(f32[128]{0:T(128)S(1)} %get-tuple-element.332) | copy-start | bytes 1540
  66.0 14.8 %collective-permute-start.1 = (f32[3,1280]{1,0:T(4,128)S(1)}, f32[3,1280]{1,0:T(4,128)S(1)}, u32[]{:S(2)}, u32[]{:S(2)}) collective-permute-start(f32[3,1280]{1,0:T(4,128)S(1)} %copy.495), channel_id=1, source_target_pairs={{0,4},{4,8},{8,12},{1,5},{5,9},{9,13},{2,6},{6,10},{10,14},{3,7},{... | collective-permute-start | bytes 46088 | tf_op jit(solution)/shard_map/ppermute | solution.py:251
  73.2 29.7 %copy-start.141 = (f32[512,16]{0,1:T(8,128)}, f32[512,16]{0,1:T(8,128)S(1)}, u32[]{:S(2)}) copy-start(f32[512,16]{0,1:T(8,128)S(1)} %get-tuple-element.226) | copy-start | bytes 98308
  79.3 53.7 %copy-start.173 = (f32[2,256,16]{1,2,0:T(8,128)}, f32[2,256,16]{1,2,0:T(8,128)S(1)}, u32[]{:S(2)}) copy-start(f32[2,256,16]{1,2,0:T(8,128)S(1)} %get-tuple-element.275) | copy-start | bytes 98308
  90.9 42.1 %copy-start.9 = (f32[2,256,16,64]{1,0,3,2:T(2,128)}, f32[2,256,16,64]{1,0,3,2:T(2,128)S(1)}, u32[]{:S(2)}) copy-start(f32[2,256,16,64]{1,0,3,2:T(2,128)S(1)} %reshape.967) | copy-start | bytes 6291460
  93.9 35.4 %copy-start.65 = (f32[2,16,64,128]{3,2,1,0:T(8,128)}, f32[2,16,64,128]{3,2,1,0:T(8,128)S(1)}, u32[]{:S(2)}) copy-start(f32[2,16,64,128]{3,2,1,0:T(8,128)S(1)} %fusion.154) | copy-start | bytes 3145732
  95.6 228.2 %all-gather.17.cloned.1.call-start = ((), (), s32[]{:S(2)}) async-start(), calls=%async_computation.1 | async-start | bytes 2621440 | tf_op jit(solution)/shard_map/all_gather | solution.py:256
  160.7 29.7 %copy-start.51 = (bf16[2,128,2048]{2,1,0:T(8,128)(2,1)S(1)}, bf16[2,128,2048]{2,1,0:T(8,128)(2,1)}, u32[]{:S(2)}) copy-start(bf16[2,128,2048]{2,1,0:T(8,128)(2,1)} %param.19) | copy-start | bytes 3145732
  191.7 3.8 collective-permute-start.2
  194.7 70.1 %copy-start.262 = (f32[2,256]{1,0:T(2,128)}, f32[2,256]{1,0:T(2,128)S(1)}, u32[]{:S(2)}) copy-start(f32[2,256]{1,0:T(2,128)S(1)} %get-tuple-element.342) | copy-start | bytes 6148
  194.7 70.1 %copy-start.304 = (f32[2,256]{1,0:T(2,128)}, f32[2,256]{1,0:T(2,128)S(1)}, u32[]{:S(2)}) copy-start(f32[2,256]{1,0:T(2,128)S(1)} %get-tuple-element.343) | copy-start | bytes 6148
  195.4 73.8 %copy-start.240 = (f32[512]{0:T(512)}, f32[512]{0:T(512)S(1)}, u32[]{:S(2)}) copy-start(f32[512]{0:T(512)S(1)} %get-tuple-element.286) | copy-start | bytes 6148
  195.4 73.9 %copy-start.242 = (f32[512]{0:T(512)}, f32[512]{0:T(512)S(1)}, u32[]{:S(2)}) copy-start(f32[512]{0:T(512)S(1)} %get-tuple-element.287) | copy-start | bytes 6148
  195.4 73.9 %copy-start.244 = (f32[512]{0:T(512)}, f32[512]{0:T(512)S(1)}, u32[]{:S(2)}) copy-start(f32[512]{0:T(512)S(1)} %get-tuple-element.288) | copy-start | bytes 6148
  195.7 197.2 %copy-start.26 = (f32[128,2048]{1,0:T(8,128)}, f32[128,2048]{1,0:T(8,128)S(1)}, u32[]{:S(2)}) copy-start(f32[128,2048]{1,0:T(8,128)S(1)} %get-tuple-element.218) | copy-start | bytes 3145732
  196.3 57.3 %copy-start.351 = (f32[128]{0:T(128)}, f32[128]{0:T(128)S(1)}, u32[]{:S(2)}) copy-start(f32[128]{0:T(128)S(1)} %get-tuple-element.334) | copy-start | bytes 1540
  258.2 10.8 collective-permute-start.4
  262.5 40.6 %copy-start.143 = (f32[512,16]{0,1:T(8,128)}, f32[512,16]{0,1:T(8,128)S(1)}, u32[]{:S(2)}) copy-start(f32[512,16]{0,1:T(8,128)S(1)} %get-tuple-element.214) | copy-start | bytes 98308
  264.9 62.7 %copy-start.177 = (f32[2,256,16]{1,2,0:T(8,128)}, f32[2,256,16]{1,2,0:T(8,128)S(1)}, u32[]{:S(2)}) copy-start(f32[2,256,16]{1,2,0:T(8,128)S(1)} %get-tuple-element.273) | copy-start | bytes 98308
  284.0 43.6 %copy-start.11 = (f32[2,256,16,64]{1,0,3,2:T(2,128)}, f32[2,256,16,64]{1,0,3,2:T(2,128)S(1)}, u32[]{:S(2)}) copy-start(f32[2,256,16,64]{1,0,3,2:T(2,128)S(1)} %reshape.979) | copy-start | bytes 6291460
  288.9 212.9 %all-gather.19.cloned.1.call-start = ((), (), s32[]{:S(2)}) async-start(), calls=%async_computation.2 | async-start | bytes 2621440 | tf_op jit(solution)/shard_map/all_gather | solution.py:256
  290.3 106.9 %collective-permute-start.6 = (f32[3]{0:T(128)}, f32[3]{0:T(128)}, u32[]{:S(2)}, u32[]{:S(2)}) collective-permute-start(f32[3]{0:T(128)} %slice.682), channel_id=1, source_target_pairs={{0,4},{4,8},{8,12},{1,5},{5,9},{9,13},{2,6},{6,10},{10,14},{3,7},{... | collective-permute-start | bytes 44 | tf_op jit(solution)/shard_map/ppermute | solution.py:251
  357.3 35.6 %copy-start.108 = (f32[1,128,2048]{2,1,0:T(8,128)S(1)}, f32[1,128,2048]{2,1,0:T(8,128)}, u32[]{:S(2)}) copy-start(f32[1,128,2048]{2,1,0:T(8,128)} %constant_dynamic-slice_fusion.3) | copy-start | bytes 3145732
  395.7 3.8 collective-permute-start.5
  397.1 28.4 %copy-start.384 = (f32[2]{0:T(128)}, f32[2]{0:T(128)S(1)}, u32[]{:S(2)}) copy-start(f32[2]{0:T(128)S(1)} %fusion.364) | copy-start | bytes 28
  398.6 31.2 %copy-start.246 = (f32[512]{0:T(512)}, f32[512]{0:T(512)S(1)}, u32[]{:S(2)}) copy-start(f32[512]{0:T(512)S(1)} %get-tuple-element.280) | copy-start | bytes 6148
  398.6 31.2 %copy-start.248 = (f32[512]{0:T(512)}, f32[512]{0:T(512)S(1)}, u32[]{:S(2)}) copy-start(f32[512]{0:T(512)S(1)} %get-tuple-element.281) | copy-start | bytes 6148
  398.6 31.2 %copy-start.250 = (f32[512]{0:T(512)}, f32[512]{0:T(512)S(1)}, u32[]{:S(2)}) copy-start(f32[512]{0:T(512)S(1)} %get-tuple-element.282) | copy-start | bytes 6148
  419.7 9.8 collective-permute-start.7
  439.5 167.8 %copy-start.14 = (f32[2,256,16,64]{1,0,3,2:T(2,128)}, f32[2,256,16,64]{1,0,3,2:T(2,128)S(1)}, u32[]{:S(2)}) copy-start(f32[2,256,16,64]{1,0,3,2:T(2,128)S(1)} %reshape.991) | copy-start | bytes 6291460
  442.5 59.3 %copy-start.68 = (f32[2,16,64,128]{3,2,1,0:T(8,128)}, f32[2,16,64,128]{3,2,1,0:T(8,128)S(1)}, u32[]{:S(2)}) copy-start(f32[2,16,64,128]{3,2,1,0:T(8,128)S(1)} %fusion.146) | copy-start | bytes 3145732
  443.7 162.1 %all-gather.21.cloned.1.call-start = ((), (), s32[]{:S(2)}) async-start(), calls=%async_computation.3 | async-start | bytes 1310720 | tf_op jit(solution)/shard_map/all_gather | solution.py:274
  557.2 246.9 %all-gather.23.cloned.1.call-start = ((), (), s32[]{:S(2)}) async-start(), calls=%async_computation.4 | async-start | bytes 1310720 | tf_op jit(solution)/shard_map/all_gather | solution.py:274
  627.9 27.3 %copy-start.214 = (f32[1280]{0:T(1024)}, f32[1280]{0:T(1024)S(1)}, u32[]{:S(2)}) copy-start(f32[1280]{0:T(1024)S(1)} %get-tuple-element.135) | copy-start | bytes 15364
  637.9 18.0 %collective-permute-start.8 = (f32[3,1280]{1,0:T(4,128)}, f32[3,1280]{1,0:T(4,128)}, u32[]{:S(2)}, u32[]{:S(2)}) collective-permute-start(f32[3,1280]{1,0:T(4,128)} %copy.559), channel_id=1, source_target_pairs={{4,0},{8,4},{12,8},{5,1},{9,5},{13,9},{6,2},{10,6},{14,10},{7,3},{... | collective-permute-start | bytes 46088 | tf_op jit(solution)/shard_map/ppermute | solution.py:251
  676.9 26.5 %collective-permute-start.9 = (bf16[128,2048]{1,0:T(8,128)(2,1)S(1)}, bf16[128,2048]{1,0:T(8,128)(2,1)S(1)}, u32[]{:S(2)}, u32[]{:S(2)}) collective-permute-start(bf16[128,2048]{1,0:T(8,128)(2,1)S(1)} %get-tuple-element.193), channel_id=1, source_target_pairs={{16,0},{17,1},{18,2},{19,3},{20,4},{21,5},{22,6},{23,7},{24,8},{25... | collective-permute-start | bytes 1572872 | tf_op jit(solution)/shard_map/ppermute | solution.py:251
  691.6 48.9 %copy-start.319 = (f32[512]{0:T(512)S(1)}, f32[512]{0:T(512)}, u32[]{:S(2)}) copy-start(f32[512]{0:T(512)} %copy-done.318) | copy-start | bytes 6148
  773.4 250.0 %all-gather.25.cloned.1.call-start = ((), (), s32[]{:S(2)}) async-start(), calls=%async_computation.5 | async-start | bytes 1310720 | tf_op jit(solution)/shard_map/all_gather | solution.py:274
  826.4 25.9 %copy-start.216 = (f32[1280]{0:T(1024)}, f32[1280]{0:T(1024)S(1)}, u32[]{:S(2)}) copy-start(f32[1280]{0:T(1024)S(1)} %get-tuple-element.136) | copy-start | bytes 15364
  836.3 16.6 %collective-permute-start.10 = (f32[3,1280]{1,0:T(4,128)}, f32[3,1280]{1,0:T(4,128)}, u32[]{:S(2)}, u32[]{:S(2)}) collective-permute-start(f32[3,1280]{1,0:T(4,128)} %copy.582), channel_id=1, source_target_pairs={{4,0},{8,4},{12,8},{5,1},{9,5},{13,9},{6,2},{10,6},{14,10},{7,3},{... | collective-permute-start | bytes 46088 | tf_op jit(solution)/shard_map/ppermute | solution.py:251
  867.0 40.9 %copy-start.27 = (f32[128,2048]{1,0:T(8,128)S(1)}, f32[128,2048]{1,0:T(8,128)}, u32[]{:S(2)}) copy-start(f32[128,2048]{1,0:T(8,128)} %copy-done.26) | copy-start | bytes 3145732
  867.1 40.9 %copy-start.352 = (f32[128]{0:T(128)S(1)}, f32[128]{0:T(128)}, u32[]{:S(2)}) copy-start(f32[128]{0:T(128)} %copy-done.351) | copy-start | bytes 1540
  867.1 43.1 %copy-start.70 = (bf16[2,128,2048]{2,1,0:T(8,128)(2,1)S(1)}, bf16[2,128,2048]{2,1,0:T(8,128)(2,1)}, u32[]{:S(2)}) copy-start(bf16[2,128,2048]{2,1,0:T(8,128)(2,1)} %param.20) | copy-start | bytes 3145732
  867.1 43.1 %copy-start.134 = (bf16[128,2048]{1,0:T(8,128)(2,1)S(1)}, bf16[128,2048]{1,0:T(8,128)(2,1)}, u32[]{:S(2)}) copy-start(bf16[128,2048]{1,0:T(8,128)(2,1)} %copy-done.133) | copy-start | bytes 1572868
  867.1 43.1 %copy-start.393 = (f32[128]{0:T(128)S(1)}, f32[128]{0:T(128)}, u32[]{:S(2)}) copy-start(f32[128]{0:T(128)} %get-tuple-element.333) | copy-start | bytes 1540
  911.6 14.7 %collective-permute-start.11 = (bf16[128,2048]{1,0:T(8,128)(2,1)S(1)}, bf16[128,2048]{1,0:T(8,128)(2,1)S(1)}, u32[]{:S(2)}, u32[]{:S(2)}) collective-permute-start(bf16[128,2048]{1,0:T(8,128)(2,1)S(1)} %get-tuple-element.189), channel_id=1, source_target_pairs={{16,0},{17,1},{18,2},{19,3},{20,4},{21,5},{22,6},{23,7},{24,8},{25... | collective-permute-start | bytes 1572872 | tf_op jit(solution)/shard_map/ppermute | solution.py:251
  926.4 30.3 %copy-start.317 = (f32[512]{0:T(512)S(1)}, f32[512]{0:T(512)}, u32[]{:S(2)}) copy-start(f32[512]{0:T(512)} %copy-done.316) | copy-start | bytes 6148
  997.3 133.2 %all-reduce.69.cloned.1.call-start = ((), (), s32[]{:S(2)}) async-start(), calls=%async_computation.6 | async-start | bytes 8388608 | tf_op jit(solution)/shard_map/psum | solution.py:747
  1012.2 148.9 %all-gather.27.cloned.1.call-start = ((), (), s32[]{:S(2)}) async-start(), calls=%async_computation.7 | async-start | bytes 1331200 | tf_op jit(solution)/shard_map/all_gather | solution.py:617
  1057.5 12.9 collective-permute-start.12
  1086.9 47.8 %copy-start.150 = (bf16[512,1024]{0,1:T(8,128)(2,1)S(1)}, bf16[512,1024]{0,1:T(8,128)(2,1)}, u32[]{:S(2)}) copy-start(bf16[512,1024]{0,1:T(8,128)(2,1)} %get-tuple-element.231) | copy-start | bytes 3145732
  1086.9 47.8 %copy-start.321 = (bf16[512,16]{0,1:T(8,128)(2,1)S(1)}, bf16[512,16]{0,1:T(8,128)(2,1)}, u32[]{:S(2)}) copy-start(bf16[512,16]{0,1:T(8,128)(2,1)} %get-tuple-element.183) | copy-start | bytes 49156
  1134.2 225.8 %all-reduce.71.cloned.1.call-start = ((), (), s32[]{:S(2)}) async-start(), calls=%async_computation.8 | async-start | bytes 16908288 | tf_op jit(solution)/shard_map/psum | solution.py:622
  1240.7 30.4 %copy-start.53 = (bf16[2,128,2048]{2,1,0:T(8,128)(2,1)S(1)}, bf16[2,128,2048]{2,1,0:T(8,128)(2,1)}, u32[]{:S(2)}) copy-start(bf16[2,128,2048]{2,1,0:T(8,128)(2,1)} %param.19) | copy-start | bytes 3145732
  1240.7 30.4 %copy-start.160 = (f32[1,2048]{1,0:T(1,128)S(1)}, f32[1,2048]{1,0:T(1,128)}, u32[]{:S(2)}) copy-start(f32[1,2048]{1,0:T(1,128)} %param.23) | copy-start | bytes 24580
  1240.7 30.4 %copy-start.338 = (f32[128]{0:T(128)S(1)}, f32[128]{0:T(128)}, u32[]{:S(2)}) copy-start(f32[128]{0:T(128)} %copy-done.337) | copy-start | bytes 1540
  1240.7 32.0 %copy-start.268 = (f32[2048]{0:T(1024)S(1)}, f32[2048]{0:T(1024)}, u32[]{:S(2)}) copy-start(f32[2048]{0:T(1024)} %get-tuple-element.141) | copy-start | bytes 24580
  1240.7 32.0 %copy-start.269 = (f32[2048]{0:T(1024)S(1)}, f32[2048]{0:T(1024)}, u32[]{:S(2)}) copy-start(f32[2048]{0:T(1024)} %get-tuple-element.143) | copy-start | bytes 24580
  1240.7 72.4 %copy-start.392 = (f32[128]{0:T(128)S(1)}, f32[128]{0:T(128)}, u32[]{:S(2)}) copy-start(f32[128]{0:T(128)} %get-tuple-element.331) | copy-start | bytes 1540
  (365 other events, 2153.1 us)
Sparse Core Ops, SparseCore 0:
  95.7 33.5 all-gather.14
  289.1 34.7 all-gather.16
  443.8 57.9 all-gather.18
  557.3 48.4 all-gather.20
  773.5 30.5 all-gather.22
  997.4 25.8 all-gather.24
  1026.6 103.8 all-reduce.68
  1134.3 26.7 all-gather.26
  1184.6 175.3 all-reduce.70

commit v16 on v15

--- a/solution.py
+++ b/solution.py
@@ -242,7 +242,7 @@
 
 norm_eps = 1e-05
 far_below = -1e30
-highest = lax.Precision.HIGH
+highest = lax.Precision.DEFAULT
 
 
 def shifted(value, axis, by):

time: 1390 us -> 1380 us (level)
  matrix products: 254 us -> 231 us
  waiting for transfers between devices: 136 us -> 151 us
    unnamed x830 -> x876, local copies, waits for them, and re-layouts: 63 us -> 66.6 us
  transfers between devices with their start and end apart: 22 -> 22, of which waited for: 11 -> 11; matrix products, arithmetic and copies ran while one was open for 24% -> 23% of each run, Pallas kernels for 11% -> 11%
where the time goes in v16:
time: 1380 us; the launch traced here: 1370 us
  Pallas kernels  337 us (24%)
  other arithmetic  253 us (18%)
  matrix products  231 us (17%)
  local copies, waits for them, and re-layouts  174 us (13%)
  blocking collectives  165 us (12%)
  waiting for transfers between devices  151 us (11%)
  starting transfers between devices  34.8 us (3%)
  between operations  22 us (2%)
    pallas_call x7, Pallas kernels, head_gather(): pl.pallas_call(functools.partial(gather_body, n, tick), out_shape=jax.Sha...  171 us
    pallas_call x7, Pallas kernels, head_scatter(): pl.pallas_call(functools.partial(scatter_body, n, tick), out_shape=jax.Sh...  166 us
    unnamed x876, local copies, waits for them, and re-layouts  66.6 us
    all_gather x3, waiting for transfers between devices, entering(): everything = jax.tree.map(lambda part: lax.all_gather(part, axis), value)  50.2 us
    all_gather x3, waiting for transfers between devices, entering_2(): lax.all_gather(a.astype(kind), axis)  48.2 us
    dot_general x9, matrix products, block_output(): jnp.einsum('cijh,cjhp->cihp', weights, x_blocks, precision=lax.Precision....  43.7 us
    psum x1, blocking collectives, reduce_grads(): norm_sum = lax.psum(norm_part, ('seq', 'head'))  40.1 us
    dot_general x3, matrix products, mixer_forward(): projected = jnp.dot(gathered, w_main, preferred_element_type=jnp.float32)  38.1 us
  transfers between devices with their start and end apart: 22, of which 11 were waited for; matrix products, arithmetic and copies ran while one was open for 23% of the time, Pallas kernels for 11%

profile of v16, /device:TPU:0, one launch (start us, length us, event | category | flops | bytes accessed | tf_op | source)
XLA Modules:
  0.0 1368.2 jit_solution(12315975264350829407)
XLA Ops:
  20.4 29.3 %shard_map.297 = bf16[4,128,2048]{2,1,0:T(8,128)(2,1)} custom-call(bf16[128,2048]{1,0:T(8,128)(2,1)} %fusion.219.x_ref), custom_call_target="tpu_custom_call" | custom-call | tf_op jit(solution)/shard_map/pallas_call | solution.py:113
  50.0 12.7 fusion.412
  93.6 6.6 all-gather.1
  107.4 19.8 %all-gather.15.cloned.1.call-done = f32[4,16,64,128]{3,2,1,0:T(8,128)} async-done(((f32[1,16,64,128]{3,2,1,0:T(8,128)}), f32[4,16,64,128]{3,2,1,0:T(8,128)}) %all-gather.15.cloned.1.call-update) | async-done | bytes 2097168 | tf_op jit(solution)/shard_map/all_gather | solution.py:256
  137.8 11.7 psum.119
  151.1 6.9 fusion.40.p_ref
  158.0 28.0 %shard_map.298 = f32[128,2048]{1,0:T(8,128)} custom-call(f32[4,128,2048]{2,1,0:T(8,128)} %fusion.40.p_ref), custom_call_target="tpu_custom_call" | custom-call | tf_op jit(solution)/shard_map/pallas_call | solution.py:224
  194.4 43.4 %shard_map.299 = bf16[4,128,2048]{2,1,0:T(8,128)(2,1)} custom-call(bf16[128,2048]{1,0:T(8,128)(2,1)} %multiply_convert_fusion.7.x_ref), custom_call_target="tpu_custom_call" | custom-call | tf_op jit(solution)/shard_map/pallas_call | solution.py:113
  237.8 12.9 fusion.411
  266.5 9.3 fusion.112
  291.1 6.6 all-gather.2
  302.0 17.2 %all-gather.17.cloned.1.call-done = f32[4,16,64,128]{3,2,1,0:T(8,128)} async-done(((f32[1,16,64,128]{3,2,1,0:T(8,128)}), f32[4,16,64,128]{3,2,1,0:T(8,128)}) %all-gather.17.cloned.1.call-update) | async-done | bytes 2097168 | tf_op jit(solution)/shard_map/all_gather | solution.py:256
  329.8 11.7 psum.120
  345.1 6.9 fusion.38.p_ref
  351.9 35.4 %shard_map.300 = f32[128,2048]{1,0:T(8,128)} custom-call(f32[4,128,2048]{2,1,0:T(8,128)} %fusion.38.p_ref), custom_call_target="tpu_custom_call" | custom-call | tf_op jit(solution)/shard_map/pallas_call | solution.py:224
  398.9 12.5 fusion.410
  436.6 7.9 all-gather.6
  450.2 7.0 all-gather.5
  458.4 7.8 all-gather.4
  466.2 7.4 all-gather.3
  481.5 13.2 all-gather.19.cloned.1.call-done
  506.5 11.7 psum.121
  518.2 7.9 multiply_reduce_fusion.20
  526.1 8.3 psum.122
  534.5 6.9 multiply_reduce_fusion.23
  549.1 8.0 fusion.30
  561.9 5.7 fusion.449
  567.6 28.1 %all-gather.21.cloned.1.call-done = bf16[4,16,64,128]{3,2,1,0:T(8,128)(2,1)} async-done(((bf16[1,16,64,128]{3,2,1,0:T(8,128)(2,1)}), bf16[4,16,64,128]{3,2,1,0:T(8,128)(2,1)}) %all-gather.21.cloned.1.call-update) | async-done | bytes 1048592 | tf_op jit(solution)/shard_map/all_gather | solution.py:274
  609.4 6.7 multiply_reduce_fusion.13
  666.8 11.2 fusion.246
  680.2 11.8 collective-permute-done.9
  693.8 35.4 %shard_map.305 = bf16[4,128,2048]{2,1,0:T(8,128)(2,1)} custom-call(bf16[128,2048]{1,0:T(8,128)(2,1)} %fusion.237.x_ref), custom_call_target="tpu_custom_call" | custom-call | tf_op jit(solution)/shard_map/pallas_call | solution.py:113
  729.2 8.0 multiply_reduce_fusion.19
  737.2 10.5 psum.123
  747.8 6.1 multiply_reduce_fusion.22
  761.6 8.3 fusion.32
  774.6 5.7 fusion.450
  780.3 11.9 all-gather.23.cloned.1.call-done
  805.5 6.8 multiply_reduce_fusion.9
  854.3 40.9 %shard_map.306 = f32[128,2048]{1,0:T(8,128)} custom-call(f32[4,128,2048]{2,1,0:T(8,128)} %bitcast.977), custom_call_target="tpu_custom_call" | custom-call | tf_op jit(solution)/shard_map/pallas_call | solution.py:224
  900.5 11.0 fusion.244
  915.4 28.6 %shard_map.307 = bf16[4,128,2048]{2,1,0:T(8,128)(2,1)} custom-call(bf16[128,2048]{1,0:T(8,128)(2,1)} %fusion.238.x_ref), custom_call_target="tpu_custom_call" | custom-call | tf_op jit(solution)/shard_map/pallas_call | solution.py:113
  944.0 8.0 multiply_reduce_fusion.18
  952.1 11.0 psum.124
  963.1 6.0 multiply_reduce_fusion.21
  972.8 7.9 fusion.34
  990.9 10.4 add_convert_fusion
  1001.9 8.2 all-gather.25.cloned.1.call-done
  1044.4 6.0 pad_add_fusion
  1059.2 6.2 concatenate.67
  1068.5 24.1 %shard_map.308 = f32[520,256]{1,0:T(8,128)} custom-call(f32[4,520,256]{2,1,0:T(8,128)} %bitcast.984), custom_call_target="tpu_custom_call" | custom-call | tf_op jit(solution)/shard_map/pallas_call | solution.py:224
  1092.6 24.7 %all-reduce.69.cloned.1.call-done = bf16[1024,2048]{1,0:T(8,128)(2,1)} async-done(((bf16[1024,2048]{1,0:T(8,128)(2,1)}), bf16[1024,2048]{1,0:T(8,128)(2,1)}) %all-reduce.69.cloned.1.call-update) | async-done | bytes 4194320 | tf_op jit(solution)/shard_map/psum | solution.py:747
  1121.3 6.0 fusion.242
  1127.3 5.9 copy-done.49
  1134.8 13.1 all-gather.27.cloned.1.call-done
  1149.8 21.5 %fusion.35 = (bf16[1,2048,1024]{1,2,0:T(8,128)(2,1)}, bf16[1,2048,1024]{1,2,0:T(8,128)(2,1)}) fusion(f32[2048,2064]{0,1:T(8,128)} %copy-done.49, f32[2048,2064]{0,1:T(8,128)} %fusion.244, f32[2048,2064]{0,1:T(8,128)} %fusion.246, f32[]{:T(128)S(6)} %convert_element_type.616, f32[]{:T(128)S(6)} %convert_element_type.615, f32[]{:T(128)S(6)} %convert_element_type.614, ...), kind=kLoop, calls=%fused_computation.59 | loop fusion | flops 29360128 | bytes 58720276 | tf_op jit(solution)/shard_map/broadcast_in_dim | solution.py:775
  1174.5 7.1 fusion.36.p_ref
  1196.2 16.8 %all-reduce.64 = (bf16[1,4,1024]{2,1,0:T(4,128)(2,1)S(1)}, bf16[1,1024]{1,0:T(2,128)(2,1)S(1)}, bf16[1,16]{1,0:T(2,128)(2,1)S(1)}, bf16[1,16]{1,0:T(2,128)(2,1)S...) all-reduce(bf16[1,4,1024]{2,1,0:T(4,128)(2,1)S(1)} %fusion.333, ...), channel_id=1, replica_groups=mesh['section'=2,'seq'=4,'head'=4] {'seq'}, use_global_device_ids=true, to_apply=%region_95.97 | all-reduce | flops 6192 | bytes 24768 | tf_op jit(solution)/shard_map/psum | solution.py:627
  1218.2 8.2 fusion.243
  1229.3 30.4 %shard_map.309 = f32[128,2048]{1,0:T(8,128)} custom-call(f32[4,128,2048]{2,1,0:T(8,128)} %bitcast.975), custom_call_target="tpu_custom_call" | custom-call | tf_op jit(solution)/shard_map/pallas_call | solution.py:224
  1261.2 40.1 %psum.125 = f32[1,2048]{1,0:T(1,128)} all-reduce(f32[1,2048]{1,0:T(1,128)S(1)} %bitcast.1094), channel_id=1, replica_groups=mesh['section'=2,'seq'=4,'head'=4] {'seq','head'}, use_global_device_ids=true, to_apply=%region_90.92 | all-reduce | flops 2048 | bytes 16384 | tf_op jit(solution)/shard_map/psum | solution.py:631
  1309.8 29.1 %shard_map.310 = f32[4,520,256]{2,1,0:T(8,128)} custom-call(f32[520,256]{1,0:T(8,128)} %add_add_fusion.4.x_ref), custom_call_target="tpu_custom_call" | custom-call | tf_op jit(solution)/shard_map/pallas_call | solution.py:113
  1346.7 6.9 copy.616
  1353.6 6.9 copy.617
  (1319 shorter events, 448.1 us)
Async XLA Ops:
  7.2 42.5 %copy-start.226 = (bf16[1,2048,16]{1,2,0:T(8,128)(2,1)S(1)}, bf16[1,2048,16]{1,2,0:T(8,128)(2,1)}, u32[]{:S(2)}) copy-start(bf16[1,2048,16]{1,2,0:T(8,128)(2,1)} %param.27) | copy-start | bytes 196612
  7.2 42.8 %copy-start.60 = (bf16[1,2048,256]{2,1,0:T(8,128)(2,1)S(1)}, bf16[1,2048,256]{2,1,0:T(8,128)(2,1)}, u32[]{:S(2)}) copy-start(bf16[1,2048,256]{2,1,0:T(8,128)(2,1)} %param.26) | copy-start | bytes 3145732
  7.2 120.0 %all-gather.15.cloned.1.call-start = ((), (), s32[]{:S(2)}) async-start(), calls=%async_computation | async-start | bytes 2621440 | tf_op jit(solution)/shard_map/all_gather | solution.py:256
  8.1 92.8 %copy-start.294 = (s32[1,512]{1,0:T(1,128)}, s32[1,512]{1,0:T(1,128)S(1)}, u32[]{:S(2)}) copy-start(s32[1,512]{1,0:T(1,128)S(1)} %get-tuple-element.283) | copy-start | bytes 6148
  8.2 71.2 %collective-permute-start = (f32[3]{0:T(128)S(1)}, f32[3]{0:T(128)S(1)}, u32[]{:S(2)}, u32[]{:S(2)}) collective-permute-start(f32[3]{0:T(128)S(1)} %slice.608), channel_id=1, source_target_pairs={{0,4},{4,8},{8,12},{1,5},{5,9},{9,13},{2,6},{6,10},{10,14},{3,7},{... | collective-permute-start | bytes 44 | tf_op jit(solution)/shard_map/ppermute | solution.py:251
  13.1 66.3 %collective-permute-start.3 = (f32[3]{0:T(128)S(1)}, f32[3]{0:T(128)S(1)}, u32[]{:S(2)}, u32[]{:S(2)}) collective-permute-start(f32[3]{0:T(128)S(1)} %slice.647), channel_id=1, source_target_pairs={{0,4},{4,8},{8,12},{1,5},{5,9},{9,13},{2,6},{6,10},{10,14},{3,7},{... | collective-permute-start | bytes 44 | tf_op jit(solution)/shard_map/ppermute | solution.py:251
  18.4 31.4 %copy-start.356 = (f32[128]{0:T(128)}, f32[128]{0:T(128)S(1)}, u32[]{:S(2)}) copy-start(f32[128]{0:T(128)S(1)} %get-tuple-element.332) | copy-start | bytes 1540
  65.5 15.4 %collective-permute-start.1 = (f32[3,1280]{1,0:T(4,128)S(1)}, f32[3,1280]{1,0:T(4,128)S(1)}, u32[]{:S(2)}, u32[]{:S(2)}) collective-permute-start(f32[3,1280]{1,0:T(4,128)S(1)} %copy.495), channel_id=1, source_target_pairs={{0,4},{4,8},{8,12},{1,5},{5,9},{9,13},{2,6},{6,10},{10,14},{3,7},{... | collective-permute-start | bytes 46088 | tf_op jit(solution)/shard_map/ppermute | solution.py:251
  91.6 38.6 %copy-start.9 = (f32[2,256,16,64]{1,0,3,2:T(2,128)}, f32[2,256,16,64]{1,0,3,2:T(2,128)S(1)}, u32[]{:S(2)}) copy-start(f32[2,256,16,64]{1,0,3,2:T(2,128)S(1)} %reshape.967) | copy-start | bytes 6291460
  92.3 36.8 %copy-start.65 = (f32[2,16,64,128]{3,2,1,0:T(8,128)}, f32[2,16,64,128]{3,2,1,0:T(8,128)S(1)}, u32[]{:S(2)}) copy-start(f32[2,16,64,128]{3,2,1,0:T(8,128)S(1)} %fusion.154) | copy-start | bytes 3145732
  93.5 225.6 %all-gather.17.cloned.1.call-start = ((), (), s32[]{:S(2)}) async-start(), calls=%async_computation.1 | async-start | bytes 2621440 | tf_op jit(solution)/shard_map/all_gather | solution.py:256
  158.0 29.6 %copy-start.51 = (bf16[2,128,2048]{2,1,0:T(8,128)(2,1)S(1)}, bf16[2,128,2048]{2,1,0:T(8,128)(2,1)}, u32[]{:S(2)}) copy-start(bf16[2,128,2048]{2,1,0:T(8,128)(2,1)} %param.19) | copy-start | bytes 3145732
  188.8 3.7 collective-permute-start.2
  191.8 70.1 %copy-start.279 = (f32[2,256]{1,0:T(2,128)}, f32[2,256]{1,0:T(2,128)S(1)}, u32[]{:S(2)}) copy-start(f32[2,256]{1,0:T(2,128)S(1)} %get-tuple-element.342) | copy-start | bytes 6148
  191.8 70.1 %copy-start.318 = (f32[2,256]{1,0:T(2,128)}, f32[2,256]{1,0:T(2,128)S(1)}, u32[]{:S(2)}) copy-start(f32[2,256]{1,0:T(2,128)S(1)} %get-tuple-element.343) | copy-start | bytes 6148
  192.5 74.0 %copy-start.258 = (f32[512]{0:T(512)}, f32[512]{0:T(512)S(1)}, u32[]{:S(2)}) copy-start(f32[512]{0:T(512)S(1)} %get-tuple-element.286) | copy-start | bytes 6148
  192.5 74.0 %copy-start.260 = (f32[512]{0:T(512)}, f32[512]{0:T(512)S(1)}, u32[]{:S(2)}) copy-start(f32[512]{0:T(512)S(1)} %get-tuple-element.287) | copy-start | bytes 6148
  192.5 74.0 %copy-start.262 = (f32[512]{0:T(512)}, f32[512]{0:T(512)S(1)}, u32[]{:S(2)}) copy-start(f32[512]{0:T(512)S(1)} %get-tuple-element.288) | copy-start | bytes 6148
  192.8 194.5 %copy-start.26 = (f32[128,2048]{1,0:T(8,128)}, f32[128,2048]{1,0:T(8,128)S(1)}, u32[]{:S(2)}) copy-start(f32[128,2048]{1,0:T(8,128)S(1)} %get-tuple-element.218) | copy-start | bytes 3145732
  193.5 57.3 %copy-start.384 = (f32[128]{0:T(128)}, f32[128]{0:T(128)S(1)}, u32[]{:S(2)}) copy-start(f32[128]{0:T(128)S(1)} %get-tuple-element.334) | copy-start | bytes 1540
  255.3 10.9 collective-permute-start.4
  259.5 38.1 %copy-start.119 = (f32[512,16]{0,1:T(8,128)}, f32[512,16]{0,1:T(8,128)S(1)}, u32[]{:S(2)}) copy-start(f32[512,16]{0,1:T(8,128)S(1)} %get-tuple-element.214) | copy-start | bytes 98308
  281.5 40.7 %copy-start.11 = (f32[2,256,16,64]{1,0,3,2:T(2,128)}, f32[2,256,16,64]{1,0,3,2:T(2,128)S(1)}, u32[]{:S(2)}) copy-start(f32[2,256,16,64]{1,0,3,2:T(2,128)S(1)} %reshape.979) | copy-start | bytes 6291460
  284.3 210.4 %all-gather.19.cloned.1.call-start = ((), (), s32[]{:S(2)}) async-start(), calls=%async_computation.2 | async-start | bytes 2621440 | tf_op jit(solution)/shard_map/all_gather | solution.py:256
  284.9 106.9 %collective-permute-start.6 = (f32[3]{0:T(128)}, f32[3]{0:T(128)}, u32[]{:S(2)}, u32[]{:S(2)}) collective-permute-start(f32[3]{0:T(128)} %slice.682), channel_id=1, source_target_pairs={{0,4},{4,8},{8,12},{1,5},{5,9},{9,13},{2,6},{6,10},{10,14},{3,7},{... | collective-permute-start | bytes 44 | tf_op jit(solution)/shard_map/ppermute | solution.py:251
  351.9 35.4 %copy-start.96 = (f32[1,128,2048]{2,1,0:T(8,128)S(1)}, f32[1,128,2048]{2,1,0:T(8,128)}, u32[]{:S(2)}) copy-start(f32[1,128,2048]{2,1,0:T(8,128)} %constant_dynamic-slice_fusion.3) | copy-start | bytes 3145732
  390.2 3.8 collective-permute-start.5
  391.8 28.2 %copy-start.408 = (f32[2]{0:T(128)}, f32[2]{0:T(128)S(1)}, u32[]{:S(2)}) copy-start(f32[2]{0:T(128)S(1)} %fusion.364) | copy-start | bytes 28
  393.3 30.9 %copy-start.264 = (f32[512]{0:T(512)}, f32[512]{0:T(512)S(1)}, u32[]{:S(2)}) copy-start(f32[512]{0:T(512)S(1)} %get-tuple-element.280) | copy-start | bytes 6148
  393.3 31.0 %copy-start.266 = (f32[512]{0:T(512)}, f32[512]{0:T(512)S(1)}, u32[]{:S(2)}) copy-start(f32[512]{0:T(512)S(1)} %get-tuple-element.281) | copy-start | bytes 6148
  393.3 31.0 %copy-start.268 = (f32[512]{0:T(512)}, f32[512]{0:T(512)S(1)}, u32[]{:S(2)}) copy-start(f32[512]{0:T(512)S(1)} %get-tuple-element.282) | copy-start | bytes 6148
  414.1 9.8 collective-permute-start.7
  434.7 162.7 %copy-start.14 = (f32[2,256,16,64]{1,0,3,2:T(2,128)}, f32[2,256,16,64]{1,0,3,2:T(2,128)S(1)}, u32[]{:S(2)}) copy-start(f32[2,256,16,64]{1,0,3,2:T(2,128)S(1)} %reshape.991) | copy-start | bytes 6291460
  435.3 59.4 %copy-start.68 = (f32[2,16,64,128]{3,2,1,0:T(8,128)}, f32[2,16,64,128]{3,2,1,0:T(8,128)S(1)}, u32[]{:S(2)}) copy-start(f32[2,16,64,128]{3,2,1,0:T(8,128)S(1)} %fusion.146) | copy-start | bytes 3145732
  436.5 159.3 %all-gather.21.cloned.1.call-start = ((), (), s32[]{:S(2)}) async-start(), calls=%async_computation.3 | async-start | bytes 1310720 | tf_op jit(solution)/shard_map/all_gather | solution.py:274
  548.9 243.3 %all-gather.23.cloned.1.call-start = ((), (), s32[]{:S(2)}) async-start(), calls=%async_computation.4 | async-start | bytes 1310720 | tf_op jit(solution)/shard_map/all_gather | solution.py:274
  561.9 33.9 %copy-start.353 = (f32[16]{0:T(128)S(1)}, f32[16]{0:T(128)}, u32[]{:S(2)}) copy-start(f32[16]{0:T(128)} %get-tuple-element.328) | copy-start | bytes 196
  561.9 33.9 %copy-start.372 = (f32[16]{0:T(128)S(1)}, f32[16]{0:T(128)}, u32[]{:S(2)}) copy-start(f32[16]{0:T(128)} %get-tuple-element.296) | copy-start | bytes 196
  561.9 33.9 %copy-start.374 = (f32[16]{0:T(128)S(1)}, f32[16]{0:T(128)}, u32[]{:S(2)}) copy-start(f32[16]{0:T(128)} %get-tuple-element.297) | copy-start | bytes 196
  561.9 33.9 %copy-start.404 = (f32[16]{0:T(128)S(1)}, f32[16]{0:T(128)}, u32[]{:S(2)}) copy-start(f32[16]{0:T(128)} %fusion.374) | copy-start | bytes 196
  626.0 18.6 %collective-permute-start.8 = (f32[3,1280]{1,0:T(4,128)}, f32[3,1280]{1,0:T(4,128)}, u32[]{:S(2)}, u32[]{:S(2)}) collective-permute-start(f32[3,1280]{1,0:T(4,128)} %copy.559), channel_id=1, source_target_pairs={{4,0},{8,4},{12,8},{5,1},{9,5},{13,9},{6,2},{10,6},{14,10},{7,3},{... | collective-permute-start | bytes 46088 | tf_op jit(solution)/shard_map/ppermute | solution.py:251
  665.5 26.5 %collective-permute-start.9 = (bf16[128,2048]{1,0:T(8,128)(2,1)S(1)}, bf16[128,2048]{1,0:T(8,128)(2,1)S(1)}, u32[]{:S(2)}, u32[]{:S(2)}) collective-permute-start(bf16[128,2048]{1,0:T(8,128)(2,1)S(1)} %get-tuple-element.193), channel_id=1, source_target_pairs={{16,0},{17,1},{18,2},{19,3},{20,4},{21,5},{22,6},{23,7},{24,8},{25... | collective-permute-start | bytes 1572872 | tf_op jit(solution)/shard_map/ppermute | solution.py:251
  680.2 49.0 %copy-start.333 = (f32[512]{0:T(512)S(1)}, f32[512]{0:T(512)}, u32[]{:S(2)}) copy-start(f32[512]{0:T(512)} %copy-done.332) | copy-start | bytes 6148
  761.5 248.6 %all-gather.25.cloned.1.call-start = ((), (), s32[]{:S(2)}) async-start(), calls=%async_computation.5 | async-start | bytes 1310720 | tf_op jit(solution)/shard_map/all_gather | solution.py:274
  822.3 17.8 %collective-permute-start.10 = (f32[3,1280]{1,0:T(4,128)}, f32[3,1280]{1,0:T(4,128)}, u32[]{:S(2)}, u32[]{:S(2)}) collective-permute-start(f32[3,1280]{1,0:T(4,128)} %copy.582), channel_id=1, source_target_pairs={{4,0},{8,4},{12,8},{5,1},{9,5},{13,9},{6,2},{10,6},{14,10},{7,3},{... | collective-permute-start | bytes 46088 | tf_op jit(solution)/shard_map/ppermute | solution.py:251
  854.2 40.9 %copy-start.27 = (f32[128,2048]{1,0:T(8,128)S(1)}, f32[128,2048]{1,0:T(8,128)}, u32[]{:S(2)}) copy-start(f32[128,2048]{1,0:T(8,128)} %copy-done.26) | copy-start | bytes 3145732
  854.2 40.9 %copy-start.385 = (f32[128]{0:T(128)S(1)}, f32[128]{0:T(128)}, u32[]{:S(2)}) copy-start(f32[128]{0:T(128)} %copy-done.384) | copy-start | bytes 1540
  854.2 43.1 %copy-start.70 = (bf16[2,128,2048]{2,1,0:T(8,128)(2,1)S(1)}, bf16[2,128,2048]{2,1,0:T(8,128)(2,1)}, u32[]{:S(2)}) copy-start(bf16[2,128,2048]{2,1,0:T(8,128)(2,1)} %param.20) | copy-start | bytes 3145732
  854.2 43.1 %copy-start.116 = (bf16[128,2048]{1,0:T(8,128)(2,1)S(1)}, bf16[128,2048]{1,0:T(8,128)(2,1)}, u32[]{:S(2)}) copy-start(bf16[128,2048]{1,0:T(8,128)(2,1)} %copy-done.115) | copy-start | bytes 1572868
  854.3 43.2 %copy-start.417 = (f32[128]{0:T(128)S(1)}, f32[128]{0:T(128)}, u32[]{:S(2)}) copy-start(f32[128]{0:T(128)} %get-tuple-element.333) | copy-start | bytes 1540
  898.8 14.8 %collective-permute-start.11 = (bf16[128,2048]{1,0:T(8,128)(2,1)S(1)}, bf16[128,2048]{1,0:T(8,128)(2,1)S(1)}, u32[]{:S(2)}, u32[]{:S(2)}) collective-permute-start(bf16[128,2048]{1,0:T(8,128)(2,1)S(1)} %get-tuple-element.189), channel_id=1, source_target_pairs={{16,0},{17,1},{18,2},{19,3},{20,4},{21,5},{22,6},{23,7},{24,8},{25... | collective-permute-start | bytes 1572872 | tf_op jit(solution)/shard_map/ppermute | solution.py:251
  913.6 30.4 %copy-start.331 = (f32[512]{0:T(512)S(1)}, f32[512]{0:T(512)}, u32[]{:S(2)}) copy-start(f32[512]{0:T(512)} %copy-done.330) | copy-start | bytes 6148
  984.1 133.2 %all-reduce.69.cloned.1.call-start = ((), (), s32[]{:S(2)}) async-start(), calls=%async_computation.6 | async-start | bytes 8388608 | tf_op jit(solution)/shard_map/psum | solution.py:747
  1001.4 146.5 %all-gather.27.cloned.1.call-start = ((), (), s32[]{:S(2)}) async-start(), calls=%async_computation.7 | async-start | bytes 1331200 | tf_op jit(solution)/shard_map/all_gather | solution.py:617
  1040.0 12.1 collective-permute-start.12
  1068.5 52.8 %copy-start.150 = (bf16[512,1024]{0,1:T(8,128)(2,1)S(1)}, bf16[512,1024]{0,1:T(8,128)(2,1)}, u32[]{:S(2)}) copy-start(bf16[512,1024]{0,1:T(8,128)(2,1)} %get-tuple-element.231) | copy-start | bytes 3145732
  1068.5 52.8 %copy-start.336 = (bf16[512,16]{0,1:T(8,128)(2,1)S(1)}, bf16[512,16]{0,1:T(8,128)(2,1)}, u32[]{:S(2)}) copy-start(bf16[512,16]{0,1:T(8,128)(2,1)} %get-tuple-element.183) | copy-start | bytes 49156
  1121.0 225.8 %all-reduce.71.cloned.1.call-start = ((), (), s32[]{:S(2)}) async-start(), calls=%async_computation.8 | async-start | bytes 16908288 | tf_op jit(solution)/shard_map/psum | solution.py:622
  1229.2 30.4 %copy-start.53 = (bf16[2,128,2048]{2,1,0:T(8,128)(2,1)S(1)}, bf16[2,128,2048]{2,1,0:T(8,128)(2,1)}, u32[]{:S(2)}) copy-start(bf16[2,128,2048]{2,1,0:T(8,128)(2,1)} %param.19) | copy-start | bytes 3145732
  1229.2 30.4 %copy-start.164 = (f32[1,2048]{1,0:T(1,128)S(1)}, f32[1,2048]{1,0:T(1,128)}, u32[]{:S(2)}) copy-start(f32[1,2048]{1,0:T(1,128)} %param.23) | copy-start | bytes 24580
  1229.2 30.4 %copy-start.357 = (f32[128]{0:T(128)S(1)}, f32[128]{0:T(128)}, u32[]{:S(2)}) copy-start(f32[128]{0:T(128)} %copy-done.356) | copy-start | bytes 1540
  1229.2 32.0 %copy-start.283 = (f32[2048]{0:T(1024)S(1)}, f32[2048]{0:T(1024)}, u32[]{:S(2)}) copy-start(f32[2048]{0:T(1024)} %get-tuple-element.141) | copy-start | bytes 24580
  1229.2 32.0 %copy-start.284 = (f32[2048]{0:T(1024)S(1)}, f32[2048]{0:T(1024)}, u32[]{:S(2)}) copy-start(f32[2048]{0:T(1024)} %get-tuple-element.143) | copy-start | bytes 24580
  1229.2 72.1 %copy-start.416 = (f32[128]{0:T(128)S(1)}, f32[128]{0:T(128)}, u32[]{:S(2)}) copy-start(f32[128]{0:T(128)} %get-tuple-element.331) | copy-start | bytes 1540
  (388 other events, 2331.4 us)
Sparse Core Ops, SparseCore 0:
  93.6 33.5 all-gather.14
  284.4 34.7 all-gather.16
  436.6 57.9 all-gather.18
  549.0 46.7 all-gather.20
  761.6 30.5 all-gather.22
  984.2 25.8 all-gather.24
  1013.4 103.8 all-reduce.68
  1121.1 26.7 all-gather.26
  1171.4 175.3 all-reduce.70

commit v17 on v16

--- a/solution.py
+++ b/solution.py
@@ -550,9 +550,6 @@
     grad_bc = grad_pre[:, inner_width:]
     grad_low = jnp.concatenate([grad_gate, grad_inner, grad_dt_pre.astype(jnp.bfloat16)], axis=1)
     w_bc_float = w_bc.astype(jnp.float32)
-    g_low = lax.dot_general(
-        gathered, grad_low, (((0,), (0,)), ((), ())), preferred_element_type=jnp.float32
-    )
     g_w_bc = lax.dot_general(
         gathered,
         grad_bc.astype(jnp.bfloat16),
@@ -584,9 +581,6 @@
         - stream * scale_in**3 * jnp.mean(weighted_in * stream, axis=-1, keepdims=True)
     )
     head_part = (
-        g_low[:, :inner_width],
-        g_low[:, inner_width : 2 * inner_width],
-        g_low[:, 2 * inner_width :],
         g_conv_w[:, :inner_width],
         g_conv_b[:inner_width],
         g_dt_bias,
@@ -595,7 +589,7 @@
         g_gate_gain,
     )
     shared_part = (g_norm_gain, g_w_bc, g_conv_w[:, inner_width:], g_conv_b[inner_width:])
-    return (grad_stream, head_part, shared_part, g_w_out)
+    return (grad_stream, head_part, shared_part, g_w_out, (gathered, grad_low))
 
 
 def pack_rows(members, width, multiple):
@@ -708,6 +702,7 @@
     input_grads = jnp.zeros((micro_count,) + row_shape, jnp.float32)
     head_count = lax.axis_size("head")
     bc_box = []
+    low_pairs = []
     head_total = ()
     shared_total = ()
     for tick_index in range(tick_count):
@@ -730,7 +725,7 @@
                 bc_box.append((part, [member.shape for member in totals]))
                 return part[0, 0] * 0.0
 
-        grad_stream, head_part, shared_part, out_part = mixer_backward(
+        grad_stream, head_part, shared_part, out_part, low_pair = mixer_backward(
             grad_next,
             layer_weights,
             saved,
@@ -745,6 +740,7 @@
             out_total = out_total + out_part
         if tick_index + 1 == tick_count:
             out_total = lax.psum(out_total.astype(jnp.bfloat16), "seq")
+        low_pairs.append((low_pair[0], low_pair[1] * is_valid.astype(low_pair[1].dtype)))
         head_part = tuple((member * mask_value for member in head_part))
         shared_part = tuple((member * mask_value for member in shared_part))
         if tick_index == 0:
@@ -760,8 +756,19 @@
             back_arrived = shifted(grad_stream.astype(jnp.bfloat16), "section", -1).astype(
                 grad_stream.dtype
             )
+    inner_width = w_out.shape[1]
+    g_low = lax.dot_general(
+        jnp.concatenate([pair[0] for pair in low_pairs], axis=0),
+        jnp.concatenate([pair[1] for pair in low_pairs], axis=0),
+        (((0,), (0,)), ((), ())),
+        preferred_element_type=jnp.float32,
+    )
     anchor = out_total[0, 0].astype(jnp.float32) * 0.0
-    head_total = (head_total[0] + anchor,) + head_total[1:]
+    head_total = (
+        g_low[:, :inner_width] + anchor,
+        g_low[:, inner_width : 2 * inner_width],
+        g_low[:, 2 * inner_width :],
+    ) + head_total
     bc_part, bc_shapes = bc_box[0]
     bc_part = bc_part + anchor
     head_total, norm_sum, bc_rows = reduce_grads(head_total, shared_total[0], bc_part, tick_count)

time: 1380 us -> 1360 us (0.986)
    broadcast_in_dim x1, other arithmetic: 21.5 us -> 6.66 us  [on_device(): head_total[0][None]]
    dot_general x3 -> x1, matrix products: 28.2 us -> 21.6 us  [on_device(): lax.dot_general(jnp.concatenate([pair[0] for pair in low_pairs], axis=0),...]
    unnamed x876 -> x910, local copies, waits for them, and re-layouts: 66.6 us -> 61.2 us
  transfers between devices with their start and end apart: 22 -> 22, of which waited for: 11 -> 10; matrix products, arithmetic and copies ran while one was open for 23% -> 23% of each run, Pallas kernels for 11% -> 11%
where the time goes in v17:
time: 1360 us; the launch traced here: 1350 us
  Pallas kernels  344 us (25%)
  other arithmetic  242 us (18%)
  matrix products  224 us (16%)
  local copies, waits for them, and re-layouts  172 us (13%)
  blocking collectives  163 us (12%)
  waiting for transfers between devices  145 us (11%)
  starting transfers between devices  34.5 us (3%)
  between operations  22.1 us (2%)
    pallas_call x7, Pallas kernels, head_gather(): pl.pallas_call(functools.partial(gather_body, n, tick), out_shape=jax.Sha...  178 us
    pallas_call x7, Pallas kernels, head_scatter(): pl.pallas_call(functools.partial(scatter_body, n, tick), out_shape=jax.Sh...  166 us
    unnamed x910, local copies, waits for them, and re-layouts  61.2 us
    all_gather x3, waiting for transfers between devices, entering(): everything = jax.tree.map(lambda part: lax.all_gather(part, axis), value)  50.2 us
    all_gather x3, waiting for transfers between devices, entering_2(): lax.all_gather(a.astype(kind), axis)  44.6 us
    dot_general x9, matrix products, block_output(): jnp.einsum('cijh,cjhp->cihp', weights, x_blocks, precision=lax.Precision....  43.4 us
    psum x1, blocking collectives, reduce_grads(): norm_sum = lax.psum(norm_part, ('seq', 'head'))  40.3 us
    dot_general x3, matrix products, mixer_forward(): projected = jnp.dot(gathered, w_main, preferred_element_type=jnp.float32)  38.1 us
  transfers between devices with their start and end apart: 22, of which 10 were waited for; matrix products, arithmetic and copies ran while one was open for 23% of the time, Pallas kernels for 11%

profile of v17, /device:TPU:0, one launch (start us, length us, event | category | flops | bytes accessed | tf_op | source)
XLA Modules:
  0.0 1347.7 jit_solution(9132129885146448204)
XLA Ops:
  20.4 29.3 %shard_map.297 = bf16[4,128,2048]{2,1,0:T(8,128)(2,1)} custom-call(bf16[128,2048]{1,0:T(8,128)(2,1)} %fusion.223.x_ref), custom_call_target="tpu_custom_call" | custom-call | tf_op jit(solution)/shard_map/pallas_call | solution.py:113
  50.0 12.7 fusion.407
  93.6 6.6 all-gather.1
  107.3 19.9 %all-gather.15.cloned.1.call-done = f32[4,16,64,128]{3,2,1,0:T(8,128)} async-done(((f32[1,16,64,128]{3,2,1,0:T(8,128)}), f32[4,16,64,128]{3,2,1,0:T(8,128)}) %all-gather.15.cloned.1.call-update) | async-done | bytes 2097168 | tf_op jit(solution)/shard_map/all_gather | solution.py:256
  137.8 11.7 psum.119
  151.1 6.9 fusion.45.p_ref
  158.0 28.0 %shard_map.298 = f32[128,2048]{1,0:T(8,128)} custom-call(f32[4,128,2048]{2,1,0:T(8,128)} %fusion.45.p_ref), custom_call_target="tpu_custom_call" | custom-call | tf_op jit(solution)/shard_map/pallas_call | solution.py:224
  194.3 43.4 %shard_map.299 = bf16[4,128,2048]{2,1,0:T(8,128)(2,1)} custom-call(bf16[128,2048]{1,0:T(8,128)(2,1)} %multiply_convert_fusion.7.x_ref), custom_call_target="tpu_custom_call" | custom-call | tf_op jit(solution)/shard_map/pallas_call | solution.py:113
  237.7 12.9 fusion.406
  266.3 9.2 fusion.116
  290.8 6.6 all-gather.2
  301.7 17.1 %all-gather.17.cloned.1.call-done = f32[4,16,64,128]{3,2,1,0:T(8,128)} async-done(((f32[1,16,64,128]{3,2,1,0:T(8,128)}), f32[4,16,64,128]{3,2,1,0:T(8,128)}) %all-gather.17.cloned.1.call-update) | async-done | bytes 2097168 | tf_op jit(solution)/shard_map/all_gather | solution.py:256
  329.5 11.7 psum.120
  344.7 6.9 fusion.43.p_ref
  351.6 35.4 %shard_map.300 = f32[128,2048]{1,0:T(8,128)} custom-call(f32[4,128,2048]{2,1,0:T(8,128)} %fusion.43.p_ref), custom_call_target="tpu_custom_call" | custom-call | tf_op jit(solution)/shard_map/pallas_call | solution.py:224
  398.5 12.5 fusion.405
  436.3 7.9 all-gather.6
  450.0 7.0 all-gather.5
  458.2 7.8 all-gather.4
  465.9 7.5 all-gather.3
  481.2 13.2 all-gather.19.cloned.1.call-done
  506.2 11.7 psum.121
  517.9 7.9 multiply_reduce_fusion.20
  525.8 8.3 psum.122
  534.2 6.8 multiply_reduce_fusion.23
  548.8 8.0 fusion.35
  561.5 5.7 fusion.445
  567.3 28.2 %all-gather.21.cloned.1.call-done = bf16[4,16,64,128]{3,2,1,0:T(8,128)(2,1)} async-done(((bf16[1,16,64,128]{3,2,1,0:T(8,128)(2,1)}), bf16[4,16,64,128]{3,2,1,0:T(8,128)(2,1)}) %all-gather.21.cloned.1.call-update) | async-done | bytes 1048592 | tf_op jit(solution)/shard_map/all_gather | solution.py:274
  609.1 6.7 multiply_reduce_fusion.13
  630.3 5.4 reduce-window.115
  650.1 5.2 fusion.248
  670.7 21.1 %collective-permute-done.9 = bf16[128,2048]{1,0:T(8,128)(2,1)S(1)} collective-permute-done((bf16[128,2048]{1,0:T(8,128)(2,1)S(1)}, bf16[128,2048]{1,0:T(8,128)(2,1)S(1)}, u32[]{:S(2)}, u32[]{:S(2)}) %collective-permute-start.9) | collective-permute-done | bytes 524320 | tf_op jit(solution)/shard_map/ppermute | solution.py:251
  693.5 42.3 %shard_map.305 = bf16[4,128,2048]{2,1,0:T(8,128)(2,1)} custom-call(bf16[128,2048]{1,0:T(8,128)(2,1)} %fusion.241.x_ref), custom_call_target="tpu_custom_call" | custom-call | tf_op jit(solution)/shard_map/pallas_call | solution.py:113
  735.9 8.0 multiply_reduce_fusion.19
  743.9 9.8 psum.123
  753.7 6.0 multiply_reduce_fusion.22
  767.4 8.0 fusion.37
  779.9 5.7 fusion.446
  785.6 8.1 all-gather.23.cloned.1.call-done
  807.1 6.8 multiply_reduce_fusion.9
  828.5 5.2 reduce-window.119
  847.7 5.2 fusion.247
  855.8 40.9 %shard_map.306 = f32[128,2048]{1,0:T(8,128)} custom-call(f32[4,128,2048]{2,1,0:T(8,128)} %bitcast.974), custom_call_target="tpu_custom_call" | custom-call | tf_op jit(solution)/shard_map/pallas_call | solution.py:224
  908.8 28.7 %shard_map.307 = bf16[4,128,2048]{2,1,0:T(8,128)(2,1)} custom-call(bf16[128,2048]{1,0:T(8,128)(2,1)} %fusion.242.x_ref), custom_call_target="tpu_custom_call" | custom-call | tf_op jit(solution)/shard_map/pallas_call | solution.py:113
  937.5 8.0 multiply_reduce_fusion.18
  945.5 10.7 psum.124
  956.3 6.0 multiply_reduce_fusion.21
  966.0 7.9 fusion.39
  984.6 10.4 add_convert_fusion
  995.0 8.3 all-gather.25.cloned.1.call-done
  1017.6 7.0 multiply_reduce_fusion.5
  1039.9 6.0 pad_add_fusion
  1059.8 23.8 %shard_map.308 = f32[520,256]{1,0:T(8,128)} custom-call(f32[4,520,256]{2,1,0:T(8,128)} %bitcast.981), custom_call_target="tpu_custom_call" | custom-call | tf_op jit(solution)/shard_map/pallas_call | solution.py:224
  1086.7 23.8 %all-reduce.69.cloned.1.call-done = bf16[1024,2048]{1,0:T(8,128)(2,1)} async-done(((bf16[1024,2048]{1,0:T(8,128)(2,1)}), bf16[1024,2048]{1,0:T(8,128)(2,1)}) %all-reduce.69.cloned.1.call-update) | async-done | bytes 4194320 | tf_op jit(solution)/shard_map/psum | solution.py:742
  1114.2 21.6 %fusion.441 = (bf16[2048,2064]{0,1:T(8,128)(2,1)}, f32[2048,2064]{0,1:T(8,128)}) fusion(bf16[512,2048]{1,0:T(8,128)(2,1)S(1)} %bitcast.968, bf16[512,2048]{1,0:T(8,128)(2,1)} %bitcast.970, bf16[512,2048]{1,0:T(8,128)(2,1)} %bitcast.976, bf16[512,2064]{0,1:T(8,128)(2,1)} %broadcast_multiply_fusion.3, bf16[512,2064]{0,1:T(8,128)(2,1)} %broadcast_multiply_fusion.4, ...), kind=kOutput, calls=%fused_computation.841 | convolution fusion | flops 13027688448 | bytes 37994496 | tf_op jit(solution)/shard_map/dot_general | solution.py:760
  1143.9 6.7 fusion.40
  1154.5 7.1 fusion.41.p_ref
  1173.6 15.8 %all-reduce.64 = (bf16[1,4,1024]{2,1,0:T(4,128)(2,1)S(1)}, bf16[1,1024]{1,0:T(2,128)(2,1)S(1)}, bf16[1,16]{1,0:T(2,128)(2,1)S(1)}, bf16[1,16]{1,0:T(2,128)(2,1)S...) all-reduce(bf16[1,4,1024]{2,1,0:T(4,128)(2,1)S(1)} %fusion.330, ...), channel_id=1, replica_groups=mesh['section'=2,'seq'=4,'head'=4] {'seq'}, use_global_device_ids=true, to_apply=%region_95.97 | all-reduce | flops 6192 | bytes 24768 | tf_op jit(solution)/shard_map/psum | solution.py:621
  1194.7 8.1 fusion.246
  1205.5 30.4 %shard_map.309 = f32[128,2048]{1,0:T(8,128)} custom-call(f32[4,128,2048]{2,1,0:T(8,128)} %bitcast.972), custom_call_target="tpu_custom_call" | custom-call | tf_op jit(solution)/shard_map/pallas_call | solution.py:224
  1237.6 40.3 %psum.125 = f32[1,2048]{1,0:T(1,128)} all-reduce(f32[1,2048]{1,0:T(1,128)S(1)} %bitcast.1091), channel_id=1, replica_groups=mesh['section'=2,'seq'=4,'head'=4] {'seq','head'}, use_global_device_ids=true, to_apply=%region_90.92 | all-reduce | flops 2048 | bytes 16384 | tf_op jit(solution)/shard_map/psum | solution.py:625
  1287.1 29.2 %shard_map.310 = f32[4,520,256]{2,1,0:T(8,128)} custom-call(f32[520,256]{1,0:T(8,128)} %add_add_fusion.4.x_ref), custom_call_target="tpu_custom_call" | custom-call | tf_op jit(solution)/shard_map/pallas_call | solution.py:113
  1326.3 6.9 copy.616
  1333.2 6.9 copy.617
  (1355 shorter events, 437.1 us)
Async XLA Ops:
  7.2 42.5 %copy-start.228 = (bf16[1,2048,16]{1,2,0:T(8,128)(2,1)S(1)}, bf16[1,2048,16]{1,2,0:T(8,128)(2,1)}, u32[]{:S(2)}) copy-start(bf16[1,2048,16]{1,2,0:T(8,128)(2,1)} %param.27) | copy-start | bytes 196612
  7.2 42.8 %copy-start.61 = (bf16[1,2048,256]{2,1,0:T(8,128)(2,1)S(1)}, bf16[1,2048,256]{2,1,0:T(8,128)(2,1)}, u32[]{:S(2)}) copy-start(bf16[1,2048,256]{2,1,0:T(8,128)(2,1)} %param.26) | copy-start | bytes 3145732
  7.2 120.0 %all-gather.15.cloned.1.call-start = ((), (), s32[]{:S(2)}) async-start(), calls=%async_computation | async-start | bytes 2621440 | tf_op jit(solution)/shard_map/all_gather | solution.py:256
  8.1 92.8 %copy-start.308 = (s32[1,512]{1,0:T(1,128)}, s32[1,512]{1,0:T(1,128)S(1)}, u32[]{:S(2)}) copy-start(s32[1,512]{1,0:T(1,128)S(1)} %get-tuple-element.281) | copy-start | bytes 6148
  8.2 71.3 %collective-permute-start = (f32[3]{0:T(128)S(1)}, f32[3]{0:T(128)S(1)}, u32[]{:S(2)}, u32[]{:S(2)}) collective-permute-start(f32[3]{0:T(128)S(1)} %slice.592), channel_id=1, source_target_pairs={{0,4},{4,8},{8,12},{1,5},{5,9},{9,13},{2,6},{6,10},{10,14},{3,7},{... | collective-permute-start | bytes 44 | tf_op jit(solution)/shard_map/ppermute | solution.py:251
  13.1 66.3 %collective-permute-start.3 = (f32[3]{0:T(128)S(1)}, f32[3]{0:T(128)S(1)}, u32[]{:S(2)}, u32[]{:S(2)}) collective-permute-start(f32[3]{0:T(128)S(1)} %slice.631), channel_id=1, source_target_pairs={{0,4},{4,8},{8,12},{1,5},{5,9},{9,13},{2,6},{6,10},{10,14},{3,7},{... | collective-permute-start | bytes 44 | tf_op jit(solution)/shard_map/ppermute | solution.py:251
  18.3 31.4 %copy-start.368 = (f32[128]{0:T(128)}, f32[128]{0:T(128)S(1)}, u32[]{:S(2)}) copy-start(f32[128]{0:T(128)S(1)} %get-tuple-element.330) | copy-start | bytes 1540
  65.4 15.4 %collective-permute-start.1 = (f32[3,1280]{1,0:T(4,128)S(1)}, f32[3,1280]{1,0:T(4,128)S(1)}, u32[]{:S(2)}, u32[]{:S(2)}) collective-permute-start(f32[3,1280]{1,0:T(4,128)S(1)} %copy.495), channel_id=1, source_target_pairs={{0,4},{4,8},{8,12},{1,5},{5,9},{9,13},{2,6},{6,10},{10,14},{3,7},{... | collective-permute-start | bytes 46088 | tf_op jit(solution)/shard_map/ppermute | solution.py:251
  72.6 27.6 %copy-start.125 = (f32[512,16]{0,1:T(8,128)}, f32[512,16]{0,1:T(8,128)S(1)}, u32[]{:S(2)}) copy-start(f32[512,16]{0,1:T(8,128)S(1)} %get-tuple-element.226) | copy-start | bytes 98308
  91.6 38.6 %copy-start.9 = (f32[2,256,16,64]{1,0,3,2:T(2,128)}, f32[2,256,16,64]{1,0,3,2:T(2,128)S(1)}, u32[]{:S(2)}) copy-start(f32[2,256,16,64]{1,0,3,2:T(2,128)S(1)} %reshape.967) | copy-start | bytes 6291460
  92.3 36.7 %copy-start.66 = (f32[2,16,64,128]{3,2,1,0:T(8,128)}, f32[2,16,64,128]{3,2,1,0:T(8,128)S(1)}, u32[]{:S(2)}) copy-start(f32[2,16,64,128]{3,2,1,0:T(8,128)S(1)} %fusion.158) | copy-start | bytes 3145732
  93.5 225.3 %all-gather.17.cloned.1.call-start = ((), (), s32[]{:S(2)}) async-start(), calls=%async_computation.1 | async-start | bytes 2621440 | tf_op jit(solution)/shard_map/all_gather | solution.py:256
  103.2 27.0 %copy-start.372 = (f32[16]{0:T(128)}, f32[16]{0:T(128)S(1)}, u32[]{:S(2)}) copy-start(f32[16]{0:T(128)S(1)} %get-tuple-element.309) | copy-start | bytes 196
  158.0 29.6 %copy-start.51 = (bf16[2,128,2048]{2,1,0:T(8,128)(2,1)S(1)}, bf16[2,128,2048]{2,1,0:T(8,128)(2,1)}, u32[]{:S(2)}) copy-start(bf16[2,128,2048]{2,1,0:T(8,128)(2,1)} %param.19) | copy-start | bytes 3145732
  188.9 3.7 collective-permute-start.2
  191.8 69.9 %copy-start.293 = (f32[2,256]{1,0:T(2,128)}, f32[2,256]{1,0:T(2,128)S(1)}, u32[]{:S(2)}) copy-start(f32[2,256]{1,0:T(2,128)S(1)} %get-tuple-element.342) | copy-start | bytes 6148
  191.8 69.9 %copy-start.332 = (f32[2,256]{1,0:T(2,128)}, f32[2,256]{1,0:T(2,128)S(1)}, u32[]{:S(2)}) copy-start(f32[2,256]{1,0:T(2,128)S(1)} %get-tuple-element.343) | copy-start | bytes 6148
  192.5 73.7 %copy-start.272 = (f32[512]{0:T(512)}, f32[512]{0:T(512)S(1)}, u32[]{:S(2)}) copy-start(f32[512]{0:T(512)S(1)} %get-tuple-element.284) | copy-start | bytes 6148
  192.5 73.7 %copy-start.274 = (f32[512]{0:T(512)}, f32[512]{0:T(512)S(1)}, u32[]{:S(2)}) copy-start(f32[512]{0:T(512)S(1)} %get-tuple-element.285) | copy-start | bytes 6148
  192.5 73.7 %copy-start.276 = (f32[512]{0:T(512)}, f32[512]{0:T(512)S(1)}, u32[]{:S(2)}) copy-start(f32[512]{0:T(512)S(1)} %get-tuple-element.286) | copy-start | bytes 6148
  192.8 194.2 %copy-start.26 = (f32[128,2048]{1,0:T(8,128)}, f32[128,2048]{1,0:T(8,128)S(1)}, u32[]{:S(2)}) copy-start(f32[128,2048]{1,0:T(8,128)S(1)} %get-tuple-element.218) | copy-start | bytes 3145732
  193.3 57.3 %copy-start.396 = (f32[128]{0:T(128)}, f32[128]{0:T(128)S(1)}, u32[]{:S(2)}) copy-start(f32[128]{0:T(128)S(1)} %get-tuple-element.332) | copy-start | bytes 1540
  255.1 10.8 collective-permute-start.4
  259.4 38.0 %copy-start.127 = (f32[512,16]{0,1:T(8,128)}, f32[512,16]{0,1:T(8,128)S(1)}, u32[]{:S(2)}) copy-start(f32[512,16]{0,1:T(8,128)S(1)} %get-tuple-element.214) | copy-start | bytes 98308
  281.2 40.7 %copy-start.11 = (f32[2,256,16,64]{1,0,3,2:T(2,128)}, f32[2,256,16,64]{1,0,3,2:T(2,128)S(1)}, u32[]{:S(2)}) copy-start(f32[2,256,16,64]{1,0,3,2:T(2,128)S(1)} %reshape.979) | copy-start | bytes 6291460
  283.9 210.5 %all-gather.19.cloned.1.call-start = ((), (), s32[]{:S(2)}) async-start(), calls=%async_computation.2 | async-start | bytes 2621440 | tf_op jit(solution)/shard_map/all_gather | solution.py:256
  284.6 106.9 %collective-permute-start.6 = (f32[3]{0:T(128)}, f32[3]{0:T(128)}, u32[]{:S(2)}, u32[]{:S(2)}) collective-permute-start(f32[3]{0:T(128)} %slice.666), channel_id=1, source_target_pairs={{0,4},{4,8},{8,12},{1,5},{5,9},{9,13},{2,6},{6,10},{10,14},{3,7},{... | collective-permute-start | bytes 44 | tf_op jit(solution)/shard_map/ppermute | solution.py:251
  351.6 35.4 %copy-start.102 = (f32[1,128,2048]{2,1,0:T(8,128)S(1)}, f32[1,128,2048]{2,1,0:T(8,128)}, u32[]{:S(2)}) copy-start(f32[1,128,2048]{2,1,0:T(8,128)} %constant_dynamic-slice_fusion.3) | copy-start | bytes 3145732
  389.9 3.8 collective-permute-start.5
  391.5 28.2 %copy-start.424 = (f32[2]{0:T(128)}, f32[2]{0:T(128)S(1)}, u32[]{:S(2)}) copy-start(f32[2]{0:T(128)S(1)} %fusion.361) | copy-start | bytes 28
  392.9 31.0 %copy-start.278 = (f32[512]{0:T(512)}, f32[512]{0:T(512)S(1)}, u32[]{:S(2)}) copy-start(f32[512]{0:T(512)S(1)} %get-tuple-element.278) | copy-start | bytes 6148
  392.9 31.0 %copy-start.280 = (f32[512]{0:T(512)}, f32[512]{0:T(512)S(1)}, u32[]{:S(2)}) copy-start(f32[512]{0:T(512)S(1)} %get-tuple-element.279) | copy-start | bytes 6148
  392.9 31.1 %copy-start.282 = (f32[512]{0:T(512)}, f32[512]{0:T(512)S(1)}, u32[]{:S(2)}) copy-start(f32[512]{0:T(512)S(1)} %get-tuple-element.280) | copy-start | bytes 6148
  413.7 9.9 collective-permute-start.7
  434.4 162.6 %copy-start.14 = (f32[2,256,16,64]{1,0,3,2:T(2,128)}, f32[2,256,16,64]{1,0,3,2:T(2,128)S(1)}, u32[]{:S(2)}) copy-start(f32[2,256,16,64]{1,0,3,2:T(2,128)S(1)} %reshape.991) | copy-start | bytes 6291460
  435.0 59.4 %copy-start.69 = (f32[2,16,64,128]{3,2,1,0:T(8,128)}, f32[2,16,64,128]{3,2,1,0:T(8,128)S(1)}, u32[]{:S(2)}) copy-start(f32[2,16,64,128]{3,2,1,0:T(8,128)S(1)} %fusion.150) | copy-start | bytes 3145732
  436.3 159.1 %all-gather.21.cloned.1.call-start = ((), (), s32[]{:S(2)}) async-start(), calls=%async_computation.3 | async-start | bytes 1310720 | tf_op jit(solution)/shard_map/all_gather | solution.py:274
  548.5 245.2 %all-gather.23.cloned.1.call-start = ((), (), s32[]{:S(2)}) async-start(), calls=%async_computation.4 | async-start | bytes 1310720 | tf_op jit(solution)/shard_map/all_gather | solution.py:274
  561.5 33.9 %copy-start.365 = (f32[16]{0:T(128)S(1)}, f32[16]{0:T(128)}, u32[]{:S(2)}) copy-start(f32[16]{0:T(128)} %get-tuple-element.326) | copy-start | bytes 196
  561.5 33.9 %copy-start.384 = (f32[16]{0:T(128)S(1)}, f32[16]{0:T(128)}, u32[]{:S(2)}) copy-start(f32[16]{0:T(128)} %get-tuple-element.294) | copy-start | bytes 196
  561.5 33.9 %copy-start.386 = (f32[16]{0:T(128)S(1)}, f32[16]{0:T(128)}, u32[]{:S(2)}) copy-start(f32[16]{0:T(128)} %get-tuple-element.295) | copy-start | bytes 196
  561.5 33.9 %copy-start.416 = (f32[16]{0:T(128)S(1)}, f32[16]{0:T(128)}, u32[]{:S(2)}) copy-start(f32[16]{0:T(128)} %fusion.371) | copy-start | bytes 196
  625.6 18.7 %collective-permute-start.8 = (f32[3,1280]{1,0:T(4,128)}, f32[3,1280]{1,0:T(4,128)}, u32[]{:S(2)}, u32[]{:S(2)}) collective-permute-start(f32[3,1280]{1,0:T(4,128)} %copy.559), channel_id=1, source_target_pairs={{4,0},{8,4},{12,8},{5,1},{9,5},{13,9},{6,2},{10,6},{14,10},{7,3},{... | collective-permute-start | bytes 46088 | tf_op jit(solution)/shard_map/ppermute | solution.py:251
  665.2 26.6 %collective-permute-start.9 = (bf16[128,2048]{1,0:T(8,128)(2,1)S(1)}, bf16[128,2048]{1,0:T(8,128)(2,1)S(1)}, u32[]{:S(2)}, u32[]{:S(2)}) collective-permute-start(bf16[128,2048]{1,0:T(8,128)(2,1)S(1)} %get-tuple-element.193), channel_id=1, source_target_pairs={{16,0},{17,1},{18,2},{19,3},{20,4},{21,5},{22,6},{23,7},{24,8},{25... | collective-permute-start | bytes 1572872 | tf_op jit(solution)/shard_map/ppermute | solution.py:251
  670.7 65.1 %copy-start.347 = (f32[512]{0:T(512)S(1)}, f32[512]{0:T(512)}, u32[]{:S(2)}) copy-start(f32[512]{0:T(512)} %copy-done.346) | copy-start | bytes 6148
  767.3 236.0 %all-gather.25.cloned.1.call-start = ((), (), s32[]{:S(2)}) async-start(), calls=%async_computation.5 | async-start | bytes 1310720 | tf_op jit(solution)/shard_map/all_gather | solution.py:274
  813.9 27.1 %copy-start.238 = (f32[1280]{0:T(1024)}, f32[1280]{0:T(1024)S(1)}, u32[]{:S(2)}) copy-start(f32[1280]{0:T(1024)S(1)} %get-tuple-element.136) | copy-start | bytes 15364
  823.8 17.8 %collective-permute-start.10 = (f32[3,1280]{1,0:T(4,128)}, f32[3,1280]{1,0:T(4,128)}, u32[]{:S(2)}, u32[]{:S(2)}) collective-permute-start(f32[3,1280]{1,0:T(4,128)} %copy.582), channel_id=1, source_target_pairs={{4,0},{8,4},{12,8},{5,1},{9,5},{13,9},{6,2},{10,6},{14,10},{7,3},{... | collective-permute-start | bytes 46088 | tf_op jit(solution)/shard_map/ppermute | solution.py:251
  855.8 40.9 %copy-start.27 = (f32[128,2048]{1,0:T(8,128)S(1)}, f32[128,2048]{1,0:T(8,128)}, u32[]{:S(2)}) copy-start(f32[128,2048]{1,0:T(8,128)} %copy-done.26) | copy-start | bytes 3145732
  855.8 40.9 %copy-start.397 = (f32[128]{0:T(128)S(1)}, f32[128]{0:T(128)}, u32[]{:S(2)}) copy-start(f32[128]{0:T(128)} %copy-done.396) | copy-start | bytes 1540
  855.8 43.1 %copy-start.71 = (bf16[2,128,2048]{2,1,0:T(8,128)(2,1)S(1)}, bf16[2,128,2048]{2,1,0:T(8,128)(2,1)}, u32[]{:S(2)}) copy-start(bf16[2,128,2048]{2,1,0:T(8,128)(2,1)} %param.20) | copy-start | bytes 3145732
  855.8 43.1 %copy-start.433 = (f32[128]{0:T(128)S(1)}, f32[128]{0:T(128)}, u32[]{:S(2)}) copy-start(f32[128]{0:T(128)} %get-tuple-element.331) | copy-start | bytes 1540
  901.6 5.5 collective-permute-start.11
  907.0 30.4 %copy-start.345 = (f32[512]{0:T(512)S(1)}, f32[512]{0:T(512)}, u32[]{:S(2)}) copy-start(f32[512]{0:T(512)} %copy-done.344) | copy-start | bytes 6148
  977.3 133.2 %all-reduce.69.cloned.1.call-start = ((), (), s32[]{:S(2)}) async-start(), calls=%async_computation.6 | async-start | bytes 8388608 | tf_op jit(solution)/shard_map/psum | solution.py:742
  995.0 147.1 %all-gather.27.cloned.1.call-start = ((), (), s32[]{:S(2)}) async-start(), calls=%async_computation.7 | async-start | bytes 1331200 | tf_op jit(solution)/shard_map/all_gather | solution.py:611
  1036.3 11.3 collective-permute-start.12
  1085.0 29.3 %copy-start.48 = (bf16[4,128,2048]{2,1,0:T(8,128)(2,1)S(1)}, bf16[4,128,2048]{2,1,0:T(8,128)(2,1)}, u32[]{:S(2)}) copy-start(bf16[4,128,2048]{2,1,0:T(8,128)(2,1)} %shard_map.297) | copy-start | bytes 6291460
  1114.2 212.2 %all-reduce.71.cloned.1.call-start = ((), (), s32[]{:S(2)}) async-start(), calls=%async_computation.8 | async-start | bytes 16908288 | tf_op jit(solution)/shard_map/psum | solution.py:616
  1205.5 30.5 %copy-start.53 = (bf16[2,128,2048]{2,1,0:T(8,128)(2,1)S(1)}, bf16[2,128,2048]{2,1,0:T(8,128)(2,1)}, u32[]{:S(2)}) copy-start(bf16[2,128,2048]{2,1,0:T(8,128)(2,1)} %param.19) | copy-start | bytes 3145732
  1205.5 30.5 %copy-start.369 = (f32[128]{0:T(128)S(1)}, f32[128]{0:T(128)}, u32[]{:S(2)}) copy-start(f32[128]{0:T(128)} %copy-done.368) | copy-start | bytes 1540
  1205.5 32.0 %copy-start.297 = (f32[2048]{0:T(1024)S(1)}, f32[2048]{0:T(1024)}, u32[]{:S(2)}) copy-start(f32[2048]{0:T(1024)} %get-tuple-element.141) | copy-start | bytes 24580
  1205.5 32.0 %copy-start.298 = (f32[2048]{0:T(1024)S(1)}, f32[2048]{0:T(1024)}, u32[]{:S(2)}) copy-start(f32[2048]{0:T(1024)} %get-tuple-element.143) | copy-start | bytes 24580
  1205.5 72.3 %copy-start.432 = (f32[128]{0:T(128)S(1)}, f32[128]{0:T(128)}, u32[]{:S(2)}) copy-start(f32[128]{0:T(128)} %get-tuple-element.329) | copy-start | bytes 1540
  (405 other events, 2342.4 us)
Sparse Core Ops, SparseCore 0:
  93.6 33.5 all-gather.14
  284.0 34.7 all-gather.16
  436.4 57.9 all-gather.18
  548.7 46.7 all-gather.20
  767.4 26.2 all-gather.22
  977.4 25.8 all-gather.24
  1006.6 103.8 all-reduce.68
  1114.3 26.7 all-gather.26
  1150.7 175.5 all-reduce.70
